TPU v7x, 256 devices: a whole 4x4x8 slice. The times are simulated.
256 devices in a mesh: seq: 128 (over x, z, y), mp: 2 (over core).
Axes of the slice: x: 4, y: 4, z: 8, core: 2. Of those that a mesh axis runs over, the one named last changes fastest.
Arguments:
- states: bfloat16 [32768, 768], P('seq'), may hold values from -24 to 24
- qkv_weight: bfloat16 [3, 768, 768], P(None, None, 'mp'), may hold values from -0.21875 to 0.21875
- out_weight: bfloat16 [768, 768], P('mp'), may hold values from -0.21875 to 0.21875
- up_weight: bfloat16 [768, 3072], P(None, 'mp'), may hold values from -0.21875 to 0.21875
- down_weight: bfloat16 [3072, 768], P('mp'), may hold values from -0.109375 to 0.109375
- attn_gain: float32 [768], replicated, may hold values from 0.5 to 1.5
- mlp_gain: float32 [768], replicated, may hold values from 0.5 to 1.5
- global_ids: int32 [2], replicated, may hold values from 0 to 511, as said below
- random_owner: int32 [2, 512, 6, 3], P('mp', 'seq'), may hold values from 0 to 127, all different within a row; in each aligned block of 24 rows (0 to 23, 24 to 47, ..., all dimensions but the last counted through in order) at most 2 rows name the same one
- random_local: int32 [2, 512, 6, 3], P('mp', 'seq'), may hold values from 0 to 3
Outputs:
- layer_out: bfloat16 [32768, 768], P('seq')
Inputs may be any that keep to these rules, and one draw needn't show every extreme that they name: `global_ids`: 2 different block numbers; the second is 511. The random key block is random_owner * 4 + random_local. For one query block and head the 3 owners differ. Within the rows of one device (aligned blocks of 4 * K rows over the first three dimensions, K the third dimension) no owner is named more than 2 times, a bound that some block reaches.
All inputs are finite; a program needn't handle non-finite values.
Results may differ from a plain program's by a relative error of at most 0.008.
The roundings to bfloat16 on the way count: a program that leaves them out, or rounds other values in their place, can miss the bound.
Values may be sent and summed in bfloat16 or wider, within the bound.
No kernel may reach another device: no remote copies, remote signals or barrier semaphores. Data moves between devices by JAX's collectives and lax.ppermute only.
A program may use at most 192 MiB of HBM per device.

v0:
```python
import jax
import jax.numpy as jnp
from jax import lax
from jax.sharding import Mesh
from jax.sharding import PartitionSpec as P

HD = 64
BS = 64
R = 3
G = 2
SEQ = ("seq_0", "seq_1", "seq_2")


EPSILON = 1e-05
NEGATIVE = -1e30


def from_root(value, axes, root):
    value = jnp.where(lax.axis_index(axes) == root, value, jnp.zeros_like(value))
    for axis in axes:
        value = lax.psum(value, axis)
    return value


def with_halo(cells, sides, width):
    for axis, dim in sides:
        count = lax.axis_size(axis)
        ends = count - 1
        head = lax.slice_in_dim(cells, 0, width, axis=dim)
        tail = lax.slice_in_dim(cells, cells.shape[dim] - width, cells.shape[dim], axis=dim)
        cells = jnp.concatenate(
            [
                lax.ppermute(tail, axis, [(i, (i + 1) % count) for i in range(ends)]),
                cells,
                lax.ppermute(head, axis, [((i + 1) % count, i) for i in range(ends)]),
            ],
            axis=dim,
        )
    return cells


def collected_together(value, axis):
    leaves = jax.tree.leaves(value)
    order = sorted(range(len(leaves)), key=lambda k: -leaves[k].size)
    width = (1, *leaves[order[0]].shape)[-1]
    lines = [
        jnp.pad(leaves[k].reshape(-1), (0, -leaves[k].size % width)).reshape(-1, width)
        for k in order
    ]
    both, at, found = (lax.all_gather(jnp.concatenate(lines), axis), 0, {})
    for k, line in zip(order, lines):
        share = both[:, at : at + len(line)].reshape(len(both), -1)
        found[k] = share[:, : leaves[k].size].reshape(-1, *leaves[k].shape)
        at += len(line)
    numbers = iter(range(len(leaves)))
    return jax.tree.map(lambda _: found[next(numbers)], value)


def joined_all(value, axes, combine):
    for axis in axes:
        pieces = collected_together(value, axis)
        value = jax.tree.map(lambda part: part[0], pieces)
        for k in range(1, lax.axis_size(axis)):
            value = combine(value, jax.tree.map(lambda part: part[k], pieces))
    return value


def from_everyone(value, axis):
    copies = jnp.broadcast_to(value, (lax.axis_size(axis), *value.shape))
    return lax.all_to_all(copies, axis, split_axis=0, concat_axis=0, tiled=True)


def taken_together(value, axis):
    return from_everyone(value, axis).sum(axis=0)


def layer_norm(inputs, scales):
    center = jnp.mean(inputs, axis=-1, keepdims=True)
    shifted = inputs - center
    spread = jnp.mean(shifted * shifted, axis=-1, keepdims=True)
    return shifted * lax.rsqrt(spread + EPSILON) * scales


def merge_partials(earlier, later):
    high_early, total_early, acc_early = earlier
    high_late, total_late, acc_late = later
    highest = jnp.maximum(high_early, high_late)
    factor_early = jnp.exp(high_early - highest)
    factor_late = jnp.exp(high_late - highest)
    total = total_early * factor_early + total_late * factor_late
    summed = acc_early * factor_early[..., None] + acc_late * factor_late[..., None]
    return (highest, total, summed)


def fetch_global(query_blocks, pair_blocks, owner, local_block):
    query_piece = lax.dynamic_index_in_dim(query_blocks, local_block, 0, keepdims=False)
    pair_piece = lax.dynamic_index_in_dim(pair_blocks, local_block, 0, keepdims=False)
    return (from_root(query_piece, SEQ, owner), from_root(pair_piece, SEQ, owner))


def shards(
    states,
    qkv_weight,
    out_weight,
    up_weight,
    down_weight,
    attn_gain,
    mlp_gain,
    global_ids,
    random_owner,
    random_local,
):
    tokens_here = states.shape[0]
    head_width = qkv_weight.shape[2]
    head_count = head_width // HD
    block_count = tokens_here // BS
    seq_count = lax.axis_size(SEQ)
    position = lax.axis_index(SEQ)
    first_block = position * block_count
    scaling = HD ** (-0.5)
    highest = lax.Precision.HIGHEST
    queries = jnp.dot(states, qkv_weight[0], preferred_element_type=jnp.float32).astype(
        jnp.bfloat16
    )
    query_blocks = queries.reshape(block_count, BS, head_count, HD)
    key_part = jnp.dot(states, qkv_weight[1], preferred_element_type=jnp.float32).astype(
        jnp.bfloat16
    )
    value_part = jnp.dot(states, qkv_weight[2], preferred_element_type=jnp.float32).astype(
        jnp.bfloat16
    )
    key_value = jnp.concatenate(
        [
            key_part.reshape(tokens_here, head_count, HD),
            value_part.reshape(tokens_here, head_count, HD),
        ],
        axis=2,
    )
    pair_blocks = key_value.reshape(block_count, BS, head_count, 2 * HD)
    owner_of = global_ids // block_count
    local_of = global_ids % block_count
    fetched = [
        fetch_global(query_blocks, pair_blocks, owner_of[number], local_of[number])
        for number in range(G)
    ]
    global_query = jnp.stack([item[0] for item in fetched])
    global_pair = jnp.stack([item[1] for item in fetched])
    padded = with_halo(key_value, ((SEQ, 0),), BS)
    padded = padded.reshape(block_count + 2, BS, head_count, 2 * HD)
    window = jnp.stack([padded[shift_by : shift_by + block_count] for shift_by in range(3)], axis=1)
    neighbour = (
        first_block
        + jnp.arange(block_count, dtype=jnp.int32)[:, None]
        + jnp.arange(-1, 2, dtype=jnp.int32)[None, :]
    )
    inside = (neighbour >= 0) & (neighbour < seq_count * block_count)
    score_window = (
        jnp.einsum(
            "bqhd,bwkhd->bhqwk", query_blocks, window[..., :HD], preferred_element_type=jnp.float32
        )
        * scaling
    )
    score_window = jnp.where(inside[:, None, None, :, None], score_window, NEGATIVE)
    score_global = (
        jnp.einsum(
            "bqhd,gkhd->bhqgk",
            query_blocks,
            global_pair[..., :HD],
            preferred_element_type=jnp.float32,
        )
        * scaling
    )
    owner_list = random_owner.reshape(-1)
    local_list = random_local.reshape(-1)
    item_count = owner_list.shape[0]
    capacity = max(2, item_count // seq_count + 1)
    slot_total = seq_count * capacity
    head_list = jnp.broadcast_to(
        jnp.arange(head_count, dtype=jnp.int32)[None, :, None], (block_count, head_count, R)
    ).reshape(-1)
    matches = (owner_list[:, None] == jnp.arange(seq_count, dtype=jnp.int32)[None, :]).astype(
        jnp.int32
    )
    slot_rank = jnp.sum((jnp.cumsum(matches, axis=0) - matches) * matches, axis=1)
    slot_index = owner_list * capacity + slot_rank
    block_table = pair_blocks.transpose(0, 2, 1, 3).reshape(block_count * head_count, BS, 2 * HD)
    wanted = (
        jnp.zeros((slot_total,), jnp.int32).at[slot_index].set(local_list * head_count + head_list)
    )
    wanted = wanted.reshape(seq_count, capacity)
    remote = lax.all_to_all(
        block_table[lax.all_to_all(wanted, SEQ, split_axis=0, concat_axis=0, tiled=True)],
        SEQ,
        split_axis=0,
        concat_axis=0,
        tiled=True,
    ).reshape(slot_total, BS, 2 * HD)[slot_index]
    remote = remote.reshape(block_count, head_count, R, BS, 2 * HD)
    score_random = (
        jnp.einsum(
            "bqhd,bhrkd->bhqrk", query_blocks, remote[..., :HD], preferred_element_type=jnp.float32
        )
        * scaling
    )
    joined = jnp.concatenate([score_window, score_random, score_global], axis=3)
    joined_shape = joined.shape
    flat_scores = joined.reshape(joined_shape[0], joined_shape[1], joined_shape[2], -1)
    row_high = jnp.max(flat_scores, axis=-1, keepdims=True)
    raised = jnp.exp(flat_scores - row_high)
    weights = (
        (raised / jnp.sum(raised, axis=-1, keepdims=True))
        .astype(jnp.bfloat16)
        .reshape(joined_shape)
    )
    mixed = jnp.einsum(
        "bhqwk,bwkhd->bqhd",
        weights[:, :, :, :3],
        window[..., HD:],
        preferred_element_type=jnp.float32,
    )
    mixed = mixed + jnp.einsum(
        "bhqrk,bhrkd->bqhd",
        weights[:, :, :, 3 : 3 + R],
        remote[..., HD:],
        preferred_element_type=jnp.float32,
    )
    mixed = mixed + jnp.einsum(
        "bhqgk,gkhd->bqhd",
        weights[:, :, :, 3 + R :],
        global_pair[..., HD:],
        preferred_element_type=jnp.float32,
    )
    global_scores = (
        jnp.einsum(
            "gqhd,khd->hgqk",
            global_query,
            key_part.reshape(tokens_here, head_count, HD),
            preferred_element_type=jnp.float32,
        )
        * scaling
    )
    local_high = jnp.max(global_scores, axis=-1)
    global_raised = jnp.exp(global_scores - local_high[..., None])
    local_total = jnp.sum(global_raised, axis=-1)
    local_acc = jnp.einsum(
        "hgqk,khd->hgqd",
        global_raised,
        value_part.reshape(tokens_here, head_count, HD).astype(jnp.float32),
        precision=highest,
    )
    merged_high, merged_total, merged_acc = joined_all(
        (local_high, local_total, local_acc), SEQ, merge_partials
    )
    global_out = merged_acc / merged_total[..., None]
    placed_here = (
        global_ids[:, None] == first_block + jnp.arange(block_count, dtype=jnp.int32)[None, :]
    ).astype(jnp.float32)
    keep_rows = 1.0 - jnp.sum(placed_here, axis=0)
    placed = jnp.einsum("gb,hgqd->bqhd", placed_here, global_out, precision=highest)
    attended = (
        (mixed * keep_rows[:, None, None, None] + placed)
        .astype(jnp.bfloat16)
        .reshape(tokens_here, head_width)
    )
    projected = taken_together(
        jnp.dot(attended, out_weight, preferred_element_type=jnp.float32), "mp"
    )
    normed = layer_norm(states.astype(jnp.float32) + projected, attn_gain).astype(jnp.bfloat16)
    hidden = jax.nn.gelu(
        jnp.dot(normed, up_weight, preferred_element_type=jnp.float32), approximate=False
    ).astype(jnp.bfloat16)
    expanded = taken_together(
        jnp.dot(hidden, down_weight, preferred_element_type=jnp.float32), "mp"
    )
    return layer_norm(normed.astype(jnp.float32) + expanded, mlp_gain).astype(jnp.bfloat16)


def solution(mesh):
    split = Mesh(mesh.devices.reshape(4, 8, 4, mesh.shape["mp"]), ("seq_0", "seq_1", "seq_2", "mp"))
    placed = (
        P(SEQ, None),
        P(None, None, "mp"),
        P("mp", None),
        P(None, "mp"),
        P("mp", None),
        P(),
        P(),
        P(),
        P("mp", SEQ, None, None),
        P("mp", SEQ, None, None),
    )
    return jax.shard_map(
        shards, mesh=split, in_specs=placed, out_specs=P(SEQ, None), check_vma=False
    )
```

profile of v0, /device:TPU:1, one launch (start us, length us, event | category | flops | bytes accessed | tf_op | source)
XLA Modules:
  0.0 507.3 jit_solution(957818700047756081)
XLA Ops:
  11.5 16.9 %all-to-all-start = ((s32[128,1,2]{2,1,0:T(1,128)}), s32[128,1,2]{2,1,0:T(1,128)}, u32[]{:S(2)}, u32[]{:S(2)}) async-start(s32[128,1,2]{2,1,0:T(1,128)} %bitcast.15), calls=%async_computation | async-start | bytes 131072 | tf_op jit(solution)/shard_map/all_to_all | solution.py:192
  38.2 2.1 convolution_convert_fusion.2
  40.3 2.1 convolution_convert_fusion.1
  45.6 2.1 reshape.969
  48.8 35.2 %all-reduce.21.cloned.1.call-done = (bf16[64,6,64]{2,0,1:T(8,128)(2,1)}, bf16[64,6,64]{2,0,1:T(8,128)(2,1)}) async-done(((bf16[64,6,64]{2,0,1:T(8,128)(2,1)}, bf16[64,6,64]{2,0,1:T(8,128)(2,1)}), (bf16[64,6,64]{2,0,1:T(8,128)(2,1)}, bf16[64,6,64]{2,0,1:T(8,128)(2,1)})) %all-reduce.21.cloned.1.call-update) | async-done | bytes 98320 | tf_op jit(solution)/shard_map/psum | solution.py:21
  86.2 70.2 %all-reduce.13.cloned.1.call-done = (bf16[64,6,64]{2,0,1:T(8,128)(2,1)}, bf16[64,6,64]{2,0,1:T(8,128)(2,1)}) async-done(((bf16[64,6,64]{2,0,1:T(8,128)(2,1)}, bf16[64,6,64]{2,0,1:T(8,128)(2,1)}), (bf16[64,6,64]{2,0,1:T(8,128)(2,1)}, bf16[64,6,64]{2,0,1:T(8,128)(2,1)})) %all-reduce.13.cloned.1.call-update) | async-done | bytes 98320 | tf_op jit(solution)/shard_map/psum | solution.py:21
  156.4 3.1 gather_fusion
  159.5 12.3 %all-to-all-start.1 = ((bf16[128,2,64,128]{3,2,1,0:T(8,128)(2,1)}), bf16[128,2,64,128]{3,2,1,0:T(8,128)(2,1)}, u32[]{:S(2)}, u32[]{:S(2)}) async-start(bf16[128,2,64,128]{3,2,1,0:T(8,128)(2,1)} %bitcast.514), calls=%async_computation.1 | async-start | bytes 8388608 | tf_op jit(solution)/shard_map/all_to_all | solution.py:191
  172.9 39.6 %all-reduce.23.cloned.1.call-done = (bf16[64,6,128]{2,0,1:T(8,128)(2,1)}, bf16[64,6,128]{2,0,1:T(8,128)(2,1)}) async-done(((bf16[64,6,128]{2,0,1:T(8,128)(2,1)}, bf16[64,6,128]{2,0,1:T(8,128)(2,1)}), (bf16[64,6,128]{2,0,1:T(8,128)(2,1)}, bf16[64,6,128]{2,0,1:T(8,128)(2,1)})) %all-reduce.23.cloned.1.call-update) | async-done | bytes 196624 | tf_op jit(solution)/shard_map/psum | solution.py:21
  212.6 51.9 %all-reduce.17.cloned.1.call-done = (bf16[1,64,6,64]{3,1,0,2:T(8,128)(2,1)}, bf16[1,64,6,64]{3,1,2,0:T(8,128)(2,1)}) async-done(((bf16[1,64,6,64]{3,1,0,2:T(8,128)(2,1)}, bf16[1,64,6,64]{3,1,2,0:T(8,128)(2,1)}), (bf16[1,64,6,64]{3,1,0,2:T(8,128)(2,1)}, bf16[1,64,6,64]{3,1,2,0:T(8,128)(2,1)})) %all-reduce.17.cloned.1.call-update) | async-done | bytes 98320 | tf_op jit(solution)/shard_map/psum | solution.py:21
  266.3 2.3 fusion.27
  269.9 12.6 %all-gather.3 = f32[4,792,64]{1,2,0:T(8,128)S(1)} all-gather(f32[1,792,64]{1,2,0:T(8,128)S(1)} %maximum_bitcast_fusion), channel_id=2, replica_groups=mesh['seq_0'=4,'seq_1'=8,'seq_2'=4,'mp'=2] {'seq_0'}, dimensions={0}, use_global_device_ids=true | all-gather | bytes 1013760 | tf_op jit(solution)/shard_map/all_gather | solution.py:50
  286.0 50.0 %all-reduce.15.cloned.1.call-done = (bf16[64,6,128]{2,0,1:T(8,128)(2,1)}, bf16[64,6,128]{2,0,1:T(8,128)(2,1)}) async-done(((bf16[64,6,128]{2,0,1:T(8,128)(2,1)}, bf16[64,6,128]{2,0,1:T(8,128)(2,1)}), (bf16[64,6,128]{2,0,1:T(8,128)(2,1)}, bf16[64,6,128]{2,0,1:T(8,128)(2,1)})) %all-reduce.15.cloned.1.call-update) | async-done | bytes 196624 | tf_op jit(solution)/shard_map/psum | solution.py:21
  339.8 3.8 collective-permute-start
  353.4 2.4 pad_maximum_fusion.3
  362.5 24.5 %all-reduce.19.cloned.1.call-done = (bf16[1,64,6,128]{3,1,0,2:T(8,128)(2,1)}, bf16[1,64,6,128]{3,1,2,0:T(8,128)(2,1)}) async-done(((bf16[1,64,6,128]{3,1,0,2:T(8,128)(2,1)}, bf16[1,64,6,128]{3,1,2,0:T(8,128)(2,1)}), (bf16[1,64,6,128]{3,1,0,2:T(8,128)(2,1)}, bf16[1,64,6,128]{3,1,2,0:T(8,128)(2,1)})) %all-reduce.19.cloned.1.call-update) | async-done | bytes 196624 | tf_op jit(solution)/shard_map/psum | solution.py:21
  387.0 3.2 fusion.189
  390.2 38.0 %all-gather.8.cloned.1.call-done = f32[8,792,64]{1,2,0:T(8,128)} async-done(((f32[1,792,64]{1,2,0:T(8,128)}), f32[8,792,64]{1,2,0:T(8,128)}) %all-gather.8.cloned.1.call-update) | async-done | bytes 1622032 | tf_op jit(solution)/shard_map/all_gather | solution.py:50
  433.3 11.9 %all-gather.5 = f32[4,792,64]{1,2,0:T(8,128)S(1)} all-gather(f32[1,792,64]{1,2,0:T(8,128)S(1)} %maximum_bitcast_fusion.2), channel_id=4, replica_groups=mesh['seq_0'=4,'seq_1'=8,'seq_2'=4,'mp'=2] {'seq_2'}, dimensions={0}, use_global_device_ids=true | all-gather | bytes 1013760 | tf_op jit(solution)/shard_map/all_gather | solution.py:50
  453.7 3.7 fusion.34
  457.4 3.1 gather_fusion.1
  469.4 12.9 %all_to_all.27 = f32[2,256,768]{2,1,0:T(8,128)} all-to-all(f32[2,256,768]{2,1,0:T(8,128)S(1)} %broadcast_in_dim.24), channel_id=1, replica_groups=mesh['seq_0'=4,'seq_1'=8,'seq_2'=4,'mp'=2] {'mp'}, dimensions={0} | all-to-all | bytes 3145728 | tf_op jit(solution)/shard_map/all_to_all | solution.py:70
  485.1 6.2 %fusion.24 = f32[256,768]{1,0:T(8,128)S(1)} fusion(bf16[1536,768]{1,0:T(8,128)(2,1)S(1)} %copy-done, bf16[256,768]{1,0:T(8,128)(2,1)S(1)} %multiply_convert_fusion.1, bf16[768,1536]{1,0:T(8,128)(2,1)} %param.13), kind=kOutput, calls=%fused_computation.56 | convolution fusion | flops 1233518592 | bytes 5898240 | tf_op jit(solution)/shard_map/dot_general | solution.py:273
  491.5 5.7 %all_to_all.28 = f32[2,256,768]{2,1,0:T(8,128)} all-to-all(f32[2,256,768]{2,1,0:T(8,128)S(1)} %broadcast_in_dim.25), channel_id=1, replica_groups=mesh['seq_0'=4,'seq_1'=8,'seq_2'=4,'mp'=2] {'mp'}, dimensions={0} | all-to-all | bytes 3145728 | tf_op jit(solution)/shard_map/all_to_all | solution.py:70
  (233 shorter events, 71.9 us)
Async XLA Ops:
  6.5 478.6 %copy-start = (bf16[1536,768]{1,0:T(8,128)(2,1)S(1)}, bf16[1536,768]{1,0:T(8,128)(2,1)}, u32[]{:S(2)}) copy-start(bf16[1536,768]{1,0:T(8,128)(2,1)} %param.14) | copy-start | bytes 7077892
  9.9 21.9 %copy-start.26 = (s32[72]{0:T(128)}, s32[72]{0:T(128)S(1)}, u32[]{:S(2)}) copy-start(s32[72]{0:T(128)S(1)} %fusion.141) | copy-start | bytes 868
  11.5 73.7 %all-to-all-start = ((s32[128,1,2]{2,1,0:T(1,128)}), s32[128,1,2]{2,1,0:T(1,128)}, u32[]{:S(2)}, u32[]{:S(2)}) async-start(s32[128,1,2]{2,1,0:T(1,128)} %bitcast.15), calls=%async_computation | async-start | bytes 131072 | tf_op jit(solution)/shard_map/all_to_all | solution.py:192
  28.4 55.6 %all-reduce.21.cloned.1.call-start = ((), (), s32[]{:S(2)}) async-start(), calls=%async_computation.9 | async-start | bytes 393216 | tf_op jit(solution)/shard_map/psum | solution.py:21
  32.5 5.7 %copy-start.7 = (bf16[256,768]{1,0:T(8,128)(2,1)S(1)}, bf16[256,768]{1,0:T(8,128)(2,1)}, u32[]{:S(2)}) copy-start(bf16[256,768]{1,0:T(8,128)(2,1)} %param.10) | copy-start | bytes 1179652
  34.4 7.9 %copy-start.5 = (bf16[4,64,6,64]{1,0,3,2:T(4,128)(2,1)}, bf16[4,64,6,64]{1,0,3,2:T(4,128)(2,1)S(1)}, u32[]{:S(2)}) copy-start(bf16[4,64,6,64]{1,0,3,2:T(4,128)(2,1)S(1)} %reshape.908) | copy-start | bytes 589828
  36.0 6.4 %copy-start.11 = (bf16[4,64,6,64]{3,1,2,0:T(8,128)(2,1)}, bf16[4,64,6,64]{3,1,2,0:T(8,128)(2,1)S(1)}, u32[]{:S(2)}) copy-start(bf16[4,64,6,64]{3,1,2,0:T(8,128)(2,1)S(1)} %copy.275) | copy-start | bytes 589828
  38.1 118.3 %all-reduce.13.cloned.1.call-start = ((), (), s32[]{:S(2)}) async-start(), calls=%async_computation.5 | async-start | bytes 393216 | tf_op jit(solution)/shard_map/psum | solution.py:21
  84.0 128.5 %all-reduce.23.cloned.1.call-start = ((), (), s32[]{:S(2)}) async-start(), calls=%async_computation.10 | async-start | bytes 393216 | tf_op jit(solution)/shard_map/psum | solution.py:21
  84.9 179.6 %all-reduce.17.cloned.1.call-start = ((), (), s32[]{:S(2)}) async-start(), calls=%async_computation.7 | async-start | bytes 393216 | tf_op jit(solution)/shard_map/psum | solution.py:21
  159.5 12.3 %copy-start.13 = (bf16[256,384]{1,0:T(8,128)(2,1)S(1)}, bf16[256,384]{1,0:T(8,128)(2,1)}, u32[]{:S(2)}) copy-start(bf16[256,384]{1,0:T(8,128)(2,1)} %convolution_convert_fusion.2) | copy-start | bytes 589828
  159.5 12.5 %copy-start.15 = (bf16[256,384]{1,0:T(8,128)(2,1)S(1)}, bf16[256,384]{1,0:T(8,128)(2,1)}, u32[]{:S(2)}) copy-start(bf16[256,384]{1,0:T(8,128)(2,1)} %convolution_convert_fusion.1) | copy-start | bytes 589828
  159.5 297.9 %all-to-all-start.1 = ((bf16[128,2,64,128]{3,2,1,0:T(8,128)(2,1)}), bf16[128,2,64,128]{3,2,1,0:T(8,128)(2,1)}, u32[]{:S(2)}, u32[]{:S(2)}) async-start(bf16[128,2,64,128]{3,2,1,0:T(8,128)(2,1)} %bitcast.514), calls=%async_computation.1 | async-start | bytes 8388608 | tf_op jit(solution)/shard_map/all_to_all | solution.py:191
  171.8 164.2 %all-reduce.15.cloned.1.call-start = ((), (), s32[]{:S(2)}) async-start(), calls=%async_computation.6 | async-start | bytes 393216 | tf_op jit(solution)/shard_map/psum | solution.py:21
  212.5 174.5 %all-reduce.19.cloned.1.call-start = ((), (), s32[]{:S(2)}) async-start(), calls=%async_computation.8 | async-start | bytes 393216 | tf_op jit(solution)/shard_map/psum | solution.py:21
  336.0 92.2 %all-gather.8.cloned.1.call-start = ((), (), s32[]{:S(2)}) async-start(), calls=%async_computation.4 | async-start | bytes 2064384 | tf_op jit(solution)/shard_map/all_gather | solution.py:50
  336.2 8.9 %copy-start.16 = (bf16[256,384]{1,0:T(8,128)(2,1)S(1)}, bf16[256,384]{1,0:T(8,128)(2,1)}, u32[]{:S(2)}) copy-start(bf16[256,384]{1,0:T(8,128)(2,1)} %convolution_convert_fusion.1) | copy-start | bytes 589828
  336.2 10.0 %copy-start.14 = (bf16[256,384]{1,0:T(8,128)(2,1)S(1)}, bf16[256,384]{1,0:T(8,128)(2,1)}, u32[]{:S(2)}) copy-start(bf16[256,384]{1,0:T(8,128)(2,1)} %convolution_convert_fusion.2) | copy-start | bytes 589828
  336.2 11.1 %copy-start.6 = (bf16[4,64,6,64]{1,0,3,2:T(4,128)(2,1)S(1)}, bf16[4,64,6,64]{1,0,3,2:T(4,128)(2,1)}, u32[]{:S(2)}) copy-start(bf16[4,64,6,64]{1,0,3,2:T(4,128)(2,1)} %copy-done.5) | copy-start | bytes 589828
  339.8 13.6 %collective-permute-start = (bf16[64,6,128]{0,2,1:T(8,128)(2,1)}, bf16[64,6,128]{0,2,1:T(8,128)(2,1)}, u32[]{:S(2)}, u32[]{:S(2)}) collective-permute-start(bf16[64,6,128]{0,2,1:T(8,128)(2,1)} %get-tuple-element.74), channel_id=1, source_target_pairs={{0,2},{2,4},{4,6},{6,8},{8,10},{10,12},{12,14},{14,16},{16,18},{18... | collective-permute-start | bytes 294920 | tf_op jit(solution)/shard_map/ppermute | solution.py:33
  343.6 9.9 %collective-permute-start.1 = (bf16[64,6,128]{0,2,1:T(8,128)(2,1)}, bf16[64,6,128]{0,2,1:T(8,128)(2,1)}, u32[]{:S(2)}, u32[]{:S(2)}) collective-permute-start(bf16[64,6,128]{0,2,1:T(8,128)(2,1)} %get-tuple-element.75), channel_id=1, source_target_pairs={{2,0},{4,2},{6,4},{8,6},{10,8},{12,10},{14,12},{16,14},{18,16},{20... | collective-permute-start | bytes 294920 | tf_op jit(solution)/shard_map/ppermute | solution.py:35
  346.2 5.4 %copy-start.28 = (s32[2]{0:T(128)S(1)}, s32[2]{0:T(128)}, u32[]{:S(2)}) copy-start(s32[2]{0:T(128)} %param.17) | copy-start | bytes 28
  346.2 6.6 %copy-start.27 = (s32[72]{0:T(128)S(1)}, s32[72]{0:T(128)}, u32[]{:S(2)}) copy-start(s32[72]{0:T(128)} %copy-done.26) | copy-start | bytes 868
  347.6 39.4 %copy-start.10 = (bf16[4,64,6,64,1]{3,1,4,2,0:T(8,128)(2,1)}, bf16[4,64,6,64,1]{3,1,4,2,0:T(8,128)(2,1)S(1)}, u32[]{:S(2)}) copy-start(bf16[4,64,6,64,1]{3,1,4,2,0:T(8,128)(2,1)S(1)} %copy.333) | copy-start | bytes 589828
  (17 other events, 24.8 us)
Sparse Core Ops, SparseCore 0:
  38.2 45.6 all-reduce.20
  86.5 69.8 all-reduce.12
  158.7 53.7 all-reduce.22
  214.8 49.6 all-reduce.16
  266.7 69.2 all-reduce.14
  338.3 48.6 all-reduce.18
  388.8 39.4 all-gather.7
where the time goes:
time: 509 us; the launch traced here: 507 us
  waiting for transfers between devices  310 us (61%)
  local copies, waits for them, and re-layouts  45.3 us (9%)
  blocking collectives  43.1 us (8%)
  starting transfers between devices  34.7 us (7%)
  matrix products  27.7 us (5%)
  other arithmetic  27.3 us (5%)
  between operations  19.6 us (4%)
    psum x6, waiting for transfers between devices, from_root(): value = lax.psum(value, axis)  271 us
    all_gather x1, waiting for transfers between devices, collected_together(): both, at, found = (lax.all_gather(jnp.concatenate(lines), axis), 0, {})  38 us
    all_gather x2, blocking collectives, collected_together(): both, at, found = (lax.all_gather(jnp.concatenate(lines), axis), 0, {})  24.5 us
    all_to_all x2, blocking collectives, from_everyone(): return lax.all_to_all(copies, axis, split_axis=0, concat_axis=0, tiled=True)  18.6 us
    all_to_all x1, starting transfers between devices, shards(): lax.all_to_all(wanted, SEQ, split_axis=0, concat_axis=0, tiled=True)  16.9 us
    concatenate x8, local copies, waits for them, and re-layouts, shards(): jnp.concatenate([key_part.reshape(tokens_here, head_count, HD), value_par...  12.6 us
    all_to_all x1, starting transfers between devices, shards(): lax.all_to_all(block_table[lax.all_to_all(wanted, SEQ, split_axis=0, conc...  12.3 us
  transfers between devices with their start and end apart: 11, of which 7 were waited for; matrix products, arithmetic and copies ran while one was open for 14% of the time, Pallas kernels for 0%

commit v1 on v0

v1 whole, which is shorter than its diff:
```python
import functools

import jax
import jax.numpy as jnp
from jax import lax
from jax.experimental import pallas as pl
from jax.experimental.pallas import tpu as pltpu
from jax.sharding import Mesh
from jax.sharding import PartitionSpec as P

SEQ = ("x", "z", "y")
PLANE = ("x", "y")
EPSILON = 1e-05
NEGATIVE = -1e30
HEADS = 6
BF16 = jnp.bfloat16
F32 = jnp.float32
LIMIT = 48 * 1024 * 1024
VMEM = pl.BlockSpec(memory_space=pltpu.VMEM)
SMEM = pl.BlockSpec(memory_space=pltpu.SMEM)


def nt(a, b):
    return lax.dot_general(a, b, (((1,), (1,)), ((), ())), preferred_element_type=F32)


def nn(a, b):
    return jnp.dot(a, b, preferred_element_type=F32)


def call(kernel, outs, in_specs, out_specs, scratch, cost, *args):
    return pl.pallas_call(
        kernel,
        out_shape=outs,
        in_specs=in_specs,
        out_specs=out_specs,
        scratch_shapes=scratch,
        cost_estimate=pl.CostEstimate(flops=cost[0], bytes_accessed=cost[1], transcendentals=cost[2]),
        compiler_params=pltpu.CompilerParams(vmem_limit_bytes=LIMIT),
    )(*args)


def prepare_kernel(states_ref, weight_ref, wq_ref, wkv_ref, q_ref, kv_ref):
    wq_ref[...] = jnp.zeros_like(wq_ref)
    for h in range(HEADS):
        part = slice(64 * h, 64 * h + 64)
        wq_ref[:, 128 * h : 128 * h + 64] = weight_ref[0, :, part] * BF16(0.125)
        wkv_ref[:, 128 * h : 128 * h + 64] = weight_ref[1, :, part]
        wkv_ref[:, 128 * h + 64 : 128 * h + 128] = weight_ref[2, :, part]
    states = states_ref[...]
    query = nn(states, wq_ref[...]).astype(BF16)
    pair = nn(states, wkv_ref[...]).astype(BF16)
    for h in range(HEADS):
        q_ref[h] = query[:, 128 * h : 128 * h + 128]
        kv_ref[h] = pair[:, 128 * h : 128 * h + 128]


def prepare(states, weight):
    shape = jax.ShapeDtypeStruct
    return call(
        prepare_kernel,
        (shape((768, 768), BF16), shape((768, 768), BF16), shape((HEADS, 256, 128), BF16), shape((HEADS, 256, 128), BF16)),
        [VMEM] * 2,
        [VMEM] * 4,
        [],
        (600_000_000, 6_000_000, 0),
        states,
        weight,
    )


def column_kernel(own_ref, other_ref, wkv_ref, wanted_ref, kv_ref, items_ref):
    for half, source in enumerate((own_ref, other_ref)):

        @pl.loop(0, 4)
        def _(i):
            rows = pl.multiple_of(i * 256, 256)
            pair = nn(source[pl.ds(rows, 256), :], wkv_ref[...]).astype(BF16)
            for h in range(HEADS):
                kv_ref[pl.ds(h * 2048 + half * 1024 + rows, 256), :] = pair[:, 128 * h : 128 * h + 128]

    @pl.loop(0, 32)
    def _(i):
        for k in range(8):
            s = i * 8 + k
            at = pl.multiple_of(wanted_ref[0, s] * 64, 64)
            items_ref[s] = kv_ref[pl.ds(at, 64), :]


def column(own, other, wkv, wanted):
    shape = jax.ShapeDtypeStruct
    return call(
        column_kernel,
        (shape((HEADS * 2048, 128), BF16), shape((256, 64, 128), BF16)),
        [VMEM, VMEM, VMEM, SMEM],
        [VMEM, VMEM],
        [],
        (2_400_000_000, 12_000_000, 0),
        own,
        other,
        wkv,
        wanted,
    )


def partial_kernel(own_ref, other_ref, wq_ref, wkv_ref, kv_ref, out_ref, pair_ref, q_ref, s_ref, ml_ref):
    for half, source in enumerate((own_ref, other_ref)):
        rows = slice(64 * half, 64 * half + 64)
        query = nn(source[...], wq_ref[...]).astype(BF16)
        pair = nn(source[...], wkv_ref[...]).astype(BF16)
        for h in range(HEADS):
            q_ref[h, rows, :] = query[:, 128 * h : 128 * h + 128]
            pair_ref[h, rows, :] = pair[:, 128 * h : 128 * h + 128]
    lane = lax.broadcasted_iota(jnp.int32, (128, 128), 1)
    stats = jnp.zeros((128, 128), F32)
    for h in range(HEADS):
        high = jnp.full((128, 1), NEGATIVE, F32)
        for c in range(4):
            s = nt(q_ref[h], kv_ref[h * 2048 + c * 512 : h * 2048 + c * 512 + 512, :])
            s_ref[h % 2, :, c * 512 : c * 512 + 512] = s
            high = jnp.maximum(high, jnp.max(s, axis=1, keepdims=True))
        total = jnp.zeros((128, 1), F32)
        acc = jnp.zeros((128, 128), F32)
        for c in range(4):
            p = jnp.exp(s_ref[h % 2, :, c * 512 : c * 512 + 512] - high)
            total = total + jnp.sum(p, axis=1, keepdims=True)
            head = p.astype(BF16)
            rest = (p - head.astype(F32)).astype(BF16)
            keys = kv_ref[h * 2048 + c * 512 : h * 2048 + c * 512 + 512, :]
            acc = acc + nn(head, keys) + nn(rest, keys)
        out_ref[h // 2, :, (h % 2) * 64 : (h % 2) * 64 + 64] = acc[:, 64:128]
        stats = jnp.where(lane == h, high, jnp.where(lane == 64 + h, total, stats))
    out_ref[3] = stats


def partial(own, other, wq, wkv, kv):
    shape = jax.ShapeDtypeStruct
    return call(
        partial_kernel,
        (shape((4, 128, 128), F32), shape((HEADS, 128, 128), BF16)),
        [VMEM] * 5,
        [VMEM] * 2,
        [
            pltpu.VMEM((HEADS, 128, 128), BF16),
            pltpu.VMEM((2, 128, 2048), F32),
            pltpu.VMEM((8, 128), F32),
        ],
        (2_000_000_000, 5_000_000, 1_600_000),
        own,
        other,
        wq,
        wkv,
        kv,
    )


def merged(refs):
    stats = [r[3] for r in refs]
    highs, totals, factors = [], [], []
    for h in range(HEADS):
        high = functools.reduce(jnp.maximum, [s[:, h : h + 1] for s in stats])
        factor = [jnp.exp(s[:, h : h + 1] - high) for s in stats]
        highs.append(high)
        factors.append(factor)
        totals.append(sum(s[:, 64 + h : 65 + h] * f for s, f in zip(stats, factor)))
    sums = []
    for h in range(HEADS):
        lanes = slice((h % 2) * 64, (h % 2) * 64 + 64)
        sums.append(sum(r[h // 2, :, lanes] * f for r, f in zip(refs, factors[h])))
    return highs, totals, sums


def merge_kernel(a_ref, b_ref, c_ref, d_ref, out_ref):
    highs, totals, sums = merged((a_ref, b_ref, c_ref, d_ref))
    lane = lax.broadcasted_iota(jnp.int32, (128, 128), 1)
    stats = jnp.zeros((128, 128), F32)
    for h in range(HEADS):
        stats = jnp.where(lane == h, highs[h], jnp.where(lane == 64 + h, totals[h], stats))
        out_ref[h // 2, :, (h % 2) * 64 : (h % 2) * 64 + 64] = sums[h]
    out_ref[3] = stats


def merge(pieces):
    return call(
        merge_kernel,
        jax.ShapeDtypeStruct((4, 128, 128), F32),
        [VMEM] * 4,
        VMEM,
        [],
        (2_000_000, 1_300_000, 10_000),
        *pieces,
    )


def place_kernel(a_ref, b_ref, c_ref, d_ref, attended_ref, place_ref, out_ref, rows_ref):
    _, totals, sums = merged((a_ref, b_ref, c_ref, d_ref))
    for h in range(HEADS):
        rows_ref[:, 64 * h : 64 * h + 64] = (sums[h] / totals[h]).astype(BF16)
    out_ref[...] = attended_ref[...]
    core = place_ref[0, 2]
    for g in range(2):

        @pl.when(place_ref[0, g] >= 0)
        def _():
            start = place_ref[0, g] * 64
            for half, side in ((0, core), (1, 1 - core)):
                at = pl.multiple_of(start + side * 32, 32)
                out_ref[pl.ds(at, 32), :] = rows_ref[half * 64 + g * 32 : half * 64 + g * 32 + 32, :]


def place(pieces, attended, where):
    return call(
        place_kernel,
        jax.ShapeDtypeStruct((256, 384), BF16),
        [VMEM] * 5 + [SMEM],
        VMEM,
        [pltpu.VMEM((128, 384), BF16)],
        (2_000_000, 1_500_000, 10_000),
        *pieces,
        attended,
        where,
    )


def attend_kernel(q_ref, kv_ref, before_ref, after_ref, wkv_ref, remote_ref, pair_ref, slot_ref, edge_ref, out_ref, ext_ref, keys_ref):
    before = nn(before_ref[...], wkv_ref[...]).astype(BF16)
    after = nn(after_ref[...], wkv_ref[...]).astype(BF16)
    for h in range(HEADS):
        ext_ref[h, 0:64, :] = before[:, 128 * h : 128 * h + 128]
        ext_ref[h, 64:320, :] = kv_ref[h]
        ext_ref[h, 320:384, :] = after[:, 128 * h : 128 * h + 128]
    lane = lax.broadcasted_iota(jnp.int32, (64, 512), 1)

    @pl.loop(0, HEADS // 2)
    def _(pair):
        for b in range(4):
            outs = []
            for k in range(2):
                h = pair * 2 + k
                buf = keys_ref.at[b * 2 + k]
                buf[0:192, :] = ext_ref[h, b * 64 : b * 64 + 192, :]
                for r in range(3):
                    slot = slot_ref[0, (b * HEADS + h) * 3 + r]
                    buf[192 + 64 * r : 256 + 64 * r, :] = remote_ref[slot]
                buf[384:512, :] = pair_ref[h]
                keys = buf[...]
                s = nt(q_ref[h, b * 64 : b * 64 + 64, :], keys)
                if b == 0:
                    s = jnp.where((lane < 64) & (edge_ref[0, 0] > 0), NEGATIVE, s)
                if b == 3:
                    s = jnp.where((lane >= 128) & (lane < 192) & (edge_ref[0, 1] > 0), NEGATIVE, s)
                p = jnp.exp(s - jnp.max(s, axis=1, keepdims=True))
                w = (p / jnp.sum(p, axis=1, keepdims=True)).astype(BF16)
                outs.append(nn(w, keys)[:, 64:128])
            lanes = pl.ds(pl.multiple_of(pair * 128, 128), 128)
            out_ref[b * 64 : b * 64 + 64, lanes] = jnp.concatenate(outs, axis=1).astype(BF16)


def attend(q, kv, before, after, wkv, remote, pair, slots, edges):
    return call(
        attend_kernel,
        jax.ShapeDtypeStruct((256, 384), BF16),
        [VMEM] * 7 + [SMEM] * 2,
        VMEM,
        [pltpu.VMEM((HEADS, 384, 128), BF16), pltpu.VMEM((8, 512, 128), BF16)],
        (600_000_000, 7_000_000, 800_000),
        q,
        kv,
        before,
        after,
        wkv,
        remote,
        pair,
        slots,
        edges,
    )


def norm(v, gain):
    shifted = v - jnp.mean(v, axis=1, keepdims=True)
    spread = jnp.mean(shifted * shifted, axis=1, keepdims=True)
    return shifted * lax.rsqrt(spread + EPSILON) * gain


CHUNK = 512
STEPS = 1536 // CHUNK


def finish_kernel(
    own_ref, other_ref, states_ref, wo_own, wo_other, gain_ref, gain2_ref, up_own, up_other, down_own, down_other, out_ref, normed_ref, sum_ref
):
    step = pl.program_id(0)

    @pl.when(step == 0)
    def _():
        projected = nn(own_ref[...], wo_own[...]) + nn(other_ref[...], wo_other[...])
        normed_ref[...] = norm(states_ref[...].astype(F32) + projected, gain_ref[...]).astype(BF16)
        sum_ref[...] = jnp.zeros_like(sum_ref)

    def half(k, up, down):
        v = nn(normed_ref[...], up[...])
        hidden = (v * (1.0 + lax.erf(v * 0.7071067811865476)) * 0.5).astype(BF16)
        sum_ref[k] += nn(hidden, down[...])

    @pl.when(step < STEPS)
    def _():
        half(0, up_own, down_own)

    @pl.when(step >= STEPS)
    def _():
        half(1, up_other, down_other)

    @pl.when(step == 2 * STEPS - 1)
    def _():
        total = normed_ref[...].astype(F32) + (sum_ref[0] + sum_ref[1])
        out_ref[...] = norm(total, gain2_ref[...]).astype(BF16)


def finish(own, other, states, wo_own, wo_other, gain, gain2, up_own, up_other, down_own, down_other):
    whole = lambda *shape: pl.BlockSpec(shape, lambda s: (0, 0), pipeline_mode=pl.Buffered(1))
    first = lambda s: jnp.minimum(s, STEPS - 1)
    second = lambda s: jnp.maximum(s - STEPS, 0)
    return pl.pallas_call(
        finish_kernel,
        out_shape=jax.ShapeDtypeStruct((256, 768), BF16),
        grid=(2 * STEPS,),
        in_specs=[
            whole(256, 384),
            whole(256, 384),
            whole(256, 768),
            whole(384, 768),
            whole(384, 768),
            whole(1, 768),
            whole(1, 768),
            pl.BlockSpec((768, CHUNK), lambda s: (0, first(s))),
            pl.BlockSpec((768, CHUNK), lambda s: (0, second(s))),
            pl.BlockSpec((CHUNK, 768), lambda s: (first(s), 0)),
            pl.BlockSpec((CHUNK, 768), lambda s: (second(s), 0)),
        ],
        out_specs=pl.BlockSpec((256, 768), lambda s: (0, 0)),
        scratch_shapes=[pltpu.VMEM((256, 768), BF16), pltpu.VMEM((2, 256, 768), F32)],
        cost_estimate=pl.CostEstimate(flops=2_700_000_000, bytes_accessed=12_000_000, transcendentals=800_000),
        compiler_params=pltpu.CompilerParams(dimension_semantics=("arbitrary",), vmem_limit_bytes=LIMIT),
    )(own, other, states, wo_own, wo_other, gain, gain2, up_own, up_other, down_own, down_other)


def turned(value, axis, shift):
    count = lax.axis_size(axis)
    return lax.ppermute(value, axis, [(i, (i + shift) % count) for i in range(count)])


def swapped(value):
    return lax.ppermute(value, "mp", [(0, 1), (1, 0)])


def picked(pieces, number, per):
    rows = []
    for g in range(2):
        part = pieces[0][g * per : g * per + per]
        for k in range(1, len(pieces)):
            part = jnp.where(number[g] == k, pieces[k][g * per : g * per + per], part)
        rows.append(part)
    return jnp.concatenate(rows)


def everywhere(rows, here, root, per):
    for axis in ("y", "x"):
        pieces = [rows] + [turned(rows, axis, k) for k in (1, 2, 3)]
        rows = picked(pieces, (here[axis] - root[axis]) & 3, per)
    return rows


def shards(
    states, qkv_weight, out_weight, up_weight, down_weight, attn_gain, mlp_gain, global_ids, random_owner, random_local
):
    here = {axis: lax.axis_index(axis) for axis in ("x", "z", "y", "mp")}
    core = here["mp"]
    seq = (here["x"] * 8 + here["z"]) * 4 + here["y"]

    mine = lax.dynamic_slice_in_dim(states, core * 128, 128, 0)
    ups, downs = [mine], [mine]
    for _ in range(4):
        ups.append(turned(ups[-1], "z", 1))
    for _ in range(3):
        downs.append(turned(downs[-1], "z", -1))
    own = jnp.concatenate(ups + [downs[3], downs[2], downs[1]])
    other = swapped(own)

    owner = random_owner.reshape(-1)
    local = random_local.reshape(-1)
    head = jnp.broadcast_to(jnp.arange(HEADS, dtype=jnp.int32)[None, :, None], (4, HEADS, 3)).reshape(-1)

    def place_in_column(block_owner, block_local):
        away = (here["z"] - ((block_owner >> 2) & 7)) & 7
        far = ((block_local >> 1) != core).astype(jnp.int32)
        return far * 16 + away * 2 + (block_local & 1)

    item = head * 32 + place_in_column(owner, local)
    group = (owner >> 5) * 4 + (owner & 3)
    count = owner.shape[0]
    number = jnp.arange(count, dtype=jnp.int32)
    same = (group[:, None] == group[None, :]) & (number[None, :] < number[:, None])
    slots = group * 16 + jnp.sum(same.astype(jnp.int32), axis=1)
    chosen = slots[:, None] == jnp.arange(256, dtype=jnp.int32)[None, :]
    wanted = jnp.sum(jnp.where(chosen, item[:, None], 0), axis=0).reshape(16, 16)
    wanted = lax.all_to_all(wanted, PLANE, split_axis=0, concat_axis=0, tiled=True)

    ends = [(i, i + 1) for i in range(127)]
    before = lax.ppermute(states[192:], SEQ, ends)
    after = lax.ppermute(states[:64], SEQ, [(j, i) for i, j in ends])
    wo_other, up_other, down_other = swapped(out_weight), swapped(up_weight), swapped(down_weight)

    wq, wkv, q, kv = prepare(states, qkv_weight)
    pairs, items = column(own, other, wkv, wanted.reshape(1, 256))
    remote = lax.all_to_all(items.reshape(16, 1024, 128), PLANE, split_axis=0, concat_axis=0, tiled=True)

    root_owner, root_local = global_ids >> 2, global_ids & 3
    root = {"x": root_owner >> 5, "y": root_owner & 3}
    at = place_in_column(root_owner, root_local)
    parts = []
    for g in range(2):
        start = (at[g] & 15) * 64 + core * 32
        near = lax.dynamic_slice_in_dim(own, start, 32, 0)
        far = lax.dynamic_slice_in_dim(other, start, 32, 0)
        parts.append(jnp.where(at[g] >= 16, far, near))
    rows = everywhere(jnp.concatenate(parts), here, root, 32)
    part, pair = partial(rows, swapped(rows), wq, wkv, pairs)
    part = merge([part] + [turned(part, "y", k) for k in (1, 2, 3)])
    last = [part] + [turned(part, "x", k) for k in (1, 2, 3)]

    edges = jnp.stack([seq == 0, seq == 127]).astype(jnp.int32).reshape(1, 2)
    attended = attend(q, kv, before, after, wkv, remote.reshape(256, 64, 128), pair, slots.reshape(1, -1), edges)
    block = jnp.where(root_owner == seq, root_local, -1)
    where = jnp.concatenate([block, core[None]]).astype(jnp.int32).reshape(1, 3)
    attended = place(last, attended, where)
    return finish(
        attended,
        swapped(attended),
        states,
        out_weight,
        wo_other,
        attn_gain.reshape(1, -1),
        mlp_gain.reshape(1, -1),
        up_weight,
        up_other,
        down_weight,
        down_other,
    )


def solution(mesh):
    split = Mesh(mesh.devices.reshape(4, 8, 4, mesh.shape["mp"]), ("x", "z", "y", "mp"))
    placed = (
        P(SEQ, None),
        P(None, None, "mp"),
        P("mp", None),
        P(None, "mp"),
        P("mp", None),
        P(),
        P(),
        P(),
        P("mp", SEQ, None, None),
        P("mp", SEQ, None, None),
    )
    return jax.shard_map(shards, mesh=split, in_specs=placed, out_specs=P(SEQ, None), check_vma=False)
```

time: 509 us -> 216 us (0.42)
  waiting for transfers between devices: 310 us -> 73 us
  blocking collectives: 43.1 us -> 0 us
  Pallas kernels: 0 us -> 39.3 us
  starting transfers between devices: 34.7 us -> 69.4 us
  matrix products: 27.7 us -> 0 us
  other arithmetic: 27.3 us -> 2.24 us
  local copies, waits for them, and re-layouts: 45.3 us -> 21.3 us
  between operations: 19.6 us -> 10.3 us
    psum x6 -> x0, waiting for transfers between devices: 271 us -> none  [from_root(): value = lax.psum(value, axis)]
    ppermute x2 -> x27, waiting for transfers between devices: 0.01 us -> 70.3 us  [the longest x19 62.6 us: turned(): lax.ppermute(value, axis, [(i, (i + shift) % count) for i in range(count)])]
    ppermute x2 -> x27, starting transfers between devices: 5.25 us -> 58 us  [the longest x19 37 us: turned(): lax.ppermute(value, axis, [(i, (i + shift) % count) for i in range(count)])]
    pallas_call x0 -> x7, Pallas kernels: none -> 39.3 us  [the longest x6 29.7 us: call(): pl.pallas_call(kernel, out_shape=outs, in_specs=in_specs, out_specs=out_s...]
    all_gather x1 -> x0, waiting for transfers between devices: 38 us -> none  [collected_together(): both, at, found = (lax.all_gather(jnp.concatenate(lines), axis), 0, {})]
    dot_general x13 -> x0, matrix products: 27.2 us -> none  [the longest x1 6.22 us: shards(): jnp.dot(hidden, down_weight, preferred_element_type=jnp.float32)]
    all_gather x2 -> x0, blocking collectives: 24.5 us -> none  [collected_together(): both, at, found = (lax.all_gather(jnp.concatenate(lines), axis), 0, {})]
    all_to_all x2 -> x0, blocking collectives: 18.6 us -> none  [from_everyone(): return lax.all_to_all(copies, axis, split_axis=0, concat_axis=0, tiled=True)]
  transfers between devices with their start and end apart: 11 -> 29, of which waited for: 7 -> 13; matrix products, arithmetic and copies ran while one was open for 14% -> 4% of each run, Pallas kernels for 0% -> 9%
where the time goes in v1:
time: 216 us
  waiting for transfers between devices  73 us (34%)
  starting transfers between devices  69.4 us (32%)
  Pallas kernels  39.3 us (18%)
  local copies, waits for them, and re-layouts  21.3 us (10%)
  between operations  10.3 us (5%)
  other arithmetic  2.24 us (1%)
    ppermute x19, waiting for transfers between devices, turned(): lax.ppermute(value, axis, [(i, (i + shift) % count) for i in range(count)])  62.6 us
    ppermute x19, starting transfers between devices, turned(): lax.ppermute(value, axis, [(i, (i + shift) % count) for i in range(count)])  37 us
    pallas_call x6, Pallas kernels, call(): pl.pallas_call(kernel, out_shape=outs, in_specs=in_specs, out_specs=out_s...  29.7 us
    ppermute x6, starting transfers between devices, swapped(): return lax.ppermute(value, 'mp', [(0, 1), (1, 0)])  17 us
    unnamed x47, local copies, waits for them, and re-layouts  16.6 us
    pallas_call x1, Pallas kernels, finish(): pl.pallas_call(finish_kernel, out_shape=jax.ShapeDtypeStruct((256, 768),...  9.59 us
    all_to_all x1, starting transfers between devices, shards(): lax.all_to_all(wanted, PLANE, split_axis=0, concat_axis=0, tiled=True)  6.75 us
    ppermute x1, waiting for transfers between devices, shards(): after = lax.ppermute(states[:64], SEQ, [(j, i) for i, j in ends])  4.97 us
  transfers between devices with their start and end apart: 29, of which 13 were waited for; matrix products, arithmetic and copies ran while one was open for 4% of the time, Pallas kernels for 9%

profile of v1, /device:TPU:1, one launch (start us, length us, event | category | flops | bytes accessed | tf_op | source)
XLA Modules:
  0.0 215.5 jit_solution(13627301201321347719)
XLA Ops:
  4.1 3.9 %collective-permute-start.4 = (bf16[128,768]{1,0:T(8,128)(2,1)S(1)}, bf16[128,768]{1,0:T(8,128)(2,1)S(1)}, u32[]{:S(2)}, u32[]{:S(2)}) collective-permute-start(bf16[128,768]{1,0:T(8,128)(2,1)S(1)} %get-tuple-element.22), channel_id=1, source_target_pairs={{0,56},{8,0},{16,8},{24,16},{32,24},{40,32},{48,40},{56,48},{1,57}... | collective-permute-start | bytes 589832 | tf_op jit(solution)/shard_map/ppermute | solution.py:349
  8.1 4.6 %collective-permute-done = bf16[128,768]{1,0:T(8,128)(2,1)S(1)} collective-permute-done((bf16[128,768]{1,0:T(8,128)(2,1)S(1)}, bf16[128,768]{1,0:T(8,128)(2,1)S(1)}, u32[]{:S(2)}, u32[]{:S(2)}) %collective-permute-start) | collective-permute-done | bytes 196640 | tf_op jit(solution)/shard_map/ppermute | solution.py:349
  12.7 2.7 %collective-permute-start.5 = (bf16[128,768]{1,0:T(8,128)(2,1)S(1)}, bf16[128,768]{1,0:T(8,128)(2,1)S(1)}, u32[]{:S(2)}, u32[]{:S(2)}) collective-permute-start(bf16[128,768]{1,0:T(8,128)(2,1)S(1)} %collective-permute-done.4), channel_id=1, source_target_pairs={{0,56},{8,0},{16,8},{24,16},{32,24},{40,32},{48,40},{56,48},{1,57}... | collective-permute-start | bytes 589832 | tf_op jit(solution)/shard_map/ppermute | solution.py:349
  15.4 3.7 %collective-permute-done.1 = bf16[128,768]{1,0:T(8,128)(2,1)S(1)} collective-permute-done((bf16[128,768]{1,0:T(8,128)(2,1)S(1)}, bf16[128,768]{1,0:T(8,128)(2,1)S(1)}, u32[]{:S(2)}, u32[]{:S(2)}) %collective-permute-start.1) | collective-permute-done | bytes 196640 | tf_op jit(solution)/shard_map/ppermute | solution.py:349
  19.8 2.7 %collective-permute-start.6 = (bf16[128,768]{1,0:T(8,128)(2,1)S(1)}, bf16[128,768]{1,0:T(8,128)(2,1)S(1)}, u32[]{:S(2)}, u32[]{:S(2)}) collective-permute-start(bf16[128,768]{1,0:T(8,128)(2,1)S(1)} %collective-permute-done.5), channel_id=1, source_target_pairs={{0,56},{8,0},{16,8},{24,16},{32,24},{40,32},{48,40},{56,48},{1,57}... | collective-permute-start | bytes 589832 | tf_op jit(solution)/shard_map/ppermute | solution.py:349
  26.2 4.3 %collective-permute-done.3 = bf16[128,768]{1,0:T(8,128)(2,1)S(1)} collective-permute-done((bf16[128,768]{1,0:T(8,128)(2,1)S(1)}, bf16[128,768]{1,0:T(8,128)(2,1)S(1)}, u32[]{:S(2)}, u32[]{:S(2)}) %collective-permute-start.3) | collective-permute-done | bytes 196640 | tf_op jit(solution)/shard_map/ppermute | solution.py:349
  33.3 4.4 %collective-permute-start.7 = (bf16[1024,768]{1,0:T(8,128)(2,1)}, bf16[1024,768]{1,0:T(8,128)(2,1)}, u32[]{:S(2)}, u32[]{:S(2)}) collective-permute-start(bf16[1024,768]{1,0:T(8,128)(2,1)} %constant_dynamic-update-slice_fusion.own_ref), channel_id=1, source_target_pairs={{0,1},{1,0},{2,3},{3,2},{4,5},{5,4},{6,7},{7,6},{8,9},{9,8},{10,11... | collective-permute-start | bytes 4718600 | tf_op jit(solution)/shard_map/ppermute | solution.py:353
  39.3 6.8 %all-to-all-start = ((s32[16,1,16]{2,1,0:T(1,128)}), s32[16,1,16]{2,1,0:T(1,128)S(1)}, u32[]{:S(2)}, u32[]{:S(2)}) async-start(s32[16,1,16]{2,1,0:T(1,128)} %all_to_all.9), calls=%async_computation | async-start | bytes 16384 | tf_op jit(solution)/shard_map/all_to_all | solution.py:406
  49.8 2.6 %all-to-all-done = s32[16,1,16]{2,1,0:T(1,128)S(1)} async-done(((s32[16,1,16]{2,1,0:T(1,128)}), s32[16,1,16]{2,1,0:T(1,128)S(1)}, u32[]{:S(2)}, u32[]{:S(2)}) %all-to-all-start) | async-done | bytes 1056 | tf_op jit(solution)/shard_map/all_to_all | solution.py:406
  53.9 9.4 %shard_map.101 = (bf16[12288,128]{1,0:T(8,128)(2,1)}, bf16[256,64,128]{2,1,0:T(8,128)(2,1)}) custom-call(bf16[1024,768]{1,0:T(8,128)(2,1)} %constant_dynamic-update-slice_fusion.own_ref, bf16[1024,768]{1,0:T(8,128)(2,1)} %collective-permute-done.7.other_ref, bf16[768,768]{1,0:T(8,128)(2,1)S(1)} %get-tuple-element.14.wkv_ref, s32[1,256]{1,0:T(1,128)S(1)} %reshape.218.wanted_ref), custom_call_target="tpu_custom_call" | custom-call | flops 2400000000 | bytes 12000000 | tf_op jit(solution)/shard_map/pallas_call | solution.py:32
  63.3 4.7 %all-to-all-start.1 = ((bf16[16,1024,128]{2,1,0:T(8,128)(2,1)}), bf16[16,1024,128]{2,1,0:T(8,128)(2,1)}, u32[]{:S(2)}, u32[]{:S(2)}) async-start(bf16[16,1024,128]{2,1,0:T(8,128)(2,1)} %bitcast.25), calls=%async_computation.1 | async-start | bytes 8388608 | tf_op jit(solution)/shard_map/all_to_all | solution.py:415
  82.4 35.0 %collective-permute-done.10 = bf16[64,768]{1,0:T(8,128)(2,1)S(1)} collective-permute-done((bf16[64,768]{1,0:T(8,128)(2,1)S(1)}, bf16[64,768]{1,0:T(8,128)(2,1)S(1)}, u32[]{:S(2)}, u32[]{:S(2)}) %collective-permute-start.10) | collective-permute-done | bytes 98336 | tf_op jit(solution)/shard_map/ppermute | solution.py:349
  117.5 7.1 %collective-permute-start.11 = (bf16[64,768]{1,0:T(8,128)(2,1)S(1)}, bf16[64,768]{1,0:T(8,128)(2,1)S(1)}, u32[]{:S(2)}, u32[]{:S(2)}) collective-permute-start(bf16[64,768]{1,0:T(8,128)(2,1)S(1)} %pad_maximum_fusion.1), channel_id=1, source_target_pairs={{0,192},{64,0},{128,64},{192,128},{1,193},{65,1},{129,65},{193,129... | collective-permute-start | bytes 294920 | tf_op jit(solution)/shard_map/ppermute | solution.py:349
  131.3 6.1 %collective-permute-start.14 = (bf16[64,768]{1,0:T(8,128)(2,1)S(1)}, bf16[64,768]{1,0:T(8,128)(2,1)S(1)}, u32[]{:S(2)}, u32[]{:S(2)}) collective-permute-start(bf16[64,768]{1,0:T(8,128)(2,1)S(1)} %pad_maximum_fusion.2.own_ref), channel_id=1, source_target_pairs={{0,1},{1,0},{2,3},{3,2},{4,5},{5,4},{6,7},{7,6},{8,9},{9,8},{10,11... | collective-permute-start | bytes 294920 | tf_op jit(solution)/shard_map/ppermute | solution.py:353
  141.4 4.9 %shard_map.102 = (f32[4,128,128]{2,1,0:T(8,128)S(1)}, bf16[6,128,128]{2,1,0:T(8,128)(2,1)S(1)}) custom-call(bf16[64,768]{1,0:T(8,128)(2,1)S(1)} %pad_maximum_fusion.2.own_ref, bf16[64,768]{1,0:T(8,128)(2,1)S(1)} %collective-permute-done.14.other_ref, bf16[768,768]{1,0:T(8,128)(2,1)S(1)} %copy-done.13, bf16[768,768]{1,0:T(8,128)(2,1)S(1)} %copy-done.3, ...), custom_call_target="tpu_custom_call" | custom-call | flops 2000000000 | bytes 5000000 | tf_op jit(solution)/shard_map/pallas_call | solution.py:32
  147.3 4.3 %collective-permute-start.16 = (f32[4,128,128]{2,1,0:T(8,128)S(1)}, f32[4,128,128]{2,1,0:T(8,128)S(1)}, u32[]{:S(2)}, u32[]{:S(2)}) collective-permute-start(f32[4,128,128]{2,1,0:T(8,128)S(1)} %get-tuple-element.16.a_ref), channel_id=1, source_target_pairs={{0,4},{2,6},{4,0},{6,2},{1,5},{3,7},{5,1},{7,3},{8,12},{10,14},{12... | collective-permute-start | bytes 786440 | tf_op jit(solution)/shard_map/ppermute | solution.py:349
  151.6 5.2 %collective-permute-done.15.b_ref = f32[4,128,128]{2,1,0:T(8,128)S(1)} collective-permute-done((f32[4,128,128]{2,1,0:T(8,128)S(1)}, f32[4,128,128]{2,1,0:T(8,128)S(1)}, u32[]{:S(2)}, u32[]{:S(2)}) %collective-permute-start.15) | collective-permute-done | bytes 262176 | tf_op jit(solution)/shard_map/ppermute | solution.py:349
  156.8 6.5 %collective-permute-done.16.c_ref = f32[4,128,128]{2,1,0:T(8,128)S(1)} collective-permute-done((f32[4,128,128]{2,1,0:T(8,128)S(1)}, f32[4,128,128]{2,1,0:T(8,128)S(1)}, u32[]{:S(2)}, u32[]{:S(2)}) %collective-permute-start.16) | collective-permute-done | bytes 262176 | tf_op jit(solution)/shard_map/ppermute | solution.py:349
  164.9 2.7 %collective-permute-start.21 = (bf16[64,768]{1,0:T(8,128)(2,1)}, bf16[64,768]{1,0:T(8,128)(2,1)S(1)}, u32[]{:S(2)}, u32[]{:S(2)}) collective-permute-start(bf16[64,768]{1,0:T(8,128)(2,1)} %get-tuple-element.26), channel_id=1, source_target_pairs={{0,2},{2,4},{4,6},{6,8},{8,10},{10,12},{12,14},{14,16},{16,18},{18... | collective-permute-start | bytes 294920 | tf_op jit(solution)/shard_map/ppermute | solution.py:409
  170.9 5.0 %collective-permute-done.22.after_ref = bf16[64,768]{1,0:T(8,128)(2,1)S(1)} collective-permute-done((bf16[64,768]{1,0:T(8,128)(2,1)}, bf16[64,768]{1,0:T(8,128)(2,1)S(1)}, u32[]{:S(2)}, u32[]{:S(2)}) %collective-permute-start.22) | collective-permute-done | bytes 98336 | tf_op jit(solution)/shard_map/ppermute | solution.py:410
  176.5 6.4 %collective-permute-start.19 = (f32[4,128,128]{2,1,0:T(8,128)S(1)}, f32[4,128,128]{2,1,0:T(8,128)}, u32[]{:S(2)}, u32[]{:S(2)}) collective-permute-start(f32[4,128,128]{2,1,0:T(8,128)S(1)} %shard_map.103.a_ref), channel_id=1, source_target_pairs={{0,128},{64,192},{128,0},{192,64},{1,129},{65,193},{129,1},{193,65... | collective-permute-start | bytes 786440 | tf_op jit(solution)/shard_map/ppermute | solution.py:349
  187.6 11.3 %shard_map.104.attended_ref = bf16[256,384]{1,0:T(8,128)(2,1)S(1)} custom-call(bf16[6,256,128]{2,1,0:T(8,128)(2,1)S(1)} %get-tuple-element.17.q_ref, bf16[6,256,128]{2,1,0:T(8,128)(2,1)S(1)} %copy-done.6, bf16[64,768]{1,0:T(8,128)(2,1)S(1)} %collective-permute-done.21.before_ref, bf16[64,768]{1,0:T(8,128)(2,1)S(1)} %copy-done.10, ...), custom_call_target="tpu_custom_call" | custom-call | flops 600000000 | bytes 7000000 | tf_op jit(solution)/shard_map/pallas_call | solution.py:32
  200.7 4.1 %collective-permute-start.23 = (bf16[256,384]{1,0:T(8,128)(2,1)S(1)}, bf16[256,384]{1,0:T(8,128)(2,1)S(1)}, u32[]{:S(2)}, u32[]{:S(2)}) collective-permute-start(bf16[256,384]{1,0:T(8,128)(2,1)S(1)} %shard_map.105.own_ref), channel_id=1, source_target_pairs={{0,1},{1,0},{2,3},{3,2},{4,5},{5,4},{6,7},{7,6},{8,9},{9,8},{10,11... | collective-permute-start | bytes 589832 | tf_op jit(solution)/shard_map/ppermute | solution.py:353
  205.9 9.6 %shard_map.106 = bf16[256,768]{1,0:T(8,128)(2,1)} custom-call(bf16[256,384]{1,0:T(8,128)(2,1)S(1)} %shard_map.105.own_ref, bf16[256,384]{1,0:T(8,128)(2,1)S(1)} %collective-permute-done.23.other_ref, bf16[256,768]{1,0:T(8,128)(2,1)S(1)} %copy-done.1, bf16[384,768]{1,0:T(8,128)(2,1)} %wo_own.1, bf16[384,768]{1,0:T(8,128)(2,1)} %collective-permute-done.24.wo_other, ...), custom_call_target="tpu_custom_call" | custom-call | flops 2700000000 | bytes 12000000 | tf_op jit(solution)/shard_map/pallas_call | solution.py:323
  (121 shorter events, 47.2 us)
Async XLA Ops:
  1.7 11.0 %collective-permute-start = (bf16[128,768]{1,0:T(8,128)(2,1)S(1)}, bf16[128,768]{1,0:T(8,128)(2,1)S(1)}, u32[]{:S(2)}, u32[]{:S(2)}) collective-permute-start(bf16[128,768]{1,0:T(8,128)(2,1)S(1)} %get-tuple-element.22), channel_id=1, source_target_pairs={{0,8},{8,16},{16,24},{24,32},{32,40},{40,48},{48,56},{56,0},{1,9},... | collective-permute-start | bytes 589832 | tf_op jit(solution)/shard_map/ppermute | solution.py:349
  4.1 8.6 %collective-permute-start.4 = (bf16[128,768]{1,0:T(8,128)(2,1)S(1)}, bf16[128,768]{1,0:T(8,128)(2,1)S(1)}, u32[]{:S(2)}, u32[]{:S(2)}) collective-permute-start(bf16[128,768]{1,0:T(8,128)(2,1)S(1)} %get-tuple-element.22), channel_id=1, source_target_pairs={{0,56},{8,0},{16,8},{24,16},{32,24},{40,32},{48,40},{56,48},{1,57}... | collective-permute-start | bytes 589832 | tf_op jit(solution)/shard_map/ppermute | solution.py:349
  12.7 6.4 %collective-permute-start.1 = (bf16[128,768]{1,0:T(8,128)(2,1)S(1)}, bf16[128,768]{1,0:T(8,128)(2,1)S(1)}, u32[]{:S(2)}, u32[]{:S(2)}) collective-permute-start(bf16[128,768]{1,0:T(8,128)(2,1)S(1)} %collective-permute-done), channel_id=1, source_target_pairs={{0,8},{8,16},{16,24},{24,32},{32,40},{40,48},{48,56},{56,0},{1,9},... | collective-permute-start | bytes 589832 | tf_op jit(solution)/shard_map/ppermute | solution.py:349
  12.7 7.1 %collective-permute-start.5 = (bf16[128,768]{1,0:T(8,128)(2,1)S(1)}, bf16[128,768]{1,0:T(8,128)(2,1)S(1)}, u32[]{:S(2)}, u32[]{:S(2)}) collective-permute-start(bf16[128,768]{1,0:T(8,128)(2,1)S(1)} %collective-permute-done.4), channel_id=1, source_target_pairs={{0,56},{8,0},{16,8},{24,16},{32,24},{40,32},{48,40},{56,48},{1,57}... | collective-permute-start | bytes 589832 | tf_op jit(solution)/shard_map/ppermute | solution.py:349
  19.8 11.5 %collective-permute-start.6 = (bf16[128,768]{1,0:T(8,128)(2,1)S(1)}, bf16[128,768]{1,0:T(8,128)(2,1)S(1)}, u32[]{:S(2)}, u32[]{:S(2)}) collective-permute-start(bf16[128,768]{1,0:T(8,128)(2,1)S(1)} %collective-permute-done.5), channel_id=1, source_target_pairs={{0,56},{8,0},{16,8},{24,16},{32,24},{40,32},{48,40},{56,48},{1,57}... | collective-permute-start | bytes 589832 | tf_op jit(solution)/shard_map/ppermute | solution.py:349
  33.3 20.5 %collective-permute-start.7 = (bf16[1024,768]{1,0:T(8,128)(2,1)}, bf16[1024,768]{1,0:T(8,128)(2,1)}, u32[]{:S(2)}, u32[]{:S(2)}) collective-permute-start(bf16[1024,768]{1,0:T(8,128)(2,1)} %constant_dynamic-update-slice_fusion.own_ref), channel_id=1, source_target_pairs={{0,1},{1,0},{2,3},{3,2},{4,5},{5,4},{6,7},{7,6},{8,9},{9,8},{10,11... | collective-permute-start | bytes 4718600 | tf_op jit(solution)/shard_map/ppermute | solution.py:353
  39.3 13.2 %all-to-all-start = ((s32[16,1,16]{2,1,0:T(1,128)}), s32[16,1,16]{2,1,0:T(1,128)S(1)}, u32[]{:S(2)}, u32[]{:S(2)}) async-start(s32[16,1,16]{2,1,0:T(1,128)} %all_to_all.9), calls=%async_computation | async-start | bytes 16384 | tf_op jit(solution)/shard_map/all_to_all | solution.py:406
  63.3 120.2 %all-to-all-start.1 = ((bf16[16,1024,128]{2,1,0:T(8,128)(2,1)}), bf16[16,1024,128]{2,1,0:T(8,128)(2,1)}, u32[]{:S(2)}, u32[]{:S(2)}) async-start(bf16[16,1024,128]{2,1,0:T(8,128)(2,1)} %bitcast.25), calls=%async_computation.1 | async-start | bytes 8388608 | tf_op jit(solution)/shard_map/all_to_all | solution.py:415
  68.0 136.9 %collective-permute-start.25 = (bf16[768,1536]{1,0:T(8,128)(2,1)S(1)}, bf16[768,1536]{1,0:T(8,128)(2,1)}, u32[]{:S(2)}, u32[]{:S(2)}) collective-permute-start(bf16[768,1536]{1,0:T(8,128)(2,1)S(1)} %copy-done), channel_id=1, source_target_pairs={{0,1},{1,0},{2,3},{3,2},{4,5},{5,4},{6,7},{7,6},{8,9},{9,8},{10,11... | collective-permute-start | bytes 7077896 | tf_op jit(solution)/shard_map/ppermute | solution.py:353
  69.4 135.5 %collective-permute-start.26 = (bf16[1536,768]{1,0:T(8,128)(2,1)}, bf16[1536,768]{1,0:T(8,128)(2,1)}, u32[]{:S(2)}, u32[]{:S(2)}) collective-permute-start(bf16[1536,768]{1,0:T(8,128)(2,1)} %down_own.1), channel_id=1, source_target_pairs={{0,1},{1,0},{2,3},{3,2},{4,5},{5,4},{6,7},{7,6},{8,9},{9,8},{10,11... | collective-permute-start | bytes 7077896 | tf_op jit(solution)/shard_map/ppermute | solution.py:353
  73.7 43.8 %collective-permute-start.10 = (bf16[64,768]{1,0:T(8,128)(2,1)S(1)}, bf16[64,768]{1,0:T(8,128)(2,1)S(1)}, u32[]{:S(2)}, u32[]{:S(2)}) collective-permute-start(bf16[64,768]{1,0:T(8,128)(2,1)S(1)} %pad_maximum_fusion), channel_id=1, source_target_pairs={{0,2},{2,4},{4,6},{6,0},{1,3},{3,5},{5,7},{7,1},{8,10},{10,12},{12... | collective-permute-start | bytes 294920 | tf_op jit(solution)/shard_map/ppermute | solution.py:349
  75.2 42.3 %collective-permute-start.8 = (bf16[64,768]{1,0:T(8,128)(2,1)S(1)}, bf16[64,768]{1,0:T(8,128)(2,1)S(1)}, u32[]{:S(2)}, u32[]{:S(2)}) collective-permute-start(bf16[64,768]{1,0:T(8,128)(2,1)S(1)} %pad_maximum_fusion), channel_id=1, source_target_pairs={{0,6},{2,0},{4,2},{6,4},{1,7},{3,1},{5,3},{7,5},{8,14},{10,8},{12,... | collective-permute-start | bytes 294920 | tf_op jit(solution)/shard_map/ppermute | solution.py:349
  76.5 41.0 %collective-permute-start.9 = (bf16[64,768]{1,0:T(8,128)(2,1)S(1)}, bf16[64,768]{1,0:T(8,128)(2,1)S(1)}, u32[]{:S(2)}, u32[]{:S(2)}) collective-permute-start(bf16[64,768]{1,0:T(8,128)(2,1)S(1)} %pad_maximum_fusion), channel_id=1, source_target_pairs={{0,4},{2,6},{4,0},{6,2},{1,5},{3,7},{5,1},{7,3},{8,12},{10,14},{12... | collective-permute-start | bytes 294920 | tf_op jit(solution)/shard_map/ppermute | solution.py:349
  117.5 12.8 %collective-permute-start.11 = (bf16[64,768]{1,0:T(8,128)(2,1)S(1)}, bf16[64,768]{1,0:T(8,128)(2,1)S(1)}, u32[]{:S(2)}, u32[]{:S(2)}) collective-permute-start(bf16[64,768]{1,0:T(8,128)(2,1)S(1)} %pad_maximum_fusion.1), channel_id=1, source_target_pairs={{0,192},{64,0},{128,64},{192,128},{1,193},{65,1},{129,65},{193,129... | collective-permute-start | bytes 294920 | tf_op jit(solution)/shard_map/ppermute | solution.py:349
  124.6 5.7 %collective-permute-start.12 = (bf16[64,768]{1,0:T(8,128)(2,1)S(1)}, bf16[64,768]{1,0:T(8,128)(2,1)S(1)}, u32[]{:S(2)}, u32[]{:S(2)}) collective-permute-start(bf16[64,768]{1,0:T(8,128)(2,1)S(1)} %pad_maximum_fusion.1), channel_id=1, source_target_pairs={{0,128},{64,192},{128,0},{192,64},{1,129},{65,193},{129,1},{193,65... | collective-permute-start | bytes 294920 | tf_op jit(solution)/shard_map/ppermute | solution.py:349
  131.3 7.0 %collective-permute-start.14 = (bf16[64,768]{1,0:T(8,128)(2,1)S(1)}, bf16[64,768]{1,0:T(8,128)(2,1)S(1)}, u32[]{:S(2)}, u32[]{:S(2)}) collective-permute-start(bf16[64,768]{1,0:T(8,128)(2,1)S(1)} %pad_maximum_fusion.2.own_ref), channel_id=1, source_target_pairs={{0,1},{1,0},{2,3},{3,2},{4,5},{5,4},{6,7},{7,6},{8,9},{9,8},{10,11... | collective-permute-start | bytes 294920 | tf_op jit(solution)/shard_map/ppermute | solution.py:353
  147.0 9.8 %collective-permute-start.15 = (f32[4,128,128]{2,1,0:T(8,128)S(1)}, f32[4,128,128]{2,1,0:T(8,128)S(1)}, u32[]{:S(2)}, u32[]{:S(2)}) collective-permute-start(f32[4,128,128]{2,1,0:T(8,128)S(1)} %get-tuple-element.16.a_ref), channel_id=1, source_target_pairs={{0,2},{2,4},{4,6},{6,0},{1,3},{3,5},{5,7},{7,1},{8,10},{10,12},{12... | collective-permute-start | bytes 786440 | tf_op jit(solution)/shard_map/ppermute | solution.py:349
  147.3 16.0 %collective-permute-start.16 = (f32[4,128,128]{2,1,0:T(8,128)S(1)}, f32[4,128,128]{2,1,0:T(8,128)S(1)}, u32[]{:S(2)}, u32[]{:S(2)}) collective-permute-start(f32[4,128,128]{2,1,0:T(8,128)S(1)} %get-tuple-element.16.a_ref), channel_id=1, source_target_pairs={{0,4},{2,6},{4,0},{6,2},{1,5},{3,7},{5,1},{7,3},{8,12},{10,14},{12... | collective-permute-start | bytes 786440 | tf_op jit(solution)/shard_map/ppermute | solution.py:349
  151.6 11.7 %collective-permute-start.17 = (f32[4,128,128]{2,1,0:T(8,128)S(1)}, f32[4,128,128]{2,1,0:T(8,128)S(1)}, u32[]{:S(2)}, u32[]{:S(2)}) collective-permute-start(f32[4,128,128]{2,1,0:T(8,128)S(1)} %get-tuple-element.16.a_ref), channel_id=1, source_target_pairs={{0,6},{2,0},{4,2},{6,4},{1,7},{3,1},{5,3},{7,5},{8,14},{10,8},{12,... | collective-permute-start | bytes 786440 | tf_op jit(solution)/shard_map/ppermute | solution.py:349
  164.1 18.9 %collective-permute-start.18 = (f32[4,128,128]{2,1,0:T(8,128)S(1)}, f32[4,128,128]{2,1,0:T(8,128)}, u32[]{:S(2)}, u32[]{:S(2)}) collective-permute-start(f32[4,128,128]{2,1,0:T(8,128)S(1)} %shard_map.103.a_ref), channel_id=1, source_target_pairs={{0,64},{64,128},{128,192},{192,0},{1,65},{65,129},{129,193},{193,1... | collective-permute-start | bytes 786440 | tf_op jit(solution)/shard_map/ppermute | solution.py:349
  167.6 37.3 %collective-permute-start.24 = (bf16[384,768]{1,0:T(8,128)(2,1)}, bf16[384,768]{1,0:T(8,128)(2,1)}, u32[]{:S(2)}, u32[]{:S(2)}) collective-permute-start(bf16[384,768]{1,0:T(8,128)(2,1)} %wo_own.1), channel_id=1, source_target_pairs={{0,1},{1,0},{2,3},{3,2},{4,5},{5,4},{6,7},{7,6},{8,9},{9,8},{10,11... | collective-permute-start | bytes 1769480 | tf_op jit(solution)/shard_map/ppermute | solution.py:353
  169.5 6.3 %collective-permute-start.22 = (bf16[64,768]{1,0:T(8,128)(2,1)}, bf16[64,768]{1,0:T(8,128)(2,1)S(1)}, u32[]{:S(2)}, u32[]{:S(2)}) collective-permute-start(bf16[64,768]{1,0:T(8,128)(2,1)} %get-tuple-element.25), channel_id=1, source_target_pairs={{2,0},{4,2},{6,4},{8,6},{10,8},{12,10},{14,12},{16,14},{18,16},{20... | collective-permute-start | bytes 294920 | tf_op jit(solution)/shard_map/ppermute | solution.py:410
  176.5 22.4 %collective-permute-start.19 = (f32[4,128,128]{2,1,0:T(8,128)S(1)}, f32[4,128,128]{2,1,0:T(8,128)}, u32[]{:S(2)}, u32[]{:S(2)}) collective-permute-start(f32[4,128,128]{2,1,0:T(8,128)S(1)} %shard_map.103.a_ref), channel_id=1, source_target_pairs={{0,128},{64,192},{128,0},{192,64},{1,129},{65,193},{129,1},{193,65... | collective-permute-start | bytes 786440 | tf_op jit(solution)/shard_map/ppermute | solution.py:349
  183.0 15.9 %collective-permute-start.20 = (f32[4,128,128]{2,1,0:T(8,128)S(1)}, f32[4,128,128]{2,1,0:T(8,128)}, u32[]{:S(2)}, u32[]{:S(2)}) collective-permute-start(f32[4,128,128]{2,1,0:T(8,128)S(1)} %shard_map.103.a_ref), channel_id=1, source_target_pairs={{0,192},{64,0},{128,64},{192,128},{1,193},{65,1},{129,65},{193,129... | collective-permute-start | bytes 786440 | tf_op jit(solution)/shard_map/ppermute | solution.py:349
  (25 other events, 294.8 us)

commit v2 on v1

v2 whole, which is shorter than its diff:
```python
import functools

import jax
import jax.numpy as jnp
from jax import lax
from jax.experimental import pallas as pl
from jax.experimental.pallas import tpu as pltpu
from jax.sharding import Mesh
from jax.sharding import PartitionSpec as P

SEQ = ("x", "z", "y")
PLANE = ("x", "y")
EPSILON = 1e-05
NEGATIVE = -1e30
HEADS = 6
BF16 = jnp.bfloat16
F32 = jnp.float32
LIMIT = 48 * 1024 * 1024
VMEM = pl.BlockSpec(memory_space=pltpu.VMEM)
SMEM = pl.BlockSpec(memory_space=pltpu.SMEM)


def nt(a, b):
    return lax.dot_general(a, b, (((1,), (1,)), ((), ())), preferred_element_type=F32)


def nn(a, b):
    return jnp.dot(a, b, preferred_element_type=F32)


def call(kernel, outs, in_specs, out_specs, scratch, cost, *args):
    return pl.pallas_call(
        kernel,
        out_shape=outs,
        in_specs=in_specs,
        out_specs=out_specs,
        scratch_shapes=scratch,
        cost_estimate=pl.CostEstimate(flops=cost[0], bytes_accessed=cost[1], transcendentals=cost[2]),
        compiler_params=pltpu.CompilerParams(vmem_limit_bytes=LIMIT),
    )(*args)


def prepare_kernel(states_ref, weight_ref, wq_ref, wkv_ref, q_ref, kv_ref):
    wq_ref[...] = jnp.zeros_like(wq_ref)
    for h in range(HEADS):
        part = slice(64 * h, 64 * h + 64)
        wq_ref[:, 128 * h : 128 * h + 64] = weight_ref[0, :, part] * BF16(0.125)
        wkv_ref[:, 128 * h : 128 * h + 64] = weight_ref[1, :, part]
        wkv_ref[:, 128 * h + 64 : 128 * h + 128] = weight_ref[2, :, part]
    states = states_ref[...]
    query = nn(states, wq_ref[...]).astype(BF16)
    pair = nn(states, wkv_ref[...]).astype(BF16)
    for h in range(HEADS):
        q_ref[h] = query[:, 128 * h : 128 * h + 128]
        kv_ref[h] = pair[:, 128 * h : 128 * h + 128]


def prepare(states, weight):
    shape = jax.ShapeDtypeStruct
    return call(
        prepare_kernel,
        (shape((768, 768), BF16), shape((768, 768), BF16), shape((HEADS, 256, 128), BF16), shape((HEADS, 256, 128), BF16)),
        [VMEM] * 2,
        [VMEM] * 4,
        [],
        (600_000_000, 6_000_000, 0),
        states,
        weight,
    )


def early_kernel(*refs):
    wkv_ref, kv_ref = refs[10:]
    for p in range(10):
        pair = nn(refs[p][...], wkv_ref[...]).astype(BF16)
        for h in range(HEADS):
            kv_ref[p, h] = pair[:, 128 * h : 128 * h + 128]


def early(pieces, wkv):
    return call(
        early_kernel,
        jax.ShapeDtypeStruct((10, HEADS, 128, 128), BF16),
        [VMEM] * 11,
        VMEM,
        [],
        (1_500_000_000, 5_000_000, 0),
        *pieces,
        wkv,
    )


def scatter_kernel(*refs):
    wanted_ref, where_ref, out_ref, rows_ref, sem = refs[16:]
    for g in range(2):
        for p in range(16):

            @pl.when(where_ref[0, 2 * g] == p)
            def _():
                start = pl.multiple_of(where_ref[0, 2 * g + 1] * 64, 64)
                pltpu.make_async_copy(refs[p].at[pl.ds(start, 64), :], rows_ref.at[pl.ds(g * 64, 64), :], sem.at[g]).start()

    for g in range(2):
        pltpu.make_async_copy(refs[0].at[pl.ds(0, 64), :], rows_ref.at[pl.ds(g * 64, 64), :], sem.at[g]).wait()
    for p in range(16):
        for c in range(3):
            lanes = (p % 2) * 384 + c * 128
            out_ref[p, 16 * c : 16 * c + 16, :] = rows_ref[p // 2 * 16 : p // 2 * 16 + 16, lanes : lanes + 128]
        out_ref[p, 48:64, :] = jnp.broadcast_to(wanted_ref[p : p + 1, :], (16, 128)).astype(BF16)


def scatter(pieces, wanted, where):
    return call(
        scatter_kernel,
        jax.ShapeDtypeStruct((16, 64, 128), BF16),
        [pl.BlockSpec(memory_space=pl.ANY)] * 16 + [VMEM, SMEM],
        VMEM,
        [pltpu.VMEM((128, 768), BF16), pltpu.SemaphoreType.DMA((2,))],
        (0, 700_000, 0),
        *pieces,
        wanted,
        where,
    )


def column_kernel(*refs):
    wkv_ref, early_ref, received_ref, wanted_ref, kv_ref, items_ref, sem = refs[6:]
    copy = pltpu.make_async_copy(early_ref, kv_ref.at[pl.ds(0, 10 * HEADS)], sem)
    copy.start()
    for p in range(6):
        pair = nn(refs[p][...], wkv_ref[...]).astype(BF16)
        for h in range(HEADS):
            kv_ref[(10 + p) * HEADS + h] = pair[:, 128 * h : 128 * h + 128]
    copy.wait()
    share = received_ref[wanted_ref[0, 256], 0:48, :]
    for p in range(16):
        items_ref[p, 1024:1072, :] = share

    @pl.loop(0, 16)
    def _(p):
        for k in range(16):
            item = wanted_ref[0, p * 16 + k]
            at = pl.multiple_of((item & 1) * 64, 64)
            items_ref[p, 64 * k : 64 * k + 64, :] = kv_ref[item >> 1, pl.ds(at, 64), :]


def column(pieces, wkv, first, received, wanted):
    shape = jax.ShapeDtypeStruct
    return call(
        column_kernel,
        (shape((16 * HEADS, 128, 128), BF16), shape((16, 1072, 128), BF16)),
        [VMEM] * 7 + [pl.BlockSpec(memory_space=pl.ANY), VMEM, SMEM],
        [VMEM, VMEM],
        [pltpu.SemaphoreType.DMA],
        (1_000_000_000, 12_000_000, 0),
        *pieces,
        wkv,
        first,
        received,
        wanted,
    )


def partial_kernel(remote_ref, wq_ref, wkv_ref, kv_ref, out_ref, pair_ref, share_ref, rows_ref, q_ref, s_ref, sem):
    copies = [pltpu.make_async_copy(remote_ref.at[p, pl.ds(1024, 48), :], share_ref.at[p], sem.at[p]) for p in range(16)]
    for copy in copies:
        copy.start()
    for p, copy in enumerate(copies):
        copy.wait()
        for c in range(3):
            lanes = (p % 2) * 384 + c * 128
            rows_ref[p // 2 * 16 : p // 2 * 16 + 16, lanes : lanes + 128] = share_ref[p, 16 * c : 16 * c + 16, :]
    query = nn(rows_ref[...], wq_ref[...]).astype(BF16)
    pair = nn(rows_ref[...], wkv_ref[...]).astype(BF16)
    for h in range(HEADS):
        q_ref[h] = query[:, 128 * h : 128 * h + 128]
        pair_ref[h] = pair[:, 128 * h : 128 * h + 128]
    lane = lax.broadcasted_iota(jnp.int32, (128, 128), 1)
    highs = jnp.zeros((128, 128), F32)
    totals = jnp.zeros((128, 128), F32)
    for h in range(HEADS):
        keys = [kv_ref[4 * c : 4 * c + 4, h].reshape(512, 128) for c in range(4)]
        high = jnp.full((128, 1), NEGATIVE, F32)
        for c in range(4):
            s = nt(q_ref[h], keys[c])
            s_ref[h % 2, :, c * 512 : c * 512 + 512] = s
            high = jnp.maximum(high, jnp.max(s, axis=1, keepdims=True))
        total = jnp.zeros((128, 1), F32)
        acc = jnp.zeros((128, 128), F32)
        for c in range(4):
            p = jnp.exp(s_ref[h % 2, :, c * 512 : c * 512 + 512] - high)
            total = total + jnp.sum(p, axis=1, keepdims=True)
            head = p.astype(BF16)
            rest = (p - head.astype(F32)).astype(BF16)
            acc = acc + nn(head, keys[c]) + nn(rest, keys[c])
        out_ref[:, 64 * h : 64 * h + 64] = acc[:, 64:128]
        highs = jnp.where(lane == h, high, highs)
        totals = jnp.where(lane == h, total, totals)
    out_ref[:, 384:512] = highs
    out_ref[:, 512:640] = totals


def partial(remote, wq, wkv, kv):
    shape = jax.ShapeDtypeStruct
    return call(
        partial_kernel,
        (shape((128, 640), F32), shape((HEADS, 128, 128), BF16)),
        [pl.BlockSpec(memory_space=pl.ANY)] + [VMEM] * 3,
        [VMEM] * 2,
        [
            pltpu.VMEM((16, 48, 128), BF16),
            pltpu.VMEM((128, 768), BF16),
            pltpu.VMEM((HEADS, 128, 128), BF16),
            pltpu.VMEM((2, 128, 2048), F32),
            pltpu.SemaphoreType.DMA((16,)),
        ],
        (2_000_000_000, 5_000_000, 1_600_000),
        remote,
        wq,
        wkv,
        kv,
    )


def merge_kernel(parts_ref, out_ref):
    highs = parts_ref[:, :, 384:512]
    factor = jnp.exp(highs - jnp.max(highs, axis=0, keepdims=True))
    total = jnp.sum(factor * parts_ref[:, :, 512:640], axis=0)
    outs = []
    for h in range(HEADS):
        acc = jnp.sum(parts_ref[:, :, 64 * h : 64 * h + 64] * factor[:, :, h : h + 1], axis=0)
        outs.append(acc / total[:, h : h + 1])
    rows = jnp.concatenate(outs, axis=1).astype(BF16)
    for p in range(32):
        out_ref[p] = rows


def merge(parts):
    return call(
        merge_kernel,
        jax.ShapeDtypeStruct((32, 8, 384), BF16),
        [VMEM],
        VMEM,
        [],
        (2_000_000, 600_000, 10_000),
        parts,
    )


def attend_kernel(q_ref, kv_ref, before_ref, after_ref, wkv_ref, remote_ref, pair_ref, slot_ref, edge_ref, out_ref, ext_ref, keys_ref):
    before = nn(before_ref[...], wkv_ref[...]).astype(BF16)
    after = nn(after_ref[...], wkv_ref[...]).astype(BF16)
    for h in range(HEADS):
        ext_ref[h, 0:64, :] = before[:, 128 * h : 128 * h + 128]
        ext_ref[h, 64:320, :] = kv_ref[h]
        ext_ref[h, 320:384, :] = after[:, 128 * h : 128 * h + 128]
    lane = lax.broadcasted_iota(jnp.int32, (64, 512), 1)

    @pl.loop(0, HEADS // 2)
    def _(pair):
        for b in range(4):
            outs = []
            for k in range(2):
                h = pair * 2 + k
                buf = keys_ref.at[b * 2 + k]
                buf[0:192, :] = ext_ref[h, b * 64 : b * 64 + 192, :]
                for r in range(3):
                    at = pl.multiple_of(slot_ref[0, (b * HEADS + h) * 3 + r], 16)
                    buf[192 + 64 * r : 256 + 64 * r, :] = remote_ref[pl.ds(at, 64), :]
                buf[384:512, :] = pair_ref[h]
                keys = buf[...]
                s = nt(q_ref[h, b * 64 : b * 64 + 64, :], keys)
                if b == 0:
                    s = jnp.where((lane < 64) & (edge_ref[0, 0] > 0), NEGATIVE, s)
                if b == 3:
                    s = jnp.where((lane >= 128) & (lane < 192) & (edge_ref[0, 1] > 0), NEGATIVE, s)
                p = jnp.exp(s - jnp.max(s, axis=1, keepdims=True))
                w = (p / jnp.sum(p, axis=1, keepdims=True)).astype(BF16)
                outs.append(nn(w, keys)[:, 64:128])
            lanes = pl.ds(pl.multiple_of(pair * 128, 128), 128)
            out_ref[b * 64 : b * 64 + 64, lanes] = jnp.concatenate(outs, axis=1).astype(BF16)


def attend(q, kv, before, after, wkv, remote, pair, slots, edges):
    return call(
        attend_kernel,
        jax.ShapeDtypeStruct((256, 384), BF16),
        [VMEM] * 7 + [SMEM] * 2,
        VMEM,
        [pltpu.VMEM((HEADS, 384, 128), BF16), pltpu.VMEM((8, 512, 128), BF16)],
        (600_000_000, 7_000_000, 800_000),
        q,
        kv,
        before,
        after,
        wkv,
        remote,
        pair,
        slots,
        edges,
    )


def norm(v, gain):
    shifted = v - jnp.mean(v, axis=1, keepdims=True)
    spread = jnp.mean(shifted * shifted, axis=1, keepdims=True)
    return shifted * lax.rsqrt(spread + EPSILON) * gain


CHUNK = 512
STEPS = 1536 // CHUNK


def finish_kernel(
    own_ref,
    other_ref,
    states_ref,
    wo_own,
    wo_other,
    gain_ref,
    gain2_ref,
    up_own,
    up_other,
    down_own,
    down_other,
    rows_ref,
    place_ref,
    out_ref,
    normed_ref,
    sum_ref,
    attended_ref,
):
    step = pl.program_id(0)

    @pl.when(step == 0)
    def _():
        attended_ref[0] = own_ref[...]
        attended_ref[1] = other_ref[...]
        core = place_ref[0, 2]
        for g in range(2):

            @pl.when(place_ref[0, g] >= 0)
            def _():
                for k, side in ((0, core), (1, 1 - core)):
                    for i in range(4):
                        first = (g * 8 + 2 * i) * 2 + side
                        at = pl.multiple_of(place_ref[0, g] * 64 + 16 * i, 16)
                        both = jnp.concatenate([rows_ref[first], rows_ref[first + 2]], axis=0)
                        attended_ref[k, pl.ds(at, 16), :] = both

        projected = nn(attended_ref[0], wo_own[...]) + nn(attended_ref[1], wo_other[...])
        normed_ref[...] = norm(states_ref[...].astype(F32) + projected, gain_ref[...]).astype(BF16)
        sum_ref[...] = jnp.zeros_like(sum_ref)

    def half(k, up, down):
        v = nn(normed_ref[...], up[...])
        hidden = (v * (1.0 + lax.erf(v * 0.7071067811865476)) * 0.5).astype(BF16)
        sum_ref[k] += nn(hidden, down[...])

    @pl.when(step < STEPS)
    def _():
        half(0, up_own, down_own)

    @pl.when(step >= STEPS)
    def _():
        half(1, up_other, down_other)

    @pl.when(step == 2 * STEPS - 1)
    def _():
        total = normed_ref[...].astype(F32) + (sum_ref[0] + sum_ref[1])
        out_ref[...] = norm(total, gain2_ref[...]).astype(BF16)


def finish(own, other, states, wo_own, wo_other, gain, gain2, up_own, up_other, down_own, down_other, rows, where):
    whole = lambda *shape: pl.BlockSpec(shape, lambda s: (0, 0), pipeline_mode=pl.Buffered(1))
    first = lambda s: jnp.minimum(s, STEPS - 1)
    second = lambda s: jnp.maximum(s - STEPS, 0)
    return pl.pallas_call(
        finish_kernel,
        out_shape=jax.ShapeDtypeStruct((256, 768), BF16),
        grid=(2 * STEPS,),
        in_specs=[
            whole(256, 384),
            whole(256, 384),
            whole(256, 768),
            whole(384, 768),
            whole(384, 768),
            whole(1, 768),
            whole(1, 768),
            pl.BlockSpec((768, CHUNK), lambda s: (0, first(s))),
            pl.BlockSpec((768, CHUNK), lambda s: (0, second(s))),
            pl.BlockSpec((CHUNK, 768), lambda s: (first(s), 0)),
            pl.BlockSpec((CHUNK, 768), lambda s: (second(s), 0)),
            pl.BlockSpec((32, 8, 384), lambda s: (0, 0, 0), pipeline_mode=pl.Buffered(1)),
            SMEM,
        ],
        out_specs=pl.BlockSpec((256, 768), lambda s: (0, 0)),
        scratch_shapes=[pltpu.VMEM((256, 768), BF16), pltpu.VMEM((2, 256, 768), F32), pltpu.VMEM((2, 256, 384), BF16)],
        cost_estimate=pl.CostEstimate(flops=2_700_000_000, bytes_accessed=12_000_000, transcendentals=800_000),
        compiler_params=pltpu.CompilerParams(dimension_semantics=("arbitrary",), vmem_limit_bytes=LIMIT),
    )(own, other, states, wo_own, wo_other, gain, gain2, up_own, up_other, down_own, down_other, rows, where)


def turned(value, axis, shift):
    count = lax.axis_size(axis)
    return lax.ppermute(value, axis, [(i, (i + shift) % count) for i in range(count)])


def exchanged(value, axes):
    return lax.all_to_all(value, axes, split_axis=0, concat_axis=0, tiled=True)


def swapped(value):
    return lax.ppermute(value, "mp", [(0, 1), (1, 0)])


def shards(
    states, qkv_weight, out_weight, up_weight, down_weight, attn_gain, mlp_gain, global_ids, random_owner, random_local
):
    here = {axis: lax.axis_index(axis) for axis in ("x", "z", "y", "mp")}
    core = here["mp"]
    seq = (here["x"] * 8 + here["z"]) * 4 + here["y"]

    mine = lax.dynamic_slice_in_dim(states, core * 128, 128, 0)
    ups, downs = [mine], [mine]
    for _ in range(4):
        ups.append(turned(ups[-1], "z", 1))
    for _ in range(3):
        downs.append(turned(downs[-1], "z", -1))
    first = [ups[0], ups[1], ups[2], downs[1], downs[2]]
    last = [ups[3], ups[4], downs[3]]
    first = first + [swapped(piece) for piece in first]
    last = last + [swapped(piece) for piece in last]

    owner = random_owner.reshape(-1)
    local = random_local.reshape(-1)
    head = jnp.broadcast_to(jnp.arange(HEADS, dtype=jnp.int32)[None, :, None], (4, HEADS, 3)).reshape(-1)

    def piece_of(block_owner, block_local):
        away = (here["z"] - ((block_owner >> 2) & 7)) & 7
        far = ((block_local >> 1) != core).astype(jnp.int32)
        soon = far * 5 + jnp.where(away >= 6, 10 - away, away)
        return jnp.where((away >= 3) & (away <= 5), 10 + far * 3 + away - 3, soon)

    item = (piece_of(owner, local) * HEADS + head) * 2 + (local & 1)
    group = (owner >> 5) * 4 + (owner & 3)
    number = jnp.arange(owner.shape[0], dtype=jnp.int32)
    same = (group[:, None] == group[None, :]) & (number[None, :] < number[:, None])
    rank = jnp.sum(same.astype(jnp.int32), axis=1)
    slots = group * 1072 + rank * 64
    lanes = jnp.arange(2048, dtype=jnp.int32)
    chosen = (group * 128 + rank)[:, None] == lanes[None, :]
    wanted = jnp.sum(jnp.where(chosen, item[:, None], 0), axis=0).astype(F32).reshape(16, 128)

    root_owner, root_local = global_ids >> 2, global_ids & 3
    pieces = piece_of(root_owner, root_local)
    where = jnp.stack([pieces[0], root_local[0] & 1, pieces[1], root_local[1] & 1]).reshape(1, 4)
    received = exchanged(scatter(first + last, wanted, where), PLANE)
    root = (root_owner >> 5) * 4 + (root_owner & 3)
    source = jnp.where(here["x"] >= 2, root[1], root[0])
    wanted = jnp.concatenate([received[:, 48, :16].astype(jnp.int32).reshape(-1), source[None]]).reshape(1, 257)

    ends = [(i, i + 1) for i in range(127)]
    before = lax.ppermute(states[192:], SEQ, ends)
    after = lax.ppermute(states[:64], SEQ, [(j, i) for i, j in ends])
    wo_other, up_other, down_other = swapped(out_weight), swapped(up_weight), swapped(down_weight)

    wq, wkv, q, kv = prepare(states, qkv_weight)
    pairs, items = column(last, wkv, early(first, wkv).reshape(10 * HEADS, 128, 128), received, wanted)
    remote = exchanged(items, PLANE)
    part, pair = partial(remote, wq, wkv, pairs.reshape(16, HEADS, 128, 128))
    rows = exchanged(merge(exchanged(part.reshape(16, 8, 640), PLANE)), PLANE + ("mp",))

    edges = jnp.stack([seq == 0, seq == 127]).astype(jnp.int32).reshape(1, 2)
    attended = attend(q, kv, before, after, wkv, remote.reshape(16 * 1072, 128), pair, slots.reshape(1, -1), edges)
    block = jnp.where(root_owner == seq, root_local, -1)
    where = jnp.concatenate([block, core[None]]).astype(jnp.int32).reshape(1, 3)
    return finish(
        attended,
        swapped(attended),
        states,
        out_weight,
        wo_other,
        attn_gain.reshape(1, -1),
        mlp_gain.reshape(1, -1),
        up_weight,
        up_other,
        down_weight,
        down_other,
        rows,
        where,
    )


def solution(mesh):
    split = Mesh(mesh.devices.reshape(4, 8, 4, mesh.shape["mp"]), ("x", "z", "y", "mp"))
    placed = (
        P(SEQ, None),
        P(None, None, "mp"),
        P("mp", None),
        P(None, "mp"),
        P("mp", None),
        P(),
        P(),
        P(),
        P("mp", SEQ, None, None),
        P("mp", SEQ, None, None),
    )
    return jax.shard_map(shards, mesh=split, in_specs=placed, out_specs=P(SEQ, None), check_vma=False)
```

time: 216 us -> 227 us (1.051)
  local copies, waits for them, and re-layouts: 21.3 us -> 47.4 us
  starting transfers between devices: 69.4 us -> 60.9 us
  between operations: 10.3 us -> 3.08 us
  waiting for transfers between devices: 73 us -> 67.9 us
  other arithmetic: 2.24 us -> 5.75 us
    all_to_all x2 -> x4, waiting for transfers between devices: 2.65 us -> 59.7 us  [exchanged(): return lax.all_to_all(value, axes, split_axis=0, concat_axis=0, tiled=True)]
    ppermute x19 -> x7, waiting for transfers between devices: 62.6 us -> 7.16 us  [turned(): lax.ppermute(value, axis, [(i, (i + shift) % count) for i in range(count)])]
    ppermute x19 -> x7, starting transfers between devices: 37 us -> 12.3 us  [turned(): lax.ppermute(value, axis, [(i, (i + shift) % count) for i in range(count)])]
    unnamed x47 -> x122, local copies, waits for them, and re-layouts: 16.6 us -> 41 us
    all_to_all x2 -> x4, starting transfers between devices: 11.4 us -> 30.8 us  [exchanged(): return lax.all_to_all(value, axes, split_axis=0, concat_axis=0, tiled=True)]
    ppermute x1, waiting for transfers between devices: 4.97 us -> 0.01 us  [shards(): after = lax.ppermute(states[:64], SEQ, [(j, i) for i, j in ends])]
    ppermute x6 -> x12, starting transfers between devices: 17 us -> 12.3 us  [swapped(): return lax.ppermute(value, 'mp', [(0, 1), (1, 0)])]
    pallas_call x6 -> x7, Pallas kernels: 29.7 us -> 30.6 us  [call(): pl.pallas_call(kernel, out_shape=outs, in_specs=in_specs, out_specs=out_s...]
  transfers between devices with their start and end apart: 29 -> 25, of which waited for: 13 -> 6; matrix products, arithmetic and copies ran while one was open for 4% -> 5% of each run, Pallas kernels for 9% -> 10%
where the time goes in v2:
time: 227 us; the launch traced here: 225 us
  waiting for transfers between devices  67.9 us (30%)
  starting transfers between devices  60.9 us (27%)
  local copies, waits for them, and re-layouts  47.4 us (21%)
  Pallas kernels  40.2 us (18%)
  other arithmetic  5.75 us (3%)
  between operations  3.08 us (1%)
    all_to_all x4, waiting for transfers between devices, exchanged(): return lax.all_to_all(value, axes, split_axis=0, concat_axis=0, tiled=True)  59.7 us
    unnamed x122, local copies, waits for them, and re-layouts  41 us
    all_to_all x4, starting transfers between devices, exchanged(): return lax.all_to_all(value, axes, split_axis=0, concat_axis=0, tiled=True)  30.8 us
    pallas_call x7, Pallas kernels, call(): pl.pallas_call(kernel, out_shape=outs, in_specs=in_specs, out_specs=out_s...  30.6 us
    ppermute x7, starting transfers between devices, turned(): lax.ppermute(value, axis, [(i, (i + shift) % count) for i in range(count)])  12.3 us
    ppermute x12, starting transfers between devices, swapped(): return lax.ppermute(value, 'mp', [(0, 1), (1, 0)])  12.3 us
    pallas_call x1, Pallas kernels, finish(): pl.pallas_call(finish_kernel, out_shape=jax.ShapeDtypeStruct((256, 768),...  9.57 us
    ppermute x7, waiting for transfers between devices, turned(): lax.ppermute(value, axis, [(i, (i + shift) % count) for i in range(count)])  7.16 us
  transfers between devices with their start and end apart: 25, of which 6 were waited for; matrix products, arithmetic and copies ran while one was open for 5% of the time, Pallas kernels for 10%

profile of v2, /device:TPU:1, one launch (start us, length us, event | category | flops | bytes accessed | tf_op | source)
XLA Modules:
  0.0 225.3 jit_solution(8491915773234360820)
XLA Ops:
  0.9 2.5 %collective-permute-start.2 = (bf16[128,768]{1,0:T(8,128)(2,1)S(1)}, bf16[128,768]{1,0:T(8,128)(2,1)S(1)}, u32[]{:S(2)}, u32[]{:S(2)}) collective-permute-start(bf16[128,768]{1,0:T(8,128)(2,1)S(1)} %constant_dynamic-slice_fusion.refs_0_), channel_id=1, source_target_pairs={{0,8},{8,16},{16,24},{24,32},{32,40},{40,48},{48,56},{56,0},{1,9},... | collective-permute-start | bytes 589832 | tf_op jit(solution)/shard_map/ppermute | solution.py:406
  3.5 4.0 %collective-permute-start.6 = (bf16[128,768]{1,0:T(8,128)(2,1)S(1)}, bf16[128,768]{1,0:T(8,128)(2,1)S(1)}, u32[]{:S(2)}, u32[]{:S(2)}) collective-permute-start(bf16[128,768]{1,0:T(8,128)(2,1)S(1)} %constant_dynamic-slice_fusion.refs_0_), channel_id=1, source_target_pairs={{0,56},{8,0},{16,8},{24,16},{32,24},{40,32},{48,40},{56,48},{1,57}... | collective-permute-start | bytes 589832 | tf_op jit(solution)/shard_map/ppermute | solution.py:406
  16.3 2.7 %collective-permute-start.7 = (bf16[128,768]{1,0:T(8,128)(2,1)S(1)}, bf16[128,768]{1,0:T(8,128)(2,1)S(1)}, u32[]{:S(2)}, u32[]{:S(2)}) collective-permute-start(bf16[128,768]{1,0:T(8,128)(2,1)S(1)} %collective-permute-done.6.refs_3_), channel_id=1, source_target_pairs={{0,56},{8,0},{16,8},{24,16},{32,24},{40,32},{48,40},{56,48},{1,57}... | collective-permute-start | bytes 589832 | tf_op jit(solution)/shard_map/ppermute | solution.py:406
  19.0 4.2 %collective-permute-done.3.refs_2_ = bf16[128,768]{1,0:T(8,128)(2,1)S(1)} collective-permute-done((bf16[128,768]{1,0:T(8,128)(2,1)S(1)}, bf16[128,768]{1,0:T(8,128)(2,1)S(1)}, u32[]{:S(2)}, u32[]{:S(2)}) %collective-permute-start.3) | collective-permute-done | bytes 196640 | tf_op jit(solution)/shard_map/ppermute | solution.py:406
  25.5 2.9 %collective-permute-start.8 = (bf16[128,768]{1,0:T(8,128)(2,1)S(1)}, bf16[128,768]{1,0:T(8,128)(2,1)S(1)}, u32[]{:S(2)}, u32[]{:S(2)}) collective-permute-start(bf16[128,768]{1,0:T(8,128)(2,1)S(1)} %collective-permute-done.7.refs_4_), channel_id=1, source_target_pairs={{0,56},{8,0},{16,8},{24,16},{32,24},{40,32},{48,40},{56,48},{1,57}... | collective-permute-start | bytes 589832 | tf_op jit(solution)/shard_map/ppermute | solution.py:406
  28.4 1.6 collective-permute-done.4.refs_10_.refs_0_
  32.2 1.7 collective-permute-start.14
  35.8 2.8 %collective-permute-start.10 = (bf16[128,768]{1,0:T(8,128)(2,1)S(1)}, bf16[128,768]{1,0:T(8,128)(2,1)S(1)}, u32[]{:S(2)}, u32[]{:S(2)}) collective-permute-start(bf16[128,768]{1,0:T(8,128)(2,1)S(1)} %collective-permute-done.5.refs_11_.refs_1_), channel_id=1, source_target_pairs={{0,1},{1,0},{2,3},{3,2},{4,5},{5,4},{6,7},{7,6},{8,9},{9,8},{10,11... | collective-permute-start | bytes 589832 | tf_op jit(solution)/shard_map/ppermute | solution.py:414
  43.4 1.8 shard_map.102
  47.3 6.8 %all-to-all-start = ((bf16[16,64,128]{2,1,0:T(8,128)(2,1)}), bf16[16,64,128]{2,1,0:T(8,128)(2,1)}, u32[]{:S(2)}, u32[]{:S(2)}) async-start(bf16[16,64,128]{2,1,0:T(8,128)(2,1)} %shard_map.102), calls=%async_computation | async-start | bytes 524288 | tf_op jit(solution)/shard_map/all_to_all | solution.py:410
  71.3 1.7 shard_map.101
  79.4 6.2 %shard_map.103 = (bf16[96,128,128]{2,1,0:T(8,128)(2,1)}, bf16[16,1072,128]{2,1,0:T(8,128)(2,1)}) custom-call(bf16[128,768]{1,0:T(8,128)(2,1)S(1)} %copy-done.10, bf16[128,768]{1,0:T(8,128)(2,1)S(1)} %copy-done.14, bf16[128,768]{1,0:T(8,128)(2,1)S(1)} %copy-done.12, bf16[128,768]{1,0:T(8,128)(2,1)S(1)} %copy-done.16, bf16[128,768]{1,0:T(8,128)(2,1)S(1)} %copy-done.20, ...), custom_call_target="tpu_custom_call" | custom-call | flops 1000000000 | bytes 12000000 | tf_op jit(solution)/shard_map/pallas_call | solution.py:32
  85.6 6.8 %all-to-all-start.1 = ((bf16[16,1072,128]{2,1,0:T(8,128)(2,1)}), bf16[16,1072,128]{2,1,0:T(8,128)(2,1)}, u32[]{:S(2)}, u32[]{:S(2)}) async-start(bf16[16,1072,128]{2,1,0:T(8,128)(2,1)} %get-tuple-element.16), calls=%async_computation.1 | async-start | bytes 8781824 | tf_op jit(solution)/shard_map/all_to_all | solution.py:410
  95.5 4.1 %collective-permute-start = (bf16[64,768]{1,0:T(8,128)(2,1)}, bf16[64,768]{1,0:T(8,128)(2,1)}, u32[]{:S(2)}, u32[]{:S(2)}) collective-permute-start(bf16[64,768]{1,0:T(8,128)(2,1)} %get-tuple-element.24), channel_id=1, source_target_pairs={{0,2},{2,4},{4,6},{6,8},{8,10},{10,12},{12,14},{14,16},{16,18},{18... | collective-permute-start | bytes 294920 | tf_op jit(solution)/shard_map/ppermute | solution.py:464
  103.1 52.2 %all-to-all-done.1.remote_ref = bf16[16,1072,128]{2,1,0:T(8,128)(2,1)} async-done(((bf16[16,1072,128]{2,1,0:T(8,128)(2,1)}), bf16[16,1072,128]{2,1,0:T(8,128)(2,1)}, u32[]{:S(2)}, u32[]{:S(2)}) %all-to-all-start.1) | async-done | bytes 4390944 | tf_op jit(solution)/shard_map/all_to_all | solution.py:410
  155.3 1.9 copy-done
  158.5 5.4 %shard_map.104 = (f32[128,640]{1,0:T(8,128)S(1)}, bf16[6,128,128]{2,1,0:T(8,128)(2,1)S(1)}) custom-call(bf16[16,1072,128]{2,1,0:T(8,128)(2,1)} %all-to-all-done.1.remote_ref, bf16[768,768]{1,0:T(8,128)(2,1)S(1)} %copy-done.5, bf16[768,768]{1,0:T(8,128)(2,1)S(1)} %get-tuple-element.15.refs_10_.refs_6_.wkv_ref, bf16[16,6,128,128]{3,2,1,0:T(8,128)(2,1)S(1)} %bitcast.18), custom_call_target="tpu_custom_call" | custom-call | flops 2000000000 | bytes 5000000 | tf_op jit(solution)/shard_map/pallas_call | solution.py:32
  165.3 9.9 %all-to-all-start.2 = ((f32[16,8,640]{2,1,0:T(8,128)}), f32[16,8,640]{2,1,0:T(8,128)}, u32[]{:S(2)}, u32[]{:S(2)}) async-start(f32[16,8,640]{2,1,0:T(8,128)} %bitcast.20), calls=%async_computation.2 | async-start | bytes 655360 | tf_op jit(solution)/shard_map/all_to_all | solution.py:410
  178.2 12.1 %shard_map.105.own_ref = bf16[256,384]{1,0:T(8,128)(2,1)} custom-call(bf16[6,256,128]{2,1,0:T(8,128)(2,1)S(1)} %copy-done.25, bf16[6,256,128]{2,1,0:T(8,128)(2,1)S(1)} %copy-done.27, bf16[64,768]{1,0:T(8,128)(2,1)} %collective-permute-done.before_ref, bf16[64,768]{1,0:T(8,128)(2,1)} %collective-permute-done.1.after_ref, ...), custom_call_target="tpu_custom_call" | custom-call | flops 600000000 | bytes 7000000 | tf_op jit(solution)/shard_map/pallas_call | solution.py:32
  190.4 3.2 %collective-permute-start.17 = (bf16[256,384]{1,0:T(8,128)(2,1)}, bf16[256,384]{1,0:T(8,128)(2,1)S(1)}, u32[]{:S(2)}, u32[]{:S(2)}) collective-permute-start(bf16[256,384]{1,0:T(8,128)(2,1)} %shard_map.105.own_ref), channel_id=1, source_target_pairs={{0,1},{1,0},{2,3},{3,2},{4,5},{5,4},{6,7},{7,6},{8,9},{9,8},{10,11... | collective-permute-start | bytes 589832 | tf_op jit(solution)/shard_map/ppermute | solution.py:414
  193.6 1.9 shard_map.106
  195.4 7.3 %all-to-all-start.3 = ((bf16[32,8,384]{2,1,0:T(8,128)(2,1)}), bf16[32,8,384]{2,1,0:T(8,128)(2,1)S(1)}, u32[]{:S(2)}, u32[]{:S(2)}) async-start(bf16[32,8,384]{2,1,0:T(8,128)(2,1)} %shard_map.106), calls=%async_computation.3 | async-start | bytes 393216 | tf_op jit(solution)/shard_map/all_to_all | solution.py:410
  203.6 7.5 %all-to-all-done.3.rows_ref = bf16[32,8,384]{2,1,0:T(8,128)(2,1)S(1)} async-done(((bf16[32,8,384]{2,1,0:T(8,128)(2,1)}), bf16[32,8,384]{2,1,0:T(8,128)(2,1)S(1)}, u32[]{:S(2)}, u32[]{:S(2)}) %all-to-all-start.3) | async-done | bytes 196640 | tf_op jit(solution)/shard_map/all_to_all | solution.py:410
  215.7 9.6 %shard_map.107 = bf16[256,768]{1,0:T(8,128)(2,1)} custom-call(bf16[256,384]{1,0:T(8,128)(2,1)} %shard_map.105.own_ref, bf16[256,384]{1,0:T(8,128)(2,1)S(1)} %copy-done.53, bf16[256,768]{1,0:T(8,128)(2,1)S(1)} %copy-done.3, bf16[384,768]{1,0:T(8,128)(2,1)S(1)} %copy-done.23, bf16[384,768]{1,0:T(8,128)(2,1)} %collective-permute-done.18.wo_other, ...), custom_call_target="tpu_custom_call" | custom-call | flops 2700000000 | bytes 12000000 | tf_op jit(solution)/shard_map/pallas_call | solution.py:378
  (192 shorter events, 61.2 us)
Async XLA Ops:
  0.9 14.5 %collective-permute-start.2 = (bf16[128,768]{1,0:T(8,128)(2,1)S(1)}, bf16[128,768]{1,0:T(8,128)(2,1)S(1)}, u32[]{:S(2)}, u32[]{:S(2)}) collective-permute-start(bf16[128,768]{1,0:T(8,128)(2,1)S(1)} %constant_dynamic-slice_fusion.refs_0_), channel_id=1, source_target_pairs={{0,8},{8,16},{16,24},{24,32},{32,40},{40,48},{48,56},{56,0},{1,9},... | collective-permute-start | bytes 589832 | tf_op jit(solution)/shard_map/ppermute | solution.py:406
  3.5 12.8 %collective-permute-start.6 = (bf16[128,768]{1,0:T(8,128)(2,1)S(1)}, bf16[128,768]{1,0:T(8,128)(2,1)S(1)}, u32[]{:S(2)}, u32[]{:S(2)}) collective-permute-start(bf16[128,768]{1,0:T(8,128)(2,1)S(1)} %constant_dynamic-slice_fusion.refs_0_), channel_id=1, source_target_pairs={{0,56},{8,0},{16,8},{24,16},{32,24},{40,32},{48,40},{56,48},{1,57}... | collective-permute-start | bytes 589832 | tf_op jit(solution)/shard_map/ppermute | solution.py:406
  7.5 24.0 %collective-permute-start.12 = (bf16[128,768]{1,0:T(8,128)(2,1)S(1)}, bf16[128,768]{1,0:T(8,128)(2,1)S(1)}, u32[]{:S(2)}, u32[]{:S(2)}) collective-permute-start(bf16[128,768]{1,0:T(8,128)(2,1)S(1)} %constant_dynamic-slice_fusion.refs_0_), channel_id=1, source_target_pairs={{0,1},{1,0},{2,3},{3,2},{4,5},{5,4},{6,7},{7,6},{8,9},{9,8},{10,11... | collective-permute-start | bytes 589832 | tf_op jit(solution)/shard_map/ppermute | solution.py:414
  15.4 7.8 %collective-permute-start.3 = (bf16[128,768]{1,0:T(8,128)(2,1)S(1)}, bf16[128,768]{1,0:T(8,128)(2,1)S(1)}, u32[]{:S(2)}, u32[]{:S(2)}) collective-permute-start(bf16[128,768]{1,0:T(8,128)(2,1)S(1)} %collective-permute-done.2.refs_1_), channel_id=1, source_target_pairs={{0,8},{8,16},{16,24},{24,32},{32,40},{40,48},{48,56},{56,0},{1,9},... | collective-permute-start | bytes 589832 | tf_op jit(solution)/shard_map/ppermute | solution.py:406
  16.3 9.2 %collective-permute-start.7 = (bf16[128,768]{1,0:T(8,128)(2,1)S(1)}, bf16[128,768]{1,0:T(8,128)(2,1)S(1)}, u32[]{:S(2)}, u32[]{:S(2)}) collective-permute-start(bf16[128,768]{1,0:T(8,128)(2,1)S(1)} %collective-permute-done.6.refs_3_), channel_id=1, source_target_pairs={{0,56},{8,0},{16,8},{24,16},{32,24},{40,32},{48,40},{56,48},{1,57}... | collective-permute-start | bytes 589832 | tf_op jit(solution)/shard_map/ppermute | solution.py:406
  23.2 6.9 %collective-permute-start.4 = (bf16[128,768]{1,0:T(8,128)(2,1)S(1)}, bf16[128,768]{1,0:T(8,128)(2,1)S(1)}, u32[]{:S(2)}, u32[]{:S(2)}) collective-permute-start(bf16[128,768]{1,0:T(8,128)(2,1)S(1)} %collective-permute-done.3.refs_2_), channel_id=1, source_target_pairs={{0,8},{8,16},{16,24},{24,32},{32,40},{40,48},{48,56},{56,0},{1,9},... | collective-permute-start | bytes 589832 | tf_op jit(solution)/shard_map/ppermute | solution.py:406
  23.2 10.6 %collective-permute-start.13 = (bf16[128,768]{1,0:T(8,128)(2,1)S(1)}, bf16[128,768]{1,0:T(8,128)(2,1)S(1)}, u32[]{:S(2)}, u32[]{:S(2)}) collective-permute-start(bf16[128,768]{1,0:T(8,128)(2,1)S(1)} %collective-permute-done.2.refs_1_), channel_id=1, source_target_pairs={{0,1},{1,0},{2,3},{3,2},{4,5},{5,4},{6,7},{7,6},{8,9},{9,8},{10,11... | collective-permute-start | bytes 589832 | tf_op jit(solution)/shard_map/ppermute | solution.py:414
  24.8 9.2 %collective-permute-start.15 = (bf16[128,768]{1,0:T(8,128)(2,1)S(1)}, bf16[128,768]{1,0:T(8,128)(2,1)S(1)}, u32[]{:S(2)}, u32[]{:S(2)}) collective-permute-start(bf16[128,768]{1,0:T(8,128)(2,1)S(1)} %collective-permute-done.6.refs_3_), channel_id=1, source_target_pairs={{0,1},{1,0},{2,3},{3,2},{4,5},{5,4},{6,7},{7,6},{8,9},{9,8},{10,11... | collective-permute-start | bytes 589832 | tf_op jit(solution)/shard_map/ppermute | solution.py:414
  25.5 8.9 %collective-permute-start.8 = (bf16[128,768]{1,0:T(8,128)(2,1)S(1)}, bf16[128,768]{1,0:T(8,128)(2,1)S(1)}, u32[]{:S(2)}, u32[]{:S(2)}) collective-permute-start(bf16[128,768]{1,0:T(8,128)(2,1)S(1)} %collective-permute-done.7.refs_4_), channel_id=1, source_target_pairs={{0,56},{8,0},{16,8},{24,16},{32,24},{40,32},{48,40},{56,48},{1,57}... | collective-permute-start | bytes 589832 | tf_op jit(solution)/shard_map/ppermute | solution.py:406
  30.1 5.7 %collective-permute-start.5 = (bf16[128,768]{1,0:T(8,128)(2,1)S(1)}, bf16[128,768]{1,0:T(8,128)(2,1)S(1)}, u32[]{:S(2)}, u32[]{:S(2)}) collective-permute-start(bf16[128,768]{1,0:T(8,128)(2,1)S(1)} %collective-permute-done.4.refs_10_.refs_0_), channel_id=1, source_target_pairs={{0,8},{8,16},{16,24},{24,32},{32,40},{40,48},{48,56},{56,0},{1,9},... | collective-permute-start | bytes 589832 | tf_op jit(solution)/shard_map/ppermute | solution.py:406
  32.2 6.5 %collective-permute-start.14 = (bf16[128,768]{1,0:T(8,128)(2,1)S(1)}, bf16[128,768]{1,0:T(8,128)(2,1)S(1)}, u32[]{:S(2)}, u32[]{:S(2)}) collective-permute-start(bf16[128,768]{1,0:T(8,128)(2,1)S(1)} %collective-permute-done.3.refs_2_), channel_id=1, source_target_pairs={{0,1},{1,0},{2,3},{3,2},{4,5},{5,4},{6,7},{7,6},{8,9},{9,8},{10,11... | collective-permute-start | bytes 589832 | tf_op jit(solution)/shard_map/ppermute | solution.py:414
  33.9 4.8 %collective-permute-start.16 = (bf16[128,768]{1,0:T(8,128)(2,1)S(1)}, bf16[128,768]{1,0:T(8,128)(2,1)S(1)}, u32[]{:S(2)}, u32[]{:S(2)}) collective-permute-start(bf16[128,768]{1,0:T(8,128)(2,1)S(1)} %collective-permute-done.7.refs_4_), channel_id=1, source_target_pairs={{0,1},{1,0},{2,3},{3,2},{4,5},{5,4},{6,7},{7,6},{8,9},{9,8},{10,11... | collective-permute-start | bytes 589832 | tf_op jit(solution)/shard_map/ppermute | solution.py:414
  34.0 4.7 %collective-permute-start.9 = (bf16[128,768]{1,0:T(8,128)(2,1)S(1)}, bf16[128,768]{1,0:T(8,128)(2,1)S(1)}, u32[]{:S(2)}, u32[]{:S(2)}) collective-permute-start(bf16[128,768]{1,0:T(8,128)(2,1)S(1)} %collective-permute-done.4.refs_10_.refs_0_), channel_id=1, source_target_pairs={{0,1},{1,0},{2,3},{3,2},{4,5},{5,4},{6,7},{7,6},{8,9},{9,8},{10,11... | collective-permute-start | bytes 589832 | tf_op jit(solution)/shard_map/ppermute | solution.py:414
  34.4 4.3 %collective-permute-start.11 = (bf16[128,768]{1,0:T(8,128)(2,1)S(1)}, bf16[128,768]{1,0:T(8,128)(2,1)S(1)}, u32[]{:S(2)}, u32[]{:S(2)}) collective-permute-start(bf16[128,768]{1,0:T(8,128)(2,1)S(1)} %collective-permute-done.8.refs_12_.refs_2_), channel_id=1, source_target_pairs={{0,1},{1,0},{2,3},{3,2},{4,5},{5,4},{6,7},{7,6},{8,9},{9,8},{10,11... | collective-permute-start | bytes 589832 | tf_op jit(solution)/shard_map/ppermute | solution.py:414
  47.3 25.7 %all-to-all-start = ((bf16[16,64,128]{2,1,0:T(8,128)(2,1)}), bf16[16,64,128]{2,1,0:T(8,128)(2,1)}, u32[]{:S(2)}, u32[]{:S(2)}) async-start(bf16[16,64,128]{2,1,0:T(8,128)(2,1)} %shard_map.102), calls=%async_computation | async-start | bytes 524288 | tf_op jit(solution)/shard_map/all_to_all | solution.py:410
  85.6 69.7 %all-to-all-start.1 = ((bf16[16,1072,128]{2,1,0:T(8,128)(2,1)}), bf16[16,1072,128]{2,1,0:T(8,128)(2,1)}, u32[]{:S(2)}, u32[]{:S(2)}) async-start(bf16[16,1072,128]{2,1,0:T(8,128)(2,1)} %get-tuple-element.16), calls=%async_computation.1 | async-start | bytes 8781824 | tf_op jit(solution)/shard_map/all_to_all | solution.py:410
  92.4 110.5 %collective-permute-start.19 = (bf16[768,1536]{1,0:T(8,128)(2,1)S(1)}, bf16[768,1536]{1,0:T(8,128)(2,1)}, u32[]{:S(2)}, u32[]{:S(2)}) collective-permute-start(bf16[768,1536]{1,0:T(8,128)(2,1)S(1)} %copy-done.1), channel_id=1, source_target_pairs={{0,1},{1,0},{2,3},{3,2},{4,5},{5,4},{6,7},{7,6},{8,9},{9,8},{10,11... | collective-permute-start | bytes 7077896 | tf_op jit(solution)/shard_map/ppermute | solution.py:414
  93.7 109.2 %collective-permute-start.20 = (bf16[1536,768]{1,0:T(8,128)(2,1)}, bf16[1536,768]{1,0:T(8,128)(2,1)}, u32[]{:S(2)}, u32[]{:S(2)}) collective-permute-start(bf16[1536,768]{1,0:T(8,128)(2,1)} %down_own.1), channel_id=1, source_target_pairs={{0,1},{1,0},{2,3},{3,2},{4,5},{5,4},{6,7},{7,6},{8,9},{9,8},{10,11... | collective-permute-start | bytes 7077896 | tf_op jit(solution)/shard_map/ppermute | solution.py:414
  95.5 79.8 %collective-permute-start = (bf16[64,768]{1,0:T(8,128)(2,1)}, bf16[64,768]{1,0:T(8,128)(2,1)}, u32[]{:S(2)}, u32[]{:S(2)}) collective-permute-start(bf16[64,768]{1,0:T(8,128)(2,1)} %get-tuple-element.24), channel_id=1, source_target_pairs={{0,2},{2,4},{4,6},{6,8},{8,10},{10,12},{12,14},{14,16},{16,18},{18... | collective-permute-start | bytes 294920 | tf_op jit(solution)/shard_map/ppermute | solution.py:464
  99.6 75.7 %collective-permute-start.1 = (bf16[64,768]{1,0:T(8,128)(2,1)}, bf16[64,768]{1,0:T(8,128)(2,1)}, u32[]{:S(2)}, u32[]{:S(2)}) collective-permute-start(bf16[64,768]{1,0:T(8,128)(2,1)} %get-tuple-element.23), channel_id=1, source_target_pairs={{2,0},{4,2},{6,4},{8,6},{10,8},{12,10},{14,12},{16,14},{18,16},{20... | collective-permute-start | bytes 294920 | tf_op jit(solution)/shard_map/ppermute | solution.py:465
  100.9 102.0 %collective-permute-start.18 = (bf16[384,768]{1,0:T(8,128)(2,1)}, bf16[384,768]{1,0:T(8,128)(2,1)}, u32[]{:S(2)}, u32[]{:S(2)}) collective-permute-start(bf16[384,768]{1,0:T(8,128)(2,1)} %wo_own.1), channel_id=1, source_target_pairs={{0,1},{1,0},{2,3},{3,2},{4,5},{5,4},{6,7},{7,6},{8,9},{9,8},{10,11... | collective-permute-start | bytes 1769480 | tf_op jit(solution)/shard_map/ppermute | solution.py:414
  165.3 28.3 %all-to-all-start.2 = ((f32[16,8,640]{2,1,0:T(8,128)}), f32[16,8,640]{2,1,0:T(8,128)}, u32[]{:S(2)}, u32[]{:S(2)}) async-start(f32[16,8,640]{2,1,0:T(8,128)} %bitcast.20), calls=%async_computation.2 | async-start | bytes 655360 | tf_op jit(solution)/shard_map/all_to_all | solution.py:410
  190.4 12.5 %collective-permute-start.17 = (bf16[256,384]{1,0:T(8,128)(2,1)}, bf16[256,384]{1,0:T(8,128)(2,1)S(1)}, u32[]{:S(2)}, u32[]{:S(2)}) collective-permute-start(bf16[256,384]{1,0:T(8,128)(2,1)} %shard_map.105.own_ref), channel_id=1, source_target_pairs={{0,1},{1,0},{2,3},{3,2},{4,5},{5,4},{6,7},{7,6},{8,9},{9,8},{10,11... | collective-permute-start | bytes 589832 | tf_op jit(solution)/shard_map/ppermute | solution.py:414
  195.4 15.7 %all-to-all-start.3 = ((bf16[32,8,384]{2,1,0:T(8,128)(2,1)}), bf16[32,8,384]{2,1,0:T(8,128)(2,1)S(1)}, u32[]{:S(2)}, u32[]{:S(2)}) async-start(bf16[32,8,384]{2,1,0:T(8,128)(2,1)} %shard_map.106), calls=%async_computation.3 | async-start | bytes 393216 | tf_op jit(solution)/shard_map/all_to_all | solution.py:410
  (62 other events, 323.9 us)

commit v3 on v2

--- a/solution.py
+++ b/solution.py
@@ -15,8 +15,8 @@
 HEADS = 6
 BF16 = jnp.bfloat16
 F32 = jnp.float32
-LIMIT = 48 * 1024 * 1024
-VMEM = pl.BlockSpec(memory_space=pltpu.VMEM)
+LIMIT = 56 * 1024 * 1024
+FAR = pl.BlockSpec(memory_space=pltpu.HBM)
 SMEM = pl.BlockSpec(memory_space=pltpu.SMEM)
 
 
@@ -28,16 +28,45 @@
     return jnp.dot(a, b, preferred_element_type=F32)
 
 
-def call(kernel, outs, in_specs, out_specs, scratch, cost, *args):
-    return pl.pallas_call(
-        kernel,
-        out_shape=outs,
-        in_specs=in_specs,
-        out_specs=out_specs,
-        scratch_shapes=scratch,
+def call(kernel, outs, scratch, cost, arrays, scalars=(), by_hand=()):
+    single = not isinstance(outs, tuple)
+    results = (outs,) if single else outs
+    count, total = len(arrays), len(arrays) + len(scalars)
+
+    def body(*refs):
+        inputs, tables = refs[:count], refs[count:total]
+        outputs = refs[total : total + len(results)]
+        held = refs[total + len(results) :]
+        near, made, (sem_in, sem_out), rest = (
+            held[:count],
+            held[count : count + len(results)],
+            held[count + len(results) : count + len(results) + 2],
+            held[count + len(results) + 2 :],
+        )
+        copies = [pltpu.make_async_copy(inputs[i], near[i], sem_in.at[i]) for i in range(count)]
+        for copy in copies:
+            copy.start()
+        for copy in copies:
+            copy.wait()
+        kernel(*near, *tables, *made, *[outputs[i] for i in by_hand], *rest)
+        copies = [pltpu.make_async_copy(made[i], outputs[i], sem_out.at[i]) for i in range(len(results)) if i not in by_hand]
+        for copy in copies:
+            copy.start()
+        for copy in copies:
+            copy.wait()
+
+    made = pl.pallas_call(
+        body,
+        out_shape=results,
+        in_specs=[FAR] * count + [SMEM] * len(scalars),
+        out_specs=(FAR,) * len(results),
+        scratch_shapes=[pltpu.VMEM(v.shape, v.dtype) for v in (*arrays, *results)]
+        + [pltpu.SemaphoreType.DMA((count,)), pltpu.SemaphoreType.DMA((len(results),))]
+        + list(scratch),
         cost_estimate=pl.CostEstimate(flops=cost[0], bytes_accessed=cost[1], transcendentals=cost[2]),
         compiler_params=pltpu.CompilerParams(vmem_limit_bytes=LIMIT),
-    )(*args)
+    )(*arrays, *scalars)
+    return made[0] if single else made
 
 
 def prepare_kernel(states_ref, weight_ref, wq_ref, wkv_ref, q_ref, kv_ref):
@@ -60,12 +89,9 @@
     return call(
         prepare_kernel,
         (shape((768, 768), BF16), shape((768, 768), BF16), shape((HEADS, 256, 128), BF16), shape((HEADS, 256, 128), BF16)),
-        [VMEM] * 2,
-        [VMEM] * 4,
         [],
         (600_000_000, 6_000_000, 0),
-        states,
-        weight,
+        [states, weight],
     )
 
 
@@ -81,27 +107,22 @@
     return call(
         early_kernel,
         jax.ShapeDtypeStruct((10, HEADS, 128, 128), BF16),
-        [VMEM] * 11,
-        VMEM,
         [],
         (1_500_000_000, 5_000_000, 0),
-        *pieces,
-        wkv,
+        [*pieces, wkv],
     )
 
 
 def scatter_kernel(*refs):
-    wanted_ref, where_ref, out_ref, rows_ref, sem = refs[16:]
+    wanted_ref, where_ref, out_ref, rows_ref = refs[16:]
     for g in range(2):
         for p in range(16):
 
             @pl.when(where_ref[0, 2 * g] == p)
             def _():
                 start = pl.multiple_of(where_ref[0, 2 * g + 1] * 64, 64)
-                pltpu.make_async_copy(refs[p].at[pl.ds(start, 64), :], rows_ref.at[pl.ds(g * 64, 64), :], sem.at[g]).start()
-
-    for g in range(2):
-        pltpu.make_async_copy(refs[0].at[pl.ds(0, 64), :], rows_ref.at[pl.ds(g * 64, 64), :], sem.at[g]).wait()
+                rows_ref[64 * g : 64 * g + 64, :] = refs[p][pl.ds(start, 64), :]
+
     for p in range(16):
         for c in range(3):
             lanes = (p % 2) * 384 + c * 128
@@ -113,18 +134,15 @@
     return call(
         scatter_kernel,
         jax.ShapeDtypeStruct((16, 64, 128), BF16),
-        [pl.BlockSpec(memory_space=pl.ANY)] * 16 + [VMEM, SMEM],
-        VMEM,
-        [pltpu.VMEM((128, 768), BF16), pltpu.SemaphoreType.DMA((2,))],
-        (0, 700_000, 0),
-        *pieces,
-        wanted,
-        where,
+        [pltpu.VMEM((128, 768), BF16)],
+        (0, 4_000_000, 0),
+        [*pieces, wanted],
+        [where],
     )
 
 
 def column_kernel(*refs):
-    wkv_ref, early_ref, received_ref, wanted_ref, kv_ref, items_ref, sem = refs[6:]
+    wkv_ref, early_ref, received_ref, wanted_ref, kv_ref, items_ref, out_ref, sem, sems = refs[6:]
     copy = pltpu.make_async_copy(early_ref, kv_ref.at[pl.ds(0, 10 * HEADS)], sem)
     copy.start()
     for p in range(6):
@@ -142,6 +160,11 @@
             item = wanted_ref[0, p * 16 + k]
             at = pl.multiple_of((item & 1) * 64, 64)
             items_ref[p, 64 * k : 64 * k + 64, :] = kv_ref[item >> 1, pl.ds(at, 64), :]
+        pltpu.make_async_copy(items_ref.at[p], out_ref.at[p], sems.at[p]).start()
+
+    @pl.loop(0, 16)
+    def _(p):
+        pltpu.make_async_copy(items_ref.at[p], out_ref.at[p], sems.at[p]).wait()
 
 
 def column(pieces, wkv, first, received, wanted):
@@ -149,27 +172,19 @@
     return call(
         column_kernel,
         (shape((16 * HEADS, 128, 128), BF16), shape((16, 1072, 128), BF16)),
-        [VMEM] * 7 + [pl.BlockSpec(memory_space=pl.ANY), VMEM, SMEM],
-        [VMEM, VMEM],
-        [pltpu.SemaphoreType.DMA],
+        [pltpu.SemaphoreType.DMA, pltpu.SemaphoreType.DMA((16,))],
         (1_000_000_000, 12_000_000, 0),
-        *pieces,
-        wkv,
-        first,
-        received,
-        wanted,
-    )
-
-
-def partial_kernel(remote_ref, wq_ref, wkv_ref, kv_ref, out_ref, pair_ref, share_ref, rows_ref, q_ref, s_ref, sem):
-    copies = [pltpu.make_async_copy(remote_ref.at[p, pl.ds(1024, 48), :], share_ref.at[p], sem.at[p]) for p in range(16)]
-    for copy in copies:
-        copy.start()
-    for p, copy in enumerate(copies):
-        copy.wait()
+        [*pieces, wkv, first, received],
+        [wanted],
+        by_hand=(1,),
+    )
+
+
+def partial_kernel(remote_ref, wq_ref, wkv_ref, kv_ref, out_ref, pair_ref, rows_ref, q_ref, s_ref):
+    for p in range(16):
         for c in range(3):
             lanes = (p % 2) * 384 + c * 128
-            rows_ref[p // 2 * 16 : p // 2 * 16 + 16, lanes : lanes + 128] = share_ref[p, 16 * c : 16 * c + 16, :]
+            rows_ref[p // 2 * 16 : p // 2 * 16 + 16, lanes : lanes + 128] = remote_ref[p, 1024 + 16 * c : 1040 + 16 * c, :]
     query = nn(rows_ref[...], wq_ref[...]).astype(BF16)
     pair = nn(rows_ref[...], wkv_ref[...]).astype(BF16)
     for h in range(HEADS):
@@ -205,20 +220,13 @@
     return call(
         partial_kernel,
         (shape((128, 640), F32), shape((HEADS, 128, 128), BF16)),
-        [pl.BlockSpec(memory_space=pl.ANY)] + [VMEM] * 3,
-        [VMEM] * 2,
         [
-            pltpu.VMEM((16, 48, 128), BF16),
             pltpu.VMEM((128, 768), BF16),
             pltpu.VMEM((HEADS, 128, 128), BF16),
             pltpu.VMEM((2, 128, 2048), F32),
-            pltpu.SemaphoreType.DMA((16,)),
         ],
-        (2_000_000_000, 5_000_000, 1_600_000),
-        remote,
-        wq,
-        wkv,
-        kv,
+        (2_000_000_000, 10_000_000, 1_600_000),
+        [remote, wq, wkv, kv],
     )
 
 
@@ -239,11 +247,9 @@
     return call(
         merge_kernel,
         jax.ShapeDtypeStruct((32, 8, 384), BF16),
-        [VMEM],
-        VMEM,
         [],
         (2_000_000, 600_000, 10_000),
-        parts,
+        [parts],
     )
 
 
@@ -285,19 +291,10 @@
     return call(
         attend_kernel,
         jax.ShapeDtypeStruct((256, 384), BF16),
-        [VMEM] * 7 + [SMEM] * 2,
-        VMEM,
         [pltpu.VMEM((HEADS, 384, 128), BF16), pltpu.VMEM((8, 512, 128), BF16)],
         (600_000_000, 7_000_000, 800_000),
-        q,
-        kv,
-        before,
-        after,
-        wkv,
-        remote,
-        pair,
-        slots,
-        edges,
+        [q, kv, before, after, wkv, remote, pair],
+        [slots, edges],
     )
 
 
@@ -308,7 +305,6 @@
 
 
 CHUNK = 512
-STEPS = 1536 // CHUNK
 
 
 def finish_kernel(
@@ -319,86 +315,109 @@
     wo_other,
     gain_ref,
     gain2_ref,
+    rows_ref,
     up_own,
     up_other,
     down_own,
     down_other,
-    rows_ref,
     place_ref,
     out_ref,
-    normed_ref,
-    sum_ref,
-    attended_ref,
+    attended,
+    states,
+    wo,
+    gains,
+    rows,
+    up,
+    down,
+    sums,
+    result,
+    sem,
+    sems,
 ):
-    step = pl.program_id(0)
-
-    @pl.when(step == 0)
-    def _():
-        attended_ref[0] = own_ref[...]
-        attended_ref[1] = other_ref[...]
-        core = place_ref[0, 2]
-        for g in range(2):
-
-            @pl.when(place_ref[0, g] >= 0)
-            def _():
-                for k, side in ((0, core), (1, 1 - core)):
-                    for i in range(4):
-                        first = (g * 8 + 2 * i) * 2 + side
-                        at = pl.multiple_of(place_ref[0, g] * 64 + 16 * i, 16)
-                        both = jnp.concatenate([rows_ref[first], rows_ref[first + 2]], axis=0)
-                        attended_ref[k, pl.ds(at, 16), :] = both
-
-        projected = nn(attended_ref[0], wo_own[...]) + nn(attended_ref[1], wo_other[...])
-        normed_ref[...] = norm(states_ref[...].astype(F32) + projected, gain_ref[...]).astype(BF16)
-        sum_ref[...] = jnp.zeros_like(sum_ref)
-
-    def half(k, up, down):
-        v = nn(normed_ref[...], up[...])
+    copies = [
+        pltpu.make_async_copy(source, target, sem.at[i])
+        for i, (source, target) in enumerate(
+            [
+                (own_ref, attended.at[0]),
+                (other_ref, attended.at[1]),
+                (rows_ref, rows),
+                (wo_own, wo.at[0]),
+                (wo_other, wo.at[1]),
+                (states_ref, states),
+                (gain_ref, gains.at[0]),
+                (gain2_ref, gains.at[1]),
+            ]
+        )
+    ]
+    chunks = []
+    for half, (above, below) in enumerate(((up_own, down_own), (up_other, down_other))):
+        for i in range(0, 1536, CHUNK):
+            number = len(chunks)
+            part = pl.ds(i, CHUNK)
+            chunks.append(
+                (
+                    pltpu.make_async_copy(above.at[:, part], up.at[number], sems.at[2 * number]),
+                    pltpu.make_async_copy(below.at[part, :], down.at[number], sems.at[2 * number + 1]),
+                )
+            )
+    for copy in copies:
+        copy.start()
+    for chunk in chunks:
+        chunk[0].start()
+        chunk[1].start()
+    for copy in copies:
+        copy.wait()
+    core = place_ref[0, 2]
+    for g in range(2):
+
+        @pl.when(place_ref[0, g] >= 0)
+        def _():
+            for k, side in ((0, core), (1, 1 - core)):
+                for i in range(4):
+                    first = (g * 8 + 2 * i) * 2 + side
+                    at = pl.multiple_of(place_ref[0, g] * 64 + 16 * i, 16)
+                    attended[k, pl.ds(at, 16), :] = jnp.concatenate([rows[first], rows[first + 2]], axis=0)
+
+    projected = nn(attended[0], wo[0]) + nn(attended[1], wo[1])
+    normed = norm(states[...].astype(F32) + projected, gains[0]).astype(BF16)
+    for number, chunk in enumerate(chunks):
+        chunk[0].wait()
+        v = nn(normed, up[number])
         hidden = (v * (1.0 + lax.erf(v * 0.7071067811865476)) * 0.5).astype(BF16)
-        sum_ref[k] += nn(hidden, down[...])
-
-    @pl.when(step < STEPS)
-    def _():
-        half(0, up_own, down_own)
-
-    @pl.when(step >= STEPS)
-    def _():
-        half(1, up_other, down_other)
-
-    @pl.when(step == 2 * STEPS - 1)
-    def _():
-        total = normed_ref[...].astype(F32) + (sum_ref[0] + sum_ref[1])
-        out_ref[...] = norm(total, gain2_ref[...]).astype(BF16)
-
-
-def finish(own, other, states, wo_own, wo_other, gain, gain2, up_own, up_other, down_own, down_other, rows, where):
-    whole = lambda *shape: pl.BlockSpec(shape, lambda s: (0, 0), pipeline_mode=pl.Buffered(1))
-    first = lambda s: jnp.minimum(s, STEPS - 1)
-    second = lambda s: jnp.maximum(s - STEPS, 0)
+        chunk[1].wait()
+        piece = nn(hidden, down[number])
+        half = number // (1536 // CHUNK)
+        if number % (1536 // CHUNK) == 0:
+            sums[half] = piece
+        else:
+            sums[half] += piece
+    result[...] = norm(normed.astype(F32) + (sums[0] + sums[1]), gains[1]).astype(BF16)
+    pltpu.sync_copy(result, out_ref)
+
+
+def finish(own, other, states, wo_own, wo_other, gain, gain2, rows, up_own, up_other, down_own, down_other, where):
+    count = 2 * 1536 // CHUNK
     return pl.pallas_call(
         finish_kernel,
         out_shape=jax.ShapeDtypeStruct((256, 768), BF16),
-        grid=(2 * STEPS,),
-        in_specs=[
-            whole(256, 384),
-            whole(256, 384),
-            whole(256, 768),
-            whole(384, 768),
-            whole(384, 768),
-            whole(1, 768),
-            whole(1, 768),
-            pl.BlockSpec((768, CHUNK), lambda s: (0, first(s))),
-            pl.BlockSpec((768, CHUNK), lambda s: (0, second(s))),
-            pl.BlockSpec((CHUNK, 768), lambda s: (first(s), 0)),
-            pl.BlockSpec((CHUNK, 768), lambda s: (second(s), 0)),
-            pl.BlockSpec((32, 8, 384), lambda s: (0, 0, 0), pipeline_mode=pl.Buffered(1)),
-            SMEM,
+        in_specs=[FAR] * 12 + [SMEM],
+        out_specs=FAR,
+        scratch_shapes=[
+            pltpu.VMEM((2, 256, 384), BF16),
+            pltpu.VMEM((256, 768), BF16),
+            pltpu.VMEM((2, 384, 768), BF16),
+            pltpu.VMEM((2, 1, 768), F32),
+            pltpu.VMEM((32, 8, 384), BF16),
+            pltpu.VMEM((count, 768, CHUNK), BF16),
+            pltpu.VMEM((count, CHUNK, 768), BF16),
+            pltpu.VMEM((2, 256, 768), F32),
+            pltpu.VMEM((256, 768), BF16),
+            pltpu.SemaphoreType.DMA((8,)),
+            pltpu.SemaphoreType.DMA((2 * count,)),
         ],
-        out_specs=pl.BlockSpec((256, 768), lambda s: (0, 0)),
-        scratch_shapes=[pltpu.VMEM((256, 768), BF16), pltpu.VMEM((2, 256, 768), F32), pltpu.VMEM((2, 256, 384), BF16)],
         cost_estimate=pl.CostEstimate(flops=2_700_000_000, bytes_accessed=12_000_000, transcendentals=800_000),
-        compiler_params=pltpu.CompilerParams(dimension_semantics=("arbitrary",), vmem_limit_bytes=LIMIT),
-    )(own, other, states, wo_own, wo_other, gain, gain2, up_own, up_other, down_own, down_other, rows, where)
+        compiler_params=pltpu.CompilerParams(vmem_limit_bytes=LIMIT),
+    )(own, other, states, wo_own, wo_other, gain, gain2, rows, up_own, up_other, down_own, down_other, where)
 
 
 def turned(value, axis, shift):
@@ -455,18 +474,23 @@
     root_owner, root_local = global_ids >> 2, global_ids & 3
     pieces = piece_of(root_owner, root_local)
     where = jnp.stack([pieces[0], root_local[0] & 1, pieces[1], root_local[1] & 1]).reshape(1, 4)
-    received = exchanged(scatter(first + last, wanted, where), PLANE)
+    spread = scatter(first + last, wanted, where)
+
+    ends = [(i, i + 1) for i in range(127)]
+    before = lax.ppermute(states[192:], SEQ, ends)
+    after = lax.ppermute(states[:64], SEQ, [(j, i) for i, j in ends])
+    weights = (swapped(out_weight), swapped(up_weight), swapped(down_weight))
+    wq, wkv, q, kv = prepare(states, qkv_weight)
+    soon = early(first, wkv).reshape(10 * HEADS, 128, 128)
+    spread, soon, before, after, weights = lax.optimization_barrier((spread, soon, before, after, weights))
+    wo_other, up_other, down_other = weights
+
+    received = exchanged(spread, PLANE)
     root = (root_owner >> 5) * 4 + (root_owner & 3)
     source = jnp.where(here["x"] >= 2, root[1], root[0])
     wanted = jnp.concatenate([received[:, 48, :16].astype(jnp.int32).reshape(-1), source[None]]).reshape(1, 257)
 
-    ends = [(i, i + 1) for i in range(127)]
-    before = lax.ppermute(states[192:], SEQ, ends)
-    after = lax.ppermute(states[:64], SEQ, [(j, i) for i, j in ends])
-    wo_other, up_other, down_other = swapped(out_weight), swapped(up_weight), swapped(down_weight)
-
-    wq, wkv, q, kv = prepare(states, qkv_weight)
-    pairs, items = column(last, wkv, early(first, wkv).reshape(10 * HEADS, 128, 128), received, wanted)
+    pairs, items = column(last, wkv, soon, received, wanted)
     remote = exchanged(items, PLANE)
     part, pair = partial(remote, wq, wkv, pairs.reshape(16, HEADS, 128, 128))
     rows = exchanged(merge(exchanged(part.reshape(16, 8, 640), PLANE)), PLANE + ("mp",))
@@ -483,11 +507,11 @@
         wo_other,
         attn_gain.reshape(1, -1),
         mlp_gain.reshape(1, -1),
+        rows,
         up_weight,
         up_other,
         down_weight,
         down_other,
-        rows,
         where,
     )
 

time: 227 us -> 222 us (0.978)
  local copies, waits for them, and re-layouts: 47.4 us -> 15.2 us
  Pallas kernels: 40.2 us -> 57.3 us
  waiting for transfers between devices: 67.9 us -> 77.8 us
  other arithmetic: 5.75 us -> 10.5 us
  starting transfers between devices: 60.9 us -> 57.3 us
    unnamed x122 -> x58, local copies, waits for them, and re-layouts: 41 us -> 2.33 us
    pallas_call x7, Pallas kernels: 30.6 us -> 46.1 us  [call(): pl.pallas_call(body, out_shape=results, in_specs=[FAR] * count + [SMEM] *...]
    all_to_all x4, waiting for transfers between devices: 59.7 us -> 66.7 us  [exchanged(): return lax.all_to_all(value, axes, split_axis=0, concat_axis=0, tiled=True)]
    all_to_all x4, starting transfers between devices: 30.8 us -> 28 us  [exchanged(): return lax.all_to_all(value, axes, split_axis=0, concat_axis=0, tiled=True)]
    ppermute x7, waiting for transfers between devices: 7.16 us -> 9.44 us  [turned(): lax.ppermute(value, axis, [(i, (i + shift) % count) for i in range(count)])]
  transfers between devices with their start and end apart: 25 -> 25, of which waited for: 6 -> 8; matrix products, arithmetic and copies ran while one was open for 5% -> 10% of each run, Pallas kernels for 10% -> 13%
where the time goes in v3:
time: 222 us; the launch traced here: 221 us
  waiting for transfers between devices  77.8 us (35%)
  starting transfers between devices  57.3 us (26%)
  Pallas kernels  57.3 us (26%)
  local copies, waits for them, and re-layouts  15.2 us (7%)
  other arithmetic  10.5 us (5%)
  between operations  3.28 us (1%)
    all_to_all x4, waiting for transfers between devices, exchanged(): return lax.all_to_all(value, axes, split_axis=0, concat_axis=0, tiled=True)  66.7 us
    pallas_call x7, Pallas kernels, call(): pl.pallas_call(body, out_shape=results, in_specs=[FAR] * count + [SMEM] *...  46.1 us
    all_to_all x4, starting transfers between devices, exchanged(): return lax.all_to_all(value, axes, split_axis=0, concat_axis=0, tiled=True)  28 us
    ppermute x12, starting transfers between devices, swapped(): return lax.ppermute(value, 'mp', [(0, 1), (1, 0)])  13.8 us
    pallas_call x1, Pallas kernels, finish(): pl.pallas_call(finish_kernel, out_shape=jax.ShapeDtypeStruct((256, 768),...  11.2 us
    ppermute x7, starting transfers between devices, turned(): lax.ppermute(value, axis, [(i, (i + shift) % count) for i in range(count)])  10.2 us
    ppermute x7, waiting for transfers between devices, turned(): lax.ppermute(value, axis, [(i, (i + shift) % count) for i in range(count)])  9.44 us
  transfers between devices with their start and end apart: 25, of which 8 were waited for; matrix products, arithmetic and copies ran while one was open for 10% of the time, Pallas kernels for 13%

profile of v3, /device:TPU:1, one launch (start us, length us, event | category | flops | bytes accessed | tf_op | source)
XLA Modules:
  0.0 221.4 jit_solution(8182799951528941373)
XLA Ops:
  0.0 3.2 %collective-permute-start.18 = (bf16[768,1536]{1,0:T(8,128)(2,1)}, bf16[768,1536]{1,0:T(8,128)(2,1)S(1)}, u32[]{:S(2)}, u32[]{:S(2)}) collective-permute-start(bf16[768,1536]{1,0:T(8,128)(2,1)} %up_own.1), channel_id=1, source_target_pairs={{0,1},{1,0},{2,3},{3,2},{4,5},{5,4},{6,7},{7,6},{8,9},{9,8},{10,11... | collective-permute-start | bytes 7077896 | tf_op jit(solution)/shard_map/ppermute | solution.py:433
  4.8 3.9 %collective-permute-start.2 = (bf16[128,768]{1,0:T(8,128)(2,1)S(1)}, bf16[128,768]{1,0:T(8,128)(2,1)S(1)}, u32[]{:S(2)}, u32[]{:S(2)}) collective-permute-start(bf16[128,768]{1,0:T(8,128)(2,1)S(1)} %constant_dynamic-slice_fusion.refs_0_), channel_id=1, source_target_pairs={{0,56},{8,0},{16,8},{24,16},{32,24},{40,32},{48,40},{56,48},{1,57}... | collective-permute-start | bytes 589832 | tf_op jit(solution)/shard_map/ppermute | solution.py:425
  23.3 3.0 %collective-permute-start.3 = (bf16[128,768]{1,0:T(8,128)(2,1)S(1)}, bf16[128,768]{1,0:T(8,128)(2,1)S(1)}, u32[]{:S(2)}, u32[]{:S(2)}) collective-permute-start(bf16[128,768]{1,0:T(8,128)(2,1)S(1)} %collective-permute-done.2.refs_3_), channel_id=1, source_target_pairs={{0,56},{8,0},{16,8},{24,16},{32,24},{40,32},{48,40},{56,48},{1,57}... | collective-permute-start | bytes 589832 | tf_op jit(solution)/shard_map/ppermute | solution.py:425
  30.5 3.4 %collective-permute-start.11 = (bf16[128,768]{1,0:T(8,128)(2,1)S(1)}, bf16[128,768]{1,0:T(8,128)(2,1)S(1)}, u32[]{:S(2)}, u32[]{:S(2)}) collective-permute-start(bf16[128,768]{1,0:T(8,128)(2,1)S(1)} %collective-permute-done.3.refs_4_), channel_id=1, source_target_pairs={{0,56},{8,0},{16,8},{24,16},{32,24},{40,32},{48,40},{56,48},{1,57}... | collective-permute-start | bytes 589832 | tf_op jit(solution)/shard_map/ppermute | solution.py:425
  37.2 1.8 collective-permute-start.6
  39.0 1.8 add_bitcast_fusion.refs_17_
  40.8 4.2 %shard_map.100 = (bf16[768,768]{1,0:T(8,128)(2,1)}, bf16[768,768]{1,0:T(8,128)(2,1)}, bf16[6,256,128]{2,1,0:T(8,128)(2,1)}, bf16[6,256,128]{2,1,0:T(8,128)(2,1)}) custom-call(bf16[256,768]{1,0:T(8,128)(2,1)} %states_ref.1, bf16[3,768,384]{2,1,0:T(8,128)(2,1)} %refs_1_.1), custom_call_target="tpu_custom_call" | custom-call | flops 600000000 | bytes 6000000 | tf_op jit(solution)/shard_map/pallas_call | solution.py:58
  47.7 6.7 %collective-permute-done.10.refs_11_.refs_1_ = bf16[128,768]{1,0:T(8,128)(2,1)S(1)} collective-permute-done((bf16[128,768]{1,0:T(8,128)(2,1)S(1)}, bf16[128,768]{1,0:T(8,128)(2,1)S(1)}, u32[]{:S(2)}, u32[]{:S(2)}) %collective-permute-start.10) | collective-permute-done | bytes 196640 | tf_op jit(solution)/shard_map/ppermute | solution.py:425
  57.1 4.0 %collective-permute-start.15 = (bf16[64,768]{1,0:T(8,128)(2,1)S(1)}, bf16[64,768]{1,0:T(8,128)(2,1)S(1)}, u32[]{:S(2)}, u32[]{:S(2)}) collective-permute-start(bf16[64,768]{1,0:T(8,128)(2,1)S(1)} %get-tuple-element.38), channel_id=1, source_target_pairs={{0,2},{2,4},{4,6},{6,8},{8,10},{10,12},{12,14},{14,16},{16,18},{18... | collective-permute-start | bytes 294920 | tf_op jit(solution)/shard_map/ppermute | solution.py:480
  61.2 5.1 %shard_map.102 = bf16[10,6,128,128]{3,2,1,0:T(8,128)(2,1)} custom-call(bf16[128,768]{1,0:T(8,128)(2,1)} %copy-done.4, bf16[128,768]{1,0:T(8,128)(2,1)} %copy-done.15, bf16[128,768]{1,0:T(8,128)(2,1)} %copy-done.19, bf16[128,768]{1,0:T(8,128)(2,1)} %copy-done.14, bf16[128,768]{1,0:T(8,128)(2,1)} %copy-done.17, bf16[128,768]{1,0:T(8,128)(2,1)} %copy-done.13, ...), custom_call_target="tpu_custom_call" | custom-call | flops 1500000000 | bytes 5000000 | tf_op jit(solution)/shard_map/pallas_call | solution.py:58
  66.3 3.7 %shard_map.101 = bf16[16,64,128]{2,1,0:T(8,128)(2,1)} custom-call(bf16[128,768]{1,0:T(8,128)(2,1)} %copy-done.4, bf16[128,768]{1,0:T(8,128)(2,1)} %copy-done.15, bf16[128,768]{1,0:T(8,128)(2,1)} %copy-done.19, bf16[128,768]{1,0:T(8,128)(2,1)} %copy-done.14, bf16[128,768]{1,0:T(8,128)(2,1)} %copy-done.17, bf16[128,768]{1,0:T(8,128)(2,1)} %copy-done.13, ...), custom_call_target="tpu_custom_call" | custom-call | bytes 4000000 | tf_op jit(solution)/shard_map/pallas_call | solution.py:58
  70.9 8.7 %all-to-all-start = ((bf16[16,64,128]{2,1,0:T(8,128)(2,1)}), bf16[16,64,128]{2,1,0:T(8,128)(2,1)S(1)}, u32[]{:S(2)}, u32[]{:S(2)}) async-start(bf16[16,64,128]{2,1,0:T(8,128)(2,1)} %shard_map.101), calls=%async_computation | async-start | bytes 524288 | tf_op jit(solution)/shard_map/all_to_all | solution.py:429
  80.9 6.2 %all-to-all-done.refs_8_ = bf16[16,64,128]{2,1,0:T(8,128)(2,1)S(1)} async-done(((bf16[16,64,128]{2,1,0:T(8,128)(2,1)}), bf16[16,64,128]{2,1,0:T(8,128)(2,1)S(1)}, u32[]{:S(2)}, u32[]{:S(2)}) %all-to-all-start) | async-done | bytes 262176 | tf_op jit(solution)/shard_map/all_to_all | solution.py:429
  87.8 8.5 %shard_map.103 = (bf16[96,128,128]{2,1,0:T(8,128)(2,1)}, bf16[16,1072,128]{2,1,0:T(8,128)(2,1)}) custom-call(bf16[128,768]{1,0:T(8,128)(2,1)} %copy-done.6, bf16[128,768]{1,0:T(8,128)(2,1)} %copy-done.8, bf16[128,768]{1,0:T(8,128)(2,1)} %copy-done.5, bf16[128,768]{1,0:T(8,128)(2,1)} %copy-done.9, bf16[128,768]{1,0:T(8,128)(2,1)} %copy-done.10, ...), custom_call_target="tpu_custom_call" | custom-call | flops 1000000000 | bytes 12000000 | tf_op jit(solution)/shard_map/pallas_call | solution.py:58
  96.3 4.6 %all-to-all-start.1 = ((bf16[16,1072,128]{2,1,0:T(8,128)(2,1)}), bf16[16,1072,128]{2,1,0:T(8,128)(2,1)}, u32[]{:S(2)}, u32[]{:S(2)}) async-start(bf16[16,1072,128]{2,1,0:T(8,128)(2,1)} %get-tuple-element.27), calls=%async_computation.1 | async-start | bytes 8781824 | tf_op jit(solution)/shard_map/all_to_all | solution.py:429
  100.9 54.0 %all-to-all-done.1.refs_0_ = bf16[16,1072,128]{2,1,0:T(8,128)(2,1)} async-done(((bf16[16,1072,128]{2,1,0:T(8,128)(2,1)}), bf16[16,1072,128]{2,1,0:T(8,128)(2,1)}, u32[]{:S(2)}, u32[]{:S(2)}) %all-to-all-start.1) | async-done | bytes 4390944 | tf_op jit(solution)/shard_map/all_to_all | solution.py:429
  154.9 9.2 %shard_map.104 = (f32[128,640]{1,0:T(8,128)}, bf16[6,128,128]{2,1,0:T(8,128)(2,1)}) custom-call(bf16[16,1072,128]{2,1,0:T(8,128)(2,1)} %all-to-all-done.1.refs_0_, bf16[768,768]{1,0:T(8,128)(2,1)} %get-tuple-element.28.refs_1_, bf16[768,768]{1,0:T(8,128)(2,1)} %get-tuple-element.22.refs_10_.refs_6_.refs_2_.refs_4_, bf16[16,6,128,128]{3,2,1,0:T(8,128)(2,1)} %bitcast.18), custom_call_target="tpu_custom_call" | custom-call | flops 2000000000 | bytes 10000000 | tf_op jit(solution)/shard_map/pallas_call | solution.py:58
  164.1 7.4 %all-to-all-start.2 = ((f32[16,8,640]{2,1,0:T(8,128)}), f32[16,8,640]{2,1,0:T(8,128)S(1)}, u32[]{:S(2)}, u32[]{:S(2)}) async-start(f32[16,8,640]{2,1,0:T(8,128)} %bitcast.20), calls=%async_computation.2 | async-start | bytes 655360 | tf_op jit(solution)/shard_map/all_to_all | solution.py:429
  172.9 13.5 %shard_map.105.own_ref = bf16[256,384]{1,0:T(8,128)(2,1)} custom-call(bf16[6,256,128]{2,1,0:T(8,128)(2,1)} %get-tuple-element.20.refs_0_, bf16[6,256,128]{2,1,0:T(8,128)(2,1)} %get-tuple-element.21.refs_1_, bf16[64,768]{1,0:T(8,128)(2,1)} %copy-done.24, bf16[64,768]{1,0:T(8,128)(2,1)} %copy-done.23, ...), custom_call_target="tpu_custom_call" | custom-call | flops 600000000 | bytes 7000000 | tf_op jit(solution)/shard_map/pallas_call | solution.py:58
  186.5 4.6 %collective-permute-start.20 = (bf16[256,384]{1,0:T(8,128)(2,1)}, bf16[256,384]{1,0:T(8,128)(2,1)S(1)}, u32[]{:S(2)}, u32[]{:S(2)}) collective-permute-start(bf16[256,384]{1,0:T(8,128)(2,1)} %shard_map.105.own_ref), channel_id=1, source_target_pairs={{0,1},{1,0},{2,3},{3,2},{4,5},{5,4},{6,7},{7,6},{8,9},{9,8},{10,11... | collective-permute-start | bytes 589832 | tf_op jit(solution)/shard_map/ppermute | solution.py:433
  191.7 1.9 shard_map.106
  193.6 7.4 %all-to-all-start.3 = ((bf16[32,8,384]{2,1,0:T(8,128)(2,1)}), bf16[32,8,384]{2,1,0:T(8,128)(2,1)S(1)}, u32[]{:S(2)}, u32[]{:S(2)}) async-start(bf16[32,8,384]{2,1,0:T(8,128)(2,1)} %shard_map.106), calls=%async_computation.3 | async-start | bytes 393216 | tf_op jit(solution)/shard_map/all_to_all | solution.py:429
  202.9 6.5 %all-to-all-done.3.rows_ref = bf16[32,8,384]{2,1,0:T(8,128)(2,1)S(1)} async-done(((bf16[32,8,384]{2,1,0:T(8,128)(2,1)}), bf16[32,8,384]{2,1,0:T(8,128)(2,1)S(1)}, u32[]{:S(2)}, u32[]{:S(2)}) %all-to-all-start.3) | async-done | bytes 196640 | tf_op jit(solution)/shard_map/all_to_all | solution.py:429
  210.0 11.2 %shard_map.107 = bf16[256,768]{1,0:T(8,128)(2,1)} custom-call(bf16[256,384]{1,0:T(8,128)(2,1)} %shard_map.105.own_ref, bf16[256,384]{1,0:T(8,128)(2,1)} %copy-done.22, bf16[256,768]{1,0:T(8,128)(2,1)} %states_ref.1, bf16[384,768]{1,0:T(8,128)(2,1)} %wo_own.1, bf16[384,768]{1,0:T(8,128)(2,1)} %copy-done.12, f32[1,768]{1,0:T(1,128)} %reshape.226.gain_ref, ...), custom_call_target="tpu_custom_call" | custom-call | flops 2700000000 | bytes 12000000 | tf_op jit(solution)/shard_map/pallas_call | solution.py:400
  (128 shorter events, 33.9 us)
Async XLA Ops:
  0.0 70.1 %collective-permute-start.18 = (bf16[768,1536]{1,0:T(8,128)(2,1)}, bf16[768,1536]{1,0:T(8,128)(2,1)S(1)}, u32[]{:S(2)}, u32[]{:S(2)}) collective-permute-start(bf16[768,1536]{1,0:T(8,128)(2,1)} %up_own.1), channel_id=1, source_target_pairs={{0,1},{1,0},{2,3},{3,2},{4,5},{5,4},{6,7},{7,6},{8,9},{9,8},{10,11... | collective-permute-start | bytes 7077896 | tf_op jit(solution)/shard_map/ppermute | solution.py:433
  3.2 67.7 %collective-permute-start.19 = (bf16[1536,768]{1,0:T(8,128)(2,1)}, bf16[1536,768]{1,0:T(8,128)(2,1)}, u32[]{:S(2)}, u32[]{:S(2)}) collective-permute-start(bf16[1536,768]{1,0:T(8,128)(2,1)} %down_own.1), channel_id=1, source_target_pairs={{0,1},{1,0},{2,3},{3,2},{4,5},{5,4},{6,7},{7,6},{8,9},{9,8},{10,11... | collective-permute-start | bytes 7077896 | tf_op jit(solution)/shard_map/ppermute | solution.py:433
  4.2 19.1 %collective-permute-start.4 = (bf16[128,768]{1,0:T(8,128)(2,1)S(1)}, bf16[128,768]{1,0:T(8,128)(2,1)S(1)}, u32[]{:S(2)}, u32[]{:S(2)}) collective-permute-start(bf16[128,768]{1,0:T(8,128)(2,1)S(1)} %constant_dynamic-slice_fusion.refs_0_), channel_id=1, source_target_pairs={{0,1},{1,0},{2,3},{3,2},{4,5},{5,4},{6,7},{7,6},{8,9},{9,8},{10,11... | collective-permute-start | bytes 589832 | tf_op jit(solution)/shard_map/ppermute | solution.py:433
  4.8 18.1 %collective-permute-start.2 = (bf16[128,768]{1,0:T(8,128)(2,1)S(1)}, bf16[128,768]{1,0:T(8,128)(2,1)S(1)}, u32[]{:S(2)}, u32[]{:S(2)}) collective-permute-start(bf16[128,768]{1,0:T(8,128)(2,1)S(1)} %constant_dynamic-slice_fusion.refs_0_), channel_id=1, source_target_pairs={{0,56},{8,0},{16,8},{24,16},{32,24},{40,32},{48,40},{56,48},{1,57}... | collective-permute-start | bytes 589832 | tf_op jit(solution)/shard_map/ppermute | solution.py:425
  8.6 19.9 %collective-permute-start = (bf16[128,768]{1,0:T(8,128)(2,1)S(1)}, bf16[128,768]{1,0:T(8,128)(2,1)S(1)}, u32[]{:S(2)}, u32[]{:S(2)}) collective-permute-start(bf16[128,768]{1,0:T(8,128)(2,1)S(1)} %constant_dynamic-slice_fusion.refs_0_), channel_id=1, source_target_pairs={{0,8},{8,16},{16,24},{24,32},{32,40},{40,48},{48,56},{56,0},{1,9},... | collective-permute-start | bytes 589832 | tf_op jit(solution)/shard_map/ppermute | solution.py:425
  22.9 6.1 %collective-permute-start.7 = (bf16[128,768]{1,0:T(8,128)(2,1)S(1)}, bf16[128,768]{1,0:T(8,128)(2,1)S(1)}, u32[]{:S(2)}, u32[]{:S(2)}) collective-permute-start(bf16[128,768]{1,0:T(8,128)(2,1)S(1)} %collective-permute-done.2.refs_3_), channel_id=1, source_target_pairs={{0,1},{1,0},{2,3},{3,2},{4,5},{5,4},{6,7},{7,6},{8,9},{9,8},{10,11... | collective-permute-start | bytes 589832 | tf_op jit(solution)/shard_map/ppermute | solution.py:433
  23.3 7.2 %collective-permute-start.3 = (bf16[128,768]{1,0:T(8,128)(2,1)S(1)}, bf16[128,768]{1,0:T(8,128)(2,1)S(1)}, u32[]{:S(2)}, u32[]{:S(2)}) collective-permute-start(bf16[128,768]{1,0:T(8,128)(2,1)S(1)} %collective-permute-done.2.refs_3_), channel_id=1, source_target_pairs={{0,56},{8,0},{16,8},{24,16},{32,24},{40,32},{48,40},{56,48},{1,57}... | collective-permute-start | bytes 589832 | tf_op jit(solution)/shard_map/ppermute | solution.py:425
  28.6 6.0 %collective-permute-start.5 = (bf16[128,768]{1,0:T(8,128)(2,1)S(1)}, bf16[128,768]{1,0:T(8,128)(2,1)S(1)}, u32[]{:S(2)}, u32[]{:S(2)}) collective-permute-start(bf16[128,768]{1,0:T(8,128)(2,1)S(1)} %collective-permute-done.refs_1_), channel_id=1, source_target_pairs={{0,1},{1,0},{2,3},{3,2},{4,5},{5,4},{6,7},{7,6},{8,9},{9,8},{10,11... | collective-permute-start | bytes 589832 | tf_op jit(solution)/shard_map/ppermute | solution.py:433
  29.0 7.6 %collective-permute-start.1 = (bf16[128,768]{1,0:T(8,128)(2,1)S(1)}, bf16[128,768]{1,0:T(8,128)(2,1)S(1)}, u32[]{:S(2)}, u32[]{:S(2)}) collective-permute-start(bf16[128,768]{1,0:T(8,128)(2,1)S(1)} %collective-permute-done.refs_1_), channel_id=1, source_target_pairs={{0,8},{8,16},{16,24},{24,32},{32,40},{40,48},{48,56},{56,0},{1,9},... | collective-permute-start | bytes 589832 | tf_op jit(solution)/shard_map/ppermute | solution.py:425
  30.5 6.8 %collective-permute-start.11 = (bf16[128,768]{1,0:T(8,128)(2,1)S(1)}, bf16[128,768]{1,0:T(8,128)(2,1)S(1)}, u32[]{:S(2)}, u32[]{:S(2)}) collective-permute-start(bf16[128,768]{1,0:T(8,128)(2,1)S(1)} %collective-permute-done.3.refs_4_), channel_id=1, source_target_pairs={{0,56},{8,0},{16,8},{24,16},{32,24},{40,32},{48,40},{56,48},{1,57}... | collective-permute-start | bytes 589832 | tf_op jit(solution)/shard_map/ppermute | solution.py:425
  34.6 10.6 %collective-permute-start.8 = (bf16[128,768]{1,0:T(8,128)(2,1)S(1)}, bf16[128,768]{1,0:T(8,128)(2,1)S(1)}, u32[]{:S(2)}, u32[]{:S(2)}) collective-permute-start(bf16[128,768]{1,0:T(8,128)(2,1)S(1)} %collective-permute-done.3.refs_4_), channel_id=1, source_target_pairs={{0,1},{1,0},{2,3},{3,2},{4,5},{5,4},{6,7},{7,6},{8,9},{9,8},{10,11... | collective-permute-start | bytes 589832 | tf_op jit(solution)/shard_map/ppermute | solution.py:433
  36.6 8.7 %collective-permute-start.9 = (bf16[128,768]{1,0:T(8,128)(2,1)S(1)}, bf16[128,768]{1,0:T(8,128)(2,1)S(1)}, u32[]{:S(2)}, u32[]{:S(2)}) collective-permute-start(bf16[128,768]{1,0:T(8,128)(2,1)S(1)} %collective-permute-done.1.refs_2_), channel_id=1, source_target_pairs={{0,8},{8,16},{16,24},{24,32},{32,40},{40,48},{48,56},{56,0},{1,9},... | collective-permute-start | bytes 589832 | tf_op jit(solution)/shard_map/ppermute | solution.py:425
  37.2 8.7 %collective-permute-start.6 = (bf16[128,768]{1,0:T(8,128)(2,1)S(1)}, bf16[128,768]{1,0:T(8,128)(2,1)S(1)}, u32[]{:S(2)}, u32[]{:S(2)}) collective-permute-start(bf16[128,768]{1,0:T(8,128)(2,1)S(1)} %collective-permute-done.1.refs_2_), channel_id=1, source_target_pairs={{0,1},{1,0},{2,3},{3,2},{4,5},{5,4},{6,7},{7,6},{8,9},{9,8},{10,11... | collective-permute-start | bytes 589832 | tf_op jit(solution)/shard_map/ppermute | solution.py:433
  45.2 24.8 %collective-permute-start.17 = (bf16[384,768]{1,0:T(8,128)(2,1)}, bf16[384,768]{1,0:T(8,128)(2,1)S(1)}, u32[]{:S(2)}, u32[]{:S(2)}) collective-permute-start(bf16[384,768]{1,0:T(8,128)(2,1)} %wo_own.1), channel_id=1, source_target_pairs={{0,1},{1,0},{2,3},{3,2},{4,5},{5,4},{6,7},{7,6},{8,9},{9,8},{10,11... | collective-permute-start | bytes 1769480 | tf_op jit(solution)/shard_map/ppermute | solution.py:433
  45.9 8.5 %collective-permute-start.10 = (bf16[128,768]{1,0:T(8,128)(2,1)S(1)}, bf16[128,768]{1,0:T(8,128)(2,1)S(1)}, u32[]{:S(2)}, u32[]{:S(2)}) collective-permute-start(bf16[128,768]{1,0:T(8,128)(2,1)S(1)} %collective-permute-done.9.refs_10_.refs_0_), channel_id=1, source_target_pairs={{0,8},{8,16},{16,24},{24,32},{32,40},{40,48},{48,56},{56,0},{1,9},... | collective-permute-start | bytes 589832 | tf_op jit(solution)/shard_map/ppermute | solution.py:425
  47.6 8.2 %collective-permute-start.12 = (bf16[128,768]{1,0:T(8,128)(2,1)S(1)}, bf16[128,768]{1,0:T(8,128)(2,1)S(1)}, u32[]{:S(2)}, u32[]{:S(2)}) collective-permute-start(bf16[128,768]{1,0:T(8,128)(2,1)S(1)} %collective-permute-done.9.refs_10_.refs_0_), channel_id=1, source_target_pairs={{0,1},{1,0},{2,3},{3,2},{4,5},{5,4},{6,7},{7,6},{8,9},{9,8},{10,11... | collective-permute-start | bytes 589832 | tf_op jit(solution)/shard_map/ppermute | solution.py:433
  54.4 2.7 %collective-permute-start.13 = (bf16[128,768]{1,0:T(8,128)(2,1)S(1)}, bf16[128,768]{1,0:T(8,128)(2,1)S(1)}, u32[]{:S(2)}, u32[]{:S(2)}) collective-permute-start(bf16[128,768]{1,0:T(8,128)(2,1)S(1)} %collective-permute-done.10.refs_11_.refs_1_), channel_id=1, source_target_pairs={{0,1},{1,0},{2,3},{3,2},{4,5},{5,4},{6,7},{7,6},{8,9},{9,8},{10,11... | collective-permute-start | bytes 589832 | tf_op jit(solution)/shard_map/ppermute | solution.py:433
  55.8 14.2 %collective-permute-start.16 = (bf16[64,768]{1,0:T(8,128)(2,1)S(1)}, bf16[64,768]{1,0:T(8,128)(2,1)S(1)}, u32[]{:S(2)}, u32[]{:S(2)}) collective-permute-start(bf16[64,768]{1,0:T(8,128)(2,1)S(1)} %get-tuple-element.37), channel_id=1, source_target_pairs={{2,0},{4,2},{6,4},{8,6},{10,8},{12,10},{14,12},{16,14},{18,16},{20... | collective-permute-start | bytes 294920 | tf_op jit(solution)/shard_map/ppermute | solution.py:481
  57.1 12.9 %collective-permute-start.15 = (bf16[64,768]{1,0:T(8,128)(2,1)S(1)}, bf16[64,768]{1,0:T(8,128)(2,1)S(1)}, u32[]{:S(2)}, u32[]{:S(2)}) collective-permute-start(bf16[64,768]{1,0:T(8,128)(2,1)S(1)} %get-tuple-element.38), channel_id=1, source_target_pairs={{0,2},{2,4},{4,6},{6,8},{8,10},{10,12},{12,14},{14,16},{16,18},{18... | collective-permute-start | bytes 294920 | tf_op jit(solution)/shard_map/ppermute | solution.py:480
  70.9 16.2 %all-to-all-start = ((bf16[16,64,128]{2,1,0:T(8,128)(2,1)}), bf16[16,64,128]{2,1,0:T(8,128)(2,1)S(1)}, u32[]{:S(2)}, u32[]{:S(2)}) async-start(bf16[16,64,128]{2,1,0:T(8,128)(2,1)} %shard_map.101), calls=%async_computation | async-start | bytes 524288 | tf_op jit(solution)/shard_map/all_to_all | solution.py:429
  96.3 58.5 %all-to-all-start.1 = ((bf16[16,1072,128]{2,1,0:T(8,128)(2,1)}), bf16[16,1072,128]{2,1,0:T(8,128)(2,1)}, u32[]{:S(2)}, u32[]{:S(2)}) async-start(bf16[16,1072,128]{2,1,0:T(8,128)(2,1)} %get-tuple-element.27), calls=%async_computation.1 | async-start | bytes 8781824 | tf_op jit(solution)/shard_map/all_to_all | solution.py:429
  164.1 26.9 %all-to-all-start.2 = ((f32[16,8,640]{2,1,0:T(8,128)}), f32[16,8,640]{2,1,0:T(8,128)S(1)}, u32[]{:S(2)}, u32[]{:S(2)}) async-start(f32[16,8,640]{2,1,0:T(8,128)} %bitcast.20), calls=%async_computation.2 | async-start | bytes 655360 | tf_op jit(solution)/shard_map/all_to_all | solution.py:429
  186.5 16.4 %collective-permute-start.20 = (bf16[256,384]{1,0:T(8,128)(2,1)}, bf16[256,384]{1,0:T(8,128)(2,1)S(1)}, u32[]{:S(2)}, u32[]{:S(2)}) collective-permute-start(bf16[256,384]{1,0:T(8,128)(2,1)} %shard_map.105.own_ref), channel_id=1, source_target_pairs={{0,1},{1,0},{2,3},{3,2},{4,5},{5,4},{6,7},{7,6},{8,9},{9,8},{10,11... | collective-permute-start | bytes 589832 | tf_op jit(solution)/shard_map/ppermute | solution.py:433
  193.6 15.7 %all-to-all-start.3 = ((bf16[32,8,384]{2,1,0:T(8,128)(2,1)}), bf16[32,8,384]{2,1,0:T(8,128)(2,1)S(1)}, u32[]{:S(2)}, u32[]{:S(2)}) async-start(bf16[32,8,384]{2,1,0:T(8,128)(2,1)} %shard_map.106), calls=%async_computation.3 | async-start | bytes 393216 | tf_op jit(solution)/shard_map/all_to_all | solution.py:429
  (30 other events, 526.0 us)

commit v4 on v3

v4 whole, which is shorter than its diff:
```python
import functools

import jax
import jax.numpy as jnp
from jax import lax
from jax.experimental import pallas as pl
from jax.experimental.pallas import tpu as pltpu
from jax.sharding import Mesh
from jax.sharding import PartitionSpec as P

SEQ = ("x", "z", "y")
PLANE = ("x", "y")
EPSILON = 1e-05
NEGATIVE = -1e30
HEADS = 6
BF16 = jnp.bfloat16
F32 = jnp.float32
LIMIT = 56 * 1024 * 1024
SLOTS = 10
MORE = 16 - SLOTS
STRIDE = SLOTS * 64 + 48
FAR = pl.BlockSpec(memory_space=pltpu.HBM)
SMEM = pl.BlockSpec(memory_space=pltpu.SMEM)


def nt(a, b):
    return lax.dot_general(a, b, (((1,), (1,)), ((), ())), preferred_element_type=F32)


def nn(a, b):
    return jnp.dot(a, b, preferred_element_type=F32)


def call(kernel, outs, scratch, cost, arrays, raw=(), scalars=(), by_hand=(), tables=()):
    single = not isinstance(outs, tuple)
    results = (outs,) if single else outs
    count, total = len(arrays), len(arrays) + len(raw) + len(scalars)

    def body(*refs):
        inputs, others = refs[:count], refs[count:total]
        outputs = refs[total : total + len(results)]
        listed = refs[total + len(results) : total + len(results) + len(tables)]
        held = refs[total + len(results) + len(tables) :]
        near, made, (sem_in, sem_out), rest = (
            held[:count],
            held[count : count + len(results)],
            held[count + len(results) : count + len(results) + 2],
            held[count + len(results) + 2 :],
        )
        copies = [pltpu.make_async_copy(inputs[i], near[i], sem_in.at[i]) for i in range(count)]
        for copy in copies:
            copy.start()
        for copy in copies:
            copy.wait()
        kernel(*near, *others, *made, *[outputs[i] for i in by_hand], *listed, *rest)
        copies = [pltpu.make_async_copy(made[i], outputs[i], sem_out.at[i]) for i in range(len(results)) if i not in by_hand]
        for copy in copies:
            copy.start()
        for copy in copies:
            copy.wait()

    made = pl.pallas_call(
        body,
        out_shape=(*results, *tables),
        in_specs=[FAR] * (count + len(raw)) + [SMEM] * len(scalars),
        out_specs=(FAR,) * len(results) + (SMEM,) * len(tables),
        scratch_shapes=[pltpu.VMEM(v.shape, v.dtype) for v in (*arrays, *results)]
        + [pltpu.SemaphoreType.DMA((count,)), pltpu.SemaphoreType.DMA((len(results),))]
        + list(scratch),
        cost_estimate=pl.CostEstimate(flops=cost[0], bytes_accessed=cost[1], transcendentals=cost[2]),
        compiler_params=pltpu.CompilerParams(vmem_limit_bytes=LIMIT),
    )(*arrays, *raw, *scalars)
    return made[0] if single and not tables else made


def pick(condition, yes, no):
    return jnp.where(condition, yes, no)


def piece_of(owner, local, z, core):
    away = (z - ((owner >> 2) & 7)) & 7
    far = pick((local >> 1) == core, 0, 1)
    first = pick(away == 7, 2, away) + 3 * far
    second = pick(away == 6, 7, 6) + 2 * far
    last = 7 + away + 3 * far
    return pick((away <= 1) | (away == 7), first, pick((away == 2) | (away == 6), second, last))


def prepare_kernel(
    states_ref, weight_ref, owner_ref, local_ref, ids_ref, here_ref, wq_ref, wkv_ref, q_ref, kv_ref, spread_ref, slots_ref, count_ref, rows_ref
):
    z, core = here_ref[0, 1], here_ref[0, 3]
    for g in range(2):
        start = pl.multiple_of((ids_ref[0, g] & 3) * 64, 64)
        rows_ref[64 * g : 64 * g + 64, :] = states_ref[pl.ds(start, 64), :]
    for p in range(16):
        for c in range(3):
            lanes = (p % 2) * 384 + c * 128
            spread_ref[p, 16 * c : 16 * c + 16, :] = rows_ref[p // 2 * 16 : p // 2 * 16 + 16, lanes : lanes + 128]
        count_ref[p] = 0
    line = lax.broadcasted_iota(jnp.int32, (16, 128), 0)
    lane = lax.broadcasted_iota(jnp.int32, (16, 128), 1)
    place = line * 128 + lane
    wanted = jnp.zeros((16, 128), F32)
    most = jnp.int32(0)
    for b in range(4):
        for h in range(HEADS):
            for r in range(3):
                owner, local = owner_ref[0, b, h, r], local_ref[0, b, h, r]
                item = (piece_of(owner, local, z, core) * HEADS + h) * 2 + (local & 1)
                group = ((owner >> 5) << 2) + (owner & 3)
                rank = count_ref[group]
                count_ref[group] = rank + 1
                most = jnp.maximum(most, rank)
                near = group * STRIDE + rank * 64
                beyond = 16 * STRIDE + group * MORE * 64 + (rank - SLOTS) * 64
                slots_ref[0, (b * HEADS + h) * 3 + r] = pick(rank < SLOTS, near, beyond)
                wanted = jnp.where(place == group * 128 + rank, item.astype(F32), wanted)
    wanted = jnp.where(lane == 127, pick(most >= SLOTS, 1.0, 0.0), wanted)
    for p in range(16):
        spread_ref[p, 48:64, :] = jnp.broadcast_to(wanted[p : p + 1, :], (16, 128)).astype(BF16)
    wq_ref[...] = jnp.zeros_like(wq_ref)
    for h in range(HEADS):
        part = slice(64 * h, 64 * h + 64)
        wq_ref[:, 128 * h : 128 * h + 64] = weight_ref[0, :, part] * BF16(0.125)
        wkv_ref[:, 128 * h : 128 * h + 64] = weight_ref[1, :, part]
        wkv_ref[:, 128 * h + 64 : 128 * h + 128] = weight_ref[2, :, part]
    query = nn(states_ref[...], wq_ref[...]).astype(BF16)
    pair = nn(states_ref[...], wkv_ref[...]).astype(BF16)
    for h in range(HEADS):
        q_ref[h] = query[:, 128 * h : 128 * h + 128]
        kv_ref[h] = pair[:, 128 * h : 128 * h + 128]


def prepare(states, weight, owner, local, ids, here):
    shape = jax.ShapeDtypeStruct
    square, heads = shape((768, 768), BF16), shape((HEADS, 256, 128), BF16)
    return call(
        prepare_kernel,
        (square, square, heads, heads, shape((16, 64, 128), BF16)),
        [pltpu.SMEM((16,), jnp.int32), pltpu.VMEM((128, 768), BF16)],
        (600_000_000, 6_000_000, 0),
        [states, weight],
        scalars=[owner, local, ids, here],
        tables=(shape((1, 72), jnp.int32),),
    )


def early_kernel(*refs):
    wkv_ref, kv_ref = refs[-2:]
    for p in range(len(refs) - 2):
        pair = nn(refs[p][...], wkv_ref[...]).astype(BF16)
        for h in range(HEADS):
            kv_ref[p * HEADS + h] = pair[:, 128 * h : 128 * h + 128]


def early(pieces, wkv):
    count = len(pieces)
    return call(
        early_kernel,
        jax.ShapeDtypeStruct((count * HEADS, 128, 128), BF16),
        [],
        (count * 150_000_000, count * 500_000, 0),
        [*pieces, wkv],
    )


def column_kernel(*refs):
    (
        wkv_ref,
        received_ref,
        shares_ref,
        early_ref,
        second_ref,
        ids_ref,
        here_ref,
        kv_ref,
        items_ref,
        out_ref,
        wanted_ref,
        flag_ref,
        asked_ref,
        sem,
        sems,
    ) = refs[6:]
    copies = [
        pltpu.make_async_copy(early_ref, kv_ref.at[pl.ds(0, 6 * HEADS)], sem.at[0]),
        pltpu.make_async_copy(second_ref, kv_ref.at[pl.ds(6 * HEADS, 4 * HEADS)], sem.at[1]),
    ]
    for p in range(16):
        asked_ref[p : p + 1, :] = received_ref[p, 48:49, :].astype(F32).astype(jnp.int32)
    copies.append(pltpu.make_async_copy(asked_ref, wanted_ref, sem.at[2]))
    for copy in copies:
        copy.start()
    for p in range(6):
        pair = nn(refs[p][...], wkv_ref[...]).astype(BF16)
        for h in range(HEADS):
            kv_ref[(10 + p) * HEADS + h] = pair[:, 128 * h : 128 * h + 128]
    for copy in copies:
        copy.wait()
    flag = wanted_ref[0, 127]
    for p in range(1, 16):
        flag = jnp.maximum(flag, wanted_ref[p, 127])
    flag_ref[0, 0] = flag
    owner = pick(here_ref[0, 0] >= 2, ids_ref[0, 1], ids_ref[0, 0]) >> 2
    share = shares_ref[(owner >> 2) & 7]
    for p in range(16):
        items_ref[p, SLOTS * 64 : STRIDE, :] = share

    @pl.loop(0, 16)
    def _(p):
        for k in range(SLOTS):
            item = wanted_ref[p, k]
            at = pl.multiple_of((item & 1) * 64, 64)
            items_ref[p, 64 * k : 64 * k + 64, :] = kv_ref[item >> 1, pl.ds(at, 64), :]
        pltpu.make_async_copy(items_ref.at[p], out_ref.at[p], sems.at[p]).start()

    @pl.loop(0, 16)
    def _(p):
        pltpu.make_async_copy(items_ref.at[p], out_ref.at[p], sems.at[p]).wait()


def column(pieces, wkv, received, shares, first, second, ids, here):
    shape = jax.ShapeDtypeStruct
    return call(
        column_kernel,
        (shape((16 * HEADS, 128, 128), BF16), shape((16, STRIDE, 128), BF16)),
        [pltpu.VMEM((16, 128), jnp.int32), pltpu.SemaphoreType.DMA((3,)), pltpu.SemaphoreType.DMA((16,))],
        (1_000_000_000, 10_000_000, 0),
        [*pieces, wkv, received, shares],
        raw=[first, second],
        scalars=[ids, here],
        by_hand=(1,),
        tables=(shape((16, 128), jnp.int32), shape((1, 1), jnp.int32)),
    )


def extra_kernel(kv_ref, wanted_ref, items_ref):
    @pl.loop(0, 16)
    def _(p):
        for k in range(MORE):
            item = wanted_ref[p, SLOTS + k]
            at = pl.multiple_of((item & 1) * 64, 64)
            items_ref[p, 64 * k : 64 * k + 64, :] = kv_ref[item >> 1, pl.ds(at, 64), :]


def extra(kv, wanted):
    shape = jax.ShapeDtypeStruct((16, MORE * 64, 128), BF16)
    items = call(extra_kernel, shape, [], (0, 5_000_000, 0), [kv], scalars=[wanted])
    return exchanged(items, PLANE)


def unused_kernel(out_ref, row_ref):
    row_ref[...] = jnp.zeros_like(row_ref)
    pltpu.sync_copy(row_ref, out_ref.at[0, pl.ds(0, 16), :])


def unused():
    return pl.pallas_call(
        unused_kernel,
        out_shape=jax.ShapeDtypeStruct((16, MORE * 64, 128), BF16),
        out_specs=FAR,
        scratch_shapes=[pltpu.VMEM((16, 128), BF16)],
        compiler_params=pltpu.CompilerParams(vmem_limit_bytes=LIMIT),
    )()


def window_kernel(kv_ref, before_ref, after_ref, wkv_ref, ext_ref, rows_ref):
    rows_ref[0:64, :] = before_ref[...]
    rows_ref[64:128, :] = after_ref[...]
    pair = nn(rows_ref[...], wkv_ref[...]).astype(BF16)
    for h in range(HEADS):
        ext_ref[h, 0:64, :] = pair[0:64, 128 * h : 128 * h + 128]
        ext_ref[h, 64:320, :] = kv_ref[h]
        ext_ref[h, 320:384, :] = pair[64:128, 128 * h : 128 * h + 128]


def window(kv, before, after, wkv):
    return call(
        window_kernel,
        jax.ShapeDtypeStruct((HEADS, 384, 128), BF16),
        [pltpu.VMEM((128, 768), BF16)],
        (150_000_000, 3_000_000, 0),
        [kv, before, after, wkv],
    )


def partial_kernel(wq_ref, wkv_ref, remote_ref, kv_far, out_ref, pair_ref, share_ref, rows_ref, q_ref, s_ref, kv_ref, sem):
    copies = [pltpu.make_async_copy(remote_ref.at[p, pl.ds(SLOTS * 64, 48), :], share_ref.at[p], sem.at[p]) for p in range(16)]
    keep = pltpu.make_async_copy(kv_far, kv_ref, sem.at[16])
    for copy in copies:
        copy.start()
    keep.start()
    for p, copy in enumerate(copies):
        copy.wait()
        for c in range(3):
            lanes = (p % 2) * 384 + c * 128
            rows_ref[p // 2 * 16 : p // 2 * 16 + 16, lanes : lanes + 128] = share_ref[p, 16 * c : 16 * c + 16, :]
    query = nn(rows_ref[...], wq_ref[...]).astype(BF16)
    pair = nn(rows_ref[...], wkv_ref[...]).astype(BF16)
    for h in range(HEADS):
        q_ref[h] = query[:, 128 * h : 128 * h + 128]
        pair_ref[h] = pair[:, 128 * h : 128 * h + 128]
    keep.wait()
    lane = lax.broadcasted_iota(jnp.int32, (128, 128), 1)
    highs = jnp.zeros((128, 128), F32)
    totals = jnp.zeros((128, 128), F32)
    for h in range(HEADS):
        keys = [kv_ref[4 * c : 4 * c + 4, h].reshape(512, 128) for c in range(4)]
        high = jnp.full((128, 1), NEGATIVE, F32)
        for c in range(4):
            s = nt(q_ref[h], keys[c])
            s_ref[h % 2, :, c * 512 : c * 512 + 512] = s
            high = jnp.maximum(high, jnp.max(s, axis=1, keepdims=True))
        total = jnp.zeros((128, 1), F32)
        acc = jnp.zeros((128, 128), F32)
        for c in range(4):
            p = jnp.exp(s_ref[h % 2, :, c * 512 : c * 512 + 512] - high)
            total = total + jnp.sum(p, axis=1, keepdims=True)
            head = p.astype(BF16)
            rest = (p - head.astype(F32)).astype(BF16)
            acc = acc + nn(head, keys[c]) + nn(rest, keys[c])
        out_ref[:, 64 * h : 64 * h + 64] = acc[:, 64:128]
        highs = jnp.where(lane == h, high, highs)
        totals = jnp.where(lane == h, total, totals)
    out_ref[:, 384:512] = highs
    out_ref[:, 512:640] = totals


def partial(wq, wkv, remote, kv):
    shape = jax.ShapeDtypeStruct
    return call(
        partial_kernel,
        (shape((128, 640), F32), shape((HEADS, 128, 128), BF16)),
        [
            pltpu.VMEM((16, 48, 128), BF16),
            pltpu.VMEM((128, 768), BF16),
            pltpu.VMEM((HEADS, 128, 128), BF16),
            pltpu.VMEM((2, 128, 2048), F32),
            pltpu.VMEM((16, HEADS, 128, 128), BF16),
            pltpu.SemaphoreType.DMA((17,)),
        ],
        (2_000_000_000, 10_000_000, 1_600_000),
        [wq, wkv],
        raw=[remote, kv],
    )


def merge_kernel(parts_ref, out_ref):
    highs = parts_ref[:, :, 384:512]
    factor = jnp.exp(highs - jnp.max(highs, axis=0, keepdims=True))
    total = jnp.sum(factor * parts_ref[:, :, 512:640], axis=0)
    outs = []
    for h in range(HEADS):
        acc = jnp.sum(parts_ref[:, :, 64 * h : 64 * h + 64] * factor[:, :, h : h + 1], axis=0)
        outs.append(acc / total[:, h : h + 1])
    rows = jnp.concatenate(outs, axis=1).astype(BF16)
    for p in range(32):
        out_ref[p] = rows


def merge(parts):
    return call(
        merge_kernel,
        jax.ShapeDtypeStruct((32, 8, 384), BF16),
        [],
        (2_000_000, 600_000, 10_000),
        [parts],
    )


def attend_kernel(
    q_ref, ext_ref, pair_ref, remote_ref, more_ref, slot_ref, here_ref, flag_ref, out_ref, pool_ref, keys_ref, sem
):
    main = pltpu.make_async_copy(remote_ref, pool_ref.at[pl.ds(0, 16 * STRIDE), :], sem.at[0])
    main.start()

    @pl.when(flag_ref[0, 0] > 0)
    def _():
        pltpu.sync_copy(more_ref, pool_ref.at[pl.ds(16 * STRIDE, 16 * MORE * 64), :])

    main.wait()
    seq = (here_ref[0, 0] * 8 + here_ref[0, 1]) * 4 + here_ref[0, 2]
    lane = lax.broadcasted_iota(jnp.int32, (64, 512), 1)

    @pl.loop(0, HEADS // 2)
    def _(pair):
        for b in range(4):
            outs = []
            for k in range(2):
                h = pair * 2 + k
                buf = keys_ref.at[b * 2 + k]
                buf[0:192, :] = ext_ref[h, b * 64 : b * 64 + 192, :]
                for r in range(3):
                    at = pl.multiple_of(slot_ref[0, (b * HEADS + h) * 3 + r], 16)
                    buf[192 + 64 * r : 256 + 64 * r, :] = pool_ref[pl.ds(at, 64), :]
                buf[384:512, :] = pair_ref[h]
                keys = buf[...]
                s = nt(q_ref[h, b * 64 : b * 64 + 64, :], keys)
                if b == 0:
                    s = jnp.where((lane < 64) & (seq == 0), NEGATIVE, s)
                if b == 3:
                    s = jnp.where((lane >= 128) & (lane < 192) & (seq == 127), NEGATIVE, s)
                p = jnp.exp(s - jnp.max(s, axis=1, keepdims=True))
                w = (p * (1.0 / jnp.sum(p, axis=1, keepdims=True))).astype(BF16)
                outs.append(nn(w, keys)[:, 64:128])
            lanes = pl.ds(pl.multiple_of(pair * 128, 128), 128)
            out_ref[b * 64 : b * 64 + 64, lanes] = jnp.concatenate(outs, axis=1).astype(BF16)


def attend(q, ext, pair, remote, more, slots, here, flag):
    return call(
        attend_kernel,
        jax.ShapeDtypeStruct((256, 384), BF16),
        [
            pltpu.VMEM((16 * STRIDE + 16 * MORE * 64, 128), BF16),
            pltpu.VMEM((8, 512, 128), BF16),
            pltpu.SemaphoreType.DMA((1,)),
        ],
        (600_000_000, 7_000_000, 800_000),
        [q, ext, pair],
        raw=[remote, more],
        scalars=[slots, here, flag],
    )


def norm(v, gain):
    shifted = v - jnp.mean(v, axis=1, keepdims=True)
    spread = jnp.mean(shifted * shifted, axis=1, keepdims=True)
    return shifted * lax.rsqrt(spread + EPSILON) * gain


CHUNK = 512


def finish_kernel(
    own_ref,
    other_ref,
    states_ref,
    wo_own,
    wo_other,
    gain_ref,
    gain2_ref,
    rows_ref,
    up_own,
    up_other,
    down_own,
    down_other,
    ids_ref,
    here_ref,
    out_ref,
    attended,
    states,
    wo,
    gains,
    rows,
    up,
    down,
    sums,
    result,
    sem,
    sems,
):
    copies = [
        pltpu.make_async_copy(source, target, sem.at[i])
        for i, (source, target) in enumerate(
            [
                (own_ref, attended.at[0]),
                (other_ref, attended.at[1]),
                (rows_ref, rows),
                (wo_own, wo.at[0]),
                (wo_other, wo.at[1]),
                (states_ref, states),
                (gain_ref, gains.at[0]),
                (gain2_ref, gains.at[1]),
            ]
        )
    ]
    chunks = []
    for half, (above, below) in enumerate(((up_own, down_own), (up_other, down_other))):
        for i in range(0, 1536, CHUNK):
            number = len(chunks)
            part = pl.ds(i, CHUNK)
            chunks.append(
                (
                    pltpu.make_async_copy(above.at[:, part], up.at[number], sems.at[2 * number]),
                    pltpu.make_async_copy(below.at[part, :], down.at[number], sems.at[2 * number + 1]),
                )
            )
    for copy in copies:
        copy.start()
    for chunk in chunks:
        chunk[0].start()
        chunk[1].start()
    for copy in copies:
        copy.wait()
    core = here_ref[0, 3]
    seq = (here_ref[0, 0] * 8 + here_ref[0, 1]) * 4 + here_ref[0, 2]
    for g in range(2):

        @pl.when((ids_ref[0, g] >> 2) == seq)
        def _():
            for k, side in ((0, core), (1, 1 - core)):
                for i in range(4):
                    first = (g * 8 + 2 * i) * 2 + side
                    at = pl.multiple_of((ids_ref[0, g] & 3) * 64 + 16 * i, 16)
                    attended[k, pl.ds(at, 16), :] = jnp.concatenate([rows[first], rows[first + 2]], axis=0)

    projected = nn(attended[0], wo[0]) + nn(attended[1], wo[1])
    normed = norm(states[...].astype(F32) + projected, gains[0]).astype(BF16)
    for number, chunk in enumerate(chunks):
        chunk[0].wait()
        v = nn(normed, up[number])
        hidden = (v * (1.0 + lax.erf(v * 0.7071067811865476)) * 0.5).astype(BF16)
        chunk[1].wait()
        piece = nn(hidden, down[number])
        half = number // (1536 // CHUNK)
        if number % (1536 // CHUNK) == 0:
            sums[half] = piece
        else:
            sums[half] += piece
    result[...] = norm(normed.astype(F32) + (sums[0] + sums[1]), gains[1]).astype(BF16)
    pltpu.sync_copy(result, out_ref)


def finish(own, other, states, wo_own, wo_other, gain, gain2, rows, up_own, up_other, down_own, down_other, ids, here):
    count = 2 * 1536 // CHUNK
    return pl.pallas_call(
        finish_kernel,
        out_shape=jax.ShapeDtypeStruct((256, 768), BF16),
        in_specs=[FAR] * 12 + [SMEM] * 2,
        out_specs=FAR,
        scratch_shapes=[
            pltpu.VMEM((2, 256, 384), BF16),
            pltpu.VMEM((256, 768), BF16),
            pltpu.VMEM((2, 384, 768), BF16),
            pltpu.VMEM((2, 1, 768), F32),
            pltpu.VMEM((32, 8, 384), BF16),
            pltpu.VMEM((count, 768, CHUNK), BF16),
            pltpu.VMEM((count, CHUNK, 768), BF16),
            pltpu.VMEM((2, 256, 768), F32),
            pltpu.VMEM((256, 768), BF16),
            pltpu.SemaphoreType.DMA((8,)),
            pltpu.SemaphoreType.DMA((2 * count,)),
        ],
        cost_estimate=pl.CostEstimate(flops=2_700_000_000, bytes_accessed=12_000_000, transcendentals=800_000),
        compiler_params=pltpu.CompilerParams(vmem_limit_bytes=LIMIT),
    )(own, other, states, wo_own, wo_other, gain, gain2, rows, up_own, up_other, down_own, down_other, ids, here)


def turned(value, axis, shift):
    count = lax.axis_size(axis)
    return lax.ppermute(value, axis, [(i, (i + shift) % count) for i in range(count)])


def exchanged(value, axes):
    return lax.all_to_all(value, axes, split_axis=0, concat_axis=0, tiled=True)


def swapped(value):
    return lax.ppermute(value, "mp", [(0, 1), (1, 0)])


def shards(
    states, qkv_weight, out_weight, up_weight, down_weight, attn_gain, mlp_gain, global_ids, random_owner, random_local
):
    x, z, y, core = (lax.axis_index(axis) for axis in ("x", "z", "y", "mp"))
    here = jnp.stack([x, z, y, core]).astype(jnp.int32).reshape(1, 4)
    ids = global_ids.reshape(1, 2)
    tied = lax.optimization_barrier

    up0 = lax.dynamic_slice_in_dim(states, core * 128, 128, 0)
    up1, down1, far0 = turned(up0, "z", 1), turned(up0, "z", -1), swapped(up0)
    wq, wkv, q, kv, spread, slots = prepare(states, qkv_weight, random_owner, random_local, ids, here)
    up1, down1, far0, wkv, spread = tied((up1, down1, far0, wkv, spread))

    up2, down2 = turned(up1, "z", 1), turned(down1, "z", -1)
    far1, far7 = swapped(up1), swapped(down1)
    received = exchanged(spread, PLANE)
    up2, down2, far1, far7 = tied((up2, down2, far1, far7))

    up3, down3 = turned(up2, "z", 1), turned(down2, "z", -1)
    far2, far6 = swapped(up2), swapped(down2)
    first = early([up0, up1, down1, far0, far1, far7], wkv)
    up3, down3, far2, far6, first, received = tied((up3, down3, far2, far6, first, received))

    root_owner = pick(x >= 2, global_ids[1], global_ids[0]) >> 2
    root = (root_owner >> 5) * 4 + (root_owner & 3)
    share = lax.dynamic_slice(received, (root, 0, 0), (1, 48, 128))
    shares = exchanged(jnp.broadcast_to(share, (8, 48, 128)), "z")
    up4 = turned(up3, "z", 1)
    far3, far5 = swapped(up3), swapped(down3)
    second = early([up2, down2, far2, far6], wkv)
    ends = [(i, i + 1) for i in range(127)]
    before = lax.ppermute(states[192:], SEQ, ends)
    after = lax.ppermute(states[:64], SEQ, [(j, i) for i, j in ends])
    up4, far3, far5, second, shares, before, after = tied((up4, far3, far5, second, shares, before, after))

    pieces = [up3, up4, down3, far3, swapped(up4), far5]
    pairs, items, wanted, flag = column(pieces, wkv, received, shares, first, second, ids, here)
    more = lax.cond(flag[0, 0] > 0, lambda: extra(pairs, wanted), unused)
    items, more, weights = tied((items, more, (out_weight, up_weight, down_weight)))
    remote = exchanged(items, PLANE)
    wo_other, up_other, down_other = (swapped(weight) for weight in weights)
    ext = window(kv, before, after, wkv)
    remote, ext = tied((remote, ext))
    part, pair = partial(wq, wkv, remote, pairs.reshape(16, HEADS, 128, 128))
    rows = exchanged(merge(exchanged(part.reshape(16, 8, 640), PLANE)), PLANE + ("mp",))
    attended = attend(
        q, ext, pair, remote.reshape(16 * STRIDE, 128), more.reshape(16 * MORE * 64, 128), slots, here, flag
    )
    return finish(
        attended,
        swapped(attended),
        states,
        out_weight,
        wo_other,
        attn_gain.reshape(1, -1),
        mlp_gain.reshape(1, -1),
        rows,
        up_weight,
        up_other,
        down_weight,
        down_other,
        ids,
        here,
    )


def solution(mesh):
    split = Mesh(mesh.devices.reshape(4, 8, 4, mesh.shape["mp"]), ("x", "z", "y", "mp"))
    placed = (
        P(SEQ, None),
        P(None, None, "mp"),
        P("mp", None),
        P(None, "mp"),
        P("mp", None),
        P(),
        P(),
        P(),
        P("mp", SEQ, None, None),
        P("mp", SEQ, None, None),
    )
    return jax.shard_map(shards, mesh=split, in_specs=placed, out_specs=P(SEQ, None), check_vma=False)
```

time: 222 us -> 181 us (0.82)
  waiting for transfers between devices: 77.8 us -> 41.8 us
  other arithmetic: 10.5 us -> 0.64 us
  starting transfers between devices: 57.3 us -> 63.2 us
  local copies, waits for them, and re-layouts: 15.2 us -> 11.1 us
  Pallas kernels: 57.3 us -> 60.4 us
    all_to_all x4 -> x5, waiting for transfers between devices: 66.7 us -> 39.9 us  [exchanged(): return lax.all_to_all(value, axes, split_axis=0, concat_axis=0, tiled=True)]
    ppermute x7, waiting for transfers between devices: 9.44 us -> 0.02 us  [turned(): lax.ppermute(value, axis, [(i, (i + shift) % count) for i in range(count)])]
    all_to_all x4 -> x5, starting transfers between devices: 28 us -> 36.9 us  [exchanged(): return lax.all_to_all(value, axes, split_axis=0, concat_axis=0, tiled=True)]
    unnamed x58 -> x62, local copies, waits for them, and re-layouts: 2.33 us -> 7.75 us
    ppermute x12, starting transfers between devices: 13.8 us -> 9.04 us  [swapped(): return lax.ppermute(value, 'mp', [(0, 1), (1, 0)])]
    pallas_call x7 -> x9, Pallas kernels: 46.1 us -> 49.2 us  [the longest x8 49.2 us: call(): pl.pallas_call(body, out_shape=(*results, *tables), in_specs=[FAR] * (cou...]
    add x4 -> x0, local copies, waits for them, and re-layouts: 2.96 us -> none  [the longest x2 1.48 us: piece_of(): return jnp.where((away >= 3) & (away <= 5), 10 + far * 3 + away - 3, soon)]
    and x4 -> x0, local copies, waits for them, and re-layouts: 2.8 us -> none  [the longest x2 1.41 us: piece_of(): away = here['z'] - (block_owner >> 2 & 7) & 7]
  transfers between devices with their start and end apart: 25 -> 26, of which waited for: 8 -> 4; matrix products, arithmetic and copies ran while one was open for 10% -> 3% of each run, Pallas kernels for 13% -> 23%
where the time goes in v4:
time: 181 us; the launch traced here: 180 us
  starting transfers between devices  63.2 us (35%)
  Pallas kernels  60.4 us (33%)
  waiting for transfers between devices  41.8 us (23%)
  local copies, waits for them, and re-layouts  11.1 us (6%)
  between operations  2.6 us (1%)
    pallas_call x8, Pallas kernels, call(): pl.pallas_call(body, out_shape=(*results, *tables), in_specs=[FAR] * (cou...  49.2 us
    all_to_all x5, waiting for transfers between devices, exchanged(): return lax.all_to_all(value, axes, split_axis=0, concat_axis=0, tiled=True)  39.9 us
    all_to_all x5, starting transfers between devices, exchanged(): return lax.all_to_all(value, axes, split_axis=0, concat_axis=0, tiled=True)  36.9 us
    ppermute x7, starting transfers between devices, turned(): lax.ppermute(value, axis, [(i, (i + shift) % count) for i in range(count)])  12.3 us
    pallas_call x1, Pallas kernels, finish(): pl.pallas_call(finish_kernel, out_shape=jax.ShapeDtypeStruct((256, 768),...  11.2 us
    ppermute x12, starting transfers between devices, swapped(): return lax.ppermute(value, 'mp', [(0, 1), (1, 0)])  9.04 us
    unnamed x62, local copies, waits for them, and re-layouts  7.75 us
  transfers between devices with their start and end apart: 26, of which 4 were waited for; matrix products, arithmetic and copies ran while one was open for 3% of the time, Pallas kernels for 23%

profile of v4, /device:TPU:1, one launch (start us, length us, event | category | flops | bytes accessed | tf_op | source)
XLA Modules:
  0.0 179.7 jit_solution(15943975385886972009)
XLA Ops:
  1.0 2.5 %collective-permute-start = (bf16[128,768]{1,0:T(8,128)(2,1)S(1)}, bf16[128,768]{1,0:T(8,128)(2,1)S(1)}, u32[]{:S(2)}, u32[]{:S(2)}) collective-permute-start(bf16[128,768]{1,0:T(8,128)(2,1)S(1)} %constant_dynamic-slice_fusion.refs_0_), channel_id=1, source_target_pairs={{0,8},{8,16},{16,24},{24,32},{32,40},{40,48},{48,56},{56,0},{1,9},... | collective-permute-start | bytes 589832 | tf_op jit(solution)/shard_map/ppermute | solution.py:553
  3.5 4.0 %collective-permute-start.1 = (bf16[128,768]{1,0:T(8,128)(2,1)S(1)}, bf16[128,768]{1,0:T(8,128)(2,1)S(1)}, u32[]{:S(2)}, u32[]{:S(2)}) collective-permute-start(bf16[128,768]{1,0:T(8,128)(2,1)S(1)} %constant_dynamic-slice_fusion.refs_0_), channel_id=1, source_target_pairs={{0,56},{8,0},{16,8},{24,16},{32,24},{40,32},{48,40},{56,48},{1,57}... | collective-permute-start | bytes 589832 | tf_op jit(solution)/shard_map/ppermute | solution.py:553
  11.9 6.6 %shard_map.100 = (bf16[768,768]{1,0:T(8,128)(2,1)}, bf16[768,768]{1,0:T(8,128)(2,1)}, bf16[6,256,128]{2,1,0:T(8,128)(2,1)}, bf16[6,256,128]{2,1,0:T(8,128)(2,1)}...) custom-call(bf16[256,768]{1,0:T(8,128)(2,1)} %states_ref.1, bf16[3,768,384]{2,1,0:T(8,128)(2,1)} %refs_1_.1, ...), custom_call_target="tpu_custom_call" | custom-call | flops 600000000 | bytes 6000000 | tf_op jit(solution)/shard_map/pallas_call | solution.py:62
  18.7 2.7 %collective-permute-start.4 = (bf16[128,768]{1,0:T(8,128)(2,1)S(1)}, bf16[128,768]{1,0:T(8,128)(2,1)S(1)}, u32[]{:S(2)}, u32[]{:S(2)}) collective-permute-start(bf16[128,768]{1,0:T(8,128)(2,1)S(1)} %collective-permute-done.1.refs_2_), channel_id=1, source_target_pairs={{0,56},{8,0},{16,8},{24,16},{32,24},{40,32},{48,40},{56,48},{1,57}... | collective-permute-start | bytes 589832 | tf_op jit(solution)/shard_map/ppermute | solution.py:553
  21.9 6.8 %all-to-all-start.1 = ((bf16[16,64,128]{2,1,0:T(8,128)(2,1)}), bf16[16,64,128]{2,1,0:T(8,128)(2,1)S(1)}, u32[]{:S(2)}, u32[]{:S(2)}) async-start(bf16[16,64,128]{2,1,0:T(8,128)(2,1)} %get-tuple-element.66), calls=%async_computation.1 | async-start | bytes 524288 | tf_op jit(solution)/shard_map/all_to_all | solution.py:557
  29.7 2.9 %collective-permute-start.8 = (bf16[128,768]{1,0:T(8,128)(2,1)S(1)}, bf16[128,768]{1,0:T(8,128)(2,1)S(1)}, u32[]{:S(2)}, u32[]{:S(2)}) collective-permute-start(bf16[128,768]{1,0:T(8,128)(2,1)S(1)} %collective-permute-done.4.refs_1_), channel_id=1, source_target_pairs={{0,56},{8,0},{16,8},{24,16},{32,24},{40,32},{48,40},{56,48},{1,57}... | collective-permute-start | bytes 589832 | tf_op jit(solution)/shard_map/ppermute | solution.py:553
  34.7 4.0 %shard_map.101.refs_9_ = bf16[36,128,128]{2,1,0:T(8,128)(2,1)} custom-call(bf16[128,768]{1,0:T(8,128)(2,1)} %copy-done.5, bf16[128,768]{1,0:T(8,128)(2,1)} %copy-done.15, bf16[128,768]{1,0:T(8,128)(2,1)} %copy-done.16, bf16[128,768]{1,0:T(8,128)(2,1)} %copy-done.17, bf16[128,768]{1,0:T(8,128)(2,1)} %copy-done.18, bf16[128,768]{1,0:T(8,128)(2,1)} %copy-done.19, ...), custom_call_target="tpu_custom_call" | custom-call | flops 900000000 | bytes 3000000 | tf_op jit(solution)/shard_map/pallas_call | solution.py:62
  40.3 5.5 %all-to-all-start.2 = ((bf16[8,48,128]{2,1,0:T(8,128)(2,1)}), bf16[8,48,128]{2,1,0:T(8,128)(2,1)S(1)}, u32[]{:S(2)}, u32[]{:S(2)}) async-start(bf16[8,48,128]{2,1,0:T(8,128)(2,1)} %broadcast_in_dim.8), calls=%async_computation.2 | async-start | bytes 196608 | tf_op jit(solution)/shard_map/all_to_all | solution.py:557
  45.8 3.5 %collective-permute-start.14 = (bf16[64,768]{1,0:T(8,128)(2,1)S(1)}, bf16[64,768]{1,0:T(8,128)(2,1)S(1)}, u32[]{:S(2)}, u32[]{:S(2)}) collective-permute-start(bf16[64,768]{1,0:T(8,128)(2,1)S(1)} %get-tuple-element.97), channel_id=1, source_target_pairs={{0,2},{2,4},{4,6},{6,8},{8,10},{10,12},{12,14},{14,16},{16,18},{18... | collective-permute-start | bytes 294920 | tf_op jit(solution)/shard_map/ppermute | solution.py:595
  50.7 3.4 %shard_map.102.refs_10_ = bf16[24,128,128]{2,1,0:T(8,128)(2,1)} custom-call(bf16[128,768]{1,0:T(8,128)(2,1)} %copy-done.20, bf16[128,768]{1,0:T(8,128)(2,1)} %copy-done.21, bf16[128,768]{1,0:T(8,128)(2,1)} %copy-done.22, bf16[128,768]{1,0:T(8,128)(2,1)} %copy-done.23, bf16[768,768]{1,0:T(8,128)(2,1)} %get-tuple-element.65.refs_6_.refs_4_.refs_3_.refs_1_), custom_call_target="tpu_custom_call" | custom-call | flops 600000000 | bytes 2000000 | tf_op jit(solution)/shard_map/pallas_call | solution.py:62
  55.0 2.1 %collective-permute-start.16 = (bf16[128,768]{1,0:T(8,128)(2,1)S(1)}, bf16[128,768]{1,0:T(8,128)(2,1)S(1)}, u32[]{:S(2)}, u32[]{:S(2)}) collective-permute-start(bf16[128,768]{1,0:T(8,128)(2,1)S(1)} %collective-permute-done.11.refs_1_), channel_id=1, source_target_pairs={{0,1},{1,0},{2,3},{3,2},{4,5},{5,4},{6,7},{7,6},{8,9},{9,8},{10,11... | collective-permute-start | bytes 589832 | tf_op jit(solution)/shard_map/ppermute | solution.py:561
  58.9 8.4 %shard_map.103 = (bf16[96,128,128]{2,1,0:T(8,128)(2,1)}, bf16[16,688,128]{2,1,0:T(8,128)(2,1)}, s32[16,128]{1,0:T(8,128)S(1)}, s32[1,1]{1,0:T(1,128)}) custom-call(bf16[128,768]{1,0:T(8,128)(2,1)} %copy-done.9, bf16[128,768]{1,0:T(8,128)(2,1)} %copy-done.11, bf16[128,768]{1,0:T(8,128)(2,1)} %copy-done.10, bf16[128,768]{1,0:T(8,128)(2,1)} %copy-done.12, ...), custom_call_target="tpu_custom_call" | custom-call | flops 1000000000 | bytes 10000000 | tf_op jit(solution)/shard_map/pallas_call | solution.py:62
  69.1 8.8 %all-to-all-start.3 = ((bf16[16,688,128]{2,1,0:T(8,128)(2,1)}), bf16[16,688,128]{2,1,0:T(8,128)(2,1)S(1)}, u32[]{:S(2)}, u32[]{:S(2)}) async-start(bf16[16,688,128]{2,1,0:T(8,128)(2,1)} %get-tuple-element.82), calls=%async_computation.3 | async-start | bytes 5636096 | tf_op jit(solution)/shard_map/all_to_all | solution.py:557
  78.8 2.7 %shard_map.104.refs_1_ = bf16[6,384,128]{2,1,0:T(8,128)(2,1)} custom-call(bf16[6,256,128]{2,1,0:T(8,128)(2,1)} %get-tuple-element.83.refs_0_, bf16[64,768]{1,0:T(8,128)(2,1)} %copy-done.25, bf16[64,768]{1,0:T(8,128)(2,1)} %copy-done.26, bf16[768,768]{1,0:T(8,128)(2,1)} %get-tuple-element.65.refs_6_.refs_4_.refs_3_.refs_1_), custom_call_target="tpu_custom_call" | custom-call | flops 150000000 | bytes 3000000 | tf_op jit(solution)/shard_map/pallas_call | solution.py:62
  82.0 32.8 %all-to-all-done.3.refs_2_ = bf16[16,688,128]{2,1,0:T(8,128)(2,1)S(1)} async-done(((bf16[16,688,128]{2,1,0:T(8,128)(2,1)}), bf16[16,688,128]{2,1,0:T(8,128)(2,1)S(1)}, u32[]{:S(2)}, u32[]{:S(2)}) %all-to-all-start.3) | async-done | bytes 2818080 | tf_op jit(solution)/shard_map/all_to_all | solution.py:557
  114.8 1.6 copy-done
  116.4 8.7 %shard_map.105 = (f32[128,640]{1,0:T(8,128)}, bf16[6,128,128]{2,1,0:T(8,128)(2,1)}) custom-call(bf16[768,768]{1,0:T(8,128)(2,1)} %get-tuple-element.87.refs_0_, bf16[768,768]{1,0:T(8,128)(2,1)} %get-tuple-element.65.refs_6_.refs_4_.refs_3_.refs_1_, bf16[16,688,128]{2,1,0:T(8,128)(2,1)} %copy-done, bf16[16,6,128,128]{3,2,1,0:T(8,128)(2,1)} %bitcast.10.refs_3_), custom_call_target="tpu_custom_call" | custom-call | flops 2000000000 | bytes 10000000 | tf_op jit(solution)/shard_map/pallas_call | solution.py:62
  125.2 8.5 %all-to-all-start.4 = ((f32[16,8,640]{2,1,0:T(8,128)}), f32[16,8,640]{2,1,0:T(8,128)S(1)}, u32[]{:S(2)}, u32[]{:S(2)}) async-start(f32[16,8,640]{2,1,0:T(8,128)} %bitcast.18), calls=%async_computation.4 | async-start | bytes 655360 | tf_op jit(solution)/shard_map/all_to_all | solution.py:557
  133.7 13.5 %shard_map.106.own_ref = bf16[256,384]{1,0:T(8,128)(2,1)} custom-call(bf16[6,256,128]{2,1,0:T(8,128)(2,1)} %get-tuple-element.55.refs_0_, bf16[6,384,128]{2,1,0:T(8,128)(2,1)} %shard_map.104.refs_1_, bf16[6,128,128]{2,1,0:T(8,128)(2,1)} %get-tuple-element.89.refs_2_, bf16[11008,128]{1,0:T(8,128)(2,1)} %bitcast.16, bf16[6144,128]{1,0:T(8,128)(2,1)} %bitcast.17, ...), custom_call_target="tpu_custom_call" | custom-call | flops 600000000 | bytes 7000000 | tf_op jit(solution)/shard_map/pallas_call | solution.py:62
  147.2 2.1 %collective-permute-start.17 = (bf16[256,384]{1,0:T(8,128)(2,1)}, bf16[256,384]{1,0:T(8,128)(2,1)S(1)}, u32[]{:S(2)}, u32[]{:S(2)}) collective-permute-start(bf16[256,384]{1,0:T(8,128)(2,1)} %shard_map.106.own_ref), channel_id=1, source_target_pairs={{0,1},{1,0},{2,3},{3,2},{4,5},{5,4},{6,7},{7,6},{8,9},{9,8},{10,11... | collective-permute-start | bytes 589832 | tf_op jit(solution)/shard_map/ppermute | solution.py:561
  150.1 1.9 %shard_map.107 = bf16[32,8,384]{2,1,0:T(8,128)(2,1)} custom-call(f32[16,8,640]{2,1,0:T(8,128)} %copy-done.3), custom_call_target="tpu_custom_call" | custom-call | flops 2000000 | bytes 600000 | tf_op jit(solution)/shard_map/pallas_call | solution.py:62
  151.9 7.4 %all-to-all-start.5 = ((bf16[32,8,384]{2,1,0:T(8,128)(2,1)}), bf16[32,8,384]{2,1,0:T(8,128)(2,1)S(1)}, u32[]{:S(2)}, u32[]{:S(2)}) async-start(bf16[32,8,384]{2,1,0:T(8,128)(2,1)} %shard_map.107), calls=%async_computation.5 | async-start | bytes 393216 | tf_op jit(solution)/shard_map/all_to_all | solution.py:557
  160.6 7.1 %all-to-all-done.5.rows_ref = bf16[32,8,384]{2,1,0:T(8,128)(2,1)S(1)} async-done(((bf16[32,8,384]{2,1,0:T(8,128)(2,1)}), bf16[32,8,384]{2,1,0:T(8,128)(2,1)S(1)}, u32[]{:S(2)}, u32[]{:S(2)}) %all-to-all-start.5) | async-done | bytes 196640 | tf_op jit(solution)/shard_map/all_to_all | solution.py:557
  168.3 11.2 %shard_map.108 = bf16[256,768]{1,0:T(8,128)(2,1)} custom-call(bf16[256,384]{1,0:T(8,128)(2,1)} %shard_map.106.own_ref, bf16[256,384]{1,0:T(8,128)(2,1)} %copy-done.24, bf16[256,768]{1,0:T(8,128)(2,1)} %states_ref.1, bf16[384,768]{1,0:T(8,128)(2,1)} %wo_own.1, bf16[384,768]{1,0:T(8,128)(2,1)} %collective-permute-done.18.wo_other, f32[1,768]{1,0:T(1,128)} %reshape.33.gain_ref, ...), custom_call_target="tpu_custom_call" | custom-call | flops 2700000000 | bytes 12000000 | tf_op jit(solution)/shard_map/pallas_call | solution.py:528
  (109 shorter events, 18.4 us)
Async XLA Ops:
  1.0 17.5 %collective-permute-start = (bf16[128,768]{1,0:T(8,128)(2,1)S(1)}, bf16[128,768]{1,0:T(8,128)(2,1)S(1)}, u32[]{:S(2)}, u32[]{:S(2)}) collective-permute-start(bf16[128,768]{1,0:T(8,128)(2,1)S(1)} %constant_dynamic-slice_fusion.refs_0_), channel_id=1, source_target_pairs={{0,8},{8,16},{16,24},{24,32},{32,40},{40,48},{48,56},{56,0},{1,9},... | collective-permute-start | bytes 589832 | tf_op jit(solution)/shard_map/ppermute | solution.py:553
  3.5 15.0 %collective-permute-start.1 = (bf16[128,768]{1,0:T(8,128)(2,1)S(1)}, bf16[128,768]{1,0:T(8,128)(2,1)S(1)}, u32[]{:S(2)}, u32[]{:S(2)}) collective-permute-start(bf16[128,768]{1,0:T(8,128)(2,1)S(1)} %constant_dynamic-slice_fusion.refs_0_), channel_id=1, source_target_pairs={{0,56},{8,0},{16,8},{24,16},{32,24},{40,32},{48,40},{56,48},{1,57}... | collective-permute-start | bytes 589832 | tf_op jit(solution)/shard_map/ppermute | solution.py:553
  7.5 11.0 %collective-permute-start.2 = (bf16[128,768]{1,0:T(8,128)(2,1)S(1)}, bf16[128,768]{1,0:T(8,128)(2,1)S(1)}, u32[]{:S(2)}, u32[]{:S(2)}) collective-permute-start(bf16[128,768]{1,0:T(8,128)(2,1)S(1)} %constant_dynamic-slice_fusion.refs_0_), channel_id=1, source_target_pairs={{0,1},{1,0},{2,3},{3,2},{4,5},{5,4},{6,7},{7,6},{8,9},{9,8},{10,11... | collective-permute-start | bytes 589832 | tf_op jit(solution)/shard_map/ppermute | solution.py:561
  18.6 10.1 %collective-permute-start.3 = (bf16[128,768]{1,0:T(8,128)(2,1)S(1)}, bf16[128,768]{1,0:T(8,128)(2,1)S(1)}, u32[]{:S(2)}, u32[]{:S(2)}) collective-permute-start(bf16[128,768]{1,0:T(8,128)(2,1)S(1)} %collective-permute-done.refs_1_), channel_id=1, source_target_pairs={{0,8},{8,16},{16,24},{24,32},{32,40},{40,48},{48,56},{56,0},{1,9},... | collective-permute-start | bytes 589832 | tf_op jit(solution)/shard_map/ppermute | solution.py:553
  18.7 10.0 %collective-permute-start.4 = (bf16[128,768]{1,0:T(8,128)(2,1)S(1)}, bf16[128,768]{1,0:T(8,128)(2,1)S(1)}, u32[]{:S(2)}, u32[]{:S(2)}) collective-permute-start(bf16[128,768]{1,0:T(8,128)(2,1)S(1)} %collective-permute-done.1.refs_2_), channel_id=1, source_target_pairs={{0,56},{8,0},{16,8},{24,16},{32,24},{40,32},{48,40},{56,48},{1,57}... | collective-permute-start | bytes 589832 | tf_op jit(solution)/shard_map/ppermute | solution.py:553
  21.3 7.4 %collective-permute-start.5 = (bf16[128,768]{1,0:T(8,128)(2,1)S(1)}, bf16[128,768]{1,0:T(8,128)(2,1)S(1)}, u32[]{:S(2)}, u32[]{:S(2)}) collective-permute-start(bf16[128,768]{1,0:T(8,128)(2,1)S(1)} %collective-permute-done.refs_1_), channel_id=1, source_target_pairs={{0,1},{1,0},{2,3},{3,2},{4,5},{5,4},{6,7},{7,6},{8,9},{9,8},{10,11... | collective-permute-start | bytes 589832 | tf_op jit(solution)/shard_map/ppermute | solution.py:561
  21.9 6.8 %collective-permute-start.6 = (bf16[128,768]{1,0:T(8,128)(2,1)S(1)}, bf16[128,768]{1,0:T(8,128)(2,1)S(1)}, u32[]{:S(2)}, u32[]{:S(2)}) collective-permute-start(bf16[128,768]{1,0:T(8,128)(2,1)S(1)} %collective-permute-done.1.refs_2_), channel_id=1, source_target_pairs={{0,1},{1,0},{2,3},{3,2},{4,5},{5,4},{6,7},{7,6},{8,9},{9,8},{10,11... | collective-permute-start | bytes 589832 | tf_op jit(solution)/shard_map/ppermute | solution.py:561
  21.9 16.8 %all-to-all-start.1 = ((bf16[16,64,128]{2,1,0:T(8,128)(2,1)}), bf16[16,64,128]{2,1,0:T(8,128)(2,1)S(1)}, u32[]{:S(2)}, u32[]{:S(2)}) async-start(bf16[16,64,128]{2,1,0:T(8,128)(2,1)} %get-tuple-element.66), calls=%async_computation.1 | async-start | bytes 524288 | tf_op jit(solution)/shard_map/all_to_all | solution.py:557
  28.7 10.0 %collective-permute-start.7 = (bf16[128,768]{1,0:T(8,128)(2,1)S(1)}, bf16[128,768]{1,0:T(8,128)(2,1)S(1)}, u32[]{:S(2)}, u32[]{:S(2)}) collective-permute-start(bf16[128,768]{1,0:T(8,128)(2,1)S(1)} %collective-permute-done.3.refs_0_), channel_id=1, source_target_pairs={{0,8},{8,16},{16,24},{24,32},{32,40},{40,48},{48,56},{56,0},{1,9},... | collective-permute-start | bytes 589832 | tf_op jit(solution)/shard_map/ppermute | solution.py:553
  28.8 9.9 %collective-permute-start.9 = (bf16[128,768]{1,0:T(8,128)(2,1)S(1)}, bf16[128,768]{1,0:T(8,128)(2,1)S(1)}, u32[]{:S(2)}, u32[]{:S(2)}) collective-permute-start(bf16[128,768]{1,0:T(8,128)(2,1)S(1)} %collective-permute-done.3.refs_0_), channel_id=1, source_target_pairs={{0,1},{1,0},{2,3},{3,2},{4,5},{5,4},{6,7},{7,6},{8,9},{9,8},{10,11... | collective-permute-start | bytes 589832 | tf_op jit(solution)/shard_map/ppermute | solution.py:561
  29.7 9.0 %collective-permute-start.8 = (bf16[128,768]{1,0:T(8,128)(2,1)S(1)}, bf16[128,768]{1,0:T(8,128)(2,1)S(1)}, u32[]{:S(2)}, u32[]{:S(2)}) collective-permute-start(bf16[128,768]{1,0:T(8,128)(2,1)S(1)} %collective-permute-done.4.refs_1_), channel_id=1, source_target_pairs={{0,56},{8,0},{16,8},{24,16},{32,24},{40,32},{48,40},{56,48},{1,57}... | collective-permute-start | bytes 589832 | tf_op jit(solution)/shard_map/ppermute | solution.py:553
  32.6 6.2 %collective-permute-start.10 = (bf16[128,768]{1,0:T(8,128)(2,1)S(1)}, bf16[128,768]{1,0:T(8,128)(2,1)S(1)}, u32[]{:S(2)}, u32[]{:S(2)}) collective-permute-start(bf16[128,768]{1,0:T(8,128)(2,1)S(1)} %collective-permute-done.4.refs_1_), channel_id=1, source_target_pairs={{0,1},{1,0},{2,3},{3,2},{4,5},{5,4},{6,7},{7,6},{8,9},{9,8},{10,11... | collective-permute-start | bytes 589832 | tf_op jit(solution)/shard_map/ppermute | solution.py:561
  38.8 16.1 %collective-permute-start.11 = (bf16[128,768]{1,0:T(8,128)(2,1)S(1)}, bf16[128,768]{1,0:T(8,128)(2,1)S(1)}, u32[]{:S(2)}, u32[]{:S(2)}) collective-permute-start(bf16[128,768]{1,0:T(8,128)(2,1)S(1)} %collective-permute-done.7.refs_0_), channel_id=1, source_target_pairs={{0,8},{8,16},{16,24},{24,32},{32,40},{40,48},{48,56},{56,0},{1,9},... | collective-permute-start | bytes 589832 | tf_op jit(solution)/shard_map/ppermute | solution.py:553
  38.9 16.0 %collective-permute-start.12 = (bf16[128,768]{1,0:T(8,128)(2,1)S(1)}, bf16[128,768]{1,0:T(8,128)(2,1)S(1)}, u32[]{:S(2)}, u32[]{:S(2)}) collective-permute-start(bf16[128,768]{1,0:T(8,128)(2,1)S(1)} %collective-permute-done.7.refs_0_), channel_id=1, source_target_pairs={{0,1},{1,0},{2,3},{3,2},{4,5},{5,4},{6,7},{7,6},{8,9},{9,8},{10,11... | collective-permute-start | bytes 589832 | tf_op jit(solution)/shard_map/ppermute | solution.py:561
  39.4 15.6 %collective-permute-start.13 = (bf16[128,768]{1,0:T(8,128)(2,1)S(1)}, bf16[128,768]{1,0:T(8,128)(2,1)S(1)}, u32[]{:S(2)}, u32[]{:S(2)}) collective-permute-start(bf16[128,768]{1,0:T(8,128)(2,1)S(1)} %collective-permute-done.8.refs_2_), channel_id=1, source_target_pairs={{0,1},{1,0},{2,3},{3,2},{4,5},{5,4},{6,7},{7,6},{8,9},{9,8},{10,11... | collective-permute-start | bytes 589832 | tf_op jit(solution)/shard_map/ppermute | solution.py:561
  40.3 14.6 %all-to-all-start.2 = ((bf16[8,48,128]{2,1,0:T(8,128)(2,1)}), bf16[8,48,128]{2,1,0:T(8,128)(2,1)S(1)}, u32[]{:S(2)}, u32[]{:S(2)}) async-start(bf16[8,48,128]{2,1,0:T(8,128)(2,1)} %broadcast_in_dim.8), calls=%async_computation.2 | async-start | bytes 196608 | tf_op jit(solution)/shard_map/all_to_all | solution.py:557
  45.8 8.3 %collective-permute-start.14 = (bf16[64,768]{1,0:T(8,128)(2,1)S(1)}, bf16[64,768]{1,0:T(8,128)(2,1)S(1)}, u32[]{:S(2)}, u32[]{:S(2)}) collective-permute-start(bf16[64,768]{1,0:T(8,128)(2,1)S(1)} %get-tuple-element.97), channel_id=1, source_target_pairs={{0,2},{2,4},{4,6},{6,8},{8,10},{10,12},{12,14},{14,16},{16,18},{18... | collective-permute-start | bytes 294920 | tf_op jit(solution)/shard_map/ppermute | solution.py:595
  69.1 45.7 %all-to-all-start.3 = ((bf16[16,688,128]{2,1,0:T(8,128)(2,1)}), bf16[16,688,128]{2,1,0:T(8,128)(2,1)S(1)}, u32[]{:S(2)}, u32[]{:S(2)}) async-start(bf16[16,688,128]{2,1,0:T(8,128)(2,1)} %get-tuple-element.82), calls=%async_computation.3 | async-start | bytes 5636096 | tf_op jit(solution)/shard_map/all_to_all | solution.py:557
  78.0 82.6 %collective-permute-start.19 = (bf16[768,1536]{1,0:T(8,128)(2,1)}, bf16[768,1536]{1,0:T(8,128)(2,1)}, u32[]{:S(2)}, u32[]{:S(2)}) collective-permute-start(bf16[768,1536]{1,0:T(8,128)(2,1)} %up_own.1), channel_id=1, source_target_pairs={{0,1},{1,0},{2,3},{3,2},{4,5},{5,4},{6,7},{7,6},{8,9},{9,8},{10,11... | collective-permute-start | bytes 7077896 | tf_op jit(solution)/shard_map/ppermute | solution.py:561
  78.7 81.8 %collective-permute-start.20 = (bf16[1536,768]{1,0:T(8,128)(2,1)}, bf16[1536,768]{1,0:T(8,128)(2,1)}, u32[]{:S(2)}, u32[]{:S(2)}) collective-permute-start(bf16[1536,768]{1,0:T(8,128)(2,1)} %down_own.1), channel_id=1, source_target_pairs={{0,1},{1,0},{2,3},{3,2},{4,5},{5,4},{6,7},{7,6},{8,9},{9,8},{10,11... | collective-permute-start | bytes 7077896 | tf_op jit(solution)/shard_map/ppermute | solution.py:561
  81.5 79.0 %collective-permute-start.18 = (bf16[384,768]{1,0:T(8,128)(2,1)S(1)}, bf16[384,768]{1,0:T(8,128)(2,1)}, u32[]{:S(2)}, u32[]{:S(2)}) collective-permute-start(bf16[384,768]{1,0:T(8,128)(2,1)S(1)} %copy-done.7), channel_id=1, source_target_pairs={{0,1},{1,0},{2,3},{3,2},{4,5},{5,4},{6,7},{7,6},{8,9},{9,8},{10,11... | collective-permute-start | bytes 1769480 | tf_op jit(solution)/shard_map/ppermute | solution.py:561
  125.2 24.2 %all-to-all-start.4 = ((f32[16,8,640]{2,1,0:T(8,128)}), f32[16,8,640]{2,1,0:T(8,128)S(1)}, u32[]{:S(2)}, u32[]{:S(2)}) async-start(f32[16,8,640]{2,1,0:T(8,128)} %bitcast.18), calls=%async_computation.4 | async-start | bytes 655360 | tf_op jit(solution)/shard_map/all_to_all | solution.py:557
  147.2 13.3 %collective-permute-start.17 = (bf16[256,384]{1,0:T(8,128)(2,1)}, bf16[256,384]{1,0:T(8,128)(2,1)S(1)}, u32[]{:S(2)}, u32[]{:S(2)}) collective-permute-start(bf16[256,384]{1,0:T(8,128)(2,1)} %shard_map.106.own_ref), channel_id=1, source_target_pairs={{0,1},{1,0},{2,3},{3,2},{4,5},{5,4},{6,7},{7,6},{8,9},{9,8},{10,11... | collective-permute-start | bytes 589832 | tf_op jit(solution)/shard_map/ppermute | solution.py:561
  151.9 15.7 %all-to-all-start.5 = ((bf16[32,8,384]{2,1,0:T(8,128)(2,1)}), bf16[32,8,384]{2,1,0:T(8,128)(2,1)S(1)}, u32[]{:S(2)}, u32[]{:S(2)}) async-start(bf16[32,8,384]{2,1,0:T(8,128)(2,1)} %shard_map.107), calls=%async_computation.5 | async-start | bytes 393216 | tf_op jit(solution)/shard_map/all_to_all | solution.py:557
  (32 other events, 379.9 us)

commit v5 on v4

v5 whole, which is shorter than its diff:
```python
import functools

import jax
import jax.numpy as jnp
from jax import lax
from jax.experimental import pallas as pl
from jax.experimental.pallas import tpu as pltpu
from jax.sharding import Mesh
from jax.sharding import PartitionSpec as P

SEQ = ("x", "z", "y")
PLANE = ("x", "y")
EPSILON = 1e-05
NEGATIVE = -1e30
HEADS = 6
BF16 = jnp.bfloat16
F32 = jnp.float32
LIMIT = 51 * 1024 * 1024
SLOTS = 10
MORE = 16 - SLOTS
STRIDE = SLOTS * 64 + 48
FAR = pl.BlockSpec(memory_space=pltpu.HBM)
NEAR = pl.BlockSpec(memory_space=pltpu.VMEM)
SMEM = pl.BlockSpec(memory_space=pltpu.SMEM)


def nt(a, b):
    return lax.dot_general(a, b, (((1,), (1,)), ((), ())), preferred_element_type=F32)


def nn(a, b):
    return jnp.dot(a, b, preferred_element_type=F32)


def call(kernel, outs, scratch, cost, arrays, raw=(), near=(), scalars=(), by_hand=(), tables=()):
    single = not isinstance(outs, tuple)
    results = (outs,) if single else outs
    count, total = len(arrays), len(arrays) + len(raw) + len(near) + len(scalars)

    def body(*refs):
        inputs, others = refs[:count], refs[count:total]
        outputs = refs[total : total + len(results)]
        listed = refs[total + len(results) : total + len(results) + len(tables)]
        held = refs[total + len(results) + len(tables) :]
        copied, made, (sem_in, sem_out), rest = (
            held[:count],
            held[count : count + len(results)],
            held[count + len(results) : count + len(results) + 2],
            held[count + len(results) + 2 :],
        )
        copies = [pltpu.make_async_copy(inputs[i], copied[i], sem_in.at[i]) for i in range(count)]
        for copy in copies:
            copy.start()
        for copy in copies:
            copy.wait()
        kernel(*copied, *others, *made, *[outputs[i] for i in by_hand], *listed, *rest)
        copies = [pltpu.make_async_copy(made[i], outputs[i], sem_out.at[i]) for i in range(len(results)) if i not in by_hand]
        for copy in copies:
            copy.start()
        for copy in copies:
            copy.wait()

    made = pl.pallas_call(
        body,
        out_shape=(*results, *tables),
        in_specs=[FAR] * (count + len(raw)) + [NEAR] * len(near) + [SMEM] * len(scalars),
        out_specs=(FAR,) * len(results) + (SMEM,) * len(tables),
        scratch_shapes=[pltpu.VMEM(v.shape, v.dtype) for v in (*arrays, *results)]
        + [pltpu.SemaphoreType.DMA((max(count, 1),)), pltpu.SemaphoreType.DMA((len(results),))]
        + list(scratch),
        cost_estimate=pl.CostEstimate(flops=cost[0], bytes_accessed=cost[1], transcendentals=cost[2]),
        compiler_params=pltpu.CompilerParams(vmem_limit_bytes=LIMIT),
    )(*arrays, *raw, *near, *scalars)
    return made[0] if single and not tables else made


def pick(condition, yes, no):
    return jnp.where(condition, yes, no)


def piece_of(owner, local, z, core):
    return ((z - ((owner >> 2) & 7)) & 7) + pick((local >> 1) == core, 0, 8)


def plan_kernel(states_ref, owner_ref, local_ref, ids_ref, here_ref, spread_ref, slots_ref, count_ref, rows_ref, sem):
    z, core = here_ref[0, 1], here_ref[0, 3]
    copies = []
    for g in range(2):
        start = pl.multiple_of((ids_ref[0, g] & 3) * 64, 64)
        copies.append(pltpu.make_async_copy(states_ref.at[pl.ds(start, 64), :], rows_ref.at[pl.ds(64 * g, 64), :], sem.at[g]))
        copies[g].start()
    for p in range(16):
        count_ref[p] = 0
    line = lax.broadcasted_iota(jnp.int32, (16, 128), 0)
    lane = lax.broadcasted_iota(jnp.int32, (16, 128), 1)
    place = line * 128 + lane
    wanted = jnp.zeros((16, 128), F32)
    most = jnp.int32(0)
    for b in range(4):
        for h in range(HEADS):
            for r in range(3):
                owner, local = owner_ref[0, r, b, h], local_ref[0, r, b, h]
                item = (piece_of(owner, local, z, core) * HEADS + h) * 2 + (local & 1)
                group = ((owner >> 5) << 2) + (owner & 3)
                rank = count_ref[group]
                count_ref[group] = rank + 1
                most = jnp.maximum(most, rank)
                near = group * STRIDE + rank * 64
                beyond = 16 * STRIDE + group * MORE * 64 + (rank - SLOTS) * 64
                slots_ref[0, (b * HEADS + h) * 3 + r] = pick(rank < SLOTS, near, beyond)
                wanted = jnp.where(place == group * 128 + rank, item.astype(F32), wanted)
    wanted = jnp.where(lane == 127, pick(most >= SLOTS, 1.0, 0.0), wanted)
    for copy in copies:
        copy.wait()
    for p in range(16):
        spread_ref[p, 48:64, :] = jnp.broadcast_to(wanted[p : p + 1, :], (16, 128)).astype(BF16)
        for c in range(3):
            lanes = (p % 2) * 384 + c * 128
            spread_ref[p, 16 * c : 16 * c + 16, :] = rows_ref[p // 2 * 16 : p // 2 * 16 + 16, lanes : lanes + 128]


def plan(states, owner, local, ids, here):
    shape = jax.ShapeDtypeStruct
    return call(
        plan_kernel,
        shape((16, 64, 128), BF16),
        [pltpu.SMEM((16,), jnp.int32), pltpu.VMEM((128, 768), BF16), pltpu.SemaphoreType.DMA((2,))],
        (1_000_000, 600_000, 0),
        [],
        raw=[states],
        scalars=[owner, local, ids, here],
        tables=(shape((1, 72), jnp.int32),),
    )


def arrange_kernel(weight_ref, wq_ref, wkv_ref):
    wq_ref[...] = jnp.zeros_like(wq_ref)
    for h in range(HEADS):
        part = slice(64 * h, 64 * h + 64)
        wq_ref[:, 128 * h : 128 * h + 64] = weight_ref[0, :, part] * BF16(0.125)
        wkv_ref[:, 128 * h : 128 * h + 64] = weight_ref[1, :, part]
        wkv_ref[:, 128 * h + 64 : 128 * h + 128] = weight_ref[2, :, part]


def arrange(weight):
    square = jax.ShapeDtypeStruct((768, 768), BF16)
    return call(arrange_kernel, (square, square), [], (2_000_000, 4_000_000, 0), [weight])


def column_kernel(*refs):
    pieces = refs[1:17]
    wkv_ref = refs[0]
    (
        received_ref,
        shares_ref,
        ids_ref,
        here_ref,
        kv_ref,
        items_ref,
        out_ref,
        wanted_ref,
        flag_ref,
        asked_ref,
        rows_ref,
        sem,
        sems,
        sem_rows,
    ) = refs[17:]
    copies = [pltpu.make_async_copy(piece, rows_ref.at[pl.ds(128 * i, 128), :], sem_rows.at[i]) for i, piece in enumerate(pieces)]
    for copy in copies:
        copy.start()
    for p in range(16):
        asked_ref[p : p + 1, :] = received_ref[p, 48:49, :].astype(F32).astype(jnp.int32)
    asked = pltpu.make_async_copy(asked_ref, wanted_ref, sem.at[0])
    asked.start()
    owner = pick(here_ref[0, 0] >= 2, ids_ref[0, 1], ids_ref[0, 0]) >> 2
    share = shares_ref[(owner >> 2) & 7]
    for p in range(16):
        items_ref[p, SLOTS * 64 : STRIDE, :] = share
    for i in range(4):
        for copy in copies[4 * i : 4 * i + 4]:
            copy.wait()
        pair = nn(rows_ref[512 * i : 512 * i + 512, :], wkv_ref[...]).astype(BF16)
        for j in range(4):
            for h in range(HEADS):
                kv_ref[(4 * i + j) * HEADS + h] = pair[128 * j : 128 * j + 128, 128 * h : 128 * h + 128]
    asked.wait()
    flag = wanted_ref[0, 127]
    for p in range(1, 16):
        flag = jnp.maximum(flag, wanted_ref[p, 127])
    flag_ref[0, 0] = flag

    @pl.loop(0, 16)
    def _(p):
        for k in range(SLOTS):
            item = wanted_ref[p, k]
            at = pl.multiple_of((item & 1) * 64, 64)
            items_ref[p, 64 * k : 64 * k + 64, :] = kv_ref[item >> 1, pl.ds(at, 64), :]
        pltpu.make_async_copy(items_ref.at[p], out_ref.at[p], sems.at[p]).start()

    @pl.loop(0, 16)
    def _(p):
        pltpu.make_async_copy(items_ref.at[p], out_ref.at[p], sems.at[p]).wait()


def column(pieces, wkv, received, shares, ids, here):
    shape = jax.ShapeDtypeStruct
    return call(
        column_kernel,
        (shape((16 * HEADS, 128, 128), BF16), shape((16, STRIDE, 128), BF16)),
        [
            pltpu.VMEM((16, 128), jnp.int32),
            pltpu.VMEM((2048, 768), BF16),
            pltpu.SemaphoreType.DMA((1,)),
            pltpu.SemaphoreType.DMA((16,)),
            pltpu.SemaphoreType.DMA((16,)),
        ],
        (2_400_000_000, 10_000_000, 0),
        [wkv],
        raw=pieces,
        near=[received, shares],
        scalars=[ids, here],
        by_hand=(1,),
        tables=(shape((16, 128), jnp.int32), shape((1, 1), jnp.int32)),
    )


def extra_kernel(kv_ref, wanted_ref, items_ref):
    @pl.loop(0, 16)
    def _(p):
        for k in range(MORE):
            item = wanted_ref[p, SLOTS + k]
            at = pl.multiple_of((item & 1) * 64, 64)
            items_ref[p, 64 * k : 64 * k + 64, :] = kv_ref[item >> 1, pl.ds(at, 64), :]


def extra(kv, wanted):
    shape = jax.ShapeDtypeStruct((16, MORE * 64, 128), BF16)
    items = call(extra_kernel, shape, [], (0, 5_000_000, 0), [kv], scalars=[wanted])
    return exchanged(items, PLANE)


def unused_kernel(out_ref, row_ref):
    row_ref[...] = jnp.zeros_like(row_ref)
    pltpu.sync_copy(row_ref, out_ref.at[0, pl.ds(0, 16), :])


def unused():
    return pl.pallas_call(
        unused_kernel,
        out_shape=jax.ShapeDtypeStruct((16, MORE * 64, 128), BF16),
        out_specs=FAR,
        scratch_shapes=[pltpu.VMEM((16, 128), BF16)],
        compiler_params=pltpu.CompilerParams(vmem_limit_bytes=LIMIT),
    )()


def window_kernel(before_ref, states_ref, after_ref, wq_ref, wkv_ref, q_ref, ext_ref, rows_ref):
    rows_ref[0:64, :] = before_ref[...]
    rows_ref[64:320, :] = states_ref[...]
    rows_ref[320:384, :] = after_ref[...]
    pair = nn(rows_ref[...], wkv_ref[...]).astype(BF16)
    query = nn(states_ref[...], wq_ref[...]).astype(BF16)
    for h in range(HEADS):
        ext_ref[h] = pair[:, 128 * h : 128 * h + 128]
        q_ref[h] = query[:, 128 * h : 128 * h + 128]


def window(before, states, after, wq, wkv):
    shape = jax.ShapeDtypeStruct
    return call(
        window_kernel,
        (shape((HEADS, 256, 128), BF16), shape((HEADS, 384, 128), BF16)),
        [pltpu.VMEM((384, 768), BF16)],
        (800_000_000, 4_000_000, 0),
        [before, states, after, wq, wkv],
    )


def partial_kernel(wq_ref, wkv_ref, kv_far, remote_ref, out_ref, pair_ref, rows_ref, q_ref, s_ref, kv_ref, sem):
    keep = pltpu.make_async_copy(kv_far, kv_ref, sem.at[0])
    keep.start()
    for p in range(16):
        for c in range(3):
            lanes = (p % 2) * 384 + c * 128
            first = SLOTS * 64 + 16 * c
            rows_ref[p // 2 * 16 : p // 2 * 16 + 16, lanes : lanes + 128] = remote_ref[p, first : first + 16, :]
    query = nn(rows_ref[...], wq_ref[...]).astype(BF16)
    pair = nn(rows_ref[...], wkv_ref[...]).astype(BF16)
    for h in range(HEADS):
        q_ref[h] = query[:, 128 * h : 128 * h + 128]
        pair_ref[h] = pair[:, 128 * h : 128 * h + 128]
    keep.wait()
    lane = lax.broadcasted_iota(jnp.int32, (128, 128), 1)
    highs = jnp.zeros((128, 128), F32)
    totals = jnp.zeros((128, 128), F32)
    for h in range(HEADS):
        keys = [kv_ref[4 * c : 4 * c + 4, h].reshape(512, 128) for c in range(4)]
        high = jnp.full((128, 1), NEGATIVE, F32)
        for c in range(4):
            s = nt(q_ref[h], keys[c])
            s_ref[h % 2, :, c * 512 : c * 512 + 512] = s
            high = jnp.maximum(high, jnp.max(s, axis=1, keepdims=True))
        total = jnp.zeros((128, 1), F32)
        acc = jnp.zeros((128, 128), F32)
        for c in range(4):
            p = jnp.exp(s_ref[h % 2, :, c * 512 : c * 512 + 512] - high)
            total = total + jnp.sum(p, axis=1, keepdims=True)
            head = p.astype(BF16)
            rest = (p - head.astype(F32)).astype(BF16)
            acc = acc + nn(head, keys[c]) + nn(rest, keys[c])
        out_ref[:, 64 * h : 64 * h + 64] = acc[:, 64:128]
        highs = jnp.where(lane == h, high, highs)
        totals = jnp.where(lane == h, total, totals)
    out_ref[:, 384:512] = highs
    out_ref[:, 512:640] = totals


def partial(wq, wkv, remote, kv):
    shape = jax.ShapeDtypeStruct
    return call(
        partial_kernel,
        (shape((128, 640), F32), shape((HEADS, 128, 128), BF16)),
        [
            pltpu.VMEM((128, 768), BF16),
            pltpu.VMEM((HEADS, 128, 128), BF16),
            pltpu.VMEM((2, 128, 2048), F32),
            pltpu.VMEM((16, HEADS, 128, 128), BF16),
            pltpu.SemaphoreType.DMA((1,)),
        ],
        (2_000_000_000, 10_000_000, 1_600_000),
        [wq, wkv],
        raw=[kv],
        near=[remote],
    )


def merge_kernel(parts_ref, out_ref):
    highs = parts_ref[:, :, 384:512]
    factor = jnp.exp(highs - jnp.max(highs, axis=0, keepdims=True))
    total = jnp.sum(factor * parts_ref[:, :, 512:640], axis=0)
    outs = []
    for h in range(HEADS):
        acc = jnp.sum(parts_ref[:, :, 64 * h : 64 * h + 64] * factor[:, :, h : h + 1], axis=0)
        outs.append(acc / total[:, h : h + 1])
    rows = jnp.concatenate(outs, axis=1).astype(BF16)
    for p in range(32):
        out_ref[p] = rows


def merge(parts):
    return call(
        merge_kernel,
        jax.ShapeDtypeStruct((32, 8, 384), BF16),
        [],
        (2_000_000, 600_000, 10_000),
        [],
        near=[parts],
    )


def attend_kernel(first, count, q_ref, ext_ref, pair_ref, remote_ref, more_ref, slot_ref, here_ref, flag_ref, out_ref, items_ref, keys_ref):
    size = 16 * STRIDE

    def each(body):
        for b in range(4):
            for h in range(2 * count):
                for r in range(3):
                    body((b * 2 * count + h) * 3 + r, slot_ref[0, (b * HEADS + 2 * first + h) * 3 + r])

    def main(i, slot):
        at = pl.multiple_of(jnp.minimum(slot, size - 64), 16)
        items_ref[i] = remote_ref[pl.ds(at, 64), :]

    def beyond(i, slot):
        @pl.when(slot >= size)
        def _():
            items_ref[i] = more_ref[pl.ds(pl.multiple_of(slot - size, 64), 64), :]

    each(main)

    @pl.when(flag_ref[0, 0] > 0)
    def _():
        each(beyond)

    seq = (here_ref[0, 0] * 8 + here_ref[0, 1]) * 4 + here_ref[0, 2]
    lane = lax.broadcasted_iota(jnp.int32, (64, 512), 1)
    for pair in range(count):
        for b in range(4):
            outs = []
            for k in range(2):
                h = 2 * (first + pair) + k
                i = (b * 2 * count + 2 * pair + k) * 3
                buf = keys_ref.at[b * 2 + k]
                buf[0:192, :] = ext_ref[h, b * 64 : b * 64 + 192, :]
                for r in range(3):
                    buf[192 + 64 * r : 256 + 64 * r, :] = items_ref[i + r]
                buf[384:512, :] = pair_ref[h]
                keys = buf[...]
                s = nt(q_ref[h, b * 64 : b * 64 + 64, :], keys)
                if b == 0:
                    s = jnp.where((lane < 64) & (seq == 0), NEGATIVE, s)
                if b == 3:
                    s = jnp.where((lane >= 128) & (lane < 192) & (seq == 127), NEGATIVE, s)
                p = jnp.exp(s - jnp.max(s, axis=1, keepdims=True))
                w = (p * (1.0 / jnp.sum(p, axis=1, keepdims=True))).astype(BF16)
                outs.append(nn(w, keys)[:, 64:128])
            out_ref[b * 64 : b * 64 + 64, 128 * pair : 128 * pair + 128] = jnp.concatenate(outs, axis=1).astype(BF16)


def attend(first, count, q, ext, pair, remote, more, slots, here, flag):
    return call(
        functools.partial(attend_kernel, first, count),
        jax.ShapeDtypeStruct((256, 128 * count), BF16),
        [pltpu.VMEM((24 * count, 64, 128), BF16), pltpu.VMEM((8, 512, 128), BF16)],
        (200_000_000 * count, 1_500_000 * count, 270_000 * count),
        [q, ext, pair],
        near=[remote, more],
        scalars=[slots, here, flag],
    )


def norm(v, gain):
    shifted = v - jnp.mean(v, axis=1, keepdims=True)
    spread = jnp.mean(shifted * shifted, axis=1, keepdims=True)
    return shifted * lax.rsqrt(spread + EPSILON) * gain


CHUNK = 512


def finish_kernel(
    own_ref,
    other_ref,
    own2_ref,
    other2_ref,
    states_ref,
    wo_own,
    wo_other,
    gain_ref,
    gain2_ref,
    up_own,
    up_other,
    down_own,
    down_other,
    rows,
    ids_ref,
    here_ref,
    out_ref,
    attended,
    states,
    wo,
    gains,
    up,
    down,
    sums,
    result,
    sem,
    sems,
):
    copies = [
        pltpu.make_async_copy(source, target, sem.at[i])
        for i, (source, target) in enumerate(
            [
                (own_ref, attended.at[0, :, pl.ds(0, 256)]),
                (other_ref, attended.at[1, :, pl.ds(0, 256)]),
                (own2_ref, attended.at[0, :, pl.ds(256, 128)]),
                (other2_ref, attended.at[1, :, pl.ds(256, 128)]),
                (wo_own, wo.at[0]),
                (wo_other, wo.at[1]),
                (states_ref, states),
                (gain_ref, gains.at[0]),
                (gain2_ref, gains.at[1]),
            ]
        )
    ]
    chunks = []
    for half, (above, below) in enumerate(((up_own, down_own), (up_other, down_other))):
        for i in range(0, 1536, CHUNK):
            number = len(chunks)
            part = pl.ds(i, CHUNK)
            chunks.append(
                (
                    pltpu.make_async_copy(above.at[:, part], up.at[number], sems.at[2 * number]),
                    pltpu.make_async_copy(below.at[part, :], down.at[number], sems.at[2 * number + 1]),
                )
            )
    for copy in copies:
        copy.start()
    for chunk in chunks:
        chunk[0].start()
        chunk[1].start()
    for copy in copies:
        copy.wait()
    core = here_ref[0, 3]
    seq = (here_ref[0, 0] * 8 + here_ref[0, 1]) * 4 + here_ref[0, 2]
    for g in range(2):

        @pl.when((ids_ref[0, g] >> 2) == seq)
        def _():
            for k, side in ((0, core), (1, 1 - core)):
                for i in range(4):
                    first = (g * 8 + 2 * i) * 2 + side
                    at = pl.multiple_of((ids_ref[0, g] & 3) * 64 + 16 * i, 16)
                    attended[k, pl.ds(at, 16), :] = jnp.concatenate([rows[first], rows[first + 2]], axis=0)

    projected = nn(attended[0], wo[0]) + nn(attended[1], wo[1])
    normed = norm(states[...].astype(F32) + projected, gains[0]).astype(BF16)
    for number, chunk in enumerate(chunks):
        chunk[0].wait()
        v = nn(normed, up[number])
        hidden = (v * (1.0 + lax.erf(v * 0.7071067811865476)) * 0.5).astype(BF16)
        chunk[1].wait()
        piece = nn(hidden, down[number])
        half = number // (1536 // CHUNK)
        if number % (1536 // CHUNK) == 0:
            sums[half] = piece
        else:
            sums[half] += piece
    result[...] = norm(normed.astype(F32) + (sums[0] + sums[1]), gains[1]).astype(BF16)
    pltpu.sync_copy(result, out_ref)


def finish(*operands):
    count = 2 * 1536 // CHUNK
    return pl.pallas_call(
        finish_kernel,
        out_shape=jax.ShapeDtypeStruct((256, 768), BF16),
        in_specs=[FAR] * 13 + [NEAR] + [SMEM] * 2,
        out_specs=FAR,
        scratch_shapes=[
            pltpu.VMEM((2, 256, 384), BF16),
            pltpu.VMEM((256, 768), BF16),
            pltpu.VMEM((2, 384, 768), BF16),
            pltpu.VMEM((2, 1, 768), F32),
            pltpu.VMEM((count, 768, CHUNK), BF16),
            pltpu.VMEM((count, CHUNK, 768), BF16),
            pltpu.VMEM((2, 256, 768), F32),
            pltpu.VMEM((256, 768), BF16),
            pltpu.SemaphoreType.DMA((9,)),
            pltpu.SemaphoreType.DMA((2 * count,)),
        ],
        cost_estimate=pl.CostEstimate(flops=2_700_000_000, bytes_accessed=12_000_000, transcendentals=800_000),
        compiler_params=pltpu.CompilerParams(vmem_limit_bytes=LIMIT),
    )(*operands)


def turned(value, axis, shift):
    count = lax.axis_size(axis)
    return lax.ppermute(value, axis, [(i, (i + shift) % count) for i in range(count)])


def exchanged(value, axes):
    return lax.all_to_all(value, axes, split_axis=0, concat_axis=0, tiled=True)


def swapped(value):
    return lax.ppermute(value, "mp", [(0, 1), (1, 0)])


def shards(
    states, qkv_weight, out_weight, up_weight, down_weight, attn_gain, mlp_gain, global_ids, random_owner, random_local
):
    x, z, y, core = (lax.axis_index(axis) for axis in ("x", "z", "y", "mp"))
    here = jnp.stack([x, z, y, core]).astype(jnp.int32).reshape(1, 4)
    ids = global_ids.reshape(1, 2)
    tied = lax.optimization_barrier

    up0 = lax.dynamic_slice_in_dim(states, core * 128, 128, 0)
    up1, down1, far0 = turned(up0, "z", 1), turned(up0, "z", -1), swapped(up0)
    order = (0, 3, 1, 2)
    spread, slots = plan(states, random_owner.transpose(order), random_local.transpose(order), ids, here)
    up1, down1, far0, spread = tied((up1, down1, far0, spread))

    up2, down2 = turned(up1, "z", 1), turned(down1, "z", -1)
    far1, far7 = swapped(up1), swapped(down1)
    received = exchanged(spread, PLANE)
    wq, wkv = arrange(qkv_weight)
    up2, down2, far1, far7, wkv = tied((up2, down2, far1, far7, wkv))

    up3, down3 = turned(up2, "z", 1), turned(down2, "z", -1)
    far2, far6 = swapped(up2), swapped(down2)
    up3, down3, far2, far6, received = tied((up3, down3, far2, far6, received))

    root_owner = pick(x >= 2, global_ids[1], global_ids[0]) >> 2
    root = (root_owner >> 5) * 4 + (root_owner & 3)
    share = lax.dynamic_slice(received, (root, 0, 0), (1, 48, 128))
    up4 = turned(up3, "z", 1)
    shares = exchanged(jnp.broadcast_to(share, (8, 48, 128)), "z")
    far3, far5 = swapped(up3), swapped(down3)
    ends = [(i, i + 1) for i in range(127)]
    before = lax.ppermute(states[192:], SEQ, ends)
    after = lax.ppermute(states[:64], SEQ, [(j, i) for i, j in ends])
    up4, far3, far5, shares, before, after = tied((up4, far3, far5, shares, before, after))

    pieces = [up0, up1, up2, up3, up4, down3, down2, down1, far0, far1, far2, far3, swapped(up4), far5, far6, far7]
    pairs, items, wanted, flag = column(pieces, wkv, received, shares, ids, here)
    more = lax.cond(flag[0, 0] > 0, lambda: extra(pairs, wanted), unused)
    items, more, weights = tied((items, more, (out_weight, up_weight, down_weight)))
    remote = exchanged(items, PLANE)
    wo_other, up_other, down_other = (swapped(weight) for weight in weights)
    q, ext = window(before, states, after, wq, wkv)
    remote, ext = tied((remote, ext))
    part, pair = partial(wq, wkv, remote, pairs.reshape(16, HEADS, 128, 128))
    parts = exchanged(part.reshape(16, 8, 640), PLANE)
    rest = (q, ext, pair, remote.reshape(16 * STRIDE, 128), more.reshape(16 * MORE * 64, 128), slots, here, flag)
    attended = attend(0, 2, *rest)
    parts, attended = tied((parts, attended))
    rows = exchanged(merge(parts), PLANE + ("mp",))
    attended2 = attend(2, 1, *rest)
    return finish(
        attended,
        swapped(attended),
        attended2,
        swapped(attended2),
        states,
        out_weight,
        wo_other,
        attn_gain.reshape(1, -1),
        mlp_gain.reshape(1, -1),
        up_weight,
        up_other,
        down_weight,
        down_other,
        rows,
        ids,
        here,
    )


def solution(mesh):
    split = Mesh(mesh.devices.reshape(4, 8, 4, mesh.shape["mp"]), ("x", "z", "y", "mp"))
    placed = (
        P(SEQ, None),
        P(None, None, "mp"),
        P("mp", None),
        P(None, "mp"),
        P("mp", None),
        P(),
        P(),
        P(),
        P("mp", SEQ, None, None),
        P("mp", SEQ, None, None),
    )
    return jax.shard_map(shards, mesh=split, in_specs=placed, out_specs=P(SEQ, None), check_vma=False)
```

time: 181 us -> 176 us (0.972)
  Pallas kernels: 60.4 us -> 57 us
    all_to_all x5, waiting for transfers between devices: 39.9 us -> 32.6 us  [exchanged(): return lax.all_to_all(value, axes, split_axis=0, concat_axis=0, tiled=True)]
    ppermute x1, waiting for transfers between devices: 0.75 us -> 4.04 us  [shards(): after = lax.ppermute(states[:64], SEQ, [(j, i) for i, j in ends])]
    pallas_call x1, Pallas kernels: 11.2 us -> 8.43 us  [finish(): pl.pallas_call(finish_kernel, out_shape=jax.ShapeDtypeStruct((256, 768),...]
    all_to_all x5, starting transfers between devices: 36.9 us -> 39.1 us  [exchanged(): return lax.all_to_all(value, axes, split_axis=0, concat_axis=0, tiled=True)]
    unnamed x62 -> x30, local copies, waits for them, and re-layouts: 7.75 us -> 7.37 us
    ppermute x12 -> x13, starting transfers between devices: 9.04 us -> 8.95 us  [swapped(): return lax.ppermute(value, 'mp', [(0, 1), (1, 0)])]
  transfers between devices with their start and end apart: 26 -> 27, of which waited for: 4 -> 7; matrix products, arithmetic and copies ran while one was open for 3% -> 1% of each run, Pallas kernels for 23% -> 20%
where the time goes in v5:
time: 176 us; the launch traced here: 175 us
  starting transfers between devices  64.6 us (37%)
  Pallas kernels  57 us (32%)
  waiting for transfers between devices  40.1 us (23%)
  local copies, waits for them, and re-layouts  10.4 us (6%)
  between operations  2.34 us (1%)
    pallas_call x8, Pallas kernels, call(): pl.pallas_call(body, out_shape=(*results, *tables), in_specs=[FAR] * (cou...  47.9 us
    all_to_all x5, starting transfers between devices, exchanged(): return lax.all_to_all(value, axes, split_axis=0, concat_axis=0, tiled=True)  39.1 us
    all_to_all x5, waiting for transfers between devices, exchanged(): return lax.all_to_all(value, axes, split_axis=0, concat_axis=0, tiled=True)  32.6 us
    ppermute x7, starting transfers between devices, turned(): lax.ppermute(value, axis, [(i, (i + shift) % count) for i in range(count)])  12.1 us
    ppermute x13, starting transfers between devices, swapped(): return lax.ppermute(value, 'mp', [(0, 1), (1, 0)])  8.95 us
    pallas_call x1, Pallas kernels, finish(): pl.pallas_call(finish_kernel, out_shape=jax.ShapeDtypeStruct((256, 768),...  8.43 us
    unnamed x30, local copies, waits for them, and re-layouts  7.37 us
    ppermute x1, waiting for transfers between devices, shards(): after = lax.ppermute(states[:64], SEQ, [(j, i) for i, j in ends])  4.04 us
  transfers between devices with their start and end apart: 27, of which 7 were waited for; matrix products, arithmetic and copies ran while one was open for 1% of the time, Pallas kernels for 20%

profile of v5, /device:TPU:1, one launch (start us, length us, event | category | flops | bytes accessed | tf_op | source)
XLA Modules:
  0.0 174.5 jit_solution(3800620094534660552)
XLA Ops:
  1.0 2.5 %collective-permute-start = (bf16[128,768]{1,0:T(8,128)(2,1)S(1)}, bf16[128,768]{1,0:T(8,128)(2,1)S(1)}, u32[]{:S(2)}, u32[]{:S(2)}) collective-permute-start(bf16[128,768]{1,0:T(8,128)(2,1)S(1)} %constant_dynamic-slice_fusion.refs_1_), channel_id=1, source_target_pairs={{0,8},{8,16},{16,24},{24,32},{32,40},{40,48},{48,56},{56,0},{1,9},... | collective-permute-start | bytes 589832 | tf_op jit(solution)/shard_map/ppermute | solution.py:550
  3.6 4.0 %collective-permute-start.1 = (bf16[128,768]{1,0:T(8,128)(2,1)S(1)}, bf16[128,768]{1,0:T(8,128)(2,1)S(1)}, u32[]{:S(2)}, u32[]{:S(2)}) collective-permute-start(bf16[128,768]{1,0:T(8,128)(2,1)S(1)} %constant_dynamic-slice_fusion.refs_1_), channel_id=1, source_target_pairs={{0,56},{8,0},{16,8},{24,16},{32,24},{40,32},{48,40},{56,48},{1,57}... | collective-permute-start | bytes 589832 | tf_op jit(solution)/shard_map/ppermute | solution.py:550
  11.7 3.1 %shard_map.101 = (bf16[16,64,128]{2,1,0:T(8,128)(2,1)}, s32[1,72]{1,0:T(1,128)S(1)}) custom-call(bf16[256,768]{1,0:T(8,128)(2,1)S(1)} %copy-done, s32[1,3,4,6]{3,2,1,0:T(4,128)S(1)} %bitcast.22, s32[1,3,4,6]{3,2,1,0:T(4,128)S(1)} %bitcast.23, s32[1,2]{1,0:T(1,128)S(1)} %bitcast.19, s32[1,4]{1,0:T(1,128)S(1)} %add_bitcast_fusion.refs_4_.refs_20_.refs_6_.here_ref), custom_call_target="tpu_custom_call" | custom-call | flops 1000000 | bytes 600000 | tf_op jit(solution)/shard_map/pallas_call | solution.py:63
  14.9 2.7 %collective-permute-start.4 = (bf16[128,768]{1,0:T(8,128)(2,1)S(1)}, bf16[128,768]{1,0:T(8,128)(2,1)S(1)}, u32[]{:S(2)}, u32[]{:S(2)}) collective-permute-start(bf16[128,768]{1,0:T(8,128)(2,1)S(1)} %collective-permute-done.1.refs_8_), channel_id=1, source_target_pairs={{0,56},{8,0},{16,8},{24,16},{32,24},{40,32},{48,40},{56,48},{1,57}... | collective-permute-start | bytes 589832 | tf_op jit(solution)/shard_map/ppermute | solution.py:550
  18.1 6.8 %all-to-all-start.1 = ((bf16[16,64,128]{2,1,0:T(8,128)(2,1)}), bf16[16,64,128]{2,1,0:T(8,128)(2,1)}, u32[]{:S(2)}, u32[]{:S(2)}) async-start(bf16[16,64,128]{2,1,0:T(8,128)(2,1)} %get-tuple-element.63), calls=%async_computation.1 | async-start | bytes 524288 | tf_op jit(solution)/shard_map/all_to_all | solution.py:554
  25.0 3.0 %shard_map.100 = (bf16[768,768]{1,0:T(8,128)(2,1)S(1)}, bf16[768,768]{1,0:T(8,128)(2,1)S(1)}) custom-call(bf16[3,768,384]{2,1,0:T(8,128)(2,1)} %refs_0_.2), custom_call_target="tpu_custom_call" | custom-call | flops 2000000 | bytes 4000000 | tf_op jit(solution)/shard_map/pallas_call | solution.py:63
  29.7 2.7 %collective-permute-start.8 = (bf16[128,768]{1,0:T(8,128)(2,1)S(1)}, bf16[128,768]{1,0:T(8,128)(2,1)S(1)}, u32[]{:S(2)}, u32[]{:S(2)}) collective-permute-start(bf16[128,768]{1,0:T(8,128)(2,1)S(1)} %collective-permute-done.4.refs_7_), channel_id=1, source_target_pairs={{0,56},{8,0},{16,8},{24,16},{32,24},{40,32},{48,40},{56,48},{1,57}... | collective-permute-start | bytes 589832 | tf_op jit(solution)/shard_map/ppermute | solution.py:550
  32.4 1.3 collective-permute-start.9
  36.6 1.8 %collective-permute-start.12 = (bf16[128,768]{1,0:T(8,128)(2,1)S(1)}, bf16[128,768]{1,0:T(8,128)(2,1)}, u32[]{:S(2)}, u32[]{:S(2)}) collective-permute-start(bf16[128,768]{1,0:T(8,128)(2,1)S(1)} %collective-permute-done.7.refs_4_), channel_id=1, source_target_pairs={{0,1},{1,0},{2,3},{3,2},{4,5},{5,4},{6,7},{7,6},{8,9},{9,8},{10,11... | collective-permute-start | bytes 589832 | tf_op jit(solution)/shard_map/ppermute | solution.py:558
  39.9 6.0 %all-to-all-start.2 = ((bf16[8,48,128]{2,1,0:T(8,128)(2,1)}), bf16[8,48,128]{2,1,0:T(8,128)(2,1)S(1)}, u32[]{:S(2)}, u32[]{:S(2)}) async-start(bf16[8,48,128]{2,1,0:T(8,128)(2,1)} %broadcast_in_dim.8), calls=%async_computation.2 | async-start | bytes 196608 | tf_op jit(solution)/shard_map/all_to_all | solution.py:554
  46.0 3.2 %collective-permute-start.14 = (bf16[64,768]{1,0:T(8,128)(2,1)S(1)}, bf16[64,768]{1,0:T(8,128)(2,1)S(1)}, u32[]{:S(2)}, u32[]{:S(2)}) collective-permute-start(bf16[64,768]{1,0:T(8,128)(2,1)S(1)} %get-tuple-element.97), channel_id=1, source_target_pairs={{0,2},{2,4},{4,6},{6,8},{8,10},{10,12},{12,14},{14,16},{16,18},{18... | collective-permute-start | bytes 294920 | tf_op jit(solution)/shard_map/ppermute | solution.py:592
  49.2 1.3 collective-permute-start.15
  50.8 4.0 %collective-permute-done.15.refs_2_ = bf16[64,768]{1,0:T(8,128)(2,1)S(1)} collective-permute-done((bf16[64,768]{1,0:T(8,128)(2,1)S(1)}, bf16[64,768]{1,0:T(8,128)(2,1)S(1)}, u32[]{:S(2)}, u32[]{:S(2)}) %collective-permute-start.15) | collective-permute-done | bytes 98336 | tf_op jit(solution)/shard_map/ppermute | solution.py:593
  55.5 2.2 %collective-permute-start.16 = (bf16[128,768]{1,0:T(8,128)(2,1)}, bf16[128,768]{1,0:T(8,128)(2,1)S(1)}, u32[]{:S(2)}, u32[]{:S(2)}) collective-permute-start(bf16[128,768]{1,0:T(8,128)(2,1)} %collective-permute-done.11.refs_5_), channel_id=1, source_target_pairs={{0,1},{1,0},{2,3},{3,2},{4,5},{5,4},{6,7},{7,6},{8,9},{9,8},{10,11... | collective-permute-start | bytes 589832 | tf_op jit(solution)/shard_map/ppermute | solution.py:558
  59.0 13.3 %shard_map.102 = (bf16[96,128,128]{2,1,0:T(8,128)(2,1)}, bf16[16,688,128]{2,1,0:T(8,128)(2,1)}, s32[16,128]{1,0:T(8,128)}, s32[1,1]{1,0:T(1,128)}) custom-call(bf16[768,768]{1,0:T(8,128)(2,1)} %copy-done.2, bf16[128,768]{1,0:T(8,128)(2,1)S(1)} %constant_dynamic-slice_fusion.refs_1_, bf16[128,768]{1,0:T(8,128)(2,1)S(1)} %collective-permute-done.refs_2_, ...), custom_call_target="tpu_custom_call" | custom-call | flops 2400000000 | bytes 10000000 | tf_op jit(solution)/shard_map/pallas_call | solution.py:63
  73.4 9.0 %all-to-all-start.3 = ((bf16[16,688,128]{2,1,0:T(8,128)(2,1)}), bf16[16,688,128]{2,1,0:T(8,128)(2,1)}, u32[]{:S(2)}, u32[]{:S(2)}) async-start(bf16[16,688,128]{2,1,0:T(8,128)(2,1)} %get-tuple-element.80), calls=%async_computation.3 | async-start | bytes 5636096 | tf_op jit(solution)/shard_map/all_to_all | solution.py:554
  83.3 3.2 %shard_map.103 = (bf16[6,256,128]{2,1,0:T(8,128)(2,1)S(1)}, bf16[6,384,128]{2,1,0:T(8,128)(2,1)S(1)}) custom-call(bf16[64,768]{1,0:T(8,128)(2,1)S(1)} %collective-permute-done.14.refs_0_, bf16[256,768]{1,0:T(8,128)(2,1)S(1)} %copy-done.1, bf16[64,768]{1,0:T(8,128)(2,1)S(1)} %copy-done.11, bf16[768,768]{1,0:T(8,128)(2,1)S(1)} %get-tuple-element.55.refs_3_.refs_0_, ...), custom_call_target="tpu_custom_call" | custom-call | flops 800000000 | bytes 4000000 | tf_op jit(solution)/shard_map/pallas_call | solution.py:63
  87.0 32.3 %all-to-all-done.3.refs_3_ = bf16[16,688,128]{2,1,0:T(8,128)(2,1)} async-done(((bf16[16,688,128]{2,1,0:T(8,128)(2,1)}), bf16[16,688,128]{2,1,0:T(8,128)(2,1)}, u32[]{:S(2)}, u32[]{:S(2)}) %all-to-all-start.3) | async-done | bytes 2818080 | tf_op jit(solution)/shard_map/all_to_all | solution.py:554
  120.6 8.7 %shard_map.104 = (f32[128,640]{1,0:T(8,128)S(1)}, bf16[6,128,128]{2,1,0:T(8,128)(2,1)S(1)}) custom-call(bf16[768,768]{1,0:T(8,128)(2,1)S(1)} %get-tuple-element.55.refs_3_.refs_0_, bf16[768,768]{1,0:T(8,128)(2,1)S(1)} %copy-done.3, bf16[16,6,128,128]{3,2,1,0:T(8,128)(2,1)} %bitcast.26, bf16[16,688,128]{2,1,0:T(8,128)(2,1)} %all-to-all-done.3.refs_3_), custom_call_target="tpu_custom_call" | custom-call | flops 2000000000 | bytes 10000000 | tf_op jit(solution)/shard_map/pallas_call | solution.py:63
  130.0 8.1 %all-to-all-start.4 = ((f32[16,8,640]{2,1,0:T(8,128)}), f32[16,8,640]{2,1,0:T(8,128)S(1)}, u32[]{:S(2)}, u32[]{:S(2)}) async-start(f32[16,8,640]{2,1,0:T(8,128)} %bitcast.18), calls=%async_computation.4 | async-start | bytes 655360 | tf_op jit(solution)/shard_map/all_to_all | solution.py:554
  138.2 9.4 %shard_map.105.own_ref = bf16[256,256]{1,0:T(8,128)(2,1)S(1)} custom-call(bf16[6,256,128]{2,1,0:T(8,128)(2,1)S(1)} %get-tuple-element.86.refs_0_, bf16[6,384,128]{2,1,0:T(8,128)(2,1)S(1)} %get-tuple-element.87.refs_1_, bf16[6,128,128]{2,1,0:T(8,128)(2,1)S(1)} %get-tuple-element.88.refs_2_, bf16[11008,128]{1,0:T(8,128)(2,1)} %bitcast.14.refs_3_, ...), custom_call_target="tpu_custom_call" | custom-call | flops 400000000 | bytes 3000000 | tf_op jit(solution)/shard_map/pallas_call | solution.py:63
  148.5 9.1 %all-to-all-start.5 = ((bf16[32,8,384]{2,1,0:T(8,128)(2,1)}), bf16[32,8,384]{2,1,0:T(8,128)(2,1)S(1)}, u32[]{:S(2)}, u32[]{:S(2)}) async-start(bf16[32,8,384]{2,1,0:T(8,128)(2,1)} %shard_map.107), calls=%async_computation.5 | async-start | bytes 393216 | tf_op jit(solution)/shard_map/all_to_all | solution.py:554
  157.9 6.4 %shard_map.106.own2_ref = bf16[256,128]{1,0:T(8,128)(2,1)S(1)} custom-call(bf16[6,256,128]{2,1,0:T(8,128)(2,1)S(1)} %get-tuple-element.86.refs_0_, bf16[6,384,128]{2,1,0:T(8,128)(2,1)S(1)} %get-tuple-element.87.refs_1_, bf16[6,128,128]{2,1,0:T(8,128)(2,1)S(1)} %get-tuple-element.88.refs_2_, bf16[11008,128]{1,0:T(8,128)(2,1)} %bitcast.14.refs_3_, ...), custom_call_target="tpu_custom_call" | custom-call | flops 200000000 | bytes 1500000 | tf_op jit(solution)/shard_map/pallas_call | solution.py:63
  165.9 8.4 %shard_map.108 = bf16[256,768]{1,0:T(8,128)(2,1)} custom-call(bf16[256,256]{1,0:T(8,128)(2,1)S(1)} %shard_map.105.own_ref, bf16[256,256]{1,0:T(8,128)(2,1)S(1)} %collective-permute-done.17.other_ref, bf16[256,128]{1,0:T(8,128)(2,1)S(1)} %shard_map.106.own2_ref, bf16[256,128]{1,0:T(8,128)(2,1)S(1)} %collective-permute-done.18.other2_ref, ...), custom_call_target="tpu_custom_call" | custom-call | flops 2700000000 | bytes 12000000 | tf_op jit(solution)/shard_map/pallas_call | solution.py:526
  (79 shorter events, 20.1 us)
Async XLA Ops:
  1.0 13.8 %collective-permute-start = (bf16[128,768]{1,0:T(8,128)(2,1)S(1)}, bf16[128,768]{1,0:T(8,128)(2,1)S(1)}, u32[]{:S(2)}, u32[]{:S(2)}) collective-permute-start(bf16[128,768]{1,0:T(8,128)(2,1)S(1)} %constant_dynamic-slice_fusion.refs_1_), channel_id=1, source_target_pairs={{0,8},{8,16},{16,24},{24,32},{32,40},{40,48},{48,56},{56,0},{1,9},... | collective-permute-start | bytes 589832 | tf_op jit(solution)/shard_map/ppermute | solution.py:550
  3.6 11.2 %collective-permute-start.1 = (bf16[128,768]{1,0:T(8,128)(2,1)S(1)}, bf16[128,768]{1,0:T(8,128)(2,1)S(1)}, u32[]{:S(2)}, u32[]{:S(2)}) collective-permute-start(bf16[128,768]{1,0:T(8,128)(2,1)S(1)} %constant_dynamic-slice_fusion.refs_1_), channel_id=1, source_target_pairs={{0,56},{8,0},{16,8},{24,16},{32,24},{40,32},{48,40},{56,48},{1,57}... | collective-permute-start | bytes 589832 | tf_op jit(solution)/shard_map/ppermute | solution.py:550
  7.6 7.2 %collective-permute-start.2 = (bf16[128,768]{1,0:T(8,128)(2,1)S(1)}, bf16[128,768]{1,0:T(8,128)(2,1)S(1)}, u32[]{:S(2)}, u32[]{:S(2)}) collective-permute-start(bf16[128,768]{1,0:T(8,128)(2,1)S(1)} %constant_dynamic-slice_fusion.refs_1_), channel_id=1, source_target_pairs={{0,1},{1,0},{2,3},{3,2},{4,5},{5,4},{6,7},{7,6},{8,9},{9,8},{10,11... | collective-permute-start | bytes 589832 | tf_op jit(solution)/shard_map/ppermute | solution.py:558
  14.8 14.2 %collective-permute-start.3 = (bf16[128,768]{1,0:T(8,128)(2,1)S(1)}, bf16[128,768]{1,0:T(8,128)(2,1)S(1)}, u32[]{:S(2)}, u32[]{:S(2)}) collective-permute-start(bf16[128,768]{1,0:T(8,128)(2,1)S(1)} %collective-permute-done.refs_2_), channel_id=1, source_target_pairs={{0,8},{8,16},{16,24},{24,32},{32,40},{40,48},{48,56},{56,0},{1,9},... | collective-permute-start | bytes 589832 | tf_op jit(solution)/shard_map/ppermute | solution.py:550
  14.9 14.1 %collective-permute-start.4 = (bf16[128,768]{1,0:T(8,128)(2,1)S(1)}, bf16[128,768]{1,0:T(8,128)(2,1)S(1)}, u32[]{:S(2)}, u32[]{:S(2)}) collective-permute-start(bf16[128,768]{1,0:T(8,128)(2,1)S(1)} %collective-permute-done.1.refs_8_), channel_id=1, source_target_pairs={{0,56},{8,0},{16,8},{24,16},{32,24},{40,32},{48,40},{56,48},{1,57}... | collective-permute-start | bytes 589832 | tf_op jit(solution)/shard_map/ppermute | solution.py:550
  17.6 11.4 %collective-permute-start.5 = (bf16[128,768]{1,0:T(8,128)(2,1)S(1)}, bf16[128,768]{1,0:T(8,128)(2,1)S(1)}, u32[]{:S(2)}, u32[]{:S(2)}) collective-permute-start(bf16[128,768]{1,0:T(8,128)(2,1)S(1)} %collective-permute-done.refs_2_), channel_id=1, source_target_pairs={{0,1},{1,0},{2,3},{3,2},{4,5},{5,4},{6,7},{7,6},{8,9},{9,8},{10,11... | collective-permute-start | bytes 589832 | tf_op jit(solution)/shard_map/ppermute | solution.py:558
  18.1 10.9 %collective-permute-start.6 = (bf16[128,768]{1,0:T(8,128)(2,1)S(1)}, bf16[128,768]{1,0:T(8,128)(2,1)S(1)}, u32[]{:S(2)}, u32[]{:S(2)}) collective-permute-start(bf16[128,768]{1,0:T(8,128)(2,1)S(1)} %collective-permute-done.1.refs_8_), channel_id=1, source_target_pairs={{0,1},{1,0},{2,3},{3,2},{4,5},{5,4},{6,7},{7,6},{8,9},{9,8},{10,11... | collective-permute-start | bytes 589832 | tf_op jit(solution)/shard_map/ppermute | solution.py:558
  18.1 17.5 %all-to-all-start.1 = ((bf16[16,64,128]{2,1,0:T(8,128)(2,1)}), bf16[16,64,128]{2,1,0:T(8,128)(2,1)}, u32[]{:S(2)}, u32[]{:S(2)}) async-start(bf16[16,64,128]{2,1,0:T(8,128)(2,1)} %get-tuple-element.63), calls=%async_computation.1 | async-start | bytes 524288 | tf_op jit(solution)/shard_map/all_to_all | solution.py:554
  29.7 6.8 %collective-permute-start.7 = (bf16[128,768]{1,0:T(8,128)(2,1)S(1)}, bf16[128,768]{1,0:T(8,128)(2,1)S(1)}, u32[]{:S(2)}, u32[]{:S(2)}) collective-permute-start(bf16[128,768]{1,0:T(8,128)(2,1)S(1)} %collective-permute-done.3.refs_3_), channel_id=1, source_target_pairs={{0,8},{8,16},{16,24},{24,32},{32,40},{40,48},{48,56},{56,0},{1,9},... | collective-permute-start | bytes 589832 | tf_op jit(solution)/shard_map/ppermute | solution.py:550
  29.7 6.8 %collective-permute-start.8 = (bf16[128,768]{1,0:T(8,128)(2,1)S(1)}, bf16[128,768]{1,0:T(8,128)(2,1)S(1)}, u32[]{:S(2)}, u32[]{:S(2)}) collective-permute-start(bf16[128,768]{1,0:T(8,128)(2,1)S(1)} %collective-permute-done.4.refs_7_), channel_id=1, source_target_pairs={{0,56},{8,0},{16,8},{24,16},{32,24},{40,32},{48,40},{56,48},{1,57}... | collective-permute-start | bytes 589832 | tf_op jit(solution)/shard_map/ppermute | solution.py:550
  32.4 4.2 %collective-permute-start.9 = (bf16[128,768]{1,0:T(8,128)(2,1)S(1)}, bf16[128,768]{1,0:T(8,128)(2,1)}, u32[]{:S(2)}, u32[]{:S(2)}) collective-permute-start(bf16[128,768]{1,0:T(8,128)(2,1)S(1)} %collective-permute-done.3.refs_3_), channel_id=1, source_target_pairs={{0,1},{1,0},{2,3},{3,2},{4,5},{5,4},{6,7},{7,6},{8,9},{9,8},{10,11... | collective-permute-start | bytes 589832 | tf_op jit(solution)/shard_map/ppermute | solution.py:558
  36.5 18.9 %collective-permute-start.11 = (bf16[128,768]{1,0:T(8,128)(2,1)S(1)}, bf16[128,768]{1,0:T(8,128)(2,1)}, u32[]{:S(2)}, u32[]{:S(2)}) collective-permute-start(bf16[128,768]{1,0:T(8,128)(2,1)S(1)} %collective-permute-done.7.refs_4_), channel_id=1, source_target_pairs={{0,8},{8,16},{16,24},{24,32},{32,40},{40,48},{48,56},{56,0},{1,9},... | collective-permute-start | bytes 589832 | tf_op jit(solution)/shard_map/ppermute | solution.py:550
  36.6 18.8 %collective-permute-start.12 = (bf16[128,768]{1,0:T(8,128)(2,1)S(1)}, bf16[128,768]{1,0:T(8,128)(2,1)}, u32[]{:S(2)}, u32[]{:S(2)}) collective-permute-start(bf16[128,768]{1,0:T(8,128)(2,1)S(1)} %collective-permute-done.7.refs_4_), channel_id=1, source_target_pairs={{0,1},{1,0},{2,3},{3,2},{4,5},{5,4},{6,7},{7,6},{8,9},{9,8},{10,11... | collective-permute-start | bytes 589832 | tf_op jit(solution)/shard_map/ppermute | solution.py:558
  38.4 17.1 %collective-permute-start.13 = (bf16[128,768]{1,0:T(8,128)(2,1)S(1)}, bf16[128,768]{1,0:T(8,128)(2,1)}, u32[]{:S(2)}, u32[]{:S(2)}) collective-permute-start(bf16[128,768]{1,0:T(8,128)(2,1)S(1)} %collective-permute-done.8.refs_6_), channel_id=1, source_target_pairs={{0,1},{1,0},{2,3},{3,2},{4,5},{5,4},{6,7},{7,6},{8,9},{9,8},{10,11... | collective-permute-start | bytes 589832 | tf_op jit(solution)/shard_map/ppermute | solution.py:558
  39.9 15.6 %all-to-all-start.2 = ((bf16[8,48,128]{2,1,0:T(8,128)(2,1)}), bf16[8,48,128]{2,1,0:T(8,128)(2,1)S(1)}, u32[]{:S(2)}, u32[]{:S(2)}) async-start(bf16[8,48,128]{2,1,0:T(8,128)(2,1)} %broadcast_in_dim.8), calls=%async_computation.2 | async-start | bytes 196608 | tf_op jit(solution)/shard_map/all_to_all | solution.py:554
  46.0 4.8 %collective-permute-start.14 = (bf16[64,768]{1,0:T(8,128)(2,1)S(1)}, bf16[64,768]{1,0:T(8,128)(2,1)S(1)}, u32[]{:S(2)}, u32[]{:S(2)}) collective-permute-start(bf16[64,768]{1,0:T(8,128)(2,1)S(1)} %get-tuple-element.97), channel_id=1, source_target_pairs={{0,2},{2,4},{4,6},{6,8},{8,10},{10,12},{12,14},{14,16},{16,18},{18... | collective-permute-start | bytes 294920 | tf_op jit(solution)/shard_map/ppermute | solution.py:592
  49.2 5.7 %collective-permute-start.15 = (bf16[64,768]{1,0:T(8,128)(2,1)S(1)}, bf16[64,768]{1,0:T(8,128)(2,1)S(1)}, u32[]{:S(2)}, u32[]{:S(2)}) collective-permute-start(bf16[64,768]{1,0:T(8,128)(2,1)S(1)} %get-tuple-element.96), channel_id=1, source_target_pairs={{2,0},{4,2},{6,4},{8,6},{10,8},{12,10},{14,12},{16,14},{18,16},{20... | collective-permute-start | bytes 294920 | tf_op jit(solution)/shard_map/ppermute | solution.py:593
  73.4 46.0 %all-to-all-start.3 = ((bf16[16,688,128]{2,1,0:T(8,128)(2,1)}), bf16[16,688,128]{2,1,0:T(8,128)(2,1)}, u32[]{:S(2)}, u32[]{:S(2)}) async-start(bf16[16,688,128]{2,1,0:T(8,128)(2,1)} %get-tuple-element.80), calls=%async_computation.3 | async-start | bytes 5636096 | tf_op jit(solution)/shard_map/all_to_all | solution.py:554
  82.4 82.2 %collective-permute-start.20 = (bf16[768,1536]{1,0:T(8,128)(2,1)}, bf16[768,1536]{1,0:T(8,128)(2,1)}, u32[]{:S(2)}, u32[]{:S(2)}) collective-permute-start(bf16[768,1536]{1,0:T(8,128)(2,1)} %up_own.1), channel_id=1, source_target_pairs={{0,1},{1,0},{2,3},{3,2},{4,5},{5,4},{6,7},{7,6},{8,9},{9,8},{10,11... | collective-permute-start | bytes 7077896 | tf_op jit(solution)/shard_map/ppermute | solution.py:558
  83.2 81.5 %collective-permute-start.21 = (bf16[1536,768]{1,0:T(8,128)(2,1)}, bf16[1536,768]{1,0:T(8,128)(2,1)}, u32[]{:S(2)}, u32[]{:S(2)}) collective-permute-start(bf16[1536,768]{1,0:T(8,128)(2,1)} %down_own.1), channel_id=1, source_target_pairs={{0,1},{1,0},{2,3},{3,2},{4,5},{5,4},{6,7},{7,6},{8,9},{9,8},{10,11... | collective-permute-start | bytes 7077896 | tf_op jit(solution)/shard_map/ppermute | solution.py:558
  86.5 78.1 %collective-permute-start.19 = (bf16[384,768]{1,0:T(8,128)(2,1)S(1)}, bf16[384,768]{1,0:T(8,128)(2,1)}, u32[]{:S(2)}, u32[]{:S(2)}) collective-permute-start(bf16[384,768]{1,0:T(8,128)(2,1)S(1)} %copy-done.4), channel_id=1, source_target_pairs={{0,1},{1,0},{2,3},{3,2},{4,5},{5,4},{6,7},{7,6},{8,9},{9,8},{10,11... | collective-permute-start | bytes 1769480 | tf_op jit(solution)/shard_map/ppermute | solution.py:558
  130.0 17.5 %all-to-all-start.4 = ((f32[16,8,640]{2,1,0:T(8,128)}), f32[16,8,640]{2,1,0:T(8,128)S(1)}, u32[]{:S(2)}, u32[]{:S(2)}) async-start(f32[16,8,640]{2,1,0:T(8,128)} %bitcast.18), calls=%async_computation.4 | async-start | bytes 655360 | tf_op jit(solution)/shard_map/all_to_all | solution.py:554
  148.5 17.4 %all-to-all-start.5 = ((bf16[32,8,384]{2,1,0:T(8,128)(2,1)}), bf16[32,8,384]{2,1,0:T(8,128)(2,1)S(1)}, u32[]{:S(2)}, u32[]{:S(2)}) async-start(bf16[32,8,384]{2,1,0:T(8,128)(2,1)} %shard_map.107), calls=%async_computation.5 | async-start | bytes 393216 | tf_op jit(solution)/shard_map/all_to_all | solution.py:554
  157.6 8.0 %collective-permute-start.17 = (bf16[256,256]{1,0:T(8,128)(2,1)S(1)}, bf16[256,256]{1,0:T(8,128)(2,1)S(1)}, u32[]{:S(2)}, u32[]{:S(2)}) collective-permute-start(bf16[256,256]{1,0:T(8,128)(2,1)S(1)} %shard_map.105.own_ref), channel_id=1, source_target_pairs={{0,1},{1,0},{2,3},{3,2},{4,5},{5,4},{6,7},{7,6},{8,9},{9,8},{10,11... | collective-permute-start | bytes 393224 | tf_op jit(solution)/shard_map/ppermute | solution.py:558
  (18 other events, 122.8 us)

commit v6 on v5

--- a/solution.py
+++ b/solution.py
@@ -16,6 +16,7 @@
 BF16 = jnp.bfloat16
 F32 = jnp.float32
 LIMIT = 51 * 1024 * 1024
+HIGH = 60 * 1024 * 1024
 SLOTS = 10
 MORE = 16 - SLOTS
 STRIDE = SLOTS * 64 + 48
@@ -32,29 +33,31 @@
     return jnp.dot(a, b, preferred_element_type=F32)
 
 
-def call(kernel, outs, scratch, cost, arrays, raw=(), near=(), scalars=(), by_hand=(), tables=()):
+def call(kernel, outs, scratch, cost, arrays, raw=(), near=(), scalars=(), by_hand=(), held=(), tables=(), limit=LIMIT):
     single = not isinstance(outs, tuple)
     results = (outs,) if single else outs
+    away = [i for i in range(len(results)) if i not in held]
     count, total = len(arrays), len(arrays) + len(raw) + len(near) + len(scalars)
 
     def body(*refs):
         inputs, others = refs[:count], refs[count:total]
         outputs = refs[total : total + len(results)]
         listed = refs[total + len(results) : total + len(results) + len(tables)]
-        held = refs[total + len(results) + len(tables) :]
+        left = refs[total + len(results) + len(tables) :]
         copied, made, (sem_in, sem_out), rest = (
-            held[:count],
-            held[count : count + len(results)],
-            held[count + len(results) : count + len(results) + 2],
-            held[count + len(results) + 2 :],
+            left[:count],
+            left[count : count + len(away)],
+            left[count + len(away) : count + len(away) + 2],
+            left[count + len(away) + 2 :],
         )
         copies = [pltpu.make_async_copy(inputs[i], copied[i], sem_in.at[i]) for i in range(count)]
         for copy in copies:
             copy.start()
         for copy in copies:
             copy.wait()
-        kernel(*copied, *others, *made, *[outputs[i] for i in by_hand], *listed, *rest)
-        copies = [pltpu.make_async_copy(made[i], outputs[i], sem_out.at[i]) for i in range(len(results)) if i not in by_hand]
+        places = [made[away.index(i)] if i in away else outputs[i] for i in range(len(results))]
+        kernel(*copied, *others, *places, *[outputs[i] for i in by_hand], *listed, *rest)
+        copies = [pltpu.make_async_copy(places[i], outputs[i], sem_out.at[i]) for i in away if i not in by_hand]
         for copy in copies:
             copy.start()
         for copy in copies:
@@ -64,12 +67,12 @@
         body,
         out_shape=(*results, *tables),
         in_specs=[FAR] * (count + len(raw)) + [NEAR] * len(near) + [SMEM] * len(scalars),
-        out_specs=(FAR,) * len(results) + (SMEM,) * len(tables),
-        scratch_shapes=[pltpu.VMEM(v.shape, v.dtype) for v in (*arrays, *results)]
+        out_specs=tuple(FAR if i in away else NEAR for i in range(len(results))) + (SMEM,) * len(tables),
+        scratch_shapes=[pltpu.VMEM(v.shape, v.dtype) for v in (*arrays, *[results[i] for i in away])]
         + [pltpu.SemaphoreType.DMA((max(count, 1),)), pltpu.SemaphoreType.DMA((len(results),))]
         + list(scratch),
         cost_estimate=pl.CostEstimate(flops=cost[0], bytes_accessed=cost[1], transcendentals=cost[2]),
-        compiler_params=pltpu.CompilerParams(vmem_limit_bytes=LIMIT),
+        compiler_params=pltpu.CompilerParams(vmem_limit_bytes=limit),
     )(*arrays, *raw, *near, *scalars)
     return made[0] if single and not tables else made
 
@@ -130,26 +133,20 @@
         raw=[states],
         scalars=[owner, local, ids, here],
         tables=(shape((1, 72), jnp.int32),),
-    )
-
-
-def arrange_kernel(weight_ref, wq_ref, wkv_ref):
-    wq_ref[...] = jnp.zeros_like(wq_ref)
+        limit=HIGH,
+    )
+
+
+def interleave(weight_ref, first, wkv_ref):
     for h in range(HEADS):
         part = slice(64 * h, 64 * h + 64)
-        wq_ref[:, 128 * h : 128 * h + 64] = weight_ref[0, :, part] * BF16(0.125)
-        wkv_ref[:, 128 * h : 128 * h + 64] = weight_ref[1, :, part]
-        wkv_ref[:, 128 * h + 64 : 128 * h + 128] = weight_ref[2, :, part]
-
-
-def arrange(weight):
-    square = jax.ShapeDtypeStruct((768, 768), BF16)
-    return call(arrange_kernel, (square, square), [], (2_000_000, 4_000_000, 0), [weight])
+        wkv_ref[:, 128 * h : 128 * h + 64] = weight_ref[first, :, part]
+        wkv_ref[:, 128 * h + 64 : 128 * h + 128] = weight_ref[first + 1, :, part]
 
 
 def column_kernel(*refs):
     pieces = refs[1:17]
-    wkv_ref = refs[0]
+    weight_far = refs[0]
     (
         received_ref,
         shares_ref,
@@ -162,13 +159,15 @@
         flag_ref,
         asked_ref,
         rows_ref,
+        weight_ref,
+        wkv_ref,
         sem,
         sems,
-        sem_rows,
     ) = refs[17:]
-    copies = [pltpu.make_async_copy(piece, rows_ref.at[pl.ds(128 * i, 128), :], sem_rows.at[i]) for i, piece in enumerate(pieces)]
-    for copy in copies:
-        copy.start()
+    weight = pltpu.make_async_copy(weight_far.at[pl.ds(1, 2)], weight_ref, sem.at[1])
+    weight.start()
+    for i, piece in enumerate(pieces):
+        rows_ref[128 * i : 128 * i + 128, :] = piece[...]
     for p in range(16):
         asked_ref[p : p + 1, :] = received_ref[p, 48:49, :].astype(F32).astype(jnp.int32)
     asked = pltpu.make_async_copy(asked_ref, wanted_ref, sem.at[0])
@@ -177,13 +176,16 @@
     share = shares_ref[(owner >> 2) & 7]
     for p in range(16):
         items_ref[p, SLOTS * 64 : STRIDE, :] = share
-    for i in range(4):
-        for copy in copies[4 * i : 4 * i + 4]:
-            copy.wait()
-        pair = nn(rows_ref[512 * i : 512 * i + 512, :], wkv_ref[...]).astype(BF16)
+    weight.wait()
+    interleave(weight_ref, 0, wkv_ref)
+
+    @pl.loop(0, 4)
+    def _(i):
+        pair = nn(rows_ref[pl.ds(pl.multiple_of(i * 512, 512), 512), :], wkv_ref[...]).astype(BF16)
         for j in range(4):
             for h in range(HEADS):
                 kv_ref[(4 * i + j) * HEADS + h] = pair[128 * j : 128 * j + 128, 128 * h : 128 * h + 128]
+
     asked.wait()
     flag = wanted_ref[0, 127]
     for p in range(1, 16):
@@ -203,7 +205,7 @@
         pltpu.make_async_copy(items_ref.at[p], out_ref.at[p], sems.at[p]).wait()
 
 
-def column(pieces, wkv, received, shares, ids, here):
+def column(pieces, weight, received, shares, ids, here):
     shape = jax.ShapeDtypeStruct
     return call(
         column_kernel,
@@ -211,16 +213,18 @@
         [
             pltpu.VMEM((16, 128), jnp.int32),
             pltpu.VMEM((2048, 768), BF16),
-            pltpu.SemaphoreType.DMA((1,)),
-            pltpu.SemaphoreType.DMA((16,)),
+            pltpu.VMEM((2, 768, 384), BF16),
+            pltpu.VMEM((768, 768), BF16),
+            pltpu.SemaphoreType.DMA((2,)),
             pltpu.SemaphoreType.DMA((16,)),
         ],
         (2_400_000_000, 10_000_000, 0),
-        [wkv],
-        raw=pieces,
-        near=[received, shares],
+        [],
+        raw=[weight],
+        near=[*pieces, received, shares],
         scalars=[ids, here],
         by_hand=(1,),
+        held=(0,),
         tables=(shape((16, 128), jnp.int32), shape((1, 1), jnp.int32)),
     )
 
@@ -236,7 +240,7 @@
 
 def extra(kv, wanted):
     shape = jax.ShapeDtypeStruct((16, MORE * 64, 128), BF16)
-    items = call(extra_kernel, shape, [], (0, 5_000_000, 0), [kv], scalars=[wanted])
+    items = call(extra_kernel, shape, [], (0, 5_000_000, 0), [], near=[kv], scalars=[wanted])
     return exchanged(items, PLANE)
 
 
@@ -255,7 +259,11 @@
     )()
 
 
-def window_kernel(before_ref, states_ref, after_ref, wq_ref, wkv_ref, q_ref, ext_ref, rows_ref):
+def window_kernel(before_ref, states_ref, after_ref, weight_ref, q_ref, ext_ref, wq_ref, wkv_ref, rows_ref):
+    wq_ref[...] = jnp.zeros_like(wq_ref)
+    for h in range(HEADS):
+        wq_ref[:, 128 * h : 128 * h + 64] = weight_ref[0, :, 64 * h : 64 * h + 64] * BF16(0.125)
+    interleave(weight_ref, 1, wkv_ref)
     rows_ref[0:64, :] = before_ref[...]
     rows_ref[64:320, :] = states_ref[...]
     rows_ref[320:384, :] = after_ref[...]
@@ -266,20 +274,20 @@
         q_ref[h] = query[:, 128 * h : 128 * h + 128]
 
 
-def window(before, states, after, wq, wkv):
+def window(before, states, after, weight):
     shape = jax.ShapeDtypeStruct
+    square = shape((768, 768), BF16)
     return call(
         window_kernel,
-        (shape((HEADS, 256, 128), BF16), shape((HEADS, 384, 128), BF16)),
+        (shape((HEADS, 256, 128), BF16), shape((HEADS, 384, 128), BF16), square, square),
         [pltpu.VMEM((384, 768), BF16)],
         (800_000_000, 4_000_000, 0),
-        [before, states, after, wq, wkv],
-    )
-
-
-def partial_kernel(wq_ref, wkv_ref, kv_far, remote_ref, out_ref, pair_ref, rows_ref, q_ref, s_ref, kv_ref, sem):
-    keep = pltpu.make_async_copy(kv_far, kv_ref, sem.at[0])
-    keep.start()
+        [before, states, after, weight],
+        held=(0, 1, 2, 3),
+    )
+
+
+def partial_kernel(wq_ref, wkv_ref, kv_ref, remote_ref, out_ref, pair_ref, rows_ref, q_ref, s_ref):
     for p in range(16):
         for c in range(3):
             lanes = (p % 2) * 384 + c * 128
@@ -290,7 +298,6 @@
     for h in range(HEADS):
         q_ref[h] = query[:, 128 * h : 128 * h + 128]
         pair_ref[h] = pair[:, 128 * h : 128 * h + 128]
-    keep.wait()
     lane = lax.broadcasted_iota(jnp.int32, (128, 128), 1)
     highs = jnp.zeros((128, 128), F32)
     totals = jnp.zeros((128, 128), F32)
@@ -306,9 +313,7 @@
         for c in range(4):
             p = jnp.exp(s_ref[h % 2, :, c * 512 : c * 512 + 512] - high)
             total = total + jnp.sum(p, axis=1, keepdims=True)
-            head = p.astype(BF16)
-            rest = (p - head.astype(F32)).astype(BF16)
-            acc = acc + nn(head, keys[c]) + nn(rest, keys[c])
+            acc = acc + nn(p.astype(BF16), keys[c])
         out_ref[:, 64 * h : 64 * h + 64] = acc[:, 64:128]
         highs = jnp.where(lane == h, high, highs)
         totals = jnp.where(lane == h, total, totals)
@@ -325,13 +330,11 @@
             pltpu.VMEM((128, 768), BF16),
             pltpu.VMEM((HEADS, 128, 128), BF16),
             pltpu.VMEM((2, 128, 2048), F32),
-            pltpu.VMEM((16, HEADS, 128, 128), BF16),
-            pltpu.SemaphoreType.DMA((1,)),
         ],
         (2_000_000_000, 10_000_000, 1_600_000),
-        [wq, wkv],
-        raw=[kv],
-        near=[remote],
+        [],
+        near=[wq, wkv, kv, remote],
+        held=(1,),
     )
 
 
@@ -414,8 +417,8 @@
         jax.ShapeDtypeStruct((256, 128 * count), BF16),
         [pltpu.VMEM((24 * count, 64, 128), BF16), pltpu.VMEM((8, 512, 128), BF16)],
         (200_000_000 * count, 1_500_000 * count, 270_000 * count),
-        [q, ext, pair],
-        near=[remote, more],
+        [],
+        near=[q, ext, pair, remote, more],
         scalars=[slots, here, flag],
     )
 
@@ -567,16 +570,18 @@
     tied = lax.optimization_barrier
 
     up0 = lax.dynamic_slice_in_dim(states, core * 128, 128, 0)
+    ends = [(i, i + 1) for i in range(127)]
+    before = lax.ppermute(states[192:], SEQ, ends)
+    after = lax.ppermute(states[:64], SEQ, [(j, i) for i, j in ends])
     up1, down1, far0 = turned(up0, "z", 1), turned(up0, "z", -1), swapped(up0)
     order = (0, 3, 1, 2)
     spread, slots = plan(states, random_owner.transpose(order), random_local.transpose(order), ids, here)
-    up1, down1, far0, spread = tied((up1, down1, far0, spread))
+    up1, down1, far0, spread, before, after = tied((up1, down1, far0, spread, before, after))
 
     up2, down2 = turned(up1, "z", 1), turned(down1, "z", -1)
     far1, far7 = swapped(up1), swapped(down1)
     received = exchanged(spread, PLANE)
-    wq, wkv = arrange(qkv_weight)
-    up2, down2, far1, far7, wkv = tied((up2, down2, far1, far7, wkv))
+    up2, down2, far1, far7 = tied((up2, down2, far1, far7))
 
     up3, down3 = turned(up2, "z", 1), turned(down2, "z", -1)
     far2, far6 = swapped(up2), swapped(down2)
@@ -588,18 +593,15 @@
     up4 = turned(up3, "z", 1)
     shares = exchanged(jnp.broadcast_to(share, (8, 48, 128)), "z")
     far3, far5 = swapped(up3), swapped(down3)
-    ends = [(i, i + 1) for i in range(127)]
-    before = lax.ppermute(states[192:], SEQ, ends)
-    after = lax.ppermute(states[:64], SEQ, [(j, i) for i, j in ends])
-    up4, far3, far5, shares, before, after = tied((up4, far3, far5, shares, before, after))
+    up4, far3, far5, shares = tied((up4, far3, far5, shares))
 
     pieces = [up0, up1, up2, up3, up4, down3, down2, down1, far0, far1, far2, far3, swapped(up4), far5, far6, far7]
-    pairs, items, wanted, flag = column(pieces, wkv, received, shares, ids, here)
+    pairs, items, wanted, flag = column(pieces, qkv_weight, received, shares, ids, here)
     more = lax.cond(flag[0, 0] > 0, lambda: extra(pairs, wanted), unused)
     items, more, weights = tied((items, more, (out_weight, up_weight, down_weight)))
     remote = exchanged(items, PLANE)
     wo_other, up_other, down_other = (swapped(weight) for weight in weights)
-    q, ext = window(before, states, after, wq, wkv)
+    q, ext, wq, wkv = window(before, states, after, qkv_weight)
     remote, ext = tied((remote, ext))
     part, pair = partial(wq, wkv, remote, pairs.reshape(16, HEADS, 128, 128))
     parts = exchanged(part.reshape(16, 8, 640), PLANE)

time: 176 us -> 167 us (0.949)
  blocking collectives: 0 us -> 11.6 us
  Pallas kernels: 57 us -> 47.4 us
  waiting for transfers between devices: 40.1 us -> 35.3 us
  starting transfers between devices: 64.6 us -> 61.4 us
  local copies, waits for them, and re-layouts: 10.4 us -> 7.76 us
    all_to_all x0 -> x1, blocking collectives: none -> 11.6 us  [exchanged(): return lax.all_to_all(value, axes, split_axis=0, concat_axis=0, tiled=True)]
    pallas_call x8 -> x7, Pallas kernels: 47.9 us -> 39 us  [call(): pl.pallas_call(body, out_shape=(*results, *tables), in_specs=[FAR] * (cou...]
    all_to_all x5 -> x4, starting transfers between devices: 39.1 us -> 33.7 us  [exchanged(): return lax.all_to_all(value, axes, split_axis=0, concat_axis=0, tiled=True)]
    ppermute x1, waiting for transfers between devices: 4.04 us -> 0.88 us  [shards(): after = lax.ppermute(states[:64], SEQ, [(j, i) for i, j in ends])]
    unnamed x30 -> x28, local copies, waits for them, and re-layouts: 7.37 us -> 4.48 us
    all_to_all x5 -> x4, waiting for transfers between devices: 32.6 us -> 32.4 us  [exchanged(): return lax.all_to_all(value, axes, split_axis=0, concat_axis=0, tiled=True)]
  transfers between devices with their start and end apart: 27 -> 26, of which waited for: 7 -> 6; matrix products, arithmetic and copies ran while one was open for 1% -> 2% of each run, Pallas kernels for 20% -> 18%
where the time goes in v6:
time: 167 us
  starting transfers between devices  61.4 us (37%)
  Pallas kernels  47.4 us (28%)
  waiting for transfers between devices  35.3 us (21%)
  blocking collectives  11.6 us (7%)
  local copies, waits for them, and re-layouts  7.76 us (5%)
  between operations  2.44 us (1%)
    pallas_call x7, Pallas kernels, call(): pl.pallas_call(body, out_shape=(*results, *tables), in_specs=[FAR] * (cou...  39 us
    all_to_all x4, starting transfers between devices, exchanged(): return lax.all_to_all(value, axes, split_axis=0, concat_axis=0, tiled=True)  33.7 us
    all_to_all x4, waiting for transfers between devices, exchanged(): return lax.all_to_all(value, axes, split_axis=0, concat_axis=0, tiled=True)  32.4 us
    ppermute x7, starting transfers between devices, turned(): lax.ppermute(value, axis, [(i, (i + shift) % count) for i in range(count)])  13.3 us
    all_to_all x1, blocking collectives, exchanged(): return lax.all_to_all(value, axes, split_axis=0, concat_axis=0, tiled=True)  11.6 us
    ppermute x13, starting transfers between devices, swapped(): return lax.ppermute(value, 'mp', [(0, 1), (1, 0)])  9.9 us
    pallas_call x1, Pallas kernels, finish(): pl.pallas_call(finish_kernel, out_shape=jax.ShapeDtypeStruct((256, 768),...  8.43 us
    unnamed x28, local copies, waits for them, and re-layouts  4.48 us
  transfers between devices with their start and end apart: 26, of which 6 were waited for; matrix products, arithmetic and copies ran while one was open for 2% of the time, Pallas kernels for 18%

profile of v6, /device:TPU:1, one launch (start us, length us, event | category | flops | bytes accessed | tf_op | source)
XLA Modules:
  0.0 166.5 jit_solution(14107087093312530544)
XLA Ops:
  0.9 2.5 %collective-permute-start = (bf16[128,768]{1,0:T(8,128)(2,1)S(1)}, bf16[128,768]{1,0:T(8,128)(2,1)S(1)}, u32[]{:S(2)}, u32[]{:S(2)}) collective-permute-start(bf16[128,768]{1,0:T(8,128)(2,1)S(1)} %constant_dynamic-slice_fusion.refs_1_), channel_id=1, source_target_pairs={{0,8},{8,16},{16,24},{24,32},{32,40},{40,48},{48,56},{56,0},{1,9},... | collective-permute-start | bytes 589832 | tf_op jit(solution)/shard_map/ppermute | solution.py:553
  3.5 4.0 %collective-permute-start.1 = (bf16[128,768]{1,0:T(8,128)(2,1)S(1)}, bf16[128,768]{1,0:T(8,128)(2,1)S(1)}, u32[]{:S(2)}, u32[]{:S(2)}) collective-permute-start(bf16[128,768]{1,0:T(8,128)(2,1)S(1)} %constant_dynamic-slice_fusion.refs_1_), channel_id=1, source_target_pairs={{0,56},{8,0},{16,8},{24,16},{32,24},{40,32},{48,40},{56,48},{1,57}... | collective-permute-start | bytes 589832 | tf_op jit(solution)/shard_map/ppermute | solution.py:553
  9.4 3.2 %collective-permute-start.3 = (bf16[64,768]{1,0:T(8,128)(2,1)S(1)}, bf16[64,768]{1,0:T(8,128)(2,1)S(1)}, u32[]{:S(2)}, u32[]{:S(2)}) collective-permute-start(bf16[64,768]{1,0:T(8,128)(2,1)S(1)} %get-tuple-element.95), channel_id=1, source_target_pairs={{0,2},{2,4},{4,6},{6,8},{8,10},{10,12},{12,14},{14,16},{16,18},{18... | collective-permute-start | bytes 294920 | tf_op jit(solution)/shard_map/ppermute | solution.py:574
  12.6 1.3 collective-permute-start.4
  14.6 3.1 %shard_map.100 = (bf16[16,64,128]{2,1,0:T(8,128)(2,1)}, s32[1,72]{1,0:T(1,128)}) custom-call(bf16[256,768]{1,0:T(8,128)(2,1)} %states_ref.1, s32[1,3,4,6]{3,2,1,0:T(4,128)} %bitcast.25, s32[1,3,4,6]{3,2,1,0:T(4,128)} %bitcast.26, s32[1,2]{1,0:T(1,128)} %bitcast.19, s32[1,4]{1,0:T(1,128)} %add_bitcast_fusion.refs_4_.refs_20_.refs_6_.here_ref), custom_call_target="tpu_custom_call" | custom-call | flops 1000000 | bytes 600000 | tf_op jit(solution)/shard_map/pallas_call | solution.py:66
  18.7 2.5 %collective-permute-start.5 = (bf16[128,768]{1,0:T(8,128)(2,1)S(1)}, bf16[128,768]{1,0:T(8,128)(2,1)S(1)}, u32[]{:S(2)}, u32[]{:S(2)}) collective-permute-start(bf16[128,768]{1,0:T(8,128)(2,1)S(1)} %collective-permute-done.refs_2_), channel_id=1, source_target_pairs={{0,8},{8,16},{16,24},{24,32},{32,40},{40,48},{48,56},{56,0},{1,9},... | collective-permute-start | bytes 589832 | tf_op jit(solution)/shard_map/ppermute | solution.py:553
  21.1 1.4 collective-permute-start.6
  23.4 9.3 %all-to-all-start.1 = ((bf16[16,64,128]{2,1,0:T(8,128)(2,1)}), bf16[16,64,128]{2,1,0:T(8,128)(2,1)S(1)}, u32[]{:S(2)}, u32[]{:S(2)}) async-start(bf16[16,64,128]{2,1,0:T(8,128)(2,1)} %get-tuple-element.63), calls=%async_computation.1 | async-start | bytes 524288 | tf_op jit(solution)/shard_map/all_to_all | solution.py:557
  32.8 2.7 %collective-permute-start.10 = (bf16[128,768]{1,0:T(8,128)(2,1)S(1)}, bf16[128,768]{1,0:T(8,128)(2,1)S(1)}, u32[]{:S(2)}, u32[]{:S(2)}) collective-permute-start(bf16[128,768]{1,0:T(8,128)(2,1)S(1)} %collective-permute-done.6.refs_7_), channel_id=1, source_target_pairs={{0,56},{8,0},{16,8},{24,16},{32,24},{40,32},{48,40},{56,48},{1,57}... | collective-permute-start | bytes 589832 | tf_op jit(solution)/shard_map/ppermute | solution.py:553
  35.5 1.3 collective-permute-start.11
  36.8 1.4 fusion.1
  40.3 2.1 %collective-permute-start.14 = (bf16[128,768]{1,0:T(8,128)(2,1)S(1)}, bf16[128,768]{1,0:T(8,128)(2,1)S(1)}, u32[]{:S(2)}, u32[]{:S(2)}) collective-permute-start(bf16[128,768]{1,0:T(8,128)(2,1)S(1)} %collective-permute-done.9.refs_4_), channel_id=1, source_target_pairs={{0,1},{1,0},{2,3},{3,2},{4,5},{5,4},{6,7},{7,6},{8,9},{9,8},{10,11... | collective-permute-start | bytes 589832 | tf_op jit(solution)/shard_map/ppermute | solution.py:561
  42.5 11.6 %all_to_all.30.refs_18_ = bf16[8,48,128]{2,1,0:T(8,128)(2,1)S(1)} all-to-all(bf16[8,48,128]{2,1,0:T(8,128)(2,1)S(1)} %broadcast_in_dim.8), channel_id=1, replica_groups=mesh['x'=4,'z'=8,'y'=4,'mp'=2] {'z'}, dimensions={0} | all-to-all | bytes 196608 | tf_op jit(solution)/shard_map/all_to_all | solution.py:557
  54.1 2.3 %collective-permute-start.16 = (bf16[128,768]{1,0:T(8,128)(2,1)S(1)}, bf16[128,768]{1,0:T(8,128)(2,1)S(1)}, u32[]{:S(2)}, u32[]{:S(2)}) collective-permute-start(bf16[128,768]{1,0:T(8,128)(2,1)S(1)} %collective-permute-done.13.refs_5_), channel_id=1, source_target_pairs={{0,1},{1,0},{2,3},{3,2},{4,5},{5,4},{6,7},{7,6},{8,9},{9,8},{10,11... | collective-permute-start | bytes 589832 | tf_op jit(solution)/shard_map/ppermute | solution.py:561
  58.8 9.7 %shard_map.102 = (bf16[96,128,128]{2,1,0:T(8,128)(2,1)}, bf16[16,688,128]{2,1,0:T(8,128)(2,1)}, s32[16,128]{1,0:T(8,128)S(1)}, s32[1,1]{1,0:T(1,128)}) custom-call(bf16[3,768,384]{2,1,0:T(8,128)(2,1)} %refs_0_.3, bf16[128,768]{1,0:T(8,128)(2,1)S(1)} %constant_dynamic-slice_fusion.refs_1_, bf16[128,768]{1,0:T(8,128)(2,1)S(1)} %collective-permute-done.refs_2_, ...), custom_call_target="tpu_custom_call" | custom-call | flops 2400000000 | bytes 10000000 | tf_op jit(solution)/shard_map/pallas_call | solution.py:66
  70.3 6.8 %all-to-all-start.3 = ((bf16[16,688,128]{2,1,0:T(8,128)(2,1)}), bf16[16,688,128]{2,1,0:T(8,128)(2,1)}, u32[]{:S(2)}, u32[]{:S(2)}) async-start(bf16[16,688,128]{2,1,0:T(8,128)(2,1)} %get-tuple-element.80), calls=%async_computation.3 | async-start | bytes 5636096 | tf_op jit(solution)/shard_map/all_to_all | solution.py:557
  78.0 4.4 %shard_map.101 = (bf16[6,256,128]{2,1,0:T(8,128)(2,1)S(1)}, bf16[6,384,128]{2,1,0:T(8,128)(2,1)S(1)}, bf16[768,768]{1,0:T(8,128)(2,1)S(1)}, bf16[768,768]{1,0:T(8,128)(2,1)}) custom-call(bf16[64,768]{1,0:T(8,128)(2,1)S(1)} %collective-permute-done.3.refs_0_, bf16[256,768]{1,0:T(8,128)(2,1)S(1)} %copy-done, ...), custom_call_target="tpu_custom_call" | custom-call | flops 800000000 | bytes 4000000 | tf_op jit(solution)/shard_map/pallas_call | solution.py:66
  82.9 31.2 %all-to-all-done.3.refs_3_ = bf16[16,688,128]{2,1,0:T(8,128)(2,1)} async-done(((bf16[16,688,128]{2,1,0:T(8,128)(2,1)}), bf16[16,688,128]{2,1,0:T(8,128)(2,1)}, u32[]{:S(2)}, u32[]{:S(2)}) %all-to-all-start.3) | async-done | bytes 2818080 | tf_op jit(solution)/shard_map/all_to_all | solution.py:557
  115.3 6.3 %shard_map.103 = (f32[128,640]{1,0:T(8,128)S(1)}, bf16[6,128,128]{2,1,0:T(8,128)(2,1)S(1)}) custom-call(bf16[768,768]{1,0:T(8,128)(2,1)S(1)} %get-tuple-element.57.refs_0_, bf16[768,768]{1,0:T(8,128)(2,1)S(1)} %copy-done.1, bf16[16,6,128,128]{3,2,1,0:T(8,128)(2,1)} %bitcast.24, bf16[16,688,128]{2,1,0:T(8,128)(2,1)} %all-to-all-done.3.refs_3_), custom_call_target="tpu_custom_call" | custom-call | flops 2000000000 | bytes 10000000 | tf_op jit(solution)/shard_map/pallas_call | solution.py:66
  122.4 8.5 %all-to-all-start.4 = ((f32[16,8,640]{2,1,0:T(8,128)}), f32[16,8,640]{2,1,0:T(8,128)S(1)}, u32[]{:S(2)}, u32[]{:S(2)}) async-start(f32[16,8,640]{2,1,0:T(8,128)} %bitcast.18), calls=%async_computation.4 | async-start | bytes 655360 | tf_op jit(solution)/shard_map/all_to_all | solution.py:557
  130.9 8.7 %shard_map.104.own_ref = bf16[256,256]{1,0:T(8,128)(2,1)S(1)} custom-call(bf16[6,256,128]{2,1,0:T(8,128)(2,1)S(1)} %get-tuple-element.84.refs_0_, bf16[6,384,128]{2,1,0:T(8,128)(2,1)S(1)} %get-tuple-element.85.refs_1_, bf16[6,128,128]{2,1,0:T(8,128)(2,1)S(1)} %get-tuple-element.86.refs_2_, bf16[11008,128]{1,0:T(8,128)(2,1)} %bitcast.14.refs_3_, ...), custom_call_target="tpu_custom_call" | custom-call | flops 400000000 | bytes 3000000 | tf_op jit(solution)/shard_map/pallas_call | solution.py:66
  140.5 9.1 %all-to-all-start.5 = ((bf16[32,8,384]{2,1,0:T(8,128)(2,1)}), bf16[32,8,384]{2,1,0:T(8,128)(2,1)S(1)}, u32[]{:S(2)}, u32[]{:S(2)}) async-start(bf16[32,8,384]{2,1,0:T(8,128)(2,1)} %shard_map.106), calls=%async_computation.5 | async-start | bytes 393216 | tf_op jit(solution)/shard_map/all_to_all | solution.py:557
  150.2 5.9 %shard_map.105.own2_ref = bf16[256,128]{1,0:T(8,128)(2,1)S(1)} custom-call(bf16[6,256,128]{2,1,0:T(8,128)(2,1)S(1)} %get-tuple-element.84.refs_0_, bf16[6,384,128]{2,1,0:T(8,128)(2,1)S(1)} %get-tuple-element.85.refs_1_, bf16[6,128,128]{2,1,0:T(8,128)(2,1)S(1)} %get-tuple-element.86.refs_2_, bf16[11008,128]{1,0:T(8,128)(2,1)} %bitcast.14.refs_3_, ...), custom_call_target="tpu_custom_call" | custom-call | flops 200000000 | bytes 1500000 | tf_op jit(solution)/shard_map/pallas_call | solution.py:66
  157.9 8.4 %shard_map.107 = bf16[256,768]{1,0:T(8,128)(2,1)} custom-call(bf16[256,256]{1,0:T(8,128)(2,1)S(1)} %shard_map.104.own_ref, bf16[256,256]{1,0:T(8,128)(2,1)S(1)} %collective-permute-done.17.other_ref, bf16[256,128]{1,0:T(8,128)(2,1)S(1)} %shard_map.105.own2_ref, bf16[256,128]{1,0:T(8,128)(2,1)S(1)} %collective-permute-done.18.other2_ref, ...), custom_call_target="tpu_custom_call" | custom-call | flops 2700000000 | bytes 12000000 | tf_op jit(solution)/shard_map/pallas_call | solution.py:529
  (75 shorter events, 16.5 us)
Async XLA Ops:
  0.9 17.7 %collective-permute-start = (bf16[128,768]{1,0:T(8,128)(2,1)S(1)}, bf16[128,768]{1,0:T(8,128)(2,1)S(1)}, u32[]{:S(2)}, u32[]{:S(2)}) collective-permute-start(bf16[128,768]{1,0:T(8,128)(2,1)S(1)} %constant_dynamic-slice_fusion.refs_1_), channel_id=1, source_target_pairs={{0,8},{8,16},{16,24},{24,32},{32,40},{40,48},{48,56},{56,0},{1,9},... | collective-permute-start | bytes 589832 | tf_op jit(solution)/shard_map/ppermute | solution.py:553
  3.5 15.2 %collective-permute-start.1 = (bf16[128,768]{1,0:T(8,128)(2,1)S(1)}, bf16[128,768]{1,0:T(8,128)(2,1)S(1)}, u32[]{:S(2)}, u32[]{:S(2)}) collective-permute-start(bf16[128,768]{1,0:T(8,128)(2,1)S(1)} %constant_dynamic-slice_fusion.refs_1_), channel_id=1, source_target_pairs={{0,56},{8,0},{16,8},{24,16},{32,24},{40,32},{48,40},{56,48},{1,57}... | collective-permute-start | bytes 589832 | tf_op jit(solution)/shard_map/ppermute | solution.py:553
  7.5 11.1 %collective-permute-start.2 = (bf16[128,768]{1,0:T(8,128)(2,1)S(1)}, bf16[128,768]{1,0:T(8,128)(2,1)S(1)}, u32[]{:S(2)}, u32[]{:S(2)}) collective-permute-start(bf16[128,768]{1,0:T(8,128)(2,1)S(1)} %constant_dynamic-slice_fusion.refs_1_), channel_id=1, source_target_pairs={{0,1},{1,0},{2,3},{3,2},{4,5},{5,4},{6,7},{7,6},{8,9},{9,8},{10,11... | collective-permute-start | bytes 589832 | tf_op jit(solution)/shard_map/ppermute | solution.py:561
  9.4 8.3 %collective-permute-start.3 = (bf16[64,768]{1,0:T(8,128)(2,1)S(1)}, bf16[64,768]{1,0:T(8,128)(2,1)S(1)}, u32[]{:S(2)}, u32[]{:S(2)}) collective-permute-start(bf16[64,768]{1,0:T(8,128)(2,1)S(1)} %get-tuple-element.95), channel_id=1, source_target_pairs={{0,2},{2,4},{4,6},{6,8},{8,10},{10,12},{12,14},{14,16},{16,18},{18... | collective-permute-start | bytes 294920 | tf_op jit(solution)/shard_map/ppermute | solution.py:574
  12.6 6.0 %collective-permute-start.4 = (bf16[64,768]{1,0:T(8,128)(2,1)S(1)}, bf16[64,768]{1,0:T(8,128)(2,1)S(1)}, u32[]{:S(2)}, u32[]{:S(2)}) collective-permute-start(bf16[64,768]{1,0:T(8,128)(2,1)S(1)} %get-tuple-element.94), channel_id=1, source_target_pairs={{2,0},{4,2},{6,4},{8,6},{10,8},{12,10},{14,12},{16,14},{18,16},{20... | collective-permute-start | bytes 294920 | tf_op jit(solution)/shard_map/ppermute | solution.py:575
  18.7 14.0 %collective-permute-start.5 = (bf16[128,768]{1,0:T(8,128)(2,1)S(1)}, bf16[128,768]{1,0:T(8,128)(2,1)S(1)}, u32[]{:S(2)}, u32[]{:S(2)}) collective-permute-start(bf16[128,768]{1,0:T(8,128)(2,1)S(1)} %collective-permute-done.refs_2_), channel_id=1, source_target_pairs={{0,8},{8,16},{16,24},{24,32},{32,40},{40,48},{48,56},{56,0},{1,9},... | collective-permute-start | bytes 589832 | tf_op jit(solution)/shard_map/ppermute | solution.py:553
  21.1 11.6 %collective-permute-start.6 = (bf16[128,768]{1,0:T(8,128)(2,1)S(1)}, bf16[128,768]{1,0:T(8,128)(2,1)S(1)}, u32[]{:S(2)}, u32[]{:S(2)}) collective-permute-start(bf16[128,768]{1,0:T(8,128)(2,1)S(1)} %collective-permute-done.1.refs_8_), channel_id=1, source_target_pairs={{0,56},{8,0},{16,8},{24,16},{32,24},{40,32},{48,40},{56,48},{1,57}... | collective-permute-start | bytes 589832 | tf_op jit(solution)/shard_map/ppermute | solution.py:553
  22.5 10.2 %collective-permute-start.7 = (bf16[128,768]{1,0:T(8,128)(2,1)S(1)}, bf16[128,768]{1,0:T(8,128)(2,1)S(1)}, u32[]{:S(2)}, u32[]{:S(2)}) collective-permute-start(bf16[128,768]{1,0:T(8,128)(2,1)S(1)} %collective-permute-done.refs_2_), channel_id=1, source_target_pairs={{0,1},{1,0},{2,3},{3,2},{4,5},{5,4},{6,7},{7,6},{8,9},{9,8},{10,11... | collective-permute-start | bytes 589832 | tf_op jit(solution)/shard_map/ppermute | solution.py:561
  23.4 9.4 %collective-permute-start.8 = (bf16[128,768]{1,0:T(8,128)(2,1)S(1)}, bf16[128,768]{1,0:T(8,128)(2,1)S(1)}, u32[]{:S(2)}, u32[]{:S(2)}) collective-permute-start(bf16[128,768]{1,0:T(8,128)(2,1)S(1)} %collective-permute-done.1.refs_8_), channel_id=1, source_target_pairs={{0,1},{1,0},{2,3},{3,2},{4,5},{5,4},{6,7},{7,6},{8,9},{9,8},{10,11... | collective-permute-start | bytes 589832 | tf_op jit(solution)/shard_map/ppermute | solution.py:561
  23.4 16.8 %all-to-all-start.1 = ((bf16[16,64,128]{2,1,0:T(8,128)(2,1)}), bf16[16,64,128]{2,1,0:T(8,128)(2,1)S(1)}, u32[]{:S(2)}, u32[]{:S(2)}) async-start(bf16[16,64,128]{2,1,0:T(8,128)(2,1)} %get-tuple-element.63), calls=%async_computation.1 | async-start | bytes 524288 | tf_op jit(solution)/shard_map/all_to_all | solution.py:557
  32.7 7.4 %collective-permute-start.9 = (bf16[128,768]{1,0:T(8,128)(2,1)S(1)}, bf16[128,768]{1,0:T(8,128)(2,1)S(1)}, u32[]{:S(2)}, u32[]{:S(2)}) collective-permute-start(bf16[128,768]{1,0:T(8,128)(2,1)S(1)} %collective-permute-done.5.refs_3_), channel_id=1, source_target_pairs={{0,8},{8,16},{16,24},{24,32},{32,40},{40,48},{48,56},{56,0},{1,9},... | collective-permute-start | bytes 589832 | tf_op jit(solution)/shard_map/ppermute | solution.py:553
  32.8 7.3 %collective-permute-start.10 = (bf16[128,768]{1,0:T(8,128)(2,1)S(1)}, bf16[128,768]{1,0:T(8,128)(2,1)S(1)}, u32[]{:S(2)}, u32[]{:S(2)}) collective-permute-start(bf16[128,768]{1,0:T(8,128)(2,1)S(1)} %collective-permute-done.6.refs_7_), channel_id=1, source_target_pairs={{0,56},{8,0},{16,8},{24,16},{32,24},{40,32},{48,40},{56,48},{1,57}... | collective-permute-start | bytes 589832 | tf_op jit(solution)/shard_map/ppermute | solution.py:553
  35.5 4.7 %collective-permute-start.11 = (bf16[128,768]{1,0:T(8,128)(2,1)S(1)}, bf16[128,768]{1,0:T(8,128)(2,1)S(1)}, u32[]{:S(2)}, u32[]{:S(2)}) collective-permute-start(bf16[128,768]{1,0:T(8,128)(2,1)S(1)} %collective-permute-done.5.refs_3_), channel_id=1, source_target_pairs={{0,1},{1,0},{2,3},{3,2},{4,5},{5,4},{6,7},{7,6},{8,9},{9,8},{10,11... | collective-permute-start | bytes 589832 | tf_op jit(solution)/shard_map/ppermute | solution.py:561
  40.2 13.9 %collective-permute-start.13 = (bf16[128,768]{1,0:T(8,128)(2,1)S(1)}, bf16[128,768]{1,0:T(8,128)(2,1)S(1)}, u32[]{:S(2)}, u32[]{:S(2)}) collective-permute-start(bf16[128,768]{1,0:T(8,128)(2,1)S(1)} %collective-permute-done.9.refs_4_), channel_id=1, source_target_pairs={{0,8},{8,16},{16,24},{24,32},{32,40},{40,48},{48,56},{56,0},{1,9},... | collective-permute-start | bytes 589832 | tf_op jit(solution)/shard_map/ppermute | solution.py:553
  40.3 13.8 %collective-permute-start.14 = (bf16[128,768]{1,0:T(8,128)(2,1)S(1)}, bf16[128,768]{1,0:T(8,128)(2,1)S(1)}, u32[]{:S(2)}, u32[]{:S(2)}) collective-permute-start(bf16[128,768]{1,0:T(8,128)(2,1)S(1)} %collective-permute-done.9.refs_4_), channel_id=1, source_target_pairs={{0,1},{1,0},{2,3},{3,2},{4,5},{5,4},{6,7},{7,6},{8,9},{9,8},{10,11... | collective-permute-start | bytes 589832 | tf_op jit(solution)/shard_map/ppermute | solution.py:561
  42.4 11.7 %collective-permute-start.15 = (bf16[128,768]{1,0:T(8,128)(2,1)S(1)}, bf16[128,768]{1,0:T(8,128)(2,1)S(1)}, u32[]{:S(2)}, u32[]{:S(2)}) collective-permute-start(bf16[128,768]{1,0:T(8,128)(2,1)S(1)} %collective-permute-done.10.refs_6_), channel_id=1, source_target_pairs={{0,1},{1,0},{2,3},{3,2},{4,5},{5,4},{6,7},{7,6},{8,9},{9,8},{10,11... | collective-permute-start | bytes 589832 | tf_op jit(solution)/shard_map/ppermute | solution.py:561
  54.1 3.4 %collective-permute-start.16 = (bf16[128,768]{1,0:T(8,128)(2,1)S(1)}, bf16[128,768]{1,0:T(8,128)(2,1)S(1)}, u32[]{:S(2)}, u32[]{:S(2)}) collective-permute-start(bf16[128,768]{1,0:T(8,128)(2,1)S(1)} %collective-permute-done.13.refs_5_), channel_id=1, source_target_pairs={{0,1},{1,0},{2,3},{3,2},{4,5},{5,4},{6,7},{7,6},{8,9},{9,8},{10,11... | collective-permute-start | bytes 589832 | tf_op jit(solution)/shard_map/ppermute | solution.py:561
  70.3 43.8 %all-to-all-start.3 = ((bf16[16,688,128]{2,1,0:T(8,128)(2,1)}), bf16[16,688,128]{2,1,0:T(8,128)(2,1)}, u32[]{:S(2)}, u32[]{:S(2)}) async-start(bf16[16,688,128]{2,1,0:T(8,128)(2,1)} %get-tuple-element.80), calls=%async_computation.3 | async-start | bytes 5636096 | tf_op jit(solution)/shard_map/all_to_all | solution.py:557
  77.1 79.3 %collective-permute-start.20 = (bf16[768,1536]{1,0:T(8,128)(2,1)}, bf16[768,1536]{1,0:T(8,128)(2,1)}, u32[]{:S(2)}, u32[]{:S(2)}) collective-permute-start(bf16[768,1536]{1,0:T(8,128)(2,1)} %up_own.1), channel_id=1, source_target_pairs={{0,1},{1,0},{2,3},{3,2},{4,5},{5,4},{6,7},{7,6},{8,9},{9,8},{10,11... | collective-permute-start | bytes 7077896 | tf_op jit(solution)/shard_map/ppermute | solution.py:561
  77.9 78.6 %collective-permute-start.21 = (bf16[1536,768]{1,0:T(8,128)(2,1)}, bf16[1536,768]{1,0:T(8,128)(2,1)}, u32[]{:S(2)}, u32[]{:S(2)}) collective-permute-start(bf16[1536,768]{1,0:T(8,128)(2,1)} %down_own.1), channel_id=1, source_target_pairs={{0,1},{1,0},{2,3},{3,2},{4,5},{5,4},{6,7},{7,6},{8,9},{9,8},{10,11... | collective-permute-start | bytes 7077896 | tf_op jit(solution)/shard_map/ppermute | solution.py:561
  82.4 74.0 %collective-permute-start.19 = (bf16[384,768]{1,0:T(8,128)(2,1)S(1)}, bf16[384,768]{1,0:T(8,128)(2,1)}, u32[]{:S(2)}, u32[]{:S(2)}) collective-permute-start(bf16[384,768]{1,0:T(8,128)(2,1)S(1)} %copy-done.2), channel_id=1, source_target_pairs={{0,1},{1,0},{2,3},{3,2},{4,5},{5,4},{6,7},{7,6},{8,9},{9,8},{10,11... | collective-permute-start | bytes 1769480 | tf_op jit(solution)/shard_map/ppermute | solution.py:561
  122.4 17.2 %all-to-all-start.4 = ((f32[16,8,640]{2,1,0:T(8,128)}), f32[16,8,640]{2,1,0:T(8,128)S(1)}, u32[]{:S(2)}, u32[]{:S(2)}) async-start(f32[16,8,640]{2,1,0:T(8,128)} %bitcast.18), calls=%async_computation.4 | async-start | bytes 655360 | tf_op jit(solution)/shard_map/all_to_all | solution.py:557
  140.5 17.4 %all-to-all-start.5 = ((bf16[32,8,384]{2,1,0:T(8,128)(2,1)}), bf16[32,8,384]{2,1,0:T(8,128)(2,1)S(1)}, u32[]{:S(2)}, u32[]{:S(2)}) async-start(bf16[32,8,384]{2,1,0:T(8,128)(2,1)} %shard_map.106), calls=%async_computation.5 | async-start | bytes 393216 | tf_op jit(solution)/shard_map/all_to_all | solution.py:557
  149.6 7.8 %collective-permute-start.17 = (bf16[256,256]{1,0:T(8,128)(2,1)S(1)}, bf16[256,256]{1,0:T(8,128)(2,1)S(1)}, u32[]{:S(2)}, u32[]{:S(2)}) collective-permute-start(bf16[256,256]{1,0:T(8,128)(2,1)S(1)} %shard_map.104.own_ref), channel_id=1, source_target_pairs={{0,1},{1,0},{2,3},{3,2},{4,5},{5,4},{6,7},{7,6},{8,9},{9,8},{10,11... | collective-permute-start | bytes 393224 | tf_op jit(solution)/shard_map/ppermute | solution.py:561
  (16 other events, 117.1 us)

commit v7 on v6

--- a/solution.py
+++ b/solution.py
@@ -419,6 +419,7 @@
         (200_000_000 * count, 1_500_000 * count, 270_000 * count),
         [],
         near=[q, ext, pair, remote, more],
+        held=(0,),
         scalars=[slots, here, flag],
     )
 
@@ -576,16 +577,16 @@
     up1, down1, far0 = turned(up0, "z", 1), turned(up0, "z", -1), swapped(up0)
     order = (0, 3, 1, 2)
     spread, slots = plan(states, random_owner.transpose(order), random_local.transpose(order), ids, here)
-    up1, down1, far0, spread, before, after = tied((up1, down1, far0, spread, before, after))
+    received = exchanged(spread, PLANE)
+    up1, down1, far0 = tied((up1, down1, far0))
 
     up2, down2 = turned(up1, "z", 1), turned(down1, "z", -1)
     far1, far7 = swapped(up1), swapped(down1)
-    received = exchanged(spread, PLANE)
-    up2, down2, far1, far7 = tied((up2, down2, far1, far7))
+    up2, down2, far1, far7, received = tied((up2, down2, far1, far7, received))
 
     up3, down3 = turned(up2, "z", 1), turned(down2, "z", -1)
     far2, far6 = swapped(up2), swapped(down2)
-    up3, down3, far2, far6, received = tied((up3, down3, far2, far6, received))
+    up3, down3, far2, far6, before, after = tied((up3, down3, far2, far6, before, after))
 
     root_owner = pick(x >= 2, global_ids[1], global_ids[0]) >> 2
     root = (root_owner >> 5) * 4 + (root_owner & 3)
@@ -593,7 +594,6 @@
     up4 = turned(up3, "z", 1)
     shares = exchanged(jnp.broadcast_to(share, (8, 48, 128)), "z")
     far3, far5 = swapped(up3), swapped(down3)
-    up4, far3, far5, shares = tied((up4, far3, far5, shares))
 
     pieces = [up0, up1, up2, up3, up4, down3, down2, down1, far0, far1, far2, far3, swapped(up4), far5, far6, far7]
     pairs, items, wanted, flag = column(pieces, qkv_weight, received, shares, ids, here)

time: 167 us -> 168 us (level)
  blocking collectives: 11.6 us -> 0 us
  waiting for transfers between devices: 35.3 us -> 41.4 us
  starting transfers between devices: 61.4 us -> 67.4 us
    all_to_all x1 -> x0, blocking collectives: 11.6 us -> none  [exchanged(): return lax.all_to_all(value, axes, split_axis=0, concat_axis=0, tiled=True)]
    all_to_all x4 -> x5, starting transfers between devices: 33.7 us -> 38 us  [exchanged(): return lax.all_to_all(value, axes, split_axis=0, concat_axis=0, tiled=True)]
    ppermute x1, waiting for transfers between devices: 0.88 us -> 4.44 us  [shards(): after = lax.ppermute(states[:64], SEQ, [(j, i) for i, j in ends])]
    all_to_all x4 -> x5, waiting for transfers between devices: 32.4 us -> 35.4 us  [exchanged(): return lax.all_to_all(value, axes, split_axis=0, concat_axis=0, tiled=True)]
    unnamed x28 -> x26, local copies, waits for them, and re-layouts: 4.48 us -> 3.37 us
  transfers between devices with their start and end apart: 26 -> 27, of which waited for: 6 -> 6; matrix products, arithmetic and copies ran while one was open for 2% -> 2% of each run, Pallas kernels for 18% -> 17%
where the time goes in v7:
time: 168 us; the launch traced here: 167 us
  starting transfers between devices  67.4 us (40%)
  Pallas kernels  47.7 us (28%)
  waiting for transfers between devices  41.4 us (25%)
  local copies, waits for them, and re-layouts  7.22 us (4%)
  between operations  2.38 us (1%)
    pallas_call x7, Pallas kernels, call(): pl.pallas_call(body, out_shape=(*results, *tables), in_specs=[FAR] * (cou...  38.7 us
    all_to_all x5, starting transfers between devices, exchanged(): return lax.all_to_all(value, axes, split_axis=0, concat_axis=0, tiled=True)  38 us
    all_to_all x5, waiting for transfers between devices, exchanged(): return lax.all_to_all(value, axes, split_axis=0, concat_axis=0, tiled=True)  35.4 us
    ppermute x7, starting transfers between devices, turned(): lax.ppermute(value, axis, [(i, (i + shift) % count) for i in range(count)])  14 us
    ppermute x13, starting transfers between devices, swapped(): return lax.ppermute(value, 'mp', [(0, 1), (1, 0)])  10.6 us
    pallas_call x1, Pallas kernels, finish(): pl.pallas_call(finish_kernel, out_shape=jax.ShapeDtypeStruct((256, 768),...  8.43 us
    ppermute x1, waiting for transfers between devices, shards(): after = lax.ppermute(states[:64], SEQ, [(j, i) for i, j in ends])  4.44 us
    ppermute x1, starting transfers between devices, shards(): before = lax.ppermute(states[192:], SEQ, ends)  3.55 us
  transfers between devices with their start and end apart: 27, of which 6 were waited for; matrix products, arithmetic and copies ran while one was open for 2% of the time, Pallas kernels for 17%

profile of v7, /device:TPU:1, one launch (start us, length us, event | category | flops | bytes accessed | tf_op | source)
XLA Modules:
  0.0 166.9 jit_solution(15307977740540770716)
XLA Ops:
  0.9 2.5 %collective-permute-start = (bf16[128,768]{1,0:T(8,128)(2,1)S(1)}, bf16[128,768]{1,0:T(8,128)(2,1)S(1)}, u32[]{:S(2)}, u32[]{:S(2)}) collective-permute-start(bf16[128,768]{1,0:T(8,128)(2,1)S(1)} %constant_dynamic-slice_fusion.refs_1_), channel_id=1, source_target_pairs={{0,8},{8,16},{16,24},{24,32},{32,40},{40,48},{48,56},{56,0},{1,9},... | collective-permute-start | bytes 589832 | tf_op jit(solution)/shard_map/ppermute | solution.py:554
  3.5 4.0 %collective-permute-start.1 = (bf16[128,768]{1,0:T(8,128)(2,1)S(1)}, bf16[128,768]{1,0:T(8,128)(2,1)S(1)}, u32[]{:S(2)}, u32[]{:S(2)}) collective-permute-start(bf16[128,768]{1,0:T(8,128)(2,1)S(1)} %constant_dynamic-slice_fusion.refs_1_), channel_id=1, source_target_pairs={{0,56},{8,0},{16,8},{24,16},{32,24},{40,32},{48,40},{56,48},{1,57}... | collective-permute-start | bytes 589832 | tf_op jit(solution)/shard_map/ppermute | solution.py:554
  9.1 3.1 %shard_map.100 = (bf16[16,64,128]{2,1,0:T(8,128)(2,1)}, s32[1,72]{1,0:T(1,128)}) custom-call(bf16[256,768]{1,0:T(8,128)(2,1)} %states_ref.1, s32[1,3,4,6]{3,2,1,0:T(4,128)} %bitcast.23, s32[1,3,4,6]{3,2,1,0:T(4,128)} %bitcast.24, s32[1,2]{1,0:T(1,128)} %bitcast.19, s32[1,4]{1,0:T(1,128)} %add_bitcast_fusion.refs_4_.refs_20_.refs_6_.here_ref), custom_call_target="tpu_custom_call" | custom-call | flops 1000000 | bytes 600000 | tf_op jit(solution)/shard_map/pallas_call | solution.py:66
  12.3 6.8 %all-to-all-start.1 = ((bf16[16,64,128]{2,1,0:T(8,128)(2,1)}), bf16[16,64,128]{2,1,0:T(8,128)(2,1)S(1)}, u32[]{:S(2)}, u32[]{:S(2)}) async-start(bf16[16,64,128]{2,1,0:T(8,128)(2,1)} %get-tuple-element.51), calls=%async_computation.1 | async-start | bytes 524288 | tf_op jit(solution)/shard_map/all_to_all | solution.py:558
  19.5 2.9 %collective-permute-start.4 = (bf16[128,768]{1,0:T(8,128)(2,1)S(1)}, bf16[128,768]{1,0:T(8,128)(2,1)S(1)}, u32[]{:S(2)}, u32[]{:S(2)}) collective-permute-start(bf16[128,768]{1,0:T(8,128)(2,1)S(1)} %collective-permute-done.1.refs_8_), channel_id=1, source_target_pairs={{0,56},{8,0},{16,8},{24,16},{32,24},{40,32},{48,40},{56,48},{1,57}... | collective-permute-start | bytes 589832 | tf_op jit(solution)/shard_map/ppermute | solution.py:554
  23.6 3.6 %collective-permute-start.11 = (bf16[64,768]{1,0:T(8,128)(2,1)S(1)}, bf16[64,768]{1,0:T(8,128)(2,1)S(1)}, u32[]{:S(2)}, u32[]{:S(2)}) collective-permute-start(bf16[64,768]{1,0:T(8,128)(2,1)S(1)} %get-tuple-element.85), channel_id=1, source_target_pairs={{0,2},{2,4},{4,6},{6,8},{8,10},{10,12},{12,14},{14,16},{16,18},{18... | collective-permute-start | bytes 294920 | tf_op jit(solution)/shard_map/ppermute | solution.py:575
  27.4 3.0 %collective-permute-start.8 = (bf16[128,768]{1,0:T(8,128)(2,1)S(1)}, bf16[128,768]{1,0:T(8,128)(2,1)S(1)}, u32[]{:S(2)}, u32[]{:S(2)}) collective-permute-start(bf16[128,768]{1,0:T(8,128)(2,1)S(1)} %collective-permute-done.4.refs_7_), channel_id=1, source_target_pairs={{0,56},{8,0},{16,8},{24,16},{32,24},{40,32},{48,40},{56,48},{1,57}... | collective-permute-start | bytes 589832 | tf_op jit(solution)/shard_map/ppermute | solution.py:554
  30.3 1.5 collective-permute-start.9
  33.1 4.4 %collective-permute-done.12.refs_2_ = bf16[64,768]{1,0:T(8,128)(2,1)S(1)} collective-permute-done((bf16[64,768]{1,0:T(8,128)(2,1)S(1)}, bf16[64,768]{1,0:T(8,128)(2,1)S(1)}, u32[]{:S(2)}, u32[]{:S(2)}) %collective-permute-start.12) | collective-permute-done | bytes 98336 | tf_op jit(solution)/shard_map/ppermute | solution.py:576
  41.5 1.7 %collective-permute-start.14 = (bf16[128,768]{1,0:T(8,128)(2,1)S(1)}, bf16[128,768]{1,0:T(8,128)(2,1)S(1)}, u32[]{:S(2)}, u32[]{:S(2)}) collective-permute-start(bf16[128,768]{1,0:T(8,128)(2,1)S(1)} %collective-permute-done.7.refs_4_), channel_id=1, source_target_pairs={{0,1},{1,0},{2,3},{3,2},{4,5},{5,4},{6,7},{7,6},{8,9},{9,8},{10,11... | collective-permute-start | bytes 589832 | tf_op jit(solution)/shard_map/ppermute | solution.py:562
  44.0 2.3 %collective-permute-start.15 = (bf16[128,768]{1,0:T(8,128)(2,1)S(1)}, bf16[128,768]{1,0:T(8,128)(2,1)S(1)}, u32[]{:S(2)}, u32[]{:S(2)}) collective-permute-start(bf16[128,768]{1,0:T(8,128)(2,1)S(1)} %collective-permute-done.13.refs_5_), channel_id=1, source_target_pairs={{0,1},{1,0},{2,3},{3,2},{4,5},{5,4},{6,7},{7,6},{8,9},{9,8},{10,11... | collective-permute-start | bytes 589832 | tf_op jit(solution)/shard_map/ppermute | solution.py:562
  46.9 7.0 %all-to-all-start.2 = ((bf16[8,48,128]{2,1,0:T(8,128)(2,1)}), bf16[8,48,128]{2,1,0:T(8,128)(2,1)S(1)}, u32[]{:S(2)}, u32[]{:S(2)}) async-start(bf16[8,48,128]{2,1,0:T(8,128)(2,1)} %broadcast_in_dim.8), calls=%async_computation.2 | async-start | bytes 196608 | tf_op jit(solution)/shard_map/all_to_all | solution.py:558
  53.9 7.9 %all-to-all-done.2.refs_18_ = bf16[8,48,128]{2,1,0:T(8,128)(2,1)S(1)} async-done(((bf16[8,48,128]{2,1,0:T(8,128)(2,1)}), bf16[8,48,128]{2,1,0:T(8,128)(2,1)S(1)}, u32[]{:S(2)}, u32[]{:S(2)}) %all-to-all-start.2) | async-done | bytes 98336 | tf_op jit(solution)/shard_map/all_to_all | solution.py:558
  63.1 9.6 %shard_map.102 = (bf16[96,128,128]{2,1,0:T(8,128)(2,1)}, bf16[16,688,128]{2,1,0:T(8,128)(2,1)}, s32[16,128]{1,0:T(8,128)S(1)}, s32[1,1]{1,0:T(1,128)}) custom-call(bf16[3,768,384]{2,1,0:T(8,128)(2,1)} %refs_0_.3, bf16[128,768]{1,0:T(8,128)(2,1)S(1)} %constant_dynamic-slice_fusion.refs_1_, bf16[128,768]{1,0:T(8,128)(2,1)S(1)} %collective-permute-done.refs_2_, ...), custom_call_target="tpu_custom_call" | custom-call | flops 2400000000 | bytes 10000000 | tf_op jit(solution)/shard_map/pallas_call | solution.py:66
  74.0 7.1 %all-to-all-start.3 = ((bf16[16,688,128]{2,1,0:T(8,128)(2,1)}), bf16[16,688,128]{2,1,0:T(8,128)(2,1)}, u32[]{:S(2)}, u32[]{:S(2)}) async-start(bf16[16,688,128]{2,1,0:T(8,128)(2,1)} %get-tuple-element.70), calls=%async_computation.3 | async-start | bytes 5636096 | tf_op jit(solution)/shard_map/all_to_all | solution.py:558
  81.1 1.8 %collective-permute-start.20 = (bf16[768,1536]{1,0:T(8,128)(2,1)}, bf16[768,1536]{1,0:T(8,128)(2,1)}, u32[]{:S(2)}, u32[]{:S(2)}) collective-permute-start(bf16[768,1536]{1,0:T(8,128)(2,1)} %up_own.1), channel_id=1, source_target_pairs={{0,1},{1,0},{2,3},{3,2},{4,5},{5,4},{6,7},{7,6},{8,9},{9,8},{10,11... | collective-permute-start | bytes 7077896 | tf_op jit(solution)/shard_map/ppermute | solution.py:562
  83.1 4.4 %shard_map.101 = (bf16[6,256,128]{2,1,0:T(8,128)(2,1)S(1)}, bf16[6,384,128]{2,1,0:T(8,128)(2,1)S(1)}, bf16[768,768]{1,0:T(8,128)(2,1)S(1)}, bf16[768,768]{1,0:T(8,128)(2,1)}) custom-call(bf16[64,768]{1,0:T(8,128)(2,1)S(1)} %collective-permute-done.11.refs_0_, bf16[256,768]{1,0:T(8,128)(2,1)S(1)} %copy-done, ...), custom_call_target="tpu_custom_call" | custom-call | flops 800000000 | bytes 4000000 | tf_op jit(solution)/shard_map/pallas_call | solution.py:66
  88.0 27.0 %all-to-all-done.3.refs_3_ = bf16[16,688,128]{2,1,0:T(8,128)(2,1)} async-done(((bf16[16,688,128]{2,1,0:T(8,128)(2,1)}), bf16[16,688,128]{2,1,0:T(8,128)(2,1)}, u32[]{:S(2)}, u32[]{:S(2)}) %all-to-all-start.3) | async-done | bytes 2818080 | tf_op jit(solution)/shard_map/all_to_all | solution.py:558
  116.2 6.3 %shard_map.103 = (f32[128,640]{1,0:T(8,128)S(1)}, bf16[6,128,128]{2,1,0:T(8,128)(2,1)S(1)}) custom-call(bf16[768,768]{1,0:T(8,128)(2,1)S(1)} %get-tuple-element.56.refs_0_, bf16[768,768]{1,0:T(8,128)(2,1)S(1)} %copy-done.1, bf16[16,6,128,128]{3,2,1,0:T(8,128)(2,1)} %bitcast.22, bf16[16,688,128]{2,1,0:T(8,128)(2,1)} %all-to-all-done.3.refs_3_), custom_call_target="tpu_custom_call" | custom-call | flops 2000000000 | bytes 10000000 | tf_op jit(solution)/shard_map/pallas_call | solution.py:66
  123.3 5.6 %all-to-all-start.4 = ((f32[16,8,640]{2,1,0:T(8,128)}), f32[16,8,640]{2,1,0:T(8,128)S(1)}, u32[]{:S(2)}, u32[]{:S(2)}) async-start(f32[16,8,640]{2,1,0:T(8,128)} %bitcast.18), calls=%async_computation.4 | async-start | bytes 655360 | tf_op jit(solution)/shard_map/all_to_all | solution.py:558
  128.9 8.5 %shard_map.104.own_ref = bf16[256,256]{1,0:T(8,128)(2,1)S(1)} custom-call(bf16[6,256,128]{2,1,0:T(8,128)(2,1)S(1)} %get-tuple-element.74.refs_0_, bf16[6,384,128]{2,1,0:T(8,128)(2,1)S(1)} %get-tuple-element.75.refs_1_, bf16[6,128,128]{2,1,0:T(8,128)(2,1)S(1)} %get-tuple-element.76.refs_2_, bf16[11008,128]{1,0:T(8,128)(2,1)} %bitcast.14.refs_3_, ...), custom_call_target="tpu_custom_call" | custom-call | flops 400000000 | bytes 3000000 | tf_op jit(solution)/shard_map/pallas_call | solution.py:66
  138.4 11.5 %all-to-all-start.5 = ((bf16[32,8,384]{2,1,0:T(8,128)(2,1)}), bf16[32,8,384]{2,1,0:T(8,128)(2,1)S(1)}, u32[]{:S(2)}, u32[]{:S(2)}) async-start(bf16[32,8,384]{2,1,0:T(8,128)(2,1)} %shard_map.106), calls=%async_computation.5 | async-start | bytes 393216 | tf_op jit(solution)/shard_map/all_to_all | solution.py:558
  150.5 5.8 %shard_map.105.own2_ref = bf16[256,128]{1,0:T(8,128)(2,1)S(1)} custom-call(bf16[6,256,128]{2,1,0:T(8,128)(2,1)S(1)} %get-tuple-element.74.refs_0_, bf16[6,384,128]{2,1,0:T(8,128)(2,1)S(1)} %get-tuple-element.75.refs_1_, bf16[6,128,128]{2,1,0:T(8,128)(2,1)S(1)} %get-tuple-element.76.refs_2_, bf16[11008,128]{1,0:T(8,128)(2,1)} %bitcast.14.refs_3_, ...), custom_call_target="tpu_custom_call" | custom-call | flops 200000000 | bytes 1500000 | tf_op jit(solution)/shard_map/pallas_call | solution.py:66
  158.2 8.4 %shard_map.107 = bf16[256,768]{1,0:T(8,128)(2,1)} custom-call(bf16[256,256]{1,0:T(8,128)(2,1)S(1)} %shard_map.104.own_ref, bf16[256,256]{1,0:T(8,128)(2,1)S(1)} %collective-permute-done.17.other_ref, bf16[256,128]{1,0:T(8,128)(2,1)S(1)} %shard_map.105.own2_ref, bf16[256,128]{1,0:T(8,128)(2,1)S(1)} %collective-permute-done.18.other2_ref, ...), custom_call_target="tpu_custom_call" | custom-call | flops 2700000000 | bytes 12000000 | tf_op jit(solution)/shard_map/pallas_call | solution.py:530
  (74 shorter events, 18.2 us)
Async XLA Ops:
  0.9 18.1 %collective-permute-start = (bf16[128,768]{1,0:T(8,128)(2,1)S(1)}, bf16[128,768]{1,0:T(8,128)(2,1)S(1)}, u32[]{:S(2)}, u32[]{:S(2)}) collective-permute-start(bf16[128,768]{1,0:T(8,128)(2,1)S(1)} %constant_dynamic-slice_fusion.refs_1_), channel_id=1, source_target_pairs={{0,8},{8,16},{16,24},{24,32},{32,40},{40,48},{48,56},{56,0},{1,9},... | collective-permute-start | bytes 589832 | tf_op jit(solution)/shard_map/ppermute | solution.py:554
  3.5 15.6 %collective-permute-start.1 = (bf16[128,768]{1,0:T(8,128)(2,1)S(1)}, bf16[128,768]{1,0:T(8,128)(2,1)S(1)}, u32[]{:S(2)}, u32[]{:S(2)}) collective-permute-start(bf16[128,768]{1,0:T(8,128)(2,1)S(1)} %constant_dynamic-slice_fusion.refs_1_), channel_id=1, source_target_pairs={{0,56},{8,0},{16,8},{24,16},{32,24},{40,32},{48,40},{56,48},{1,57}... | collective-permute-start | bytes 589832 | tf_op jit(solution)/shard_map/ppermute | solution.py:554
  7.5 11.5 %collective-permute-start.2 = (bf16[128,768]{1,0:T(8,128)(2,1)S(1)}, bf16[128,768]{1,0:T(8,128)(2,1)S(1)}, u32[]{:S(2)}, u32[]{:S(2)}) collective-permute-start(bf16[128,768]{1,0:T(8,128)(2,1)S(1)} %constant_dynamic-slice_fusion.refs_1_), channel_id=1, source_target_pairs={{0,1},{1,0},{2,3},{3,2},{4,5},{5,4},{6,7},{7,6},{8,9},{9,8},{10,11... | collective-permute-start | bytes 589832 | tf_op jit(solution)/shard_map/ppermute | solution.py:562
  12.3 14.9 %all-to-all-start.1 = ((bf16[16,64,128]{2,1,0:T(8,128)(2,1)}), bf16[16,64,128]{2,1,0:T(8,128)(2,1)S(1)}, u32[]{:S(2)}, u32[]{:S(2)}) async-start(bf16[16,64,128]{2,1,0:T(8,128)(2,1)} %get-tuple-element.51), calls=%async_computation.1 | async-start | bytes 524288 | tf_op jit(solution)/shard_map/all_to_all | solution.py:558
  19.1 8.1 %collective-permute-start.3 = (bf16[128,768]{1,0:T(8,128)(2,1)S(1)}, bf16[128,768]{1,0:T(8,128)(2,1)S(1)}, u32[]{:S(2)}, u32[]{:S(2)}) collective-permute-start(bf16[128,768]{1,0:T(8,128)(2,1)S(1)} %collective-permute-done.refs_2_), channel_id=1, source_target_pairs={{0,8},{8,16},{16,24},{24,32},{32,40},{40,48},{48,56},{56,0},{1,9},... | collective-permute-start | bytes 589832 | tf_op jit(solution)/shard_map/ppermute | solution.py:554
  19.2 8.1 %collective-permute-start.5 = (bf16[128,768]{1,0:T(8,128)(2,1)S(1)}, bf16[128,768]{1,0:T(8,128)(2,1)S(1)}, u32[]{:S(2)}, u32[]{:S(2)}) collective-permute-start(bf16[128,768]{1,0:T(8,128)(2,1)S(1)} %collective-permute-done.refs_2_), channel_id=1, source_target_pairs={{0,1},{1,0},{2,3},{3,2},{4,5},{5,4},{6,7},{7,6},{8,9},{9,8},{10,11... | collective-permute-start | bytes 589832 | tf_op jit(solution)/shard_map/ppermute | solution.py:562
  19.5 7.7 %collective-permute-start.4 = (bf16[128,768]{1,0:T(8,128)(2,1)S(1)}, bf16[128,768]{1,0:T(8,128)(2,1)S(1)}, u32[]{:S(2)}, u32[]{:S(2)}) collective-permute-start(bf16[128,768]{1,0:T(8,128)(2,1)S(1)} %collective-permute-done.1.refs_8_), channel_id=1, source_target_pairs={{0,56},{8,0},{16,8},{24,16},{32,24},{40,32},{48,40},{56,48},{1,57}... | collective-permute-start | bytes 589832 | tf_op jit(solution)/shard_map/ppermute | solution.py:554
  23.6 8.2 %collective-permute-start.11 = (bf16[64,768]{1,0:T(8,128)(2,1)S(1)}, bf16[64,768]{1,0:T(8,128)(2,1)S(1)}, u32[]{:S(2)}, u32[]{:S(2)}) collective-permute-start(bf16[64,768]{1,0:T(8,128)(2,1)S(1)} %get-tuple-element.85), channel_id=1, source_target_pairs={{0,2},{2,4},{4,6},{6,8},{8,10},{10,12},{12,14},{14,16},{16,18},{18... | collective-permute-start | bytes 294920 | tf_op jit(solution)/shard_map/ppermute | solution.py:575
  27.3 10.3 %collective-permute-start.7 = (bf16[128,768]{1,0:T(8,128)(2,1)S(1)}, bf16[128,768]{1,0:T(8,128)(2,1)S(1)}, u32[]{:S(2)}, u32[]{:S(2)}) collective-permute-start(bf16[128,768]{1,0:T(8,128)(2,1)S(1)} %collective-permute-done.3.refs_3_), channel_id=1, source_target_pairs={{0,8},{8,16},{16,24},{24,32},{32,40},{40,48},{48,56},{56,0},{1,9},... | collective-permute-start | bytes 589832 | tf_op jit(solution)/shard_map/ppermute | solution.py:554
  27.4 10.2 %collective-permute-start.8 = (bf16[128,768]{1,0:T(8,128)(2,1)S(1)}, bf16[128,768]{1,0:T(8,128)(2,1)S(1)}, u32[]{:S(2)}, u32[]{:S(2)}) collective-permute-start(bf16[128,768]{1,0:T(8,128)(2,1)S(1)} %collective-permute-done.4.refs_7_), channel_id=1, source_target_pairs={{0,56},{8,0},{16,8},{24,16},{32,24},{40,32},{48,40},{56,48},{1,57}... | collective-permute-start | bytes 589832 | tf_op jit(solution)/shard_map/ppermute | solution.py:554
  30.3 7.3 %collective-permute-start.9 = (bf16[128,768]{1,0:T(8,128)(2,1)S(1)}, bf16[128,768]{1,0:T(8,128)(2,1)S(1)}, u32[]{:S(2)}, u32[]{:S(2)}) collective-permute-start(bf16[128,768]{1,0:T(8,128)(2,1)S(1)} %collective-permute-done.3.refs_3_), channel_id=1, source_target_pairs={{0,1},{1,0},{2,3},{3,2},{4,5},{5,4},{6,7},{7,6},{8,9},{9,8},{10,11... | collective-permute-start | bytes 589832 | tf_op jit(solution)/shard_map/ppermute | solution.py:562
  31.9 5.8 %collective-permute-start.10 = (bf16[128,768]{1,0:T(8,128)(2,1)S(1)}, bf16[128,768]{1,0:T(8,128)(2,1)S(1)}, u32[]{:S(2)}, u32[]{:S(2)}) collective-permute-start(bf16[128,768]{1,0:T(8,128)(2,1)S(1)} %collective-permute-done.4.refs_7_), channel_id=1, source_target_pairs={{0,1},{1,0},{2,3},{3,2},{4,5},{5,4},{6,7},{7,6},{8,9},{9,8},{10,11... | collective-permute-start | bytes 589832 | tf_op jit(solution)/shard_map/ppermute | solution.py:562
  37.6 6.3 %collective-permute-start.13 = (bf16[128,768]{1,0:T(8,128)(2,1)S(1)}, bf16[128,768]{1,0:T(8,128)(2,1)S(1)}, u32[]{:S(2)}, u32[]{:S(2)}) collective-permute-start(bf16[128,768]{1,0:T(8,128)(2,1)S(1)} %collective-permute-done.7.refs_4_), channel_id=1, source_target_pairs={{0,8},{8,16},{16,24},{24,32},{32,40},{40,48},{48,56},{56,0},{1,9},... | collective-permute-start | bytes 589832 | tf_op jit(solution)/shard_map/ppermute | solution.py:554
  41.5 20.2 %collective-permute-start.14 = (bf16[128,768]{1,0:T(8,128)(2,1)S(1)}, bf16[128,768]{1,0:T(8,128)(2,1)S(1)}, u32[]{:S(2)}, u32[]{:S(2)}) collective-permute-start(bf16[128,768]{1,0:T(8,128)(2,1)S(1)} %collective-permute-done.7.refs_4_), channel_id=1, source_target_pairs={{0,1},{1,0},{2,3},{3,2},{4,5},{5,4},{6,7},{7,6},{8,9},{9,8},{10,11... | collective-permute-start | bytes 589832 | tf_op jit(solution)/shard_map/ppermute | solution.py:562
  43.3 18.5 %collective-permute-start.16 = (bf16[128,768]{1,0:T(8,128)(2,1)S(1)}, bf16[128,768]{1,0:T(8,128)(2,1)S(1)}, u32[]{:S(2)}, u32[]{:S(2)}) collective-permute-start(bf16[128,768]{1,0:T(8,128)(2,1)S(1)} %collective-permute-done.8.refs_6_), channel_id=1, source_target_pairs={{0,1},{1,0},{2,3},{3,2},{4,5},{5,4},{6,7},{7,6},{8,9},{9,8},{10,11... | collective-permute-start | bytes 589832 | tf_op jit(solution)/shard_map/ppermute | solution.py:562
  44.0 17.8 %collective-permute-start.15 = (bf16[128,768]{1,0:T(8,128)(2,1)S(1)}, bf16[128,768]{1,0:T(8,128)(2,1)S(1)}, u32[]{:S(2)}, u32[]{:S(2)}) collective-permute-start(bf16[128,768]{1,0:T(8,128)(2,1)S(1)} %collective-permute-done.13.refs_5_), channel_id=1, source_target_pairs={{0,1},{1,0},{2,3},{3,2},{4,5},{5,4},{6,7},{7,6},{8,9},{9,8},{10,11... | collective-permute-start | bytes 589832 | tf_op jit(solution)/shard_map/ppermute | solution.py:562
  46.9 14.9 %all-to-all-start.2 = ((bf16[8,48,128]{2,1,0:T(8,128)(2,1)}), bf16[8,48,128]{2,1,0:T(8,128)(2,1)S(1)}, u32[]{:S(2)}, u32[]{:S(2)}) async-start(bf16[8,48,128]{2,1,0:T(8,128)(2,1)} %broadcast_in_dim.8), calls=%async_computation.2 | async-start | bytes 196608 | tf_op jit(solution)/shard_map/all_to_all | solution.py:558
  74.0 40.9 %all-to-all-start.3 = ((bf16[16,688,128]{2,1,0:T(8,128)(2,1)}), bf16[16,688,128]{2,1,0:T(8,128)(2,1)}, u32[]{:S(2)}, u32[]{:S(2)}) async-start(bf16[16,688,128]{2,1,0:T(8,128)(2,1)} %get-tuple-element.70), calls=%async_computation.3 | async-start | bytes 5636096 | tf_op jit(solution)/shard_map/all_to_all | solution.py:558
  81.1 75.6 %collective-permute-start.20 = (bf16[768,1536]{1,0:T(8,128)(2,1)}, bf16[768,1536]{1,0:T(8,128)(2,1)}, u32[]{:S(2)}, u32[]{:S(2)}) collective-permute-start(bf16[768,1536]{1,0:T(8,128)(2,1)} %up_own.1), channel_id=1, source_target_pairs={{0,1},{1,0},{2,3},{3,2},{4,5},{5,4},{6,7},{7,6},{8,9},{9,8},{10,11... | collective-permute-start | bytes 7077896 | tf_op jit(solution)/shard_map/ppermute | solution.py:562
  83.0 73.7 %collective-permute-start.21 = (bf16[1536,768]{1,0:T(8,128)(2,1)}, bf16[1536,768]{1,0:T(8,128)(2,1)}, u32[]{:S(2)}, u32[]{:S(2)}) collective-permute-start(bf16[1536,768]{1,0:T(8,128)(2,1)} %down_own.1), channel_id=1, source_target_pairs={{0,1},{1,0},{2,3},{3,2},{4,5},{5,4},{6,7},{7,6},{8,9},{9,8},{10,11... | collective-permute-start | bytes 7077896 | tf_op jit(solution)/shard_map/ppermute | solution.py:562
  87.5 69.2 %collective-permute-start.19 = (bf16[384,768]{1,0:T(8,128)(2,1)S(1)}, bf16[384,768]{1,0:T(8,128)(2,1)}, u32[]{:S(2)}, u32[]{:S(2)}) collective-permute-start(bf16[384,768]{1,0:T(8,128)(2,1)S(1)} %copy-done.2), channel_id=1, source_target_pairs={{0,1},{1,0},{2,3},{3,2},{4,5},{5,4},{6,7},{7,6},{8,9},{9,8},{10,11... | collective-permute-start | bytes 1769480 | tf_op jit(solution)/shard_map/ppermute | solution.py:562
  123.3 14.2 %all-to-all-start.4 = ((f32[16,8,640]{2,1,0:T(8,128)}), f32[16,8,640]{2,1,0:T(8,128)S(1)}, u32[]{:S(2)}, u32[]{:S(2)}) async-start(f32[16,8,640]{2,1,0:T(8,128)} %bitcast.18), calls=%async_computation.4 | async-start | bytes 655360 | tf_op jit(solution)/shard_map/all_to_all | solution.py:558
  138.4 19.9 %all-to-all-start.5 = ((bf16[32,8,384]{2,1,0:T(8,128)(2,1)}), bf16[32,8,384]{2,1,0:T(8,128)(2,1)S(1)}, u32[]{:S(2)}, u32[]{:S(2)}) async-start(bf16[32,8,384]{2,1,0:T(8,128)(2,1)} %shard_map.106), calls=%async_computation.5 | async-start | bytes 393216 | tf_op jit(solution)/shard_map/all_to_all | solution.py:558
  150.0 7.7 %collective-permute-start.17 = (bf16[256,256]{1,0:T(8,128)(2,1)S(1)}, bf16[256,256]{1,0:T(8,128)(2,1)S(1)}, u32[]{:S(2)}, u32[]{:S(2)}) collective-permute-start(bf16[256,256]{1,0:T(8,128)(2,1)S(1)} %shard_map.104.own_ref), channel_id=1, source_target_pairs={{0,1},{1,0},{2,3},{3,2},{4,5},{5,4},{6,7},{7,6},{8,9},{9,8},{10,11... | collective-permute-start | bytes 393224 | tf_op jit(solution)/shard_map/ppermute | solution.py:562
  (16 other events, 122.8 us)

commit v8 on v7

--- a/solution.py
+++ b/solution.py
@@ -112,6 +112,8 @@
                 beyond = 16 * STRIDE + group * MORE * 64 + (rank - SLOTS) * 64
                 slots_ref[0, (b * HEADS + h) * 3 + r] = pick(rank < SLOTS, near, beyond)
                 wanted = jnp.where(place == group * 128 + rank, item.astype(F32), wanted)
+    roots = [((ids_ref[0, g] >> 4) & 7).astype(F32) for g in range(2)]
+    wanted = jnp.where(lane == 126, jnp.where(line >= 8, roots[1], roots[0]), wanted)
     wanted = jnp.where(lane == 127, pick(most >= SLOTS, 1.0, 0.0), wanted)
     for copy in copies:
         copy.wait()
@@ -150,8 +152,6 @@
     (
         received_ref,
         shares_ref,
-        ids_ref,
-        here_ref,
         kv_ref,
         items_ref,
         out_ref,
@@ -172,10 +172,6 @@
         asked_ref[p : p + 1, :] = received_ref[p, 48:49, :].astype(F32).astype(jnp.int32)
     asked = pltpu.make_async_copy(asked_ref, wanted_ref, sem.at[0])
     asked.start()
-    owner = pick(here_ref[0, 0] >= 2, ids_ref[0, 1], ids_ref[0, 0]) >> 2
-    share = shares_ref[(owner >> 2) & 7]
-    for p in range(16):
-        items_ref[p, SLOTS * 64 : STRIDE, :] = share
     weight.wait()
     interleave(weight_ref, 0, wkv_ref)
 
@@ -191,6 +187,9 @@
     for p in range(1, 16):
         flag = jnp.maximum(flag, wanted_ref[p, 127])
     flag_ref[0, 0] = flag
+    share = shares_ref[wanted_ref[0, 126]]
+    for p in range(16):
+        items_ref[p, SLOTS * 64 : STRIDE, :] = share
 
     @pl.loop(0, 16)
     def _(p):
@@ -205,7 +204,7 @@
         pltpu.make_async_copy(items_ref.at[p], out_ref.at[p], sems.at[p]).wait()
 
 
-def column(pieces, weight, received, shares, ids, here):
+def column(pieces, weight, received, shares):
     shape = jax.ShapeDtypeStruct
     return call(
         column_kernel,
@@ -222,7 +221,6 @@
         [],
         raw=[weight],
         near=[*pieces, received, shares],
-        scalars=[ids, here],
         by_hand=(1,),
         held=(0,),
         tables=(shape((16, 128), jnp.int32), shape((1, 1), jnp.int32)),
@@ -584,19 +582,18 @@
     far1, far7 = swapped(up1), swapped(down1)
     up2, down2, far1, far7, received = tied((up2, down2, far1, far7, received))
 
-    up3, down3 = turned(up2, "z", 1), turned(down2, "z", -1)
-    far2, far6 = swapped(up2), swapped(down2)
-    up3, down3, far2, far6, before, after = tied((up3, down3, far2, far6, before, after))
-
     root_owner = pick(x >= 2, global_ids[1], global_ids[0]) >> 2
     root = (root_owner >> 5) * 4 + (root_owner & 3)
     share = lax.dynamic_slice(received, (root, 0, 0), (1, 48, 128))
+    shares = exchanged(jnp.broadcast_to(share, (8, 48, 128)), "z")
+    up3, down3 = turned(up2, "z", 1), turned(down2, "z", -1)
+    far2, far6 = swapped(up2), swapped(down2)
+    up3, down3, far2, far6, shares, before, after = tied((up3, down3, far2, far6, shares, before, after))
+
     up4 = turned(up3, "z", 1)
-    shares = exchanged(jnp.broadcast_to(share, (8, 48, 128)), "z")
     far3, far5 = swapped(up3), swapped(down3)
-
     pieces = [up0, up1, up2, up3, up4, down3, down2, down1, far0, far1, far2, far3, swapped(up4), far5, far6, far7]
-    pairs, items, wanted, flag = column(pieces, qkv_weight, received, shares, ids, here)
+    pairs, items, wanted, flag = column(pieces, qkv_weight, received, shares)
     more = lax.cond(flag[0, 0] > 0, lambda: extra(pairs, wanted), unused)
     items, more, weights = tied((items, more, (out_weight, up_weight, down_weight)))
     remote = exchanged(items, PLANE)

time: 168 us -> 165 us (0.982)
  starting transfers between devices: 67.4 us -> 64 us
  waiting for transfers between devices: 41.4 us -> 43.2 us
    ppermute x7, waiting for transfers between devices: 0.59 us -> 3.3 us  [turned(): lax.ppermute(value, axis, [(i, (i + shift) % count) for i in range(count)])]
    all_to_all x5, waiting for transfers between devices: 35.4 us -> 33.4 us  [exchanged(): return lax.all_to_all(value, axes, split_axis=0, concat_axis=0, tiled=True)]
    unnamed x26 -> x22, local copies, waits for them, and re-layouts: 3.37 us -> 2.04 us
  transfers between devices with their start and end apart: 27 -> 27, of which waited for: 6 -> 7; matrix products, arithmetic and copies ran while one was open for 2% -> 2% of each run, Pallas kernels for 17% -> 18%
where the time goes in v8:
time: 165 us; the launch traced here: 164 us
  starting transfers between devices  64 us (39%)
  Pallas kernels  47.8 us (29%)
  waiting for transfers between devices  43.2 us (26%)
  local copies, waits for them, and re-layouts  5.94 us (4%)
  between operations  2.5 us (2%)
    pallas_call x7, Pallas kernels, call(): pl.pallas_call(body, out_shape=(*results, *tables), in_specs=[FAR] * (cou...  38.8 us
    all_to_all x5, starting transfers between devices, exchanged(): return lax.all_to_all(value, axes, split_axis=0, concat_axis=0, tiled=True)  36.4 us
    all_to_all x5, waiting for transfers between devices, exchanged(): return lax.all_to_all(value, axes, split_axis=0, concat_axis=0, tiled=True)  33.4 us
    ppermute x7, starting transfers between devices, turned(): lax.ppermute(value, axis, [(i, (i + shift) % count) for i in range(count)])  12.9 us
    ppermute x13, starting transfers between devices, swapped(): return lax.ppermute(value, 'mp', [(0, 1), (1, 0)])  9.83 us
    pallas_call x1, Pallas kernels, finish(): pl.pallas_call(finish_kernel, out_shape=jax.ShapeDtypeStruct((256, 768),...  8.43 us
    ppermute x1, waiting for transfers between devices, shards(): after = lax.ppermute(states[:64], SEQ, [(j, i) for i, j in ends])  4.44 us
    ppermute x1, starting transfers between devices, shards(): before = lax.ppermute(states[192:], SEQ, ends)  3.55 us
  transfers between devices with their start and end apart: 27, of which 7 were waited for; matrix products, arithmetic and copies ran while one was open for 2% of the time, Pallas kernels for 18%

profile of v8, /device:TPU:1, one launch (start us, length us, event | category | flops | bytes accessed | tf_op | source)
XLA Modules:
  0.0 164.0 jit_solution(13260539540569682142)
XLA Ops:
  0.9 2.5 %collective-permute-start = (bf16[128,768]{1,0:T(8,128)(2,1)S(1)}, bf16[128,768]{1,0:T(8,128)(2,1)S(1)}, u32[]{:S(2)}, u32[]{:S(2)}) collective-permute-start(bf16[128,768]{1,0:T(8,128)(2,1)S(1)} %constant_dynamic-slice_fusion.refs_1_), channel_id=1, source_target_pairs={{0,8},{8,16},{16,24},{24,32},{32,40},{40,48},{48,56},{56,0},{1,9},... | collective-permute-start | bytes 589832 | tf_op jit(solution)/shard_map/ppermute | solution.py:552
  3.5 4.0 %collective-permute-start.1 = (bf16[128,768]{1,0:T(8,128)(2,1)S(1)}, bf16[128,768]{1,0:T(8,128)(2,1)S(1)}, u32[]{:S(2)}, u32[]{:S(2)}) collective-permute-start(bf16[128,768]{1,0:T(8,128)(2,1)S(1)} %constant_dynamic-slice_fusion.refs_1_), channel_id=1, source_target_pairs={{0,56},{8,0},{16,8},{24,16},{32,24},{40,32},{48,40},{56,48},{1,57}... | collective-permute-start | bytes 589832 | tf_op jit(solution)/shard_map/ppermute | solution.py:552
  9.0 3.1 %shard_map.100 = (bf16[16,64,128]{2,1,0:T(8,128)(2,1)}, s32[1,72]{1,0:T(1,128)}) custom-call(bf16[256,768]{1,0:T(8,128)(2,1)} %states_ref.1, s32[1,3,4,6]{3,2,1,0:T(4,128)} %bitcast.22, s32[1,3,4,6]{3,2,1,0:T(4,128)} %bitcast.23, s32[1,2]{1,0:T(1,128)} %bitcast.19, s32[1,4]{1,0:T(1,128)} %add_bitcast_fusion.refs_4_.refs_6_.here_ref), custom_call_target="tpu_custom_call" | custom-call | flops 1000000 | bytes 600000 | tf_op jit(solution)/shard_map/pallas_call | solution.py:66
  12.2 6.8 %all-to-all-start.1 = ((bf16[16,64,128]{2,1,0:T(8,128)(2,1)}), bf16[16,64,128]{2,1,0:T(8,128)(2,1)S(1)}, u32[]{:S(2)}, u32[]{:S(2)}) async-start(bf16[16,64,128]{2,1,0:T(8,128)(2,1)} %get-tuple-element.52), calls=%async_computation.1 | async-start | bytes 524288 | tf_op jit(solution)/shard_map/all_to_all | solution.py:556
  19.4 2.9 %collective-permute-start.4 = (bf16[128,768]{1,0:T(8,128)(2,1)S(1)}, bf16[128,768]{1,0:T(8,128)(2,1)S(1)}, u32[]{:S(2)}, u32[]{:S(2)}) collective-permute-start(bf16[128,768]{1,0:T(8,128)(2,1)S(1)} %collective-permute-done.1.refs_8_), channel_id=1, source_target_pairs={{0,56},{8,0},{16,8},{24,16},{32,24},{40,32},{48,40},{56,48},{1,57}... | collective-permute-start | bytes 589832 | tf_op jit(solution)/shard_map/ppermute | solution.py:552
  23.5 3.6 %collective-permute-start.11 = (bf16[64,768]{1,0:T(8,128)(2,1)S(1)}, bf16[64,768]{1,0:T(8,128)(2,1)S(1)}, u32[]{:S(2)}, u32[]{:S(2)}) collective-permute-start(bf16[64,768]{1,0:T(8,128)(2,1)S(1)} %get-tuple-element.87), channel_id=1, source_target_pairs={{0,2},{2,4},{4,6},{6,8},{8,10},{10,12},{12,14},{14,16},{16,18},{18... | collective-permute-start | bytes 294920 | tf_op jit(solution)/shard_map/ppermute | solution.py:573
  27.1 1.3 fusion.1
  30.4 2.9 %collective-permute-start.8 = (bf16[128,768]{1,0:T(8,128)(2,1)S(1)}, bf16[128,768]{1,0:T(8,128)(2,1)S(1)}, u32[]{:S(2)}, u32[]{:S(2)}) collective-permute-start(bf16[128,768]{1,0:T(8,128)(2,1)S(1)} %collective-permute-done.4.refs_7_), channel_id=1, source_target_pairs={{0,56},{8,0},{16,8},{24,16},{32,24},{40,32},{48,40},{56,48},{1,57}... | collective-permute-start | bytes 589832 | tf_op jit(solution)/shard_map/ppermute | solution.py:552
  34.2 5.5 %all-to-all-start.2 = ((bf16[8,48,128]{2,1,0:T(8,128)(2,1)}), bf16[8,48,128]{2,1,0:T(8,128)(2,1)S(1)}, u32[]{:S(2)}, u32[]{:S(2)}) async-start(bf16[8,48,128]{2,1,0:T(8,128)(2,1)} %broadcast_in_dim.8), calls=%async_computation.2 | async-start | bytes 196608 | tf_op jit(solution)/shard_map/all_to_all | solution.py:556
  41.0 4.4 %collective-permute-done.12.refs_2_ = bf16[64,768]{1,0:T(8,128)(2,1)S(1)} collective-permute-done((bf16[64,768]{1,0:T(8,128)(2,1)S(1)}, bf16[64,768]{1,0:T(8,128)(2,1)S(1)}, u32[]{:S(2)}, u32[]{:S(2)}) %collective-permute-start.12) | collective-permute-done | bytes 98336 | tf_op jit(solution)/shard_map/ppermute | solution.py:574
  45.5 1.7 %all-to-all-done.2.refs_18_ = bf16[8,48,128]{2,1,0:T(8,128)(2,1)S(1)} async-done(((bf16[8,48,128]{2,1,0:T(8,128)(2,1)}), bf16[8,48,128]{2,1,0:T(8,128)(2,1)S(1)}, u32[]{:S(2)}, u32[]{:S(2)}) %all-to-all-start.2) | async-done | bytes 98336 | tf_op jit(solution)/shard_map/all_to_all | solution.py:556
  47.7 2.0 %collective-permute-start.14 = (bf16[128,768]{1,0:T(8,128)(2,1)S(1)}, bf16[128,768]{1,0:T(8,128)(2,1)S(1)}, u32[]{:S(2)}, u32[]{:S(2)}) collective-permute-start(bf16[128,768]{1,0:T(8,128)(2,1)S(1)} %collective-permute-done.7.refs_4_), channel_id=1, source_target_pairs={{0,1},{1,0},{2,3},{3,2},{4,5},{5,4},{6,7},{7,6},{8,9},{9,8},{10,11... | collective-permute-start | bytes 589832 | tf_op jit(solution)/shard_map/ppermute | solution.py:560
  49.7 3.3 %collective-permute-done.13.refs_5_ = bf16[128,768]{1,0:T(8,128)(2,1)S(1)} collective-permute-done((bf16[128,768]{1,0:T(8,128)(2,1)S(1)}, bf16[128,768]{1,0:T(8,128)(2,1)S(1)}, u32[]{:S(2)}, u32[]{:S(2)}) %collective-permute-start.13) | collective-permute-done | bytes 196640 | tf_op jit(solution)/shard_map/ppermute | solution.py:552
  53.0 3.1 %collective-permute-start.15 = (bf16[128,768]{1,0:T(8,128)(2,1)S(1)}, bf16[128,768]{1,0:T(8,128)(2,1)S(1)}, u32[]{:S(2)}, u32[]{:S(2)}) collective-permute-start(bf16[128,768]{1,0:T(8,128)(2,1)S(1)} %collective-permute-done.13.refs_5_), channel_id=1, source_target_pairs={{0,1},{1,0},{2,3},{3,2},{4,5},{5,4},{6,7},{7,6},{8,9},{9,8},{10,11... | collective-permute-start | bytes 589832 | tf_op jit(solution)/shard_map/ppermute | solution.py:560
  57.2 9.6 %shard_map.102 = (bf16[96,128,128]{2,1,0:T(8,128)(2,1)}, bf16[16,688,128]{2,1,0:T(8,128)(2,1)}, s32[16,128]{1,0:T(8,128)S(1)}, s32[1,1]{1,0:T(1,128)}) custom-call(bf16[3,768,384]{2,1,0:T(8,128)(2,1)} %refs_0_.3, bf16[128,768]{1,0:T(8,128)(2,1)S(1)} %constant_dynamic-slice_fusion.refs_1_, bf16[128,768]{1,0:T(8,128)(2,1)S(1)} %collective-permute-done.refs_2_, ...), custom_call_target="tpu_custom_call" | custom-call | flops 2400000000 | bytes 10000000 | tf_op jit(solution)/shard_map/pallas_call | solution.py:66
  68.1 6.9 %all-to-all-start.3 = ((bf16[16,688,128]{2,1,0:T(8,128)(2,1)}), bf16[16,688,128]{2,1,0:T(8,128)(2,1)}, u32[]{:S(2)}, u32[]{:S(2)}) async-start(bf16[16,688,128]{2,1,0:T(8,128)(2,1)} %get-tuple-element.72), calls=%async_computation.3 | async-start | bytes 5636096 | tf_op jit(solution)/shard_map/all_to_all | solution.py:556
  75.9 4.4 %shard_map.101 = (bf16[6,256,128]{2,1,0:T(8,128)(2,1)S(1)}, bf16[6,384,128]{2,1,0:T(8,128)(2,1)S(1)}, bf16[768,768]{1,0:T(8,128)(2,1)S(1)}, bf16[768,768]{1,0:T(8,128)(2,1)}) custom-call(bf16[64,768]{1,0:T(8,128)(2,1)S(1)} %collective-permute-done.11.refs_0_, bf16[256,768]{1,0:T(8,128)(2,1)S(1)} %copy-done, ...), custom_call_target="tpu_custom_call" | custom-call | flops 800000000 | bytes 4000000 | tf_op jit(solution)/shard_map/pallas_call | solution.py:66
  80.8 31.2 %all-to-all-done.3.refs_3_ = bf16[16,688,128]{2,1,0:T(8,128)(2,1)} async-done(((bf16[16,688,128]{2,1,0:T(8,128)(2,1)}), bf16[16,688,128]{2,1,0:T(8,128)(2,1)}, u32[]{:S(2)}, u32[]{:S(2)}) %all-to-all-start.3) | async-done | bytes 2818080 | tf_op jit(solution)/shard_map/all_to_all | solution.py:556
  113.3 6.3 %shard_map.103 = (f32[128,640]{1,0:T(8,128)S(1)}, bf16[6,128,128]{2,1,0:T(8,128)(2,1)S(1)}) custom-call(bf16[768,768]{1,0:T(8,128)(2,1)S(1)} %get-tuple-element.58.refs_0_, bf16[768,768]{1,0:T(8,128)(2,1)S(1)} %copy-done.1, bf16[16,6,128,128]{3,2,1,0:T(8,128)(2,1)} %bitcast.21, bf16[16,688,128]{2,1,0:T(8,128)(2,1)} %all-to-all-done.3.refs_3_), custom_call_target="tpu_custom_call" | custom-call | flops 2000000000 | bytes 10000000 | tf_op jit(solution)/shard_map/pallas_call | solution.py:66
  120.3 8.1 %all-to-all-start.4 = ((f32[16,8,640]{2,1,0:T(8,128)}), f32[16,8,640]{2,1,0:T(8,128)S(1)}, u32[]{:S(2)}, u32[]{:S(2)}) async-start(f32[16,8,640]{2,1,0:T(8,128)} %bitcast.18), calls=%async_computation.4 | async-start | bytes 655360 | tf_op jit(solution)/shard_map/all_to_all | solution.py:556
  128.5 8.6 %shard_map.104.own_ref = bf16[256,256]{1,0:T(8,128)(2,1)S(1)} custom-call(bf16[6,256,128]{2,1,0:T(8,128)(2,1)S(1)} %get-tuple-element.76.refs_0_, bf16[6,384,128]{2,1,0:T(8,128)(2,1)S(1)} %get-tuple-element.77.refs_1_, bf16[6,128,128]{2,1,0:T(8,128)(2,1)S(1)} %get-tuple-element.78.refs_2_, bf16[11008,128]{1,0:T(8,128)(2,1)} %bitcast.14.refs_3_, ...), custom_call_target="tpu_custom_call" | custom-call | flops 400000000 | bytes 3000000 | tf_op jit(solution)/shard_map/pallas_call | solution.py:66
  138.0 9.1 %all-to-all-start.5 = ((bf16[32,8,384]{2,1,0:T(8,128)(2,1)}), bf16[32,8,384]{2,1,0:T(8,128)(2,1)S(1)}, u32[]{:S(2)}, u32[]{:S(2)}) async-start(bf16[32,8,384]{2,1,0:T(8,128)(2,1)} %shard_map.106), calls=%async_computation.5 | async-start | bytes 393216 | tf_op jit(solution)/shard_map/all_to_all | solution.py:556
  147.7 5.9 %shard_map.105.own2_ref = bf16[256,128]{1,0:T(8,128)(2,1)S(1)} custom-call(bf16[6,256,128]{2,1,0:T(8,128)(2,1)S(1)} %get-tuple-element.76.refs_0_, bf16[6,384,128]{2,1,0:T(8,128)(2,1)S(1)} %get-tuple-element.77.refs_1_, bf16[6,128,128]{2,1,0:T(8,128)(2,1)S(1)} %get-tuple-element.78.refs_2_, bf16[11008,128]{1,0:T(8,128)(2,1)} %bitcast.14.refs_3_, ...), custom_call_target="tpu_custom_call" | custom-call | flops 200000000 | bytes 1500000 | tf_op jit(solution)/shard_map/pallas_call | solution.py:66
  155.4 8.4 %shard_map.107 = bf16[256,768]{1,0:T(8,128)(2,1)} custom-call(bf16[256,256]{1,0:T(8,128)(2,1)S(1)} %shard_map.104.own_ref, bf16[256,256]{1,0:T(8,128)(2,1)S(1)} %collective-permute-done.17.other_ref, bf16[256,128]{1,0:T(8,128)(2,1)S(1)} %shard_map.105.own2_ref, bf16[256,128]{1,0:T(8,128)(2,1)S(1)} %collective-permute-done.18.other2_ref, ...), custom_call_target="tpu_custom_call" | custom-call | flops 2700000000 | bytes 12000000 | tf_op jit(solution)/shard_map/pallas_call | solution.py:528
  (70 shorter events, 16.5 us)
Async XLA Ops:
  0.9 18.0 %collective-permute-start = (bf16[128,768]{1,0:T(8,128)(2,1)S(1)}, bf16[128,768]{1,0:T(8,128)(2,1)S(1)}, u32[]{:S(2)}, u32[]{:S(2)}) collective-permute-start(bf16[128,768]{1,0:T(8,128)(2,1)S(1)} %constant_dynamic-slice_fusion.refs_1_), channel_id=1, source_target_pairs={{0,8},{8,16},{16,24},{24,32},{32,40},{40,48},{48,56},{56,0},{1,9},... | collective-permute-start | bytes 589832 | tf_op jit(solution)/shard_map/ppermute | solution.py:552
  3.5 15.5 %collective-permute-start.1 = (bf16[128,768]{1,0:T(8,128)(2,1)S(1)}, bf16[128,768]{1,0:T(8,128)(2,1)S(1)}, u32[]{:S(2)}, u32[]{:S(2)}) collective-permute-start(bf16[128,768]{1,0:T(8,128)(2,1)S(1)} %constant_dynamic-slice_fusion.refs_1_), channel_id=1, source_target_pairs={{0,56},{8,0},{16,8},{24,16},{32,24},{40,32},{48,40},{56,48},{1,57}... | collective-permute-start | bytes 589832 | tf_op jit(solution)/shard_map/ppermute | solution.py:552
  7.5 11.4 %collective-permute-start.2 = (bf16[128,768]{1,0:T(8,128)(2,1)S(1)}, bf16[128,768]{1,0:T(8,128)(2,1)S(1)}, u32[]{:S(2)}, u32[]{:S(2)}) collective-permute-start(bf16[128,768]{1,0:T(8,128)(2,1)S(1)} %constant_dynamic-slice_fusion.refs_1_), channel_id=1, source_target_pairs={{0,1},{1,0},{2,3},{3,2},{4,5},{5,4},{6,7},{7,6},{8,9},{9,8},{10,11... | collective-permute-start | bytes 589832 | tf_op jit(solution)/shard_map/ppermute | solution.py:560
  12.2 17.5 %all-to-all-start.1 = ((bf16[16,64,128]{2,1,0:T(8,128)(2,1)}), bf16[16,64,128]{2,1,0:T(8,128)(2,1)S(1)}, u32[]{:S(2)}, u32[]{:S(2)}) async-start(bf16[16,64,128]{2,1,0:T(8,128)(2,1)} %get-tuple-element.52), calls=%async_computation.1 | async-start | bytes 524288 | tf_op jit(solution)/shard_map/all_to_all | solution.py:556
  19.0 10.8 %collective-permute-start.3 = (bf16[128,768]{1,0:T(8,128)(2,1)S(1)}, bf16[128,768]{1,0:T(8,128)(2,1)S(1)}, u32[]{:S(2)}, u32[]{:S(2)}) collective-permute-start(bf16[128,768]{1,0:T(8,128)(2,1)S(1)} %collective-permute-done.refs_2_), channel_id=1, source_target_pairs={{0,8},{8,16},{16,24},{24,32},{32,40},{40,48},{48,56},{56,0},{1,9},... | collective-permute-start | bytes 589832 | tf_op jit(solution)/shard_map/ppermute | solution.py:552
  19.0 10.7 %collective-permute-start.5 = (bf16[128,768]{1,0:T(8,128)(2,1)S(1)}, bf16[128,768]{1,0:T(8,128)(2,1)S(1)}, u32[]{:S(2)}, u32[]{:S(2)}) collective-permute-start(bf16[128,768]{1,0:T(8,128)(2,1)S(1)} %collective-permute-done.refs_2_), channel_id=1, source_target_pairs={{0,1},{1,0},{2,3},{3,2},{4,5},{5,4},{6,7},{7,6},{8,9},{9,8},{10,11... | collective-permute-start | bytes 589832 | tf_op jit(solution)/shard_map/ppermute | solution.py:560
  19.4 10.3 %collective-permute-start.4 = (bf16[128,768]{1,0:T(8,128)(2,1)S(1)}, bf16[128,768]{1,0:T(8,128)(2,1)S(1)}, u32[]{:S(2)}, u32[]{:S(2)}) collective-permute-start(bf16[128,768]{1,0:T(8,128)(2,1)S(1)} %collective-permute-done.1.refs_8_), channel_id=1, source_target_pairs={{0,56},{8,0},{16,8},{24,16},{32,24},{40,32},{48,40},{56,48},{1,57}... | collective-permute-start | bytes 589832 | tf_op jit(solution)/shard_map/ppermute | solution.py:552
  22.3 7.5 %collective-permute-start.6 = (bf16[128,768]{1,0:T(8,128)(2,1)S(1)}, bf16[128,768]{1,0:T(8,128)(2,1)S(1)}, u32[]{:S(2)}, u32[]{:S(2)}) collective-permute-start(bf16[128,768]{1,0:T(8,128)(2,1)S(1)} %collective-permute-done.1.refs_8_), channel_id=1, source_target_pairs={{0,1},{1,0},{2,3},{3,2},{4,5},{5,4},{6,7},{7,6},{8,9},{9,8},{10,11... | collective-permute-start | bytes 589832 | tf_op jit(solution)/shard_map/ppermute | solution.py:560
  23.5 16.2 %collective-permute-start.11 = (bf16[64,768]{1,0:T(8,128)(2,1)S(1)}, bf16[64,768]{1,0:T(8,128)(2,1)S(1)}, u32[]{:S(2)}, u32[]{:S(2)}) collective-permute-start(bf16[64,768]{1,0:T(8,128)(2,1)S(1)} %get-tuple-element.87), channel_id=1, source_target_pairs={{0,2},{2,4},{4,6},{6,8},{8,10},{10,12},{12,14},{14,16},{16,18},{18... | collective-permute-start | bytes 294920 | tf_op jit(solution)/shard_map/ppermute | solution.py:573
  29.8 17.4 %collective-permute-start.7 = (bf16[128,768]{1,0:T(8,128)(2,1)S(1)}, bf16[128,768]{1,0:T(8,128)(2,1)S(1)}, u32[]{:S(2)}, u32[]{:S(2)}) collective-permute-start(bf16[128,768]{1,0:T(8,128)(2,1)S(1)} %collective-permute-done.3.refs_3_), channel_id=1, source_target_pairs={{0,8},{8,16},{16,24},{24,32},{32,40},{40,48},{48,56},{56,0},{1,9},... | collective-permute-start | bytes 589832 | tf_op jit(solution)/shard_map/ppermute | solution.py:552
  29.9 17.3 %collective-permute-start.9 = (bf16[128,768]{1,0:T(8,128)(2,1)S(1)}, bf16[128,768]{1,0:T(8,128)(2,1)S(1)}, u32[]{:S(2)}, u32[]{:S(2)}) collective-permute-start(bf16[128,768]{1,0:T(8,128)(2,1)S(1)} %collective-permute-done.3.refs_3_), channel_id=1, source_target_pairs={{0,1},{1,0},{2,3},{3,2},{4,5},{5,4},{6,7},{7,6},{8,9},{9,8},{10,11... | collective-permute-start | bytes 589832 | tf_op jit(solution)/shard_map/ppermute | solution.py:560
  30.4 16.7 %collective-permute-start.8 = (bf16[128,768]{1,0:T(8,128)(2,1)S(1)}, bf16[128,768]{1,0:T(8,128)(2,1)S(1)}, u32[]{:S(2)}, u32[]{:S(2)}) collective-permute-start(bf16[128,768]{1,0:T(8,128)(2,1)S(1)} %collective-permute-done.4.refs_7_), channel_id=1, source_target_pairs={{0,56},{8,0},{16,8},{24,16},{32,24},{40,32},{48,40},{56,48},{1,57}... | collective-permute-start | bytes 589832 | tf_op jit(solution)/shard_map/ppermute | solution.py:552
  33.3 13.9 %collective-permute-start.10 = (bf16[128,768]{1,0:T(8,128)(2,1)S(1)}, bf16[128,768]{1,0:T(8,128)(2,1)S(1)}, u32[]{:S(2)}, u32[]{:S(2)}) collective-permute-start(bf16[128,768]{1,0:T(8,128)(2,1)S(1)} %collective-permute-done.4.refs_7_), channel_id=1, source_target_pairs={{0,1},{1,0},{2,3},{3,2},{4,5},{5,4},{6,7},{7,6},{8,9},{9,8},{10,11... | collective-permute-start | bytes 589832 | tf_op jit(solution)/shard_map/ppermute | solution.py:560
  34.2 12.9 %all-to-all-start.2 = ((bf16[8,48,128]{2,1,0:T(8,128)(2,1)}), bf16[8,48,128]{2,1,0:T(8,128)(2,1)S(1)}, u32[]{:S(2)}, u32[]{:S(2)}) async-start(bf16[8,48,128]{2,1,0:T(8,128)(2,1)} %broadcast_in_dim.8), calls=%async_computation.2 | async-start | bytes 196608 | tf_op jit(solution)/shard_map/all_to_all | solution.py:556
  47.2 5.8 %collective-permute-start.13 = (bf16[128,768]{1,0:T(8,128)(2,1)S(1)}, bf16[128,768]{1,0:T(8,128)(2,1)S(1)}, u32[]{:S(2)}, u32[]{:S(2)}) collective-permute-start(bf16[128,768]{1,0:T(8,128)(2,1)S(1)} %collective-permute-done.7.refs_4_), channel_id=1, source_target_pairs={{0,8},{8,16},{16,24},{24,32},{32,40},{40,48},{48,56},{56,0},{1,9},... | collective-permute-start | bytes 589832 | tf_op jit(solution)/shard_map/ppermute | solution.py:552
  47.7 8.4 %collective-permute-start.14 = (bf16[128,768]{1,0:T(8,128)(2,1)S(1)}, bf16[128,768]{1,0:T(8,128)(2,1)S(1)}, u32[]{:S(2)}, u32[]{:S(2)}) collective-permute-start(bf16[128,768]{1,0:T(8,128)(2,1)S(1)} %collective-permute-done.7.refs_4_), channel_id=1, source_target_pairs={{0,1},{1,0},{2,3},{3,2},{4,5},{5,4},{6,7},{7,6},{8,9},{9,8},{10,11... | collective-permute-start | bytes 589832 | tf_op jit(solution)/shard_map/ppermute | solution.py:560
  49.7 6.4 %collective-permute-start.16 = (bf16[128,768]{1,0:T(8,128)(2,1)S(1)}, bf16[128,768]{1,0:T(8,128)(2,1)S(1)}, u32[]{:S(2)}, u32[]{:S(2)}) collective-permute-start(bf16[128,768]{1,0:T(8,128)(2,1)S(1)} %collective-permute-done.8.refs_6_), channel_id=1, source_target_pairs={{0,1},{1,0},{2,3},{3,2},{4,5},{5,4},{6,7},{7,6},{8,9},{9,8},{10,11... | collective-permute-start | bytes 589832 | tf_op jit(solution)/shard_map/ppermute | solution.py:560
  68.1 43.9 %all-to-all-start.3 = ((bf16[16,688,128]{2,1,0:T(8,128)(2,1)}), bf16[16,688,128]{2,1,0:T(8,128)(2,1)}, u32[]{:S(2)}, u32[]{:S(2)}) async-start(bf16[16,688,128]{2,1,0:T(8,128)(2,1)} %get-tuple-element.72), calls=%async_computation.3 | async-start | bytes 5636096 | tf_op jit(solution)/shard_map/all_to_all | solution.py:556
  75.1 78.8 %collective-permute-start.20 = (bf16[768,1536]{1,0:T(8,128)(2,1)}, bf16[768,1536]{1,0:T(8,128)(2,1)}, u32[]{:S(2)}, u32[]{:S(2)}) collective-permute-start(bf16[768,1536]{1,0:T(8,128)(2,1)} %up_own.1), channel_id=1, source_target_pairs={{0,1},{1,0},{2,3},{3,2},{4,5},{5,4},{6,7},{7,6},{8,9},{9,8},{10,11... | collective-permute-start | bytes 7077896 | tf_op jit(solution)/shard_map/ppermute | solution.py:560
  75.8 78.1 %collective-permute-start.21 = (bf16[1536,768]{1,0:T(8,128)(2,1)}, bf16[1536,768]{1,0:T(8,128)(2,1)}, u32[]{:S(2)}, u32[]{:S(2)}) collective-permute-start(bf16[1536,768]{1,0:T(8,128)(2,1)} %down_own.1), channel_id=1, source_target_pairs={{0,1},{1,0},{2,3},{3,2},{4,5},{5,4},{6,7},{7,6},{8,9},{9,8},{10,11... | collective-permute-start | bytes 7077896 | tf_op jit(solution)/shard_map/ppermute | solution.py:560
  80.3 73.6 %collective-permute-start.19 = (bf16[384,768]{1,0:T(8,128)(2,1)S(1)}, bf16[384,768]{1,0:T(8,128)(2,1)}, u32[]{:S(2)}, u32[]{:S(2)}) collective-permute-start(bf16[384,768]{1,0:T(8,128)(2,1)S(1)} %copy-done.2), channel_id=1, source_target_pairs={{0,1},{1,0},{2,3},{3,2},{4,5},{5,4},{6,7},{7,6},{8,9},{9,8},{10,11... | collective-permute-start | bytes 1769480 | tf_op jit(solution)/shard_map/ppermute | solution.py:560
  120.3 16.7 %all-to-all-start.4 = ((f32[16,8,640]{2,1,0:T(8,128)}), f32[16,8,640]{2,1,0:T(8,128)S(1)}, u32[]{:S(2)}, u32[]{:S(2)}) async-start(f32[16,8,640]{2,1,0:T(8,128)} %bitcast.18), calls=%async_computation.4 | async-start | bytes 655360 | tf_op jit(solution)/shard_map/all_to_all | solution.py:556
  138.0 17.4 %all-to-all-start.5 = ((bf16[32,8,384]{2,1,0:T(8,128)(2,1)}), bf16[32,8,384]{2,1,0:T(8,128)(2,1)S(1)}, u32[]{:S(2)}, u32[]{:S(2)}) async-start(bf16[32,8,384]{2,1,0:T(8,128)(2,1)} %shard_map.106), calls=%async_computation.5 | async-start | bytes 393216 | tf_op jit(solution)/shard_map/all_to_all | solution.py:556
  147.1 7.7 %collective-permute-start.17 = (bf16[256,256]{1,0:T(8,128)(2,1)S(1)}, bf16[256,256]{1,0:T(8,128)(2,1)S(1)}, u32[]{:S(2)}, u32[]{:S(2)}) collective-permute-start(bf16[256,256]{1,0:T(8,128)(2,1)S(1)} %shard_map.104.own_ref), channel_id=1, source_target_pairs={{0,1},{1,0},{2,3},{3,2},{4,5},{5,4},{6,7},{7,6},{8,9},{9,8},{10,11... | collective-permute-start | bytes 393224 | tf_op jit(solution)/shard_map/ppermute | solution.py:560
  (14 other events, 133.4 us)

commit v9 on v8

--- a/solution.py
+++ b/solution.py
@@ -588,9 +588,10 @@
     shares = exchanged(jnp.broadcast_to(share, (8, 48, 128)), "z")
     up3, down3 = turned(up2, "z", 1), turned(down2, "z", -1)
     far2, far6 = swapped(up2), swapped(down2)
-    up3, down3, far2, far6, shares, before, after = tied((up3, down3, far2, far6, shares, before, after))
+    up3, down3, far2, far6 = tied((up3, down3, far2, far6))
 
     up4 = turned(up3, "z", 1)
+    up3, down3, shares, before, after = tied((up3, down3, shares, before, after))
     far3, far5 = swapped(up3), swapped(down3)
     pieces = [up0, up1, up2, up3, up4, down3, down2, down1, far0, far1, far2, far3, swapped(up4), far5, far6, far7]
     pairs, items, wanted, flag = column(pieces, qkv_weight, received, shares)

time: 165 us -> 165 us (level)
    ppermute x7, waiting for transfers between devices: 3.3 us -> 0.02 us  [turned(): lax.ppermute(value, axis, [(i, (i + shift) % count) for i in range(count)])]
    all_to_all x5, waiting for transfers between devices: 33.4 us -> 36.1 us  [exchanged(): return lax.all_to_all(value, axes, split_axis=0, concat_axis=0, tiled=True)]
  transfers between devices with their start and end apart: 27 -> 27, of which waited for: 7 -> 9; matrix products, arithmetic and copies ran while one was open for 2% -> 2% of each run, Pallas kernels for 18% -> 18%
where the time goes in v9:
time: 165 us; the launch traced here: 164 us
  starting transfers between devices  64.1 us (39%)
  Pallas kernels  47.1 us (29%)
  waiting for transfers between devices  42.5 us (26%)
  local copies, waits for them, and re-layouts  7.08 us (4%)
  between operations  2.44 us (1%)
    pallas_call x7, Pallas kernels, call(): pl.pallas_call(body, out_shape=(*results, *tables), in_specs=[FAR] * (cou...  38.7 us
    all_to_all x5, starting transfers between devices, exchanged(): return lax.all_to_all(value, axes, split_axis=0, concat_axis=0, tiled=True)  37.7 us
    all_to_all x5, waiting for transfers between devices, exchanged(): return lax.all_to_all(value, axes, split_axis=0, concat_axis=0, tiled=True)  36.1 us
    ppermute x7, starting transfers between devices, turned(): lax.ppermute(value, axis, [(i, (i + shift) % count) for i in range(count)])  13.8 us
    ppermute x13, starting transfers between devices, swapped(): return lax.ppermute(value, 'mp', [(0, 1), (1, 0)])  8.84 us
    pallas_call x1, Pallas kernels, finish(): pl.pallas_call(finish_kernel, out_shape=jax.ShapeDtypeStruct((256, 768),...  8.43 us
    ppermute x1, waiting for transfers between devices, shards(): after = lax.ppermute(states[:64], SEQ, [(j, i) for i, j in ends])  3.87 us
  transfers between devices with their start and end apart: 27, of which 9 were waited for; matrix products, arithmetic and copies ran while one was open for 2% of the time, Pallas kernels for 18%

profile of v9, /device:TPU:1, one launch (start us, length us, event | category | flops | bytes accessed | tf_op | source)
XLA Modules:
  0.0 163.9 jit_solution(9215368402192171080)
XLA Ops:
  0.9 2.5 %collective-permute-start = (bf16[128,768]{1,0:T(8,128)(2,1)S(1)}, bf16[128,768]{1,0:T(8,128)(2,1)S(1)}, u32[]{:S(2)}, u32[]{:S(2)}) collective-permute-start(bf16[128,768]{1,0:T(8,128)(2,1)S(1)} %constant_dynamic-slice_fusion.refs_1_), channel_id=1, source_target_pairs={{0,8},{8,16},{16,24},{24,32},{32,40},{40,48},{48,56},{56,0},{1,9},... | collective-permute-start | bytes 589832 | tf_op jit(solution)/shard_map/ppermute | solution.py:552
  3.5 4.0 %collective-permute-start.1 = (bf16[128,768]{1,0:T(8,128)(2,1)S(1)}, bf16[128,768]{1,0:T(8,128)(2,1)S(1)}, u32[]{:S(2)}, u32[]{:S(2)}) collective-permute-start(bf16[128,768]{1,0:T(8,128)(2,1)S(1)} %constant_dynamic-slice_fusion.refs_1_), channel_id=1, source_target_pairs={{0,56},{8,0},{16,8},{24,16},{32,24},{40,32},{48,40},{56,48},{1,57}... | collective-permute-start | bytes 589832 | tf_op jit(solution)/shard_map/ppermute | solution.py:552
  9.1 3.1 %shard_map.100 = (bf16[16,64,128]{2,1,0:T(8,128)(2,1)}, s32[1,72]{1,0:T(1,128)}) custom-call(bf16[256,768]{1,0:T(8,128)(2,1)} %states_ref.1, s32[1,3,4,6]{3,2,1,0:T(4,128)} %bitcast.24, s32[1,3,4,6]{3,2,1,0:T(4,128)} %bitcast.25, s32[1,2]{1,0:T(1,128)} %bitcast.19, s32[1,4]{1,0:T(1,128)} %add_bitcast_fusion.refs_4_.refs_6_.here_ref), custom_call_target="tpu_custom_call" | custom-call | flops 1000000 | bytes 600000 | tf_op jit(solution)/shard_map/pallas_call | solution.py:66
  12.2 6.8 %all-to-all-start.1 = ((bf16[16,64,128]{2,1,0:T(8,128)(2,1)}), bf16[16,64,128]{2,1,0:T(8,128)(2,1)S(1)}, u32[]{:S(2)}, u32[]{:S(2)}) async-start(bf16[16,64,128]{2,1,0:T(8,128)(2,1)} %get-tuple-element.54), calls=%async_computation.1 | async-start | bytes 524288 | tf_op jit(solution)/shard_map/all_to_all | solution.py:556
  19.1 2.7 %collective-permute-start.4 = (bf16[128,768]{1,0:T(8,128)(2,1)S(1)}, bf16[128,768]{1,0:T(8,128)(2,1)S(1)}, u32[]{:S(2)}, u32[]{:S(2)}) collective-permute-start(bf16[128,768]{1,0:T(8,128)(2,1)S(1)} %collective-permute-done.1.refs_8_), channel_id=1, source_target_pairs={{0,56},{8,0},{16,8},{24,16},{32,24},{40,32},{48,40},{56,48},{1,57}... | collective-permute-start | bytes 589832 | tf_op jit(solution)/shard_map/ppermute | solution.py:552
  22.7 4.2 %all-to-all-done.1.refs_17_ = bf16[16,64,128]{2,1,0:T(8,128)(2,1)S(1)} async-done(((bf16[16,64,128]{2,1,0:T(8,128)(2,1)}), bf16[16,64,128]{2,1,0:T(8,128)(2,1)S(1)}, u32[]{:S(2)}, u32[]{:S(2)}) %all-to-all-start.1) | async-done | bytes 262176 | tf_op jit(solution)/shard_map/all_to_all | solution.py:556
  27.0 1.7 %collective-permute-start.9 = (bf16[128,768]{1,0:T(8,128)(2,1)S(1)}, bf16[128,768]{1,0:T(8,128)(2,1)S(1)}, u32[]{:S(2)}, u32[]{:S(2)}) collective-permute-start(bf16[128,768]{1,0:T(8,128)(2,1)S(1)} %collective-permute-done.3.refs_3_), channel_id=1, source_target_pairs={{0,1},{1,0},{2,3},{3,2},{4,5},{5,4},{6,7},{7,6},{8,9},{9,8},{10,11... | collective-permute-start | bytes 589832 | tf_op jit(solution)/shard_map/ppermute | solution.py:560
  28.7 2.9 %collective-permute-start.8 = (bf16[128,768]{1,0:T(8,128)(2,1)S(1)}, bf16[128,768]{1,0:T(8,128)(2,1)S(1)}, u32[]{:S(2)}, u32[]{:S(2)}) collective-permute-start(bf16[128,768]{1,0:T(8,128)(2,1)S(1)} %collective-permute-done.4.refs_7_), channel_id=1, source_target_pairs={{0,56},{8,0},{16,8},{24,16},{32,24},{40,32},{48,40},{56,48},{1,57}... | collective-permute-start | bytes 589832 | tf_op jit(solution)/shard_map/ppermute | solution.py:552
  31.8 1.4 fusion.1
  35.1 5.5 %all-to-all-start.2 = ((bf16[8,48,128]{2,1,0:T(8,128)(2,1)}), bf16[8,48,128]{2,1,0:T(8,128)(2,1)S(1)}, u32[]{:S(2)}, u32[]{:S(2)}) async-start(bf16[8,48,128]{2,1,0:T(8,128)(2,1)} %broadcast_in_dim.8), calls=%async_computation.2 | async-start | bytes 196608 | tf_op jit(solution)/shard_map/all_to_all | solution.py:556
  40.6 1.5 collective-permute-start.13
  43.1 2.4 %collective-permute-start.11 = (bf16[64,768]{1,0:T(8,128)(2,1)S(1)}, bf16[64,768]{1,0:T(8,128)(2,1)S(1)}, u32[]{:S(2)}, u32[]{:S(2)}) collective-permute-start(bf16[64,768]{1,0:T(8,128)(2,1)S(1)} %get-tuple-element.91), channel_id=1, source_target_pairs={{0,2},{2,4},{4,6},{6,8},{8,10},{10,12},{12,14},{14,16},{16,18},{18... | collective-permute-start | bytes 294920 | tf_op jit(solution)/shard_map/ppermute | solution.py:573
  47.2 3.9 %collective-permute-done.12.refs_2_ = bf16[64,768]{1,0:T(8,128)(2,1)S(1)} collective-permute-done((bf16[64,768]{1,0:T(8,128)(2,1)S(1)}, bf16[64,768]{1,0:T(8,128)(2,1)S(1)}, u32[]{:S(2)}, u32[]{:S(2)}) %collective-permute-start.12) | collective-permute-done | bytes 98336 | tf_op jit(solution)/shard_map/ppermute | solution.py:574
  51.1 2.4 %collective-permute-start.14 = (bf16[128,768]{1,0:T(8,128)(2,1)S(1)}, bf16[128,768]{1,0:T(8,128)(2,1)S(1)}, u32[]{:S(2)}, u32[]{:S(2)}) collective-permute-start(bf16[128,768]{1,0:T(8,128)(2,1)S(1)} %collective-permute-done.7.refs_4_), channel_id=1, source_target_pairs={{0,1},{1,0},{2,3},{3,2},{4,5},{5,4},{6,7},{7,6},{8,9},{9,8},{10,11... | collective-permute-start | bytes 589832 | tf_op jit(solution)/shard_map/ppermute | solution.py:560
  55.2 9.7 %shard_map.102 = (bf16[96,128,128]{2,1,0:T(8,128)(2,1)}, bf16[16,688,128]{2,1,0:T(8,128)(2,1)}, s32[16,128]{1,0:T(8,128)S(1)}, s32[1,1]{1,0:T(1,128)}) custom-call(bf16[3,768,384]{2,1,0:T(8,128)(2,1)} %refs_0_.3, bf16[128,768]{1,0:T(8,128)(2,1)S(1)} %constant_dynamic-slice_fusion.refs_1_, bf16[128,768]{1,0:T(8,128)(2,1)S(1)} %collective-permute-done.refs_2_, ...), custom_call_target="tpu_custom_call" | custom-call | flops 2400000000 | bytes 10000000 | tf_op jit(solution)/shard_map/pallas_call | solution.py:66
  66.6 8.5 %all-to-all-start.3 = ((bf16[16,688,128]{2,1,0:T(8,128)(2,1)}), bf16[16,688,128]{2,1,0:T(8,128)(2,1)}, u32[]{:S(2)}, u32[]{:S(2)}) async-start(bf16[16,688,128]{2,1,0:T(8,128)(2,1)} %get-tuple-element.76), calls=%async_computation.3 | async-start | bytes 5636096 | tf_op jit(solution)/shard_map/all_to_all | solution.py:556
  75.9 4.4 %shard_map.101 = (bf16[6,256,128]{2,1,0:T(8,128)(2,1)S(1)}, bf16[6,384,128]{2,1,0:T(8,128)(2,1)S(1)}, bf16[768,768]{1,0:T(8,128)(2,1)S(1)}, bf16[768,768]{1,0:T(8,128)(2,1)}) custom-call(bf16[64,768]{1,0:T(8,128)(2,1)S(1)} %collective-permute-done.11.refs_0_, bf16[256,768]{1,0:T(8,128)(2,1)S(1)} %copy-done, ...), custom_call_target="tpu_custom_call" | custom-call | flops 800000000 | bytes 4000000 | tf_op jit(solution)/shard_map/pallas_call | solution.py:66
  80.8 31.4 %all-to-all-done.3.refs_3_ = bf16[16,688,128]{2,1,0:T(8,128)(2,1)} async-done(((bf16[16,688,128]{2,1,0:T(8,128)(2,1)}), bf16[16,688,128]{2,1,0:T(8,128)(2,1)}, u32[]{:S(2)}, u32[]{:S(2)}) %all-to-all-start.3) | async-done | bytes 2818080 | tf_op jit(solution)/shard_map/all_to_all | solution.py:556
  113.4 6.3 %shard_map.103 = (f32[128,640]{1,0:T(8,128)S(1)}, bf16[6,128,128]{2,1,0:T(8,128)(2,1)S(1)}) custom-call(bf16[768,768]{1,0:T(8,128)(2,1)S(1)} %get-tuple-element.62.refs_0_, bf16[768,768]{1,0:T(8,128)(2,1)S(1)} %copy-done.1, bf16[16,6,128,128]{3,2,1,0:T(8,128)(2,1)} %bitcast.23, bf16[16,688,128]{2,1,0:T(8,128)(2,1)} %all-to-all-done.3.refs_3_), custom_call_target="tpu_custom_call" | custom-call | flops 2000000000 | bytes 10000000 | tf_op jit(solution)/shard_map/pallas_call | solution.py:66
  120.5 8.0 %all-to-all-start.4 = ((f32[16,8,640]{2,1,0:T(8,128)}), f32[16,8,640]{2,1,0:T(8,128)S(1)}, u32[]{:S(2)}, u32[]{:S(2)}) async-start(f32[16,8,640]{2,1,0:T(8,128)} %bitcast.18), calls=%async_computation.4 | async-start | bytes 655360 | tf_op jit(solution)/shard_map/all_to_all | solution.py:556
  128.5 8.5 %shard_map.104.own_ref = bf16[256,256]{1,0:T(8,128)(2,1)S(1)} custom-call(bf16[6,256,128]{2,1,0:T(8,128)(2,1)S(1)} %get-tuple-element.80.refs_0_, bf16[6,384,128]{2,1,0:T(8,128)(2,1)S(1)} %get-tuple-element.81.refs_1_, bf16[6,128,128]{2,1,0:T(8,128)(2,1)S(1)} %get-tuple-element.82.refs_2_, bf16[11008,128]{1,0:T(8,128)(2,1)} %bitcast.14.refs_3_, ...), custom_call_target="tpu_custom_call" | custom-call | flops 400000000 | bytes 3000000 | tf_op jit(solution)/shard_map/pallas_call | solution.py:66
  138.0 9.0 %all-to-all-start.5 = ((bf16[32,8,384]{2,1,0:T(8,128)(2,1)}), bf16[32,8,384]{2,1,0:T(8,128)(2,1)S(1)}, u32[]{:S(2)}, u32[]{:S(2)}) async-start(bf16[32,8,384]{2,1,0:T(8,128)(2,1)} %shard_map.106), calls=%async_computation.5 | async-start | bytes 393216 | tf_op jit(solution)/shard_map/all_to_all | solution.py:556
  147.6 5.8 %shard_map.105.own2_ref = bf16[256,128]{1,0:T(8,128)(2,1)S(1)} custom-call(bf16[6,256,128]{2,1,0:T(8,128)(2,1)S(1)} %get-tuple-element.80.refs_0_, bf16[6,384,128]{2,1,0:T(8,128)(2,1)S(1)} %get-tuple-element.81.refs_1_, bf16[6,128,128]{2,1,0:T(8,128)(2,1)S(1)} %get-tuple-element.82.refs_2_, bf16[11008,128]{1,0:T(8,128)(2,1)} %bitcast.14.refs_3_, ...), custom_call_target="tpu_custom_call" | custom-call | flops 200000000 | bytes 1500000 | tf_op jit(solution)/shard_map/pallas_call | solution.py:66
  155.3 8.4 %shard_map.107 = bf16[256,768]{1,0:T(8,128)(2,1)} custom-call(bf16[256,256]{1,0:T(8,128)(2,1)S(1)} %shard_map.104.own_ref, bf16[256,256]{1,0:T(8,128)(2,1)S(1)} %collective-permute-done.17.other_ref, bf16[256,128]{1,0:T(8,128)(2,1)S(1)} %shard_map.105.own2_ref, bf16[256,128]{1,0:T(8,128)(2,1)S(1)} %collective-permute-done.18.other2_ref, ...), custom_call_target="tpu_custom_call" | custom-call | flops 2700000000 | bytes 12000000 | tf_op jit(solution)/shard_map/pallas_call | solution.py:528
  (72 shorter events, 16.6 us)
Async XLA Ops:
  0.9 18.1 %collective-permute-start = (bf16[128,768]{1,0:T(8,128)(2,1)S(1)}, bf16[128,768]{1,0:T(8,128)(2,1)S(1)}, u32[]{:S(2)}, u32[]{:S(2)}) collective-permute-start(bf16[128,768]{1,0:T(8,128)(2,1)S(1)} %constant_dynamic-slice_fusion.refs_1_), channel_id=1, source_target_pairs={{0,8},{8,16},{16,24},{24,32},{32,40},{40,48},{48,56},{56,0},{1,9},... | collective-permute-start | bytes 589832 | tf_op jit(solution)/shard_map/ppermute | solution.py:552
  3.5 15.5 %collective-permute-start.1 = (bf16[128,768]{1,0:T(8,128)(2,1)S(1)}, bf16[128,768]{1,0:T(8,128)(2,1)S(1)}, u32[]{:S(2)}, u32[]{:S(2)}) collective-permute-start(bf16[128,768]{1,0:T(8,128)(2,1)S(1)} %constant_dynamic-slice_fusion.refs_1_), channel_id=1, source_target_pairs={{0,56},{8,0},{16,8},{24,16},{32,24},{40,32},{48,40},{56,48},{1,57}... | collective-permute-start | bytes 589832 | tf_op jit(solution)/shard_map/ppermute | solution.py:552
  7.5 11.5 %collective-permute-start.2 = (bf16[128,768]{1,0:T(8,128)(2,1)S(1)}, bf16[128,768]{1,0:T(8,128)(2,1)S(1)}, u32[]{:S(2)}, u32[]{:S(2)}) collective-permute-start(bf16[128,768]{1,0:T(8,128)(2,1)S(1)} %constant_dynamic-slice_fusion.refs_1_), channel_id=1, source_target_pairs={{0,1},{1,0},{2,3},{3,2},{4,5},{5,4},{6,7},{7,6},{8,9},{9,8},{10,11... | collective-permute-start | bytes 589832 | tf_op jit(solution)/shard_map/ppermute | solution.py:560
  12.2 14.6 %all-to-all-start.1 = ((bf16[16,64,128]{2,1,0:T(8,128)(2,1)}), bf16[16,64,128]{2,1,0:T(8,128)(2,1)S(1)}, u32[]{:S(2)}, u32[]{:S(2)}) async-start(bf16[16,64,128]{2,1,0:T(8,128)(2,1)} %get-tuple-element.54), calls=%async_computation.1 | async-start | bytes 524288 | tf_op jit(solution)/shard_map/all_to_all | solution.py:556
  19.0 7.8 %collective-permute-start.3 = (bf16[128,768]{1,0:T(8,128)(2,1)S(1)}, bf16[128,768]{1,0:T(8,128)(2,1)S(1)}, u32[]{:S(2)}, u32[]{:S(2)}) collective-permute-start(bf16[128,768]{1,0:T(8,128)(2,1)S(1)} %collective-permute-done.refs_2_), channel_id=1, source_target_pairs={{0,8},{8,16},{16,24},{24,32},{32,40},{40,48},{48,56},{56,0},{1,9},... | collective-permute-start | bytes 589832 | tf_op jit(solution)/shard_map/ppermute | solution.py:552
  19.1 7.7 %collective-permute-start.4 = (bf16[128,768]{1,0:T(8,128)(2,1)S(1)}, bf16[128,768]{1,0:T(8,128)(2,1)S(1)}, u32[]{:S(2)}, u32[]{:S(2)}) collective-permute-start(bf16[128,768]{1,0:T(8,128)(2,1)S(1)} %collective-permute-done.1.refs_8_), channel_id=1, source_target_pairs={{0,56},{8,0},{16,8},{24,16},{32,24},{40,32},{48,40},{56,48},{1,57}... | collective-permute-start | bytes 589832 | tf_op jit(solution)/shard_map/ppermute | solution.py:552
  21.8 5.1 %collective-permute-start.5 = (bf16[128,768]{1,0:T(8,128)(2,1)S(1)}, bf16[128,768]{1,0:T(8,128)(2,1)S(1)}, u32[]{:S(2)}, u32[]{:S(2)}) collective-permute-start(bf16[128,768]{1,0:T(8,128)(2,1)S(1)} %collective-permute-done.refs_2_), channel_id=1, source_target_pairs={{0,1},{1,0},{2,3},{3,2},{4,5},{5,4},{6,7},{7,6},{8,9},{9,8},{10,11... | collective-permute-start | bytes 589832 | tf_op jit(solution)/shard_map/ppermute | solution.py:560
  22.6 4.2 %collective-permute-start.6 = (bf16[128,768]{1,0:T(8,128)(2,1)S(1)}, bf16[128,768]{1,0:T(8,128)(2,1)S(1)}, u32[]{:S(2)}, u32[]{:S(2)}) collective-permute-start(bf16[128,768]{1,0:T(8,128)(2,1)S(1)} %collective-permute-done.1.refs_8_), channel_id=1, source_target_pairs={{0,1},{1,0},{2,3},{3,2},{4,5},{5,4},{6,7},{7,6},{8,9},{9,8},{10,11... | collective-permute-start | bytes 589832 | tf_op jit(solution)/shard_map/ppermute | solution.py:560
  26.9 13.7 %collective-permute-start.7 = (bf16[128,768]{1,0:T(8,128)(2,1)S(1)}, bf16[128,768]{1,0:T(8,128)(2,1)S(1)}, u32[]{:S(2)}, u32[]{:S(2)}) collective-permute-start(bf16[128,768]{1,0:T(8,128)(2,1)S(1)} %collective-permute-done.3.refs_3_), channel_id=1, source_target_pairs={{0,8},{8,16},{16,24},{24,32},{32,40},{40,48},{48,56},{56,0},{1,9},... | collective-permute-start | bytes 589832 | tf_op jit(solution)/shard_map/ppermute | solution.py:552
  27.0 13.6 %collective-permute-start.9 = (bf16[128,768]{1,0:T(8,128)(2,1)S(1)}, bf16[128,768]{1,0:T(8,128)(2,1)S(1)}, u32[]{:S(2)}, u32[]{:S(2)}) collective-permute-start(bf16[128,768]{1,0:T(8,128)(2,1)S(1)} %collective-permute-done.3.refs_3_), channel_id=1, source_target_pairs={{0,1},{1,0},{2,3},{3,2},{4,5},{5,4},{6,7},{7,6},{8,9},{9,8},{10,11... | collective-permute-start | bytes 589832 | tf_op jit(solution)/shard_map/ppermute | solution.py:560
  28.7 11.9 %collective-permute-start.8 = (bf16[128,768]{1,0:T(8,128)(2,1)S(1)}, bf16[128,768]{1,0:T(8,128)(2,1)S(1)}, u32[]{:S(2)}, u32[]{:S(2)}) collective-permute-start(bf16[128,768]{1,0:T(8,128)(2,1)S(1)} %collective-permute-done.4.refs_7_), channel_id=1, source_target_pairs={{0,56},{8,0},{16,8},{24,16},{32,24},{40,32},{48,40},{56,48},{1,57}... | collective-permute-start | bytes 589832 | tf_op jit(solution)/shard_map/ppermute | solution.py:552
  31.6 9.1 %collective-permute-start.10 = (bf16[128,768]{1,0:T(8,128)(2,1)S(1)}, bf16[128,768]{1,0:T(8,128)(2,1)S(1)}, u32[]{:S(2)}, u32[]{:S(2)}) collective-permute-start(bf16[128,768]{1,0:T(8,128)(2,1)S(1)} %collective-permute-done.4.refs_7_), channel_id=1, source_target_pairs={{0,1},{1,0},{2,3},{3,2},{4,5},{5,4},{6,7},{7,6},{8,9},{9,8},{10,11... | collective-permute-start | bytes 589832 | tf_op jit(solution)/shard_map/ppermute | solution.py:560
  35.1 15.9 %all-to-all-start.2 = ((bf16[8,48,128]{2,1,0:T(8,128)(2,1)}), bf16[8,48,128]{2,1,0:T(8,128)(2,1)S(1)}, u32[]{:S(2)}, u32[]{:S(2)}) async-start(bf16[8,48,128]{2,1,0:T(8,128)(2,1)} %broadcast_in_dim.8), calls=%async_computation.2 | async-start | bytes 196608 | tf_op jit(solution)/shard_map/all_to_all | solution.py:556
  40.6 12.8 %collective-permute-start.13 = (bf16[128,768]{1,0:T(8,128)(2,1)S(1)}, bf16[128,768]{1,0:T(8,128)(2,1)S(1)}, u32[]{:S(2)}, u32[]{:S(2)}) collective-permute-start(bf16[128,768]{1,0:T(8,128)(2,1)S(1)} %collective-permute-done.7.refs_4_), channel_id=1, source_target_pairs={{0,8},{8,16},{16,24},{24,32},{32,40},{40,48},{48,56},{56,0},{1,9},... | collective-permute-start | bytes 589832 | tf_op jit(solution)/shard_map/ppermute | solution.py:552
  43.1 4.1 %collective-permute-start.11 = (bf16[64,768]{1,0:T(8,128)(2,1)S(1)}, bf16[64,768]{1,0:T(8,128)(2,1)S(1)}, u32[]{:S(2)}, u32[]{:S(2)}) collective-permute-start(bf16[64,768]{1,0:T(8,128)(2,1)S(1)} %get-tuple-element.91), channel_id=1, source_target_pairs={{0,2},{2,4},{4,6},{6,8},{8,10},{10,12},{12,14},{14,16},{16,18},{18... | collective-permute-start | bytes 294920 | tf_op jit(solution)/shard_map/ppermute | solution.py:573
  45.6 5.5 %collective-permute-start.12 = (bf16[64,768]{1,0:T(8,128)(2,1)S(1)}, bf16[64,768]{1,0:T(8,128)(2,1)S(1)}, u32[]{:S(2)}, u32[]{:S(2)}) collective-permute-start(bf16[64,768]{1,0:T(8,128)(2,1)S(1)} %get-tuple-element.90), channel_id=1, source_target_pairs={{2,0},{4,2},{6,4},{8,6},{10,8},{12,10},{14,12},{16,14},{18,16},{20... | collective-permute-start | bytes 294920 | tf_op jit(solution)/shard_map/ppermute | solution.py:574
  51.1 3.4 %collective-permute-start.14 = (bf16[128,768]{1,0:T(8,128)(2,1)S(1)}, bf16[128,768]{1,0:T(8,128)(2,1)S(1)}, u32[]{:S(2)}, u32[]{:S(2)}) collective-permute-start(bf16[128,768]{1,0:T(8,128)(2,1)S(1)} %collective-permute-done.7.refs_4_), channel_id=1, source_target_pairs={{0,1},{1,0},{2,3},{3,2},{4,5},{5,4},{6,7},{7,6},{8,9},{9,8},{10,11... | collective-permute-start | bytes 589832 | tf_op jit(solution)/shard_map/ppermute | solution.py:560
  66.6 45.5 %all-to-all-start.3 = ((bf16[16,688,128]{2,1,0:T(8,128)(2,1)}), bf16[16,688,128]{2,1,0:T(8,128)(2,1)}, u32[]{:S(2)}, u32[]{:S(2)}) async-start(bf16[16,688,128]{2,1,0:T(8,128)(2,1)} %get-tuple-element.76), calls=%async_computation.3 | async-start | bytes 5636096 | tf_op jit(solution)/shard_map/all_to_all | solution.py:556
  75.1 78.6 %collective-permute-start.20 = (bf16[768,1536]{1,0:T(8,128)(2,1)}, bf16[768,1536]{1,0:T(8,128)(2,1)}, u32[]{:S(2)}, u32[]{:S(2)}) collective-permute-start(bf16[768,1536]{1,0:T(8,128)(2,1)} %up_own.1), channel_id=1, source_target_pairs={{0,1},{1,0},{2,3},{3,2},{4,5},{5,4},{6,7},{7,6},{8,9},{9,8},{10,11... | collective-permute-start | bytes 7077896 | tf_op jit(solution)/shard_map/ppermute | solution.py:560
  75.8 78.0 %collective-permute-start.21 = (bf16[1536,768]{1,0:T(8,128)(2,1)}, bf16[1536,768]{1,0:T(8,128)(2,1)}, u32[]{:S(2)}, u32[]{:S(2)}) collective-permute-start(bf16[1536,768]{1,0:T(8,128)(2,1)} %down_own.1), channel_id=1, source_target_pairs={{0,1},{1,0},{2,3},{3,2},{4,5},{5,4},{6,7},{7,6},{8,9},{9,8},{10,11... | collective-permute-start | bytes 7077896 | tf_op jit(solution)/shard_map/ppermute | solution.py:560
  80.3 73.4 %collective-permute-start.19 = (bf16[384,768]{1,0:T(8,128)(2,1)S(1)}, bf16[384,768]{1,0:T(8,128)(2,1)}, u32[]{:S(2)}, u32[]{:S(2)}) collective-permute-start(bf16[384,768]{1,0:T(8,128)(2,1)S(1)} %copy-done.2), channel_id=1, source_target_pairs={{0,1},{1,0},{2,3},{3,2},{4,5},{5,4},{6,7},{7,6},{8,9},{9,8},{10,11... | collective-permute-start | bytes 1769480 | tf_op jit(solution)/shard_map/ppermute | solution.py:560
  120.5 16.6 %all-to-all-start.4 = ((f32[16,8,640]{2,1,0:T(8,128)}), f32[16,8,640]{2,1,0:T(8,128)S(1)}, u32[]{:S(2)}, u32[]{:S(2)}) async-start(f32[16,8,640]{2,1,0:T(8,128)} %bitcast.18), calls=%async_computation.4 | async-start | bytes 655360 | tf_op jit(solution)/shard_map/all_to_all | solution.py:556
  138.0 17.3 %all-to-all-start.5 = ((bf16[32,8,384]{2,1,0:T(8,128)(2,1)}), bf16[32,8,384]{2,1,0:T(8,128)(2,1)S(1)}, u32[]{:S(2)}, u32[]{:S(2)}) async-start(bf16[32,8,384]{2,1,0:T(8,128)(2,1)} %shard_map.106), calls=%async_computation.5 | async-start | bytes 393216 | tf_op jit(solution)/shard_map/all_to_all | solution.py:556
  147.0 7.7 %collective-permute-start.17 = (bf16[256,256]{1,0:T(8,128)(2,1)S(1)}, bf16[256,256]{1,0:T(8,128)(2,1)S(1)}, u32[]{:S(2)}, u32[]{:S(2)}) collective-permute-start(bf16[256,256]{1,0:T(8,128)(2,1)S(1)} %shard_map.104.own_ref), channel_id=1, source_target_pairs={{0,1},{1,0},{2,3},{3,2},{4,5},{5,4},{6,7},{7,6},{8,9},{9,8},{10,11... | collective-permute-start | bytes 393224 | tf_op jit(solution)/shard_map/ppermute | solution.py:560
  (15 other events, 130.7 us)

commit v10 on v8

--- a/solution.py
+++ b/solution.py
@@ -17,7 +17,7 @@
 F32 = jnp.float32
 LIMIT = 51 * 1024 * 1024
 HIGH = 60 * 1024 * 1024
-SLOTS = 10
+SLOTS = 9
 MORE = 16 - SLOTS
 STRIDE = SLOTS * 64 + 48
 FAR = pl.BlockSpec(memory_space=pltpu.HBM)

time: 165 us -> 160 us (0.970)
  waiting for transfers between devices: 43.2 us -> 40.3 us
    all_to_all x5, waiting for transfers between devices: 33.4 us -> 30.5 us  [exchanged(): return lax.all_to_all(value, axes, split_axis=0, concat_axis=0, tiled=True)]
where the time goes in v10:
time: 160 us; the launch traced here: 159 us
  starting transfers between devices  62.6 us (39%)
  Pallas kernels  47.6 us (30%)
  waiting for transfers between devices  40.3 us (25%)
  local copies, waits for them, and re-layouts  5.94 us (4%)
  between operations  2.44 us (2%)
    pallas_call x7, Pallas kernels, call(): pl.pallas_call(body, out_shape=(*results, *tables), in_specs=[FAR] * (cou...  38.5 us
    all_to_all x5, starting transfers between devices, exchanged(): return lax.all_to_all(value, axes, split_axis=0, concat_axis=0, tiled=True)  34.9 us
    all_to_all x5, waiting for transfers between devices, exchanged(): return lax.all_to_all(value, axes, split_axis=0, concat_axis=0, tiled=True)  30.5 us
    ppermute x7, starting transfers between devices, turned(): lax.ppermute(value, axis, [(i, (i + shift) % count) for i in range(count)])  12.9 us
    ppermute x13, starting transfers between devices, swapped(): return lax.ppermute(value, 'mp', [(0, 1), (1, 0)])  9.83 us
    pallas_call x1, Pallas kernels, finish(): pl.pallas_call(finish_kernel, out_shape=jax.ShapeDtypeStruct((256, 768),...  8.43 us
    ppermute x1, waiting for transfers between devices, shards(): after = lax.ppermute(states[:64], SEQ, [(j, i) for i, j in ends])  4.44 us
    ppermute x1, starting transfers between devices, shards(): before = lax.ppermute(states[192:], SEQ, ends)  3.55 us
  transfers between devices with their start and end apart: 27, of which 7 were waited for; matrix products, arithmetic and copies ran while one was open for 2% of the time, Pallas kernels for 18%

profile of v10, /device:TPU:1, one launch (start us, length us, event | category | flops | bytes accessed | tf_op | source)
XLA Modules:
  0.0 159.5 jit_solution(2594408491039449246)
XLA Ops:
  0.9 2.5 %collective-permute-start = (bf16[128,768]{1,0:T(8,128)(2,1)S(1)}, bf16[128,768]{1,0:T(8,128)(2,1)S(1)}, u32[]{:S(2)}, u32[]{:S(2)}) collective-permute-start(bf16[128,768]{1,0:T(8,128)(2,1)S(1)} %constant_dynamic-slice_fusion.refs_1_), channel_id=1, source_target_pairs={{0,8},{8,16},{16,24},{24,32},{32,40},{40,48},{48,56},{56,0},{1,9},... | collective-permute-start | bytes 589832 | tf_op jit(solution)/shard_map/ppermute | solution.py:552
  3.5 4.0 %collective-permute-start.1 = (bf16[128,768]{1,0:T(8,128)(2,1)S(1)}, bf16[128,768]{1,0:T(8,128)(2,1)S(1)}, u32[]{:S(2)}, u32[]{:S(2)}) collective-permute-start(bf16[128,768]{1,0:T(8,128)(2,1)S(1)} %constant_dynamic-slice_fusion.refs_1_), channel_id=1, source_target_pairs={{0,56},{8,0},{16,8},{24,16},{32,24},{40,32},{48,40},{56,48},{1,57}... | collective-permute-start | bytes 589832 | tf_op jit(solution)/shard_map/ppermute | solution.py:552
  9.1 3.1 %shard_map.100 = (bf16[16,64,128]{2,1,0:T(8,128)(2,1)}, s32[1,72]{1,0:T(1,128)}) custom-call(bf16[256,768]{1,0:T(8,128)(2,1)} %states_ref.1, s32[1,3,4,6]{3,2,1,0:T(4,128)} %bitcast.22, s32[1,3,4,6]{3,2,1,0:T(4,128)} %bitcast.23, s32[1,2]{1,0:T(1,128)} %bitcast.19, s32[1,4]{1,0:T(1,128)} %add_bitcast_fusion.refs_4_.refs_6_.here_ref), custom_call_target="tpu_custom_call" | custom-call | flops 1000000 | bytes 600000 | tf_op jit(solution)/shard_map/pallas_call | solution.py:66
  12.2 6.8 %all-to-all-start.1 = ((bf16[16,64,128]{2,1,0:T(8,128)(2,1)}), bf16[16,64,128]{2,1,0:T(8,128)(2,1)S(1)}, u32[]{:S(2)}, u32[]{:S(2)}) async-start(bf16[16,64,128]{2,1,0:T(8,128)(2,1)} %get-tuple-element.52), calls=%async_computation.1 | async-start | bytes 524288 | tf_op jit(solution)/shard_map/all_to_all | solution.py:556
  19.5 2.9 %collective-permute-start.4 = (bf16[128,768]{1,0:T(8,128)(2,1)S(1)}, bf16[128,768]{1,0:T(8,128)(2,1)S(1)}, u32[]{:S(2)}, u32[]{:S(2)}) collective-permute-start(bf16[128,768]{1,0:T(8,128)(2,1)S(1)} %collective-permute-done.1.refs_8_), channel_id=1, source_target_pairs={{0,56},{8,0},{16,8},{24,16},{32,24},{40,32},{48,40},{56,48},{1,57}... | collective-permute-start | bytes 589832 | tf_op jit(solution)/shard_map/ppermute | solution.py:552
  23.6 3.6 %collective-permute-start.11 = (bf16[64,768]{1,0:T(8,128)(2,1)S(1)}, bf16[64,768]{1,0:T(8,128)(2,1)S(1)}, u32[]{:S(2)}, u32[]{:S(2)}) collective-permute-start(bf16[64,768]{1,0:T(8,128)(2,1)S(1)} %get-tuple-element.87), channel_id=1, source_target_pairs={{0,2},{2,4},{4,6},{6,8},{8,10},{10,12},{12,14},{14,16},{16,18},{18... | collective-permute-start | bytes 294920 | tf_op jit(solution)/shard_map/ppermute | solution.py:573
  27.2 1.3 fusion.1
  30.5 2.9 %collective-permute-start.8 = (bf16[128,768]{1,0:T(8,128)(2,1)S(1)}, bf16[128,768]{1,0:T(8,128)(2,1)S(1)}, u32[]{:S(2)}, u32[]{:S(2)}) collective-permute-start(bf16[128,768]{1,0:T(8,128)(2,1)S(1)} %collective-permute-done.4.refs_7_), channel_id=1, source_target_pairs={{0,56},{8,0},{16,8},{24,16},{32,24},{40,32},{48,40},{56,48},{1,57}... | collective-permute-start | bytes 589832 | tf_op jit(solution)/shard_map/ppermute | solution.py:552
  34.3 5.5 %all-to-all-start.2 = ((bf16[8,48,128]{2,1,0:T(8,128)(2,1)}), bf16[8,48,128]{2,1,0:T(8,128)(2,1)S(1)}, u32[]{:S(2)}, u32[]{:S(2)}) async-start(bf16[8,48,128]{2,1,0:T(8,128)(2,1)} %broadcast_in_dim.8), calls=%async_computation.2 | async-start | bytes 196608 | tf_op jit(solution)/shard_map/all_to_all | solution.py:556
  41.1 4.4 %collective-permute-done.12.refs_2_ = bf16[64,768]{1,0:T(8,128)(2,1)S(1)} collective-permute-done((bf16[64,768]{1,0:T(8,128)(2,1)S(1)}, bf16[64,768]{1,0:T(8,128)(2,1)S(1)}, u32[]{:S(2)}, u32[]{:S(2)}) %collective-permute-start.12) | collective-permute-done | bytes 98336 | tf_op jit(solution)/shard_map/ppermute | solution.py:574
  45.6 1.7 %all-to-all-done.2.refs_18_ = bf16[8,48,128]{2,1,0:T(8,128)(2,1)S(1)} async-done(((bf16[8,48,128]{2,1,0:T(8,128)(2,1)}), bf16[8,48,128]{2,1,0:T(8,128)(2,1)S(1)}, u32[]{:S(2)}, u32[]{:S(2)}) %all-to-all-start.2) | async-done | bytes 98336 | tf_op jit(solution)/shard_map/all_to_all | solution.py:556
  47.8 2.0 %collective-permute-start.14 = (bf16[128,768]{1,0:T(8,128)(2,1)S(1)}, bf16[128,768]{1,0:T(8,128)(2,1)S(1)}, u32[]{:S(2)}, u32[]{:S(2)}) collective-permute-start(bf16[128,768]{1,0:T(8,128)(2,1)S(1)} %collective-permute-done.7.refs_4_), channel_id=1, source_target_pairs={{0,1},{1,0},{2,3},{3,2},{4,5},{5,4},{6,7},{7,6},{8,9},{9,8},{10,11... | collective-permute-start | bytes 589832 | tf_op jit(solution)/shard_map/ppermute | solution.py:560
  49.8 3.3 %collective-permute-done.13.refs_5_ = bf16[128,768]{1,0:T(8,128)(2,1)S(1)} collective-permute-done((bf16[128,768]{1,0:T(8,128)(2,1)S(1)}, bf16[128,768]{1,0:T(8,128)(2,1)S(1)}, u32[]{:S(2)}, u32[]{:S(2)}) %collective-permute-start.13) | collective-permute-done | bytes 196640 | tf_op jit(solution)/shard_map/ppermute | solution.py:552
  53.1 3.1 %collective-permute-start.15 = (bf16[128,768]{1,0:T(8,128)(2,1)S(1)}, bf16[128,768]{1,0:T(8,128)(2,1)S(1)}, u32[]{:S(2)}, u32[]{:S(2)}) collective-permute-start(bf16[128,768]{1,0:T(8,128)(2,1)S(1)} %collective-permute-done.13.refs_5_), channel_id=1, source_target_pairs={{0,1},{1,0},{2,3},{3,2},{4,5},{5,4},{6,7},{7,6},{8,9},{9,8},{10,11... | collective-permute-start | bytes 589832 | tf_op jit(solution)/shard_map/ppermute | solution.py:560
  57.2 9.5 %shard_map.102 = (bf16[96,128,128]{2,1,0:T(8,128)(2,1)}, bf16[16,624,128]{2,1,0:T(8,128)(2,1)}, s32[16,128]{1,0:T(8,128)S(1)}, s32[1,1]{1,0:T(1,128)}) custom-call(bf16[3,768,384]{2,1,0:T(8,128)(2,1)} %refs_0_.3, bf16[128,768]{1,0:T(8,128)(2,1)S(1)} %constant_dynamic-slice_fusion.refs_1_, bf16[128,768]{1,0:T(8,128)(2,1)S(1)} %collective-permute-done.refs_2_, ...), custom_call_target="tpu_custom_call" | custom-call | flops 2400000000 | bytes 10000000 | tf_op jit(solution)/shard_map/pallas_call | solution.py:66
  68.0 6.9 %all-to-all-start.3 = ((bf16[16,624,128]{2,1,0:T(8,128)(2,1)}), bf16[16,624,128]{2,1,0:T(8,128)(2,1)}, u32[]{:S(2)}, u32[]{:S(2)}) async-start(bf16[16,624,128]{2,1,0:T(8,128)(2,1)} %get-tuple-element.72), calls=%async_computation.3 | async-start | bytes 5111808 | tf_op jit(solution)/shard_map/all_to_all | solution.py:556
  75.8 4.4 %shard_map.101 = (bf16[6,256,128]{2,1,0:T(8,128)(2,1)S(1)}, bf16[6,384,128]{2,1,0:T(8,128)(2,1)S(1)}, bf16[768,768]{1,0:T(8,128)(2,1)S(1)}, bf16[768,768]{1,0:T(8,128)(2,1)}) custom-call(bf16[64,768]{1,0:T(8,128)(2,1)S(1)} %collective-permute-done.11.refs_0_, bf16[256,768]{1,0:T(8,128)(2,1)S(1)} %copy-done, ...), custom_call_target="tpu_custom_call" | custom-call | flops 800000000 | bytes 4000000 | tf_op jit(solution)/shard_map/pallas_call | solution.py:66
  80.8 28.3 %all-to-all-done.3.refs_3_ = bf16[16,624,128]{2,1,0:T(8,128)(2,1)} async-done(((bf16[16,624,128]{2,1,0:T(8,128)(2,1)}), bf16[16,624,128]{2,1,0:T(8,128)(2,1)}, u32[]{:S(2)}, u32[]{:S(2)}) %all-to-all-start.3) | async-done | bytes 2555936 | tf_op jit(solution)/shard_map/all_to_all | solution.py:556
  110.3 6.2 %shard_map.103 = (f32[128,640]{1,0:T(8,128)S(1)}, bf16[6,128,128]{2,1,0:T(8,128)(2,1)S(1)}) custom-call(bf16[768,768]{1,0:T(8,128)(2,1)S(1)} %get-tuple-element.58.refs_0_, bf16[768,768]{1,0:T(8,128)(2,1)S(1)} %copy-done.1, bf16[16,6,128,128]{3,2,1,0:T(8,128)(2,1)} %bitcast.21, bf16[16,624,128]{2,1,0:T(8,128)(2,1)} %all-to-all-done.3.refs_3_), custom_call_target="tpu_custom_call" | custom-call | flops 2000000000 | bytes 10000000 | tf_op jit(solution)/shard_map/pallas_call | solution.py:66
  117.3 6.7 %all-to-all-start.4 = ((f32[16,8,640]{2,1,0:T(8,128)}), f32[16,8,640]{2,1,0:T(8,128)S(1)}, u32[]{:S(2)}, u32[]{:S(2)}) async-start(f32[16,8,640]{2,1,0:T(8,128)} %bitcast.18), calls=%async_computation.4 | async-start | bytes 655360 | tf_op jit(solution)/shard_map/all_to_all | solution.py:556
  124.0 8.5 %shard_map.104.own_ref = bf16[256,256]{1,0:T(8,128)(2,1)S(1)} custom-call(bf16[6,256,128]{2,1,0:T(8,128)(2,1)S(1)} %get-tuple-element.76.refs_0_, bf16[6,384,128]{2,1,0:T(8,128)(2,1)S(1)} %get-tuple-element.77.refs_1_, bf16[6,128,128]{2,1,0:T(8,128)(2,1)S(1)} %get-tuple-element.78.refs_2_, bf16[9984,128]{1,0:T(8,128)(2,1)} %bitcast.14.refs_3_, ...), custom_call_target="tpu_custom_call" | custom-call | flops 400000000 | bytes 3000000 | tf_op jit(solution)/shard_map/pallas_call | solution.py:66
  133.4 9.1 %all-to-all-start.5 = ((bf16[32,8,384]{2,1,0:T(8,128)(2,1)}), bf16[32,8,384]{2,1,0:T(8,128)(2,1)S(1)}, u32[]{:S(2)}, u32[]{:S(2)}) async-start(bf16[32,8,384]{2,1,0:T(8,128)(2,1)} %shard_map.106), calls=%async_computation.5 | async-start | bytes 393216 | tf_op jit(solution)/shard_map/all_to_all | solution.py:556
  143.1 5.8 %shard_map.105.own2_ref = bf16[256,128]{1,0:T(8,128)(2,1)S(1)} custom-call(bf16[6,256,128]{2,1,0:T(8,128)(2,1)S(1)} %get-tuple-element.76.refs_0_, bf16[6,384,128]{2,1,0:T(8,128)(2,1)S(1)} %get-tuple-element.77.refs_1_, bf16[6,128,128]{2,1,0:T(8,128)(2,1)S(1)} %get-tuple-element.78.refs_2_, bf16[9984,128]{1,0:T(8,128)(2,1)} %bitcast.14.refs_3_, ...), custom_call_target="tpu_custom_call" | custom-call | flops 200000000 | bytes 1500000 | tf_op jit(solution)/shard_map/pallas_call | solution.py:66
  150.9 8.4 %shard_map.107 = bf16[256,768]{1,0:T(8,128)(2,1)} custom-call(bf16[256,256]{1,0:T(8,128)(2,1)S(1)} %shard_map.104.own_ref, bf16[256,256]{1,0:T(8,128)(2,1)S(1)} %collective-permute-done.17.other_ref, bf16[256,128]{1,0:T(8,128)(2,1)S(1)} %shard_map.105.own2_ref, bf16[256,128]{1,0:T(8,128)(2,1)S(1)} %collective-permute-done.18.other2_ref, ...), custom_call_target="tpu_custom_call" | custom-call | flops 2700000000 | bytes 12000000 | tf_op jit(solution)/shard_map/pallas_call | solution.py:528
  (70 shorter events, 16.7 us)
Async XLA Ops:
  0.9 18.1 %collective-permute-start = (bf16[128,768]{1,0:T(8,128)(2,1)S(1)}, bf16[128,768]{1,0:T(8,128)(2,1)S(1)}, u32[]{:S(2)}, u32[]{:S(2)}) collective-permute-start(bf16[128,768]{1,0:T(8,128)(2,1)S(1)} %constant_dynamic-slice_fusion.refs_1_), channel_id=1, source_target_pairs={{0,8},{8,16},{16,24},{24,32},{32,40},{40,48},{48,56},{56,0},{1,9},... | collective-permute-start | bytes 589832 | tf_op jit(solution)/shard_map/ppermute | solution.py:552
  3.5 15.5 %collective-permute-start.1 = (bf16[128,768]{1,0:T(8,128)(2,1)S(1)}, bf16[128,768]{1,0:T(8,128)(2,1)S(1)}, u32[]{:S(2)}, u32[]{:S(2)}) collective-permute-start(bf16[128,768]{1,0:T(8,128)(2,1)S(1)} %constant_dynamic-slice_fusion.refs_1_), channel_id=1, source_target_pairs={{0,56},{8,0},{16,8},{24,16},{32,24},{40,32},{48,40},{56,48},{1,57}... | collective-permute-start | bytes 589832 | tf_op jit(solution)/shard_map/ppermute | solution.py:552
  7.5 11.5 %collective-permute-start.2 = (bf16[128,768]{1,0:T(8,128)(2,1)S(1)}, bf16[128,768]{1,0:T(8,128)(2,1)S(1)}, u32[]{:S(2)}, u32[]{:S(2)}) collective-permute-start(bf16[128,768]{1,0:T(8,128)(2,1)S(1)} %constant_dynamic-slice_fusion.refs_1_), channel_id=1, source_target_pairs={{0,1},{1,0},{2,3},{3,2},{4,5},{5,4},{6,7},{7,6},{8,9},{9,8},{10,11... | collective-permute-start | bytes 589832 | tf_op jit(solution)/shard_map/ppermute | solution.py:560
  12.2 17.5 %all-to-all-start.1 = ((bf16[16,64,128]{2,1,0:T(8,128)(2,1)}), bf16[16,64,128]{2,1,0:T(8,128)(2,1)S(1)}, u32[]{:S(2)}, u32[]{:S(2)}) async-start(bf16[16,64,128]{2,1,0:T(8,128)(2,1)} %get-tuple-element.52), calls=%async_computation.1 | async-start | bytes 524288 | tf_op jit(solution)/shard_map/all_to_all | solution.py:556
  19.1 10.8 %collective-permute-start.3 = (bf16[128,768]{1,0:T(8,128)(2,1)S(1)}, bf16[128,768]{1,0:T(8,128)(2,1)S(1)}, u32[]{:S(2)}, u32[]{:S(2)}) collective-permute-start(bf16[128,768]{1,0:T(8,128)(2,1)S(1)} %collective-permute-done.refs_2_), channel_id=1, source_target_pairs={{0,8},{8,16},{16,24},{24,32},{32,40},{40,48},{48,56},{56,0},{1,9},... | collective-permute-start | bytes 589832 | tf_op jit(solution)/shard_map/ppermute | solution.py:552
  19.1 10.7 %collective-permute-start.5 = (bf16[128,768]{1,0:T(8,128)(2,1)S(1)}, bf16[128,768]{1,0:T(8,128)(2,1)S(1)}, u32[]{:S(2)}, u32[]{:S(2)}) collective-permute-start(bf16[128,768]{1,0:T(8,128)(2,1)S(1)} %collective-permute-done.refs_2_), channel_id=1, source_target_pairs={{0,1},{1,0},{2,3},{3,2},{4,5},{5,4},{6,7},{7,6},{8,9},{9,8},{10,11... | collective-permute-start | bytes 589832 | tf_op jit(solution)/shard_map/ppermute | solution.py:560
  19.5 10.3 %collective-permute-start.4 = (bf16[128,768]{1,0:T(8,128)(2,1)S(1)}, bf16[128,768]{1,0:T(8,128)(2,1)S(1)}, u32[]{:S(2)}, u32[]{:S(2)}) collective-permute-start(bf16[128,768]{1,0:T(8,128)(2,1)S(1)} %collective-permute-done.1.refs_8_), channel_id=1, source_target_pairs={{0,56},{8,0},{16,8},{24,16},{32,24},{40,32},{48,40},{56,48},{1,57}... | collective-permute-start | bytes 589832 | tf_op jit(solution)/shard_map/ppermute | solution.py:552
  22.4 7.5 %collective-permute-start.6 = (bf16[128,768]{1,0:T(8,128)(2,1)S(1)}, bf16[128,768]{1,0:T(8,128)(2,1)S(1)}, u32[]{:S(2)}, u32[]{:S(2)}) collective-permute-start(bf16[128,768]{1,0:T(8,128)(2,1)S(1)} %collective-permute-done.1.refs_8_), channel_id=1, source_target_pairs={{0,1},{1,0},{2,3},{3,2},{4,5},{5,4},{6,7},{7,6},{8,9},{9,8},{10,11... | collective-permute-start | bytes 589832 | tf_op jit(solution)/shard_map/ppermute | solution.py:560
  23.6 16.2 %collective-permute-start.11 = (bf16[64,768]{1,0:T(8,128)(2,1)S(1)}, bf16[64,768]{1,0:T(8,128)(2,1)S(1)}, u32[]{:S(2)}, u32[]{:S(2)}) collective-permute-start(bf16[64,768]{1,0:T(8,128)(2,1)S(1)} %get-tuple-element.87), channel_id=1, source_target_pairs={{0,2},{2,4},{4,6},{6,8},{8,10},{10,12},{12,14},{14,16},{16,18},{18... | collective-permute-start | bytes 294920 | tf_op jit(solution)/shard_map/ppermute | solution.py:573
  29.9 17.4 %collective-permute-start.7 = (bf16[128,768]{1,0:T(8,128)(2,1)S(1)}, bf16[128,768]{1,0:T(8,128)(2,1)S(1)}, u32[]{:S(2)}, u32[]{:S(2)}) collective-permute-start(bf16[128,768]{1,0:T(8,128)(2,1)S(1)} %collective-permute-done.3.refs_3_), channel_id=1, source_target_pairs={{0,8},{8,16},{16,24},{24,32},{32,40},{40,48},{48,56},{56,0},{1,9},... | collective-permute-start | bytes 589832 | tf_op jit(solution)/shard_map/ppermute | solution.py:552
  29.9 17.3 %collective-permute-start.9 = (bf16[128,768]{1,0:T(8,128)(2,1)S(1)}, bf16[128,768]{1,0:T(8,128)(2,1)S(1)}, u32[]{:S(2)}, u32[]{:S(2)}) collective-permute-start(bf16[128,768]{1,0:T(8,128)(2,1)S(1)} %collective-permute-done.3.refs_3_), channel_id=1, source_target_pairs={{0,1},{1,0},{2,3},{3,2},{4,5},{5,4},{6,7},{7,6},{8,9},{9,8},{10,11... | collective-permute-start | bytes 589832 | tf_op jit(solution)/shard_map/ppermute | solution.py:560
  30.5 16.7 %collective-permute-start.8 = (bf16[128,768]{1,0:T(8,128)(2,1)S(1)}, bf16[128,768]{1,0:T(8,128)(2,1)S(1)}, u32[]{:S(2)}, u32[]{:S(2)}) collective-permute-start(bf16[128,768]{1,0:T(8,128)(2,1)S(1)} %collective-permute-done.4.refs_7_), channel_id=1, source_target_pairs={{0,56},{8,0},{16,8},{24,16},{32,24},{40,32},{48,40},{56,48},{1,57}... | collective-permute-start | bytes 589832 | tf_op jit(solution)/shard_map/ppermute | solution.py:552
  33.4 13.9 %collective-permute-start.10 = (bf16[128,768]{1,0:T(8,128)(2,1)S(1)}, bf16[128,768]{1,0:T(8,128)(2,1)S(1)}, u32[]{:S(2)}, u32[]{:S(2)}) collective-permute-start(bf16[128,768]{1,0:T(8,128)(2,1)S(1)} %collective-permute-done.4.refs_7_), channel_id=1, source_target_pairs={{0,1},{1,0},{2,3},{3,2},{4,5},{5,4},{6,7},{7,6},{8,9},{9,8},{10,11... | collective-permute-start | bytes 589832 | tf_op jit(solution)/shard_map/ppermute | solution.py:560
  34.3 12.9 %all-to-all-start.2 = ((bf16[8,48,128]{2,1,0:T(8,128)(2,1)}), bf16[8,48,128]{2,1,0:T(8,128)(2,1)S(1)}, u32[]{:S(2)}, u32[]{:S(2)}) async-start(bf16[8,48,128]{2,1,0:T(8,128)(2,1)} %broadcast_in_dim.8), calls=%async_computation.2 | async-start | bytes 196608 | tf_op jit(solution)/shard_map/all_to_all | solution.py:556
  47.3 5.8 %collective-permute-start.13 = (bf16[128,768]{1,0:T(8,128)(2,1)S(1)}, bf16[128,768]{1,0:T(8,128)(2,1)S(1)}, u32[]{:S(2)}, u32[]{:S(2)}) collective-permute-start(bf16[128,768]{1,0:T(8,128)(2,1)S(1)} %collective-permute-done.7.refs_4_), channel_id=1, source_target_pairs={{0,8},{8,16},{16,24},{24,32},{32,40},{40,48},{48,56},{56,0},{1,9},... | collective-permute-start | bytes 589832 | tf_op jit(solution)/shard_map/ppermute | solution.py:552
  47.8 8.4 %collective-permute-start.14 = (bf16[128,768]{1,0:T(8,128)(2,1)S(1)}, bf16[128,768]{1,0:T(8,128)(2,1)S(1)}, u32[]{:S(2)}, u32[]{:S(2)}) collective-permute-start(bf16[128,768]{1,0:T(8,128)(2,1)S(1)} %collective-permute-done.7.refs_4_), channel_id=1, source_target_pairs={{0,1},{1,0},{2,3},{3,2},{4,5},{5,4},{6,7},{7,6},{8,9},{9,8},{10,11... | collective-permute-start | bytes 589832 | tf_op jit(solution)/shard_map/ppermute | solution.py:560
  49.8 6.4 %collective-permute-start.16 = (bf16[128,768]{1,0:T(8,128)(2,1)S(1)}, bf16[128,768]{1,0:T(8,128)(2,1)S(1)}, u32[]{:S(2)}, u32[]{:S(2)}) collective-permute-start(bf16[128,768]{1,0:T(8,128)(2,1)S(1)} %collective-permute-done.8.refs_6_), channel_id=1, source_target_pairs={{0,1},{1,0},{2,3},{3,2},{4,5},{5,4},{6,7},{7,6},{8,9},{9,8},{10,11... | collective-permute-start | bytes 589832 | tf_op jit(solution)/shard_map/ppermute | solution.py:560
  68.0 41.0 %all-to-all-start.3 = ((bf16[16,624,128]{2,1,0:T(8,128)(2,1)}), bf16[16,624,128]{2,1,0:T(8,128)(2,1)}, u32[]{:S(2)}, u32[]{:S(2)}) async-start(bf16[16,624,128]{2,1,0:T(8,128)(2,1)} %get-tuple-element.72), calls=%async_computation.3 | async-start | bytes 5111808 | tf_op jit(solution)/shard_map/all_to_all | solution.py:556
  75.0 74.3 %collective-permute-start.20 = (bf16[768,1536]{1,0:T(8,128)(2,1)}, bf16[768,1536]{1,0:T(8,128)(2,1)}, u32[]{:S(2)}, u32[]{:S(2)}) collective-permute-start(bf16[768,1536]{1,0:T(8,128)(2,1)} %up_own.1), channel_id=1, source_target_pairs={{0,1},{1,0},{2,3},{3,2},{4,5},{5,4},{6,7},{7,6},{8,9},{9,8},{10,11... | collective-permute-start | bytes 7077896 | tf_op jit(solution)/shard_map/ppermute | solution.py:560
  75.7 73.6 %collective-permute-start.21 = (bf16[1536,768]{1,0:T(8,128)(2,1)}, bf16[1536,768]{1,0:T(8,128)(2,1)}, u32[]{:S(2)}, u32[]{:S(2)}) collective-permute-start(bf16[1536,768]{1,0:T(8,128)(2,1)} %down_own.1), channel_id=1, source_target_pairs={{0,1},{1,0},{2,3},{3,2},{4,5},{5,4},{6,7},{7,6},{8,9},{9,8},{10,11... | collective-permute-start | bytes 7077896 | tf_op jit(solution)/shard_map/ppermute | solution.py:560
  80.3 69.0 %collective-permute-start.19 = (bf16[384,768]{1,0:T(8,128)(2,1)S(1)}, bf16[384,768]{1,0:T(8,128)(2,1)}, u32[]{:S(2)}, u32[]{:S(2)}) collective-permute-start(bf16[384,768]{1,0:T(8,128)(2,1)S(1)} %copy-done.2), channel_id=1, source_target_pairs={{0,1},{1,0},{2,3},{3,2},{4,5},{5,4},{6,7},{7,6},{8,9},{9,8},{10,11... | collective-permute-start | bytes 1769480 | tf_op jit(solution)/shard_map/ppermute | solution.py:560
  117.3 15.2 %all-to-all-start.4 = ((f32[16,8,640]{2,1,0:T(8,128)}), f32[16,8,640]{2,1,0:T(8,128)S(1)}, u32[]{:S(2)}, u32[]{:S(2)}) async-start(f32[16,8,640]{2,1,0:T(8,128)} %bitcast.18), calls=%async_computation.4 | async-start | bytes 655360 | tf_op jit(solution)/shard_map/all_to_all | solution.py:556
  133.4 17.4 %all-to-all-start.5 = ((bf16[32,8,384]{2,1,0:T(8,128)(2,1)}), bf16[32,8,384]{2,1,0:T(8,128)(2,1)S(1)}, u32[]{:S(2)}, u32[]{:S(2)}) async-start(bf16[32,8,384]{2,1,0:T(8,128)(2,1)} %shard_map.106), calls=%async_computation.5 | async-start | bytes 393216 | tf_op jit(solution)/shard_map/all_to_all | solution.py:556
  142.6 7.7 %collective-permute-start.17 = (bf16[256,256]{1,0:T(8,128)(2,1)S(1)}, bf16[256,256]{1,0:T(8,128)(2,1)S(1)}, u32[]{:S(2)}, u32[]{:S(2)}) collective-permute-start(bf16[256,256]{1,0:T(8,128)(2,1)S(1)} %shard_map.104.own_ref), channel_id=1, source_target_pairs={{0,1},{1,0},{2,3},{3,2},{4,5},{5,4},{6,7},{7,6},{8,9},{9,8},{10,11... | collective-permute-start | bytes 393224 | tf_op jit(solution)/shard_map/ppermute | solution.py:560
  (14 other events, 130.3 us)
